TPU v7x, 32 devices: a whole 2x2x4 slice. The times are simulated.
32 devices in a mesh: expert: 8 (over y, x, core), shard: 4 (over z).
Axes of the slice: x: 2, y: 2, z: 4, core: 2. Of those that a mesh axis runs over, the one named last changes fastest.
Arguments:
- inputs: bfloat16 [32768, 768], P(('expert', 'shard')), may hold values from -4.5 to 4.5
- norm_gain: bfloat16 [768], P('shard'), may hold values from 0.25 to 1.75
- query_weight: bfloat16 [768, 768], P('shard'), may hold values from -0.21875 to 0.21875
- key_weight: bfloat16 [768, 768], P('shard'), may hold values from -0.21875 to 0.21875
- value_weight: bfloat16 [768, 768], P('shard'), may hold values from -0.21875 to 0.21875
- merge_weight: bfloat16 [768, 768], P('shard'), may hold values from -6 to 6
- bias_table: bfloat16 [32, 12], P(None, 'shard'), may hold values from -4 to 4
- expert_gain: bfloat16 [768], P('shard'), may hold values from 0.25 to 1.75
- router_weight: bfloat16 [768, 16], P('shard'), may hold values from -0.21875 to 0.21875
- up_weight: bfloat16 [16, 768, 3072], P('expert'), may hold values from -0.21875 to 0.21875
- down_weight: bfloat16 [16, 3072, 768], P('expert'), may hold values from -0.109375 to 0.109375
- routes: int32 [32768, 2], P(('expert', 'shard')), may hold values from 0 to 15, all different within a row; in each aligned block of 1024 rows (0 to 1023, 1024 to 2047, ...) at most 160 rows name the same one
- cotangent: bfloat16 [32768, 768], P(('expert', 'shard')), may hold values from -6 to 6
Outputs:
- output: bfloat16 [32768, 768], P(('expert', 'shard'))
- input_gradient: float32 [32768, 768], P(('expert', 'shard'))
- norm_gradient: float32 [768], P('shard')
- query_gradient: float32 [768, 768], P('shard')
- key_gradient: float32 [768, 768], P('shard')
- value_gradient: float32 [768, 768], P('shard')
- merge_gradient: float32 [768, 768], P('shard')
- table_gradient: float32 [32, 12], P(None, 'shard')
- gain_gradient: float32 [768], P('shard')
- router_gradient: float32 [768, 16], P('shard')
- up_gradient: float32 [16, 768, 3072], P('expert', None, 'shard')
- down_gradient: float32 [16, 3072, 768], P('expert', 'shard')
Inputs may be any that keep to these rules, and one draw needn't show every extreme that they name: In each aligned block of 1024 tokens (the tokens of one device) every expert is named by at most 160 routes, and by exactly 160 in some block; the 2 routes of a token name different experts; every expert is named by some token.
All inputs are finite; a program needn't handle non-finite values.
Results may differ from a plain program's by a relative error of at most 0.02.
Values may be sent and summed in bfloat16 or wider, within the bound.
No kernel may reach another device: no remote copies, remote signals or barrier semaphores. Data moves between devices by JAX's collectives and lax.ppermute only.
A program may use at most 448 MiB of HBM per device.

v0:
```python
from functools import partial, reduce

import jax
import jax.numpy as jnp
import numpy as np
from jax import lax
from jax.experimental import pallas as pl
from jax.experimental.pallas import tpu as pltpu
from jax.sharding import PartitionSpec as P

BUCKETS = 32
MAX_DIST = 128


epsilon = 1e-06
masked_score = -1e30


def bucket_hot(length):
    distance = np.arange(length)
    half_count = BUCKETS // 2
    clipped = np.maximum(distance, half_count)
    spread = np.log(clipped / half_count) / np.log(MAX_DIST / half_count) * (BUCKETS - half_count)
    far_bucket = np.minimum(half_count + np.floor(spread).astype(np.int32), BUCKETS - 1)
    bucket = np.where(distance < half_count, distance, far_bucket)
    return (bucket[:, None] == np.arange(BUCKETS)[None, :]).astype(np.float32)


def rms_parts(values, gain_values):
    inverse = lax.rsqrt(jnp.mean(values * values, axis=-1, keepdims=True) + epsilon)
    unit_rows = values * inverse
    return (unit_rows * gain_values, unit_rows, inverse)


def rms_back(grad_rows, unit_rows, inverse, gain_values):
    scaled = grad_rows * gain_values
    gain_grad = jnp.sum(grad_rows * unit_rows, axis=0)
    inner = jnp.mean(scaled * unit_rows, axis=-1, keepdims=True)
    return (inverse * (scaled - unit_rows * inner), gain_grad)


def dot_nt(a, b):
    return lax.dot_general(a, b, (((1,), (1,)), ((), ())), preferred_element_type=jnp.float32)

def dot_nn(a, b):
    return lax.dot_general(a, b, (((1,), (0,)), ((), ())), preferred_element_type=jnp.float32)

def near_tiles(near_ref, head, block):
    spread = jnp.broadcast_to(near_ref[0, head:head + 1, :], (block, block))
    spread = pltpu.roll(spread, 0, 1, stride=1, stride_axis=0)
    key_at = lax.broadcasted_iota(jnp.int32, (block, block), 0)
    query_at = lax.broadcasted_iota(jnp.int32, (block, block), 1)
    return (jnp.where(query_at >= key_at, spread, masked_score), jnp.where(query_at < key_at, spread, 0.0), query_at < key_at)

def diagonal_sums(tile):
    block = tile.shape[1]
    total = tile[:8]
    for start in range(8, block, 8):
        total = total + pltpu.roll(tile[start:start + 8], block - start, 1)
    row = lax.broadcasted_iota(jnp.int32, total.shape, 0)
    for step in (1, 2, 4):
        total = jnp.where((row & step) != 0, pltpu.roll(total, block - step, 1), total)
    return jnp.sum(total, axis=0, keepdims=True)

def head_part(rows, head, size):
    lane = lax.broadcasted_iota(jnp.int32, rows.shape, 1)
    return jnp.where((lane >= head * size) & (lane < (head + 1) * size), rows, jnp.zeros_like(rows))

def attend_kernel(query_ref, key_ref, value_ref, near_ref, out_ref, total_ref, *, block, size, scale):
    length, lanes = query_ref.shape
    heads = lanes // size
    count = length // block
    flipped = value_ref[...].T
    tiles = [near_tiles(near_ref, head, block) for head in range(heads)]
    for i in range(count):
        rows = pl.ds(i * block, block)
        query_rows = query_ref[rows, :] * jnp.bfloat16(scale)
        parts = []
        for head in range(heads):
            query_part = head_part(query_rows, head, size)
            scores = []
            for j in range(i + 1):
                tile = dot_nt(key_ref[pl.ds(j * block, block), :], query_part)
                if j == i:
                    tile = tile + tiles[head][0]
                elif j == i - 1:
                    tile = tile + tiles[head][1]
                scores.append(tile)
            top = reduce(jnp.maximum, scores)
            top = jnp.max(top, axis=0, keepdims=True)
            mixed = None
            total = None
            for j in range(i + 1):
                weights = jnp.exp(scores[j] - top)
                sums = jnp.sum(weights, axis=0, keepdims=True)
                part = dot_nn(flipped[head * size:(head + 1) * size, j * block:(j + 1) * block], weights.astype(jnp.bfloat16))
                mixed = part if mixed is None else mixed + part
                total = sums if total is None else total + sums
            parts.append(mixed / total)
            total_ref[0, head:head + 1, rows] = top + jnp.log(total)
        out_ref[rows, :] = jnp.concatenate(parts, axis=0).T.astype(out_ref.dtype)

def attend(queries, keys, values, near, size, block):
    length, width = queries.shape
    lanes = 128
    heads = lanes // size
    groups = width // lanes
    column = pl.BlockSpec((length, lanes), lambda g: (0, g))
    head_rows = pl.BlockSpec((1, heads, block), lambda g: (g, 0, 0))
    return pl.pallas_call(
        partial(attend_kernel, block=block, size=size, scale=size ** -0.5),
        grid=(groups,),
        in_specs=[column, column, column, head_rows],
        out_specs=[column, pl.BlockSpec((1, heads, length), lambda g: (g, 0, 0))],
        out_shape=[jax.ShapeDtypeStruct((length, width), jnp.bfloat16), jax.ShapeDtypeStruct((groups, heads, length), jnp.float32)],
        compiler_params=pltpu.CompilerParams(vmem_limit_bytes=48 << 20),
        name="attend",
    )(queries, keys, values, near)

def attend_back_kernel(query_ref, key_ref, value_ref, grad_ref, out_ref, total_ref, near_ref, dq_ref, dk_ref, dv_ref, dist_ref, key_acc, value_acc, *, block, size, scale):
    length, lanes = query_ref.shape
    heads = lanes // size
    count = length // block
    flipped = key_ref[...].T
    tiles = [near_tiles(near_ref, head, block) for head in range(heads)]
    near_acc = [None] * heads
    far_acc = [None] * heads
    for i in range(count):
        rows = pl.ds(i * block, block)
        query_rows = query_ref[rows, :] * jnp.bfloat16(scale)
        grad_rows = grad_ref[rows, :]
        products = (grad_rows.astype(jnp.float32) * out_ref[rows, :].astype(jnp.float32)).T
        query_parts = [head_part(query_rows, head, size) for head in range(heads)]
        grad_parts = [head_part(grad_rows, head, size) for head in range(heads)]
        inner = [jnp.sum(products[head * size:(head + 1) * size], axis=0, keepdims=True) for head in range(heads)]
        query_stack = jnp.concatenate(query_parts, axis=0)
        grad_stack = jnp.concatenate(grad_parts, axis=0)
        query_grads = [None] * heads
        for j in range(i + 1):
            cols = pl.ds(j * block, block)
            weight_list = []
            score_list = []
            for head in range(heads):
                tile = dot_nt(key_ref[cols, :], query_parts[head])
                if j == i:
                    tile = tile + tiles[head][0]
                elif j == i - 1:
                    tile = tile + tiles[head][1]
                weights = jnp.exp(tile - total_ref[0, head:head + 1, rows])
                grads = dot_nt(value_ref[cols, :], grad_parts[head])
                score_grads = weights * (grads - inner[head])
                low = score_grads.astype(jnp.bfloat16)
                weight_list.append(weights.astype(jnp.bfloat16))
                score_list.append(low)
                part = dot_nn(flipped[head * size:(head + 1) * size, j * block:(j + 1) * block], low)
                query_grads[head] = part if query_grads[head] is None else query_grads[head] + part
                if j == i:
                    near_acc[head] = score_grads if near_acc[head] is None else near_acc[head] + score_grads
                else:
                    far = score_grads
                    if j == i - 1:
                        close = jnp.where(tiles[head][2], score_grads, 0.0)
                        near_acc[head] = near_acc[head] + close
                        far = score_grads - close
                    far = jnp.sum(far, axis=0, keepdims=True)
                    far_acc[head] = far if far_acc[head] is None else far_acc[head] + far
            value_part = dot_nn(jnp.concatenate(weight_list, axis=1), grad_stack)
            key_part = dot_nn(jnp.concatenate(score_list, axis=1), query_stack)
            if j == i:
                value_acc[cols, :] = value_part
                key_acc[cols, :] = key_part
            else:
                value_acc[cols, :] += value_part
                key_acc[cols, :] += key_part
        dq_ref[rows, :] = (jnp.concatenate(query_grads, axis=0) * scale).T.astype(dq_ref.dtype)
    dk_ref[...] = key_acc[...].astype(dk_ref.dtype)
    dv_ref[...] = value_acc[...].astype(dv_ref.dtype)
    for head in range(heads):
        dist_ref[0, head:head + 1, :] = diagonal_sums(near_acc[head])
        dist_ref[0, heads + head:heads + head + 1, :] = far_acc[head]

def attend_back(queries, keys, values, grads, outs, totals, near, size, block):
    length, width = queries.shape
    lanes = 128
    heads = lanes // size
    groups = width // lanes
    column = pl.BlockSpec((length, lanes), lambda g: (0, g))
    head_rows = pl.BlockSpec((1, heads, block), lambda g: (g, 0, 0))
    return pl.pallas_call(
        partial(attend_back_kernel, block=block, size=size, scale=size ** -0.5),
        grid=(groups,),
        in_specs=[column] * 5 + [pl.BlockSpec((1, heads, length), lambda g: (g, 0, 0)), head_rows],
        out_specs=[column, column, column, pl.BlockSpec((1, 2 * heads, block), lambda g: (g, 0, 0))],
        out_shape=[jax.ShapeDtypeStruct((length, width), jnp.bfloat16)] * 3 + [jax.ShapeDtypeStruct((groups, 2 * heads, block), jnp.float32)],
        scratch_shapes=[pltpu.VMEM((length, lanes), jnp.float32)] * 2,
        compiler_params=pltpu.CompilerParams(vmem_limit_bytes=56 << 20),
        name="attend_back",
    )(queries, keys, values, grads, outs, totals, near)


def local(
    inputs,
    norm_gain,
    query_weight,
    key_weight,
    value_weight,
    merge_weight,
    bias_table,
    expert_gain,
    router_weight,
    up_weight,
    down_weight,
    routes,
    cotangent,
):
    gathered = (
        lax.all_gather(norm_gain, "shard", axis=0, tiled=True),
        lax.all_gather(query_weight, "shard", axis=0, tiled=True),
        lax.all_gather(key_weight, "shard", axis=0, tiled=True),
        lax.all_gather(value_weight, "shard", axis=0, tiled=True),
        lax.all_gather(merge_weight, "shard", axis=0, tiled=True),
        lax.all_gather(bias_table, "shard", axis=1, tiled=True),
        lax.all_gather(expert_gain, "shard", axis=0, tiled=True),
        lax.all_gather(router_weight, "shard", axis=0, tiled=True),
    )
    gain_one = gathered[0].astype(jnp.float32)
    query_full = gathered[1]
    key_full = gathered[2]
    value_full = gathered[3]
    merge_full = gathered[4]
    table_full = gathered[5].astype(jnp.float32)
    gain_two = gathered[6].astype(jnp.float32)
    router_full = gathered[7]
    token_count, width = inputs.shape
    head_count = table_full.shape[1]
    head_size = width // head_count
    route_count = routes.shape[1]
    local_count = up_weight.shape[0]
    owner_count = lax.axis_size("expert")
    expert_count = router_full.shape[1]
    capacity = (5 * token_count * route_count + 4 * expert_count - 1) // (4 * expert_count)
    slot_total = local_count * owner_count * capacity
    pair_count = token_count * route_count
    features = inputs.astype(jnp.float32)
    normed, unit_one, inverse_one = rms_parts(features, gain_one)
    normed_low = normed.astype(jnp.bfloat16)
    queries = jnp.dot(normed_low, query_full, preferred_element_type=jnp.float32).astype(jnp.bfloat16)
    keys = jnp.dot(normed_low, key_full, preferred_element_type=jnp.float32).astype(jnp.bfloat16)
    values = jnp.dot(normed_low, value_full, preferred_element_type=jnp.float32).astype(jnp.bfloat16)
    block = 256
    hot = bucket_hot(token_count)
    assert hot[block:, -1].all()
    near_hot = jnp.asarray(hot[:block] - hot[-1:], dtype=jnp.float32)
    group_heads = 128 // head_size
    near = jnp.dot(near_hot, table_full, precision=lax.Precision.HIGHEST).T.reshape(
        head_count // group_heads, group_heads, block
    )
    attended, log_totals = attend(queries, keys, values, near, head_size, block)
    branch = jnp.dot(attended, merge_full, preferred_element_type=jnp.float32)
    resid = features + branch
    routed, unit_two, inverse_two = rms_parts(resid, gain_two)
    routed_low = routed.astype(jnp.bfloat16)
    logits = jnp.dot(routed_low, router_full, preferred_element_type=jnp.float32)
    expert_ids = jnp.arange(expert_count, dtype=jnp.int32)
    route_hot = routes[:, :, None] == expert_ids[None, None, :]
    chosen = jnp.sum(jnp.where(route_hot, logits[:, None, :], 0.0), axis=-1)
    chosen_exp = jnp.exp(chosen - jnp.max(chosen, axis=1, keepdims=True))
    gate_values = chosen_exp / jnp.sum(chosen_exp, axis=1, keepdims=True)
    flat_routes = routes.reshape(-1)
    flat_hot = (flat_routes[:, None] == expert_ids[None, :]).astype(jnp.bfloat16)
    pair_ids = jnp.arange(pair_count, dtype=jnp.int32)
    lower_table = (pair_ids[None, :] < pair_ids[:, None]).astype(jnp.bfloat16)
    earlier = jnp.dot(lower_table, flat_hot, preferred_element_type=jnp.float32)
    position = jnp.sum(earlier * flat_hot.astype(jnp.float32), axis=1).astype(jnp.int32)
    slot_index = (
        flat_routes % local_count * owner_count + flat_routes // local_count
    ) * capacity + position
    slot_ids = jnp.arange(slot_total, dtype=jnp.int32)
    pair_hot = (slot_ids[:, None] == slot_index[None, :]).astype(jnp.bfloat16)
    token_hot = jnp.sum(
        pair_hot.reshape(slot_total, token_count, route_count), axis=2, dtype=jnp.bfloat16
    )
    send_rows = jnp.dot(token_hot, routed_low, preferred_element_type=jnp.float32).astype(
        jnp.bfloat16
    )
    arrived = lax.all_to_all(
        send_rows.reshape(local_count, owner_count, capacity, width),
        "expert",
        split_axis=1,
        concat_axis=1,
        tiled=True,
    )
    expert_rows = arrived.reshape(local_count, owner_count * capacity, width)
    pre_hidden = jnp.einsum(
        "erd,edf->erf", expert_rows, up_weight, preferred_element_type=jnp.float32
    )
    hidden = jax.nn.gelu(pre_hidden, approximate=True).astype(jnp.bfloat16)
    produced = jnp.einsum(
        "erf,efd->erd", hidden, down_weight, preferred_element_type=jnp.float32
    ).astype(jnp.bfloat16)
    returned = lax.all_to_all(
        produced.reshape(local_count, owner_count, capacity, width),
        "expert",
        split_axis=1,
        concat_axis=1,
        tiled=True,
    )
    picked = jnp.einsum(
        "sp,sd->pd",
        pair_hot,
        returned.reshape(slot_total, width),
        preferred_element_type=jnp.float32,
    ).reshape(token_count, route_count, width)
    result = resid + jnp.sum(gate_values[:, :, None] * picked, axis=1)
    output = result.astype(jnp.bfloat16)
    grad_result = cotangent.astype(jnp.float32)
    grad_gates = jnp.sum(grad_result[:, None, :] * picked, axis=-1)
    grad_chosen = gate_values * (
        grad_gates - jnp.sum(gate_values * grad_gates, axis=1, keepdims=True)
    )
    grad_logits = jnp.sum(jnp.where(route_hot, grad_chosen[:, :, None], 0.0), axis=1).astype(
        jnp.bfloat16
    )
    grad_picked = (
        (gate_values[:, :, None] * grad_result[:, None, :])
        .astype(jnp.bfloat16)
        .reshape(pair_count, width)
    )
    grad_send = jnp.dot(pair_hot, grad_picked, preferred_element_type=jnp.float32).astype(
        jnp.bfloat16
    )
    grad_arrived = lax.all_to_all(
        grad_send.reshape(local_count, owner_count, capacity, width),
        "expert",
        split_axis=1,
        concat_axis=1,
        tiled=True,
    )
    grad_produced = grad_arrived.reshape(local_count, owner_count * capacity, width)
    grad_hidden = jnp.einsum(
        "erd,efd->erf", grad_produced, down_weight, preferred_element_type=jnp.float32
    )
    activation, gelu_back = jax.vjp(partial(jax.nn.gelu, approximate=True), pre_hidden)
    hidden_again = activation.astype(jnp.bfloat16)
    grad_pre = gelu_back(grad_hidden)[0].astype(jnp.bfloat16)
    up_grad = jnp.einsum("erd,erf->edf", expert_rows, grad_pre, preferred_element_type=jnp.float32)
    down_grad = jnp.einsum(
        "erf,erd->efd", hidden_again, grad_produced, preferred_element_type=jnp.float32
    )
    grad_rows = jnp.einsum(
        "erf,edf->erd", grad_pre, up_weight, preferred_element_type=jnp.float32
    ).astype(jnp.bfloat16)
    returned_grads = lax.all_to_all(
        grad_rows.reshape(local_count, owner_count, capacity, width),
        "expert",
        split_axis=1,
        concat_axis=1,
        tiled=True,
    )
    grad_routed = jnp.einsum(
        "st,sd->td",
        token_hot,
        returned_grads.reshape(slot_total, width),
        preferred_element_type=jnp.float32,
    )
    grad_routed = grad_routed + jnp.einsum(
        "te,de->td", grad_logits, router_full, preferred_element_type=jnp.float32
    )
    router_grad = jnp.einsum(
        "td,te->de", routed_low, grad_logits, preferred_element_type=jnp.float32
    )
    grad_norm_two, gain_grad = rms_back(grad_routed, unit_two, inverse_two, gain_two)
    grad_resid = grad_result + grad_norm_two
    grad_branch = grad_resid.astype(jnp.bfloat16)
    merge_grad = jnp.einsum("ti,to->io", attended, grad_branch, preferred_element_type=jnp.float32)
    grad_attended = jnp.einsum(
        "to,io->ti", grad_branch, merge_full, preferred_element_type=jnp.float32
    ).astype(jnp.bfloat16)
    grad_queries, grad_keys, grad_values, distances = attend_back(
        queries, keys, values, grad_attended, attended, log_totals, near, head_size, block
    )
    close_sums = distances[:, :group_heads].reshape(head_count, block)
    far_sums = jnp.sum(distances[:, group_heads:].reshape(head_count, block), axis=1)
    table_grad = jnp.einsum(
        "nb,hn->bh", jnp.asarray(hot[:block]), close_sums, precision=lax.Precision.HIGHEST
    )
    table_grad = table_grad + jnp.asarray(hot[-1:]).T * far_sums[None, :]
    query_grad = jnp.einsum(
        "ti,to->io", normed_low, grad_queries, preferred_element_type=jnp.float32
    )
    key_grad = jnp.einsum("ti,to->io", normed_low, grad_keys, preferred_element_type=jnp.float32)
    value_grad = jnp.einsum(
        "ti,to->io", normed_low, grad_values, preferred_element_type=jnp.float32
    )
    grad_normed = jnp.einsum(
        "to,io->ti", grad_queries, query_full, preferred_element_type=jnp.float32
    )
    grad_normed = grad_normed + jnp.einsum(
        "to,io->ti", grad_keys, key_full, preferred_element_type=jnp.float32
    )
    grad_normed = grad_normed + jnp.einsum(
        "to,io->ti", grad_values, value_full, preferred_element_type=jnp.float32
    )
    grad_norm_one, norm_grad = rms_back(grad_normed, unit_one, inverse_one, gain_one)
    input_gradient = grad_resid + grad_norm_one
    everything = (
        lax.psum_scatter(
            norm_grad.astype(jnp.bfloat16), "shard", scatter_dimension=0, tiled=True
        ).astype(jnp.float32),
        lax.psum_scatter(
            query_grad.astype(jnp.bfloat16), "shard", scatter_dimension=0, tiled=True
        ).astype(jnp.float32),
        lax.psum_scatter(
            key_grad.astype(jnp.bfloat16), "shard", scatter_dimension=0, tiled=True
        ).astype(jnp.float32),
        lax.psum_scatter(
            value_grad.astype(jnp.bfloat16), "shard", scatter_dimension=0, tiled=True
        ).astype(jnp.float32),
        lax.psum_scatter(
            merge_grad.astype(jnp.bfloat16), "shard", scatter_dimension=0, tiled=True
        ).astype(jnp.float32),
        lax.psum_scatter(
            table_grad.astype(jnp.bfloat16), "shard", scatter_dimension=1, tiled=True
        ).astype(jnp.float32),
        lax.psum_scatter(
            gain_grad.astype(jnp.bfloat16), "shard", scatter_dimension=0, tiled=True
        ).astype(jnp.float32),
        lax.psum_scatter(
            router_grad.astype(jnp.bfloat16), "shard", scatter_dimension=0, tiled=True
        ).astype(jnp.float32),
        lax.psum_scatter(
            up_grad.astype(jnp.bfloat16), "shard", scatter_dimension=2, tiled=True
        ).astype(jnp.float32),
        lax.psum_scatter(
            down_grad.astype(jnp.bfloat16), "shard", scatter_dimension=1, tiled=True
        ).astype(jnp.float32),
    )
    layer_parts = everything[:8]
    up_part = everything[8]
    down_part = everything[9]
    totals = (
        lax.psum(layer_parts[0].astype(jnp.bfloat16), "expert").astype(jnp.float32),
        lax.psum(layer_parts[1].astype(jnp.bfloat16), "expert").astype(jnp.float32),
        lax.psum(layer_parts[2].astype(jnp.bfloat16), "expert").astype(jnp.float32),
        lax.psum(layer_parts[3].astype(jnp.bfloat16), "expert").astype(jnp.float32),
        lax.psum(layer_parts[4].astype(jnp.bfloat16), "expert").astype(jnp.float32),
        lax.psum(layer_parts[5].astype(jnp.bfloat16), "expert").astype(jnp.float32),
        lax.psum(layer_parts[6].astype(jnp.bfloat16), "expert").astype(jnp.float32),
        lax.psum(layer_parts[7].astype(jnp.bfloat16), "expert").astype(jnp.float32),
    )
    return (
        output,
        input_gradient,
        totals[0],
        totals[1],
        totals[2],
        totals[3],
        totals[4],
        totals[5],
        totals[6],
        totals[7],
        up_part,
        down_part,
    )


def solution(mesh):
    in_specs = (
        P(("expert", "shard"), None),
        P("shard"),
        P("shard", None),
        P("shard", None),
        P("shard", None),
        P("shard", None),
        P(None, "shard"),
        P("shard"),
        P("shard", None),
        P("expert", None, None),
        P("expert", None, None),
        P(("expert", "shard"), None),
        P(("expert", "shard"), None),
    )
    out_specs = (
        P(("expert", "shard"), None),
        P(("expert", "shard"), None),
        P("shard"),
        P("shard", None),
        P("shard", None),
        P("shard", None),
        P("shard", None),
        P(None, "shard"),
        P("shard"),
        P("shard", None),
        P("expert", None, "shard"),
        P("expert", "shard", None),
    )
    return jax.shard_map(local, mesh=mesh, in_specs=in_specs, out_specs=out_specs, check_vma=False)
```

profile of v0, /device:TPU:0, one launch (start us, length us, event | category | flops | bytes accessed | tf_op | source)
XLA Modules:
  0.0 976.7 jit_solution(16736297303393455007)
XLA Ops:
  12.1 12.8 %all-gather = bf16[4,3,32]{2,1,0:T(4,128)(2,1)S(1)} all-gather(bf16[1,3,32]{2,1,0:T(4,128)(2,1)S(1)} %bitcast.75), channel_id=1, replica_groups=mesh['expert'=8,'shard'=4] {'shard'}, dimensions={0}, use_global_device_ids=true | all-gather | bytes 960 | tf_op jit(solution)/shard_map/all_gather | solution.py:222
  28.9 9.2 all-reduce.8
  38.8 7.9 fusion.12
  50.7 23.3 %all-gather.9.cloned.1.call-done = bf16[768,768]{1,0:T(8,128)(2,1)} async-done(((bf16[192,768]{1,0:T(8,128)(2,1)}), bf16[768,768]{1,0:T(8,128)(2,1)}) %all-gather.9.cloned.1.call-update) | async-done | bytes 1179664 | tf_op jit(solution)/shard_map/all_gather | solution.py:219
  76.8 28.3 %all-gather.7.cloned.1.call-done = bf16[768,768]{1,0:T(8,128)(2,1)} async-done(((bf16[192,768]{1,0:T(8,128)(2,1)}), bf16[768,768]{1,0:T(8,128)(2,1)}) %all-gather.7.cloned.1.call-update) | async-done | bytes 1179664 | tf_op jit(solution)/shard_map/all_gather | solution.py:218
  107.9 22.5 %attend.1 = (bf16[1024,768]{1,0:T(8,128)(2,1)S(1)}, f32[6,2,1024]{2,1,0:T(2,128)S(1)}) custom-call(bf16[1024,768]{1,0:T(8,128)(2,1)S(1)} %convolution_convert_fusion.8.query_ref, bf16[1024,768]{1,0:T(8,128)(2,1)S(1)} %convolution_convert_fusion.7.key_ref, bf16[1024,768]{1,0:T(8,128)(2,1)} %convolution_convert_fusion.6.value_ref, ...), custom_call_target="tpu_custom_call" | custom-call | tf_op jit(solution)/shard_map/attend/pallas_call | solution.py:110
  158.8 13.1 %all-gather.1 = bf16[4,192,16]{1,2,0:T(8,128)(2,1)S(1)} all-gather(bf16[1,192,16]{1,2,0:T(8,128)(2,1)S(1)} %bitcast.74), channel_id=1, replica_groups=mesh['expert'=8,'shard'=4] {'shard'}, dimensions={0}, use_global_device_ids=true | all-gather | bytes 30720 | tf_op jit(solution)/shard_map/all_gather | solution.py:224
  172.1 7.3 mul.254.clone
  179.4 8.5 mul.255
  190.1 13.9 %fusion.14 = bf16[2560,768]{1,0:T(8,128)(2,1)S(1)} fusion(s32[2048]{0:T(1024)S(1)} %fusion.39, f32[2048,768]{1,0:T(8,128)} %mul.255, f32[2048]{0:T(1024)S(1)} %div.57), kind=kOutput, calls=%fused_computation.26 | convolution fusion | flops 8063418368 | bytes 10240000 | tf_op jit(solution)/shard_map/dot_general | solution.py:329
  206.2 4.7 all-to-all-start.2
  213.3 21.7 %fusion.55 = f32[2,1280,3072]{2,1,0:T(8,128)} fusion(bf16[2,1280,768]{2,1,0:T(8,128)(2,1)S(1)} %bitcast.64, bf16[2,768,3072]{2,1,0:T(8,128)(2,1)} %param.25), kind=kOutput, calls=%fused_computation.111 | convolution fusion | flops 12079595520 | bytes 44826624 | tf_op jit(solution)/shard_map/erd,edf->erf/dot_general | solution.py:294
  235.0 21.5 %convolution_convert_fusion.4 = bf16[2,1280,768]{2,1,0:T(8,128)(2,1)S(1)} fusion(bf16[2,3072,768]{2,1,0:T(8,128)(2,1)} %param.26, f32[2,1280,3072]{2,1,0:T(8,128)} %fusion.55), kind=kOutput, calls=%fused_computation.36 | convolution fusion | flops 12152340480 | bytes 44826624 | tf_op jit(solution)/shard_map/erf,efd->erd/dot_general | solution.py:298
  258.8 4.8 all-to-all-start.1
  267.8 33.8 %fusion.6 = bf16[2,1280,3072]{2,1,0:T(8,128)(2,1)} fusion(f32[2,1280,3072]{2,1,0:T(8,128)} %fusion.55, bf16[2,1280,768]{2,1,0:T(8,128)(2,1)S(1)} %bitcast.66, bf16[2,3072,768]{2,1,0:T(8,128)(2,1)} %param.26), kind=kOutput, calls=%fused_computation.8 | convolution fusion | flops 12236881920 | bytes 60555264 | tf_op jit(solution)/shard_map/erd,efd->erf/dot_general | solution.py:340
  301.6 19.8 %convolution_convert_fusion.3 = bf16[2,1280,768]{2,1,0:T(8,128)(2,1)} fusion(bf16[2,1280,3072]{2,1,0:T(8,128)(2,1)} %fusion.6, bf16[2,768,3072]{2,1,0:T(8,128)(2,1)} %param.25), kind=kOutput, calls=%fused_computation.35 | convolution fusion | flops 12081561600 | bytes 29097984 | tf_op jit(solution)/shard_map/erf,edf->erd/dot_general | solution.py:350
  330.8 5.3 iota_compare_fusion.2
  336.1 30.4 %eq.72 = pred[1024,2,2560]{2,1,0:T(4,128)(4,1)} reshape(pred[2048,2560]{1,0:T(8,128)(4,1)} %iota_compare_fusion.2) | data formatting | bytes 10485760 | tf_op jit(solution)/shard_map/eq | solution.py:279
  369.6 12.7 %multiply_reduce_fusion = (f32[1024,2]{0,1:T(2,128)S(1)}, f32[1024,768]{0,1:T(8,128)S(1)}) fusion(f32[1024,768]{0,1:T(8,128)S(1)} %copy-done.18, f32[1024,2]{0,1:T(2,128)S(1)} %copy-done.43, bf16[2560,768,1]{1,0,2:T(8,128)(2,1)S(1)} %bitcast.68, pred[1024,2,2560]{2,1,0:T(4,128)(4,1)} %eq.72), kind=kOutput, calls=%fused_computation.23 | convolution fusion | flops 8058566656 | bytes 15482880 | tf_op jit(solution)/shard_map/sp,sd->pd/dot_general | solution.py:308
  384.8 6.6 fusion.56
  397.7 35.8 %attend_back.1 = (bf16[1024,768]{1,0:T(8,128)(2,1)}, bf16[1024,768]{1,0:T(8,128)(2,1)}, bf16[1024,768]{1,0:T(8,128)(2,1)}, f32[6,4,256]{2,1,0:T(4,128)}) custom-call(bf16[1024,768]{1,0:T(8,128)(2,1)} %copy-done.1, bf16[1024,768]{1,0:T(8,128)(2,1)} %copy-done, bf16[1024,768]{1,0:T(8,128)(2,1)} %convolution_convert_fusion.6.value_ref, ...), custom_call_target="tpu_custom_call" | custom-call | tf_op jit(solution)/shard_map/attend_back/pallas_call | solution.py:189
  451.7 15.1 %reduce-scatter.10.cloned.1.call-done = bf16[192,768]{1,0:T(8,128)(2,1)} async-done(((bf16[768,768]{1,0:T(8,128)(2,1)}), bf16[192,768]{1,0:T(8,128)(2,1)}) %reduce-scatter.10.cloned.1.call-update) | async-done | bytes 294928 | tf_op jit(solution)/shard_map/reduce_scatter | solution.py:410
  466.8 30.7 %reduce-scatter.12.cloned.1.call-done = bf16[192,768]{1,0:T(8,128)(2,1)} async-done(((bf16[768,768]{1,0:T(8,128)(2,1)}), bf16[192,768]{1,0:T(8,128)(2,1)}) %reduce-scatter.12.cloned.1.call-update) | async-done | bytes 294928 | tf_op jit(solution)/shard_map/reduce_scatter | solution.py:413
  497.4 30.3 %reduce-scatter.14.cloned.1.call-done = bf16[192,768]{1,0:T(8,128)(2,1)} async-done(((bf16[768,768]{1,0:T(8,128)(2,1)}), bf16[192,768]{1,0:T(8,128)(2,1)}) %reduce-scatter.14.cloned.1.call-update) | async-done | bytes 294928 | tf_op jit(solution)/shard_map/reduce_scatter | solution.py:416
  527.7 30.3 %reduce-scatter.16.cloned.1.call-done = bf16[192,768]{1,0:T(8,128)(2,1)} async-done(((bf16[768,768]{1,0:T(8,128)(2,1)}), bf16[192,768]{1,0:T(8,128)(2,1)}) %reduce-scatter.16.cloned.1.call-update) | async-done | bytes 294928 | tf_op jit(solution)/shard_map/reduce_scatter | solution.py:419
  558.1 27.1 %convolution_convert_fusion = bf16[2,3072,768]{2,1,0:T(8,128)(2,1)} fusion(bf16[2,1280,768]{2,1,0:T(8,128)(2,1)} %bitcast.67, f32[2,1280,3072]{2,1,0:T(8,128)} %fusion.55), kind=kOutput, calls=%fused_computation.21 | convolution fusion | flops 12155092992 | bytes 44826624 | tf_op jit(solution)/shard_map/erf,erd->efd/dot_general | solution.py:347
  585.5 19.6 %convolution_convert_fusion.1 = bf16[2,768,3072]{2,1,0:T(8,128)(2,1)} fusion(bf16[2,1280,768]{2,1,0:T(8,128)(2,1)} %bitcast.65, bf16[2,1280,3072]{2,1,0:T(8,128)(2,1)} %fusion.6), kind=kOutput, calls=%fused_computation.22 | convolution fusion | flops 12084314112 | bytes 29097984 | tf_op jit(solution)/shard_map/erd,erf->edf/dot_general | solution.py:346
  615.2 9.6 all-reduce.7
  625.0 5.4 fusion.23
  636.6 22.8 %all-reduce.5 = (bf16[192]{0:T(256)(128)(2,1)S(1)}, bf16[32,3]{0,1:T(4,128)(2,1)S(1)}, bf16[192]{0:T(256)(128)(2,1)S(1)}, bf16[192,16]{0,1:T(8,128)(2,1)S(1)}) all-reduce(bf16[192]{0:T(256)(128)(2,1)S(1)} %dynamic-slice.3, bf16[32,3]{0,1:T(4,128)(2,1)S(1)} %constant_dynamic-slice_fusion, ...), channel_id=1, replica_groups=mesh['expert'=8,'shard'=4] {'expert'}, use_global_device_ids=true, to_apply=%region_15.16 | all-reduce | flops 3552 | bytes 14208 | tf_op jit(solution)/shard_map/psum | solution.py:442
  669.0 131.9 %reduce-scatter.20.cloned.1.call-done = bf16[2,768,768]{2,1,0:T(8,128)(2,1)} async-done(((bf16[2,3072,768]{2,1,0:T(8,128)(2,1)}), bf16[2,768,768]{2,1,0:T(8,128)(2,1)}) %reduce-scatter.20.cloned.1.call-update) | async-done | bytes 2359312 | tf_op jit(solution)/shard_map/reduce_scatter | solution.py:434
  805.1 160.2 %reduce-scatter.18.cloned.1.call-done = bf16[2,768,768]{2,1,0:T(8,128)(2,1)} async-done(((bf16[2,768,3072]{2,1,0:T(8,128)(2,1)}), bf16[2,768,768]{2,1,0:T(8,128)(2,1)}) %reduce-scatter.18.cloned.1.call-update) | async-done | bytes 2359312 | tf_op jit(solution)/shard_map/reduce_scatter | solution.py:431
  (236 shorter events, 132.6 us)
Async XLA Ops:
  7.2 17.7 %copy-start.26 = (s32[1024,2]{0,1:T(2,128)S(1)}, s32[1024,2]{0,1:T(2,128)}, u32[]{:S(2)}) copy-start(s32[1024,2]{0,1:T(2,128)} %param.27) | copy-start | bytes 24580
  7.2 39.6 %all-gather.11.cloned.1.call-start = ((), (), s32[]{:S(2)}) async-start(), calls=%async_computation.13 | async-start | bytes 1474560 | tf_op jit(solution)/shard_map/all_gather | solution.py:220
  7.9 66.0 %all-gather.9.cloned.1.call-start = ((), (), s32[]{:S(2)}) async-start(), calls=%async_computation.12 | async-start | bytes 1474560 | tf_op jit(solution)/shard_map/all_gather | solution.py:219
  8.7 96.4 %all-gather.7.cloned.1.call-start = ((), (), s32[]{:S(2)}) async-start(), calls=%async_computation.11 | async-start | bytes 1474560 | tf_op jit(solution)/shard_map/all_gather | solution.py:218
  9.4 126.6 %all-gather.13.cloned.1.call-start = ((), (), s32[]{:S(2)}) async-start(), calls=%async_computation.14 | async-start | bytes 1474560 | tf_op jit(solution)/shard_map/all_gather | solution.py:221
  11.7 93.3 %copy-start.6 = (bf16[1024,768]{0,1:T(8,128)(2,1)}, bf16[1024,768]{0,1:T(8,128)(2,1)S(1)}, u32[]{:S(2)}) copy-start(bf16[1024,768]{0,1:T(8,128)(2,1)S(1)} %copy.172) | copy-start | bytes 4718596
  27.1 77.9 %copy-start.24 = (f32[1024]{0:T(1024)}, f32[1024]{0:T(1024)S(1)}, u32[]{:S(2)}) copy-start(f32[1024]{0:T(1024)S(1)} %add_rsqrt_fusion.1) | copy-start | bytes 12292
  38.1 67.0 %copy-start.32 = (f32[768]{0:T(1024)}, f32[768]{0:T(1024)S(1)}, u32[]{:S(2)}) copy-start(f32[768]{0:T(1024)S(1)} %convert_element_type.162) | copy-start | bytes 9220
  38.1 69.8 %copy-start.4 = (f32[6,2,256]{2,1,0:T(2,128)}, f32[6,2,256]{2,1,0:T(2,128)S(1)}, u32[]{:S(2)}) copy-start(f32[6,2,256]{2,1,0:T(2,128)S(1)} %reshape.276.near_ref) | copy-start | bytes 36868
  38.1 101.5 %copy-start.36 = (f32[768]{0:T(1024)}, f32[768]{0:T(1024)S(1)}, u32[]{:S(2)}) copy-start(f32[768]{0:T(1024)S(1)} %convert_element_type.167) | copy-start | bytes 9220
  76.8 31.1 %copy-start = (bf16[1024,768]{1,0:T(8,128)(2,1)}, bf16[1024,768]{1,0:T(8,128)(2,1)S(1)}, u32[]{:S(2)}) copy-start(bf16[1024,768]{1,0:T(8,128)(2,1)S(1)} %convolution_convert_fusion.7.key_ref) | copy-start | bytes 4718596
  141.6 46.4 %copy-start.12 = (bf16[1024,768]{0,1:T(8,128)(2,1)}, bf16[1024,768]{0,1:T(8,128)(2,1)S(1)}, u32[]{:S(2)}) copy-start(bf16[1024,768]{0,1:T(8,128)(2,1)S(1)} %multiply_convert_fusion.3) | copy-start | bytes 4718596
  148.3 57.9 %all-to-all-start = ((bf16[2,8,160,768]{3,2,0,1:T(8,128)(2,1)}), bf16[2,8,160,768]{3,2,0,1:T(8,128)(2,1)}, u32[]{:S(2)}, u32[]{:S(2)}) async-start(bf16[2,8,160,768]{3,2,0,1:T(8,128)(2,1)} %copy.176), calls=%async_computation | async-start | bytes 7864320 | tf_op jit(solution)/shard_map/all_to_all | solution.py:286
  172.1 15.9 %copy-start.22 = (bf16[768,16]{0,1:T(8,128)(2,1)}, bf16[768,16]{0,1:T(8,128)(2,1)S(1)}, u32[]{:S(2)}) copy-start(bf16[768,16]{0,1:T(8,128)(2,1)S(1)} %reshape.296) | copy-start | bytes 73732
  188.0 16.0 %copy-start.40 = (s32[2048]{0:T(1024)}, s32[2048]{0:T(1024)S(1)}, u32[]{:S(2)}) copy-start(s32[2048]{0:T(1024)S(1)} %fusion.39) | copy-start | bytes 24580
  189.6 14.4 %copy-start.42 = (f32[1024,2]{0,1:T(2,128)}, f32[1024,2]{0,1:T(2,128)S(1)}, u32[]{:S(2)}) copy-start(f32[1024,2]{0,1:T(2,128)S(1)} %fusion.46) | copy-start | bytes 24580
  206.2 52.6 %all-to-all-start.2 = ((bf16[2,8,160,768]{3,2,0,1:T(8,128)(2,1)}), bf16[2,8,160,768]{3,2,0,1:T(8,128)(2,1)}, u32[]{:S(2)}, u32[]{:S(2)}) async-start(bf16[2,8,160,768]{3,2,0,1:T(8,128)(2,1)} %copy.185), calls=%async_computation.2 | async-start | bytes 7864320 | tf_op jit(solution)/shard_map/all_to_all | solution.py:332
  213.3 21.7 %copy-start.16 = (bf16[2,8,160,768]{3,2,1,0:T(8,128)(2,1)}, bf16[2,8,160,768]{3,2,1,0:T(8,128)(2,1)S(1)}, u32[]{:S(2)}) copy-start(bf16[2,8,160,768]{3,2,1,0:T(8,128)(2,1)S(1)} %copy.177) | copy-start | bytes 11796484
  258.8 66.9 %all-to-all-start.1 = ((bf16[2,8,160,768]{3,2,0,1:T(8,128)(2,1)}), bf16[2,8,160,768]{3,2,0,1:T(8,128)(2,1)}, u32[]{:S(2)}, u32[]{:S(2)}) async-start(bf16[2,8,160,768]{3,2,0,1:T(8,128)(2,1)} %copy.178), calls=%async_computation.1 | async-start | bytes 7864320 | tf_op jit(solution)/shard_map/all_to_all | solution.py:301
  325.7 56.7 %all-to-all-start.3 = ((bf16[2,8,160,768]{3,2,0,1:T(8,128)(2,1)}), bf16[2,8,160,768]{3,2,0,1:T(8,128)(2,1)}, u32[]{:S(2)}, u32[]{:S(2)}) async-start(bf16[2,8,160,768]{3,2,0,1:T(8,128)(2,1)} %copy.187), calls=%async_computation.3 | async-start | bytes 7864320 | tf_op jit(solution)/shard_map/all_to_all | solution.py:353
  330.3 136.4 %reduce-scatter.10.cloned.1.call-start = ((), (), s32[]{:S(2)}) async-start(), calls=%async_computation.15 | async-start | bytes 1474560 | tf_op jit(solution)/shard_map/reduce_scatter | solution.py:410
  369.6 12.8 %copy-start.27 = (s32[1024,2]{0,1:T(2,128)S(1)}, s32[1024,2]{0,1:T(2,128)}, u32[]{:S(2)}) copy-start(s32[1024,2]{0,1:T(2,128)} %param.27) | copy-start | bytes 24580
  397.7 35.8 %copy-start.7 = (bf16[1024,768]{0,1:T(8,128)(2,1)S(1)}, bf16[1024,768]{0,1:T(8,128)(2,1)}, u32[]{:S(2)}) copy-start(bf16[1024,768]{0,1:T(8,128)(2,1)} %copy-done.6) | copy-start | bytes 4718596
  397.7 35.8 %copy-start.25 = (f32[1024]{0:T(1024)S(1)}, f32[1024]{0:T(1024)}, u32[]{:S(2)}) copy-start(f32[1024]{0:T(1024)} %copy-done.24) | copy-start | bytes 12292
  397.7 35.8 %copy-start.33 = (f32[768]{0:T(1024)S(1)}, f32[768]{0:T(1024)}, u32[]{:S(2)}) copy-start(f32[768]{0:T(1024)} %copy-done.32) | copy-start | bytes 9220
  437.5 59.9 %reduce-scatter.12.cloned.1.call-start = ((), (), s32[]{:S(2)}) async-start(), calls=%async_computation.16 | async-start | bytes 1474560 | tf_op jit(solution)/shard_map/reduce_scatter | solution.py:413
  440.1 87.7 %reduce-scatter.14.cloned.1.call-start = ((), (), s32[]{:S(2)}) async-start(), calls=%async_computation.17 | async-start | bytes 1474560 | tf_op jit(solution)/shard_map/reduce_scatter | solution.py:416
  444.1 113.9 %reduce-scatter.16.cloned.1.call-start = ((), (), s32[]{:S(2)}) async-start(), calls=%async_computation.18 | async-start | bytes 1474560 | tf_op jit(solution)/shard_map/reduce_scatter | solution.py:419
  448.8 186.9 %reduce-scatter.22.cloned.1.call-start = ((), (), s32[]{:S(2)}) async-start(), calls=%async_computation.21 | async-start | bytes 245760
  451.6 210.1 %all-reduce.11.cloned.1.call-start = ((), (), s32[]{:S(2)}) async-start(), calls=%async_computation.22 | async-start | bytes 2359296 | tf_op jit(solution)/shard_map/psum | solution.py:443
  558.0 242.8 %reduce-scatter.20.cloned.1.call-start = ((), (), s32[]{:S(2)}) async-start(), calls=%async_computation.20 | async-start | bytes 11796480 | tf_op jit(solution)/shard_map/reduce_scatter | solution.py:434
  585.2 380.1 %reduce-scatter.18.cloned.1.call-start = ((), (), s32[]{:S(2)}) async-start(), calls=%async_computation.19 | async-start | bytes 11796480 | tf_op jit(solution)/shard_map/reduce_scatter | solution.py:431
  (42 other events, 163.9 us)
Sparse Core Ops, SparseCore 0:
  9.6 33.2 all-gather.10
  44.4 29.4 all-gather.8
  75.5 29.4 all-gather.6
  106.5 29.4 all-gather.12
  437.6 29.0 reduce-scatter.9
  469.5 27.8 reduce-scatter.11
  499.8 27.9 reduce-scatter.13
  530.0 27.9 reduce-scatter.15
  560.8 18.1 reduce-scatter.21
  582.3 55.6 all-reduce.10
  640.4 160.4 reduce-scatter.19
  803.1 162.1 reduce-scatter.17
where the time goes:
time: 982 us; the launch traced here: 977 us
  waiting for transfers between devices  456 us (46%)
  matrix products  225 us (23%)
  local copies, waits for them, and re-layouts  90.1 us (9%)
  blocking collectives  67.5 us (7%)
  Pallas kernels  58.3 us (6%)
  other arithmetic  42.1 us (4%)
  starting transfers between devices  20 us (2%)
  between operations  17.6 us (2%)
    reduce_scatter x1, waiting for transfers between devices, local(): lax.psum_scatter(up_grad.astype(jnp.bfloat16), 'shard', scatter_dimension...  160 us
    reduce_scatter x1, waiting for transfers between devices, local(): lax.psum_scatter(down_grad.astype(jnp.bfloat16), 'shard', scatter_dimensi...  132 us
    pallas_call x1, Pallas kernels, attend_back(): pl.pallas_call(partial(attend_back_kernel, block=block, size=size, scale=...  35.8 us
    dot_general x1, matrix products, local(): jnp.einsum('erd,efd->erf', grad_produced, down_weight, preferred_element_...  33.8 us
    reduce_scatter x1, waiting for transfers between devices, local(): lax.psum_scatter(key_grad.astype(jnp.bfloat16), 'shard', scatter_dimensio...  30.7 us
    eq x1, local copies, waits for them, and re-layouts, local(): pair_hot = (slot_ids[:, None] == slot_index[None, :]).astype(jnp.bfloat16)  30.4 us
    reduce_scatter x1, waiting for transfers between devices, local(): lax.psum_scatter(merge_grad.astype(jnp.bfloat16), 'shard', scatter_dimens...  30.3 us
    reduce_scatter x1, waiting for transfers between devices, local(): lax.psum_scatter(value_grad.astype(jnp.bfloat16), 'shard', scatter_dimens...  30.3 us
  transfers between devices with their start and end apart: 16, of which 9 were waited for; matrix products, arithmetic and copies ran while one was open for 32% of the time, Pallas kernels for 2%

commit v1 on v0

v1 whole, which is shorter than its diff:
```python
from functools import partial, reduce

import jax
import jax.numpy as jnp
import numpy as np
from jax import lax
from jax.experimental import pallas as pl
from jax.experimental.pallas import tpu as pltpu
from jax.sharding import PartitionSpec as P

BUCKETS = 32
MAX_DIST = 128


epsilon = 1e-06
masked_score = -1e30


def bucket_hot(length):
    distance = np.arange(length)
    half_count = BUCKETS // 2
    clipped = np.maximum(distance, half_count)
    spread = np.log(clipped / half_count) / np.log(MAX_DIST / half_count) * (BUCKETS - half_count)
    far_bucket = np.minimum(half_count + np.floor(spread).astype(np.int32), BUCKETS - 1)
    bucket = np.where(distance < half_count, distance, far_bucket)
    return (bucket[:, None] == np.arange(BUCKETS)[None, :]).astype(np.float32)


def dot_nt(a, b):
    return lax.dot_general(a, b, (((1,), (1,)), ((), ())), preferred_element_type=jnp.float32)

def dot_nn(a, b):
    return lax.dot_general(a, b, (((1,), (0,)), ((), ())), preferred_element_type=jnp.float32)

def dot_tn(a, b):
    return lax.dot_general(a, b, (((0,), (0,)), ((), ())), preferred_element_type=jnp.float32)


def slot_kernel(routes_ref, base_ref, slots_ref, *, experts):
    tokens = routes_ref.shape[1]
    expert = lax.broadcasted_iota(jnp.int32, (experts, tokens), 0)
    hits = [routes_ref[c:c + 1, :] == expert for c in range(2)]
    hot = jnp.where(hits[0] | hits[1], 1.0, 0.0).astype(jnp.bfloat16)
    earlier = lax.broadcasted_iota(jnp.int32, (tokens, tokens), 0)
    later = lax.broadcasted_iota(jnp.int32, (tokens, tokens), 1)
    before = jnp.where(earlier < later, 1.0, 0.0).astype(jnp.bfloat16)
    counts = dot_nn(hot, before)
    for c in range(2):
        position = jnp.sum(jnp.where(hits[c], counts, 0.0), axis=0, keepdims=True)
        slots_ref[c:c + 1, :] = base_ref[c:c + 1, :] + position.astype(jnp.int32)

def find_slots(routes, base, experts):
    return pl.pallas_call(
        partial(slot_kernel, experts=experts),
        out_shape=jax.ShapeDtypeStruct(routes.shape, jnp.int32),
        name="find_slots",
    )(routes, base)


def dispatch_kernel(slots_ref, rows_ref, *refs, start, gated):
    out_ref = refs[-2] if gated else refs[-1]
    block, tokens = out_ref.shape[0], rows_ref.shape[0]
    slot = lax.broadcasted_iota(jnp.int32, (block, tokens), 0) + (pl.program_id(0) * block + start)
    hits = [slot == slots_ref[c:c + 1, :] for c in range(2)]
    hot = jnp.where(hits[0] | hits[1], 1.0, 0.0).astype(jnp.bfloat16)
    out_ref[...] = dot_nn(hot, rows_ref[...]).astype(out_ref.dtype)
    if gated:
        gates_ref, gate_ref = refs[0], refs[-1]
        gate = jnp.where(hits[0], gates_ref[0:1, :], jnp.where(hits[1], gates_ref[1:2, :], 0.0))
        column = jnp.sum(gate, axis=1, keepdims=True)
        gate_ref[...] = jnp.broadcast_to(column, (block, 128)).T[0:1, :]

def dispatch(slots, rows, start, count, gates=None, block=256):
    tokens, width = rows.shape
    gated = gates is not None
    whole = lambda shape: pl.BlockSpec(shape, lambda i: (0, 0))
    out_shape = jax.ShapeDtypeStruct((count, width), rows.dtype)
    out_spec = pl.BlockSpec((block, width), lambda i: (i, 0))
    if gated:
        out_shape = [out_shape, jax.ShapeDtypeStruct((1, count), jnp.float32)]
        out_spec = [out_spec, pl.BlockSpec((1, block), lambda i: (0, i))]
    return pl.pallas_call(
        partial(dispatch_kernel, start=start, gated=gated),
        grid=(count // block,),
        in_specs=[whole(slots.shape), whole(rows.shape)] + ([whole(gates.shape)] if gated else []),
        out_specs=out_spec,
        out_shape=out_shape,
        name="dispatch",
    )(slots, rows, *([gates] if gated else []))


def gelu_pair(v):
    c = np.float32(np.sqrt(2.0 / np.pi))
    a = np.float32(0.044715)
    square = v * v
    half = 0.5 * jnp.tanh(v * (c * a * square + c)) + 0.5
    value = v * half
    slope = half + value * (1.0 - half) * (6.0 * c * a * square + 2.0 * c)
    return value, slope


def first_kernel(rows_ref, cot_ref, gate_ref, up_ref, act_ref, slope_ref, down_grad_ref, grad_ref, *, chunk):
    rows, width = rows_ref.shape
    @pl.when(pl.program_id(0) == 0)
    def _():
        column = jnp.broadcast_to(gate_ref[...], (128, rows)).T
        for start in range(0, width, 128):
            part = cot_ref[:, start:start + 128].astype(jnp.float32) * column
            grad_ref[:, start:start + 128] = part.astype(jnp.bfloat16)
    up = up_ref[0]
    for start in range(0, rows, chunk):
        pre = dot_nn(rows_ref[start:start + chunk, :], up)
        value, slope = gelu_pair(pre)
        act_ref[start:start + chunk, :] = value.astype(jnp.bfloat16)
        slope_ref[start:start + chunk, :] = slope.astype(jnp.bfloat16)
    down_grad_ref[...] = dot_tn(act_ref[...], grad_ref[...]).astype(jnp.bfloat16)

def expert_first(rows_in, cot, gate, up, which, tile=512, chunk=256):
    rows, width = rows_in.shape
    hidden = up.shape[2]
    fixed = pl.BlockSpec((rows, width), lambda i: (0, 0))
    column = pl.BlockSpec((rows, tile), lambda i: (0, i))
    return pl.pallas_call(
        partial(first_kernel, chunk=chunk),
        grid=(hidden // tile,),
        in_specs=[fixed, fixed, pl.BlockSpec((1, rows), lambda i: (0, 0)), pl.BlockSpec((1, width, tile), lambda i: (which, 0, i))],
        out_specs=[column, column, pl.BlockSpec((tile, width), lambda i: (i, 0)), fixed],
        out_shape=[jax.ShapeDtypeStruct((rows, hidden), jnp.bfloat16)] * 2 + [jax.ShapeDtypeStruct((hidden, width), jnp.bfloat16), jax.ShapeDtypeStruct((rows, width), jnp.bfloat16)],
        compiler_params=pltpu.CompilerParams(vmem_limit_bytes=56 << 20),
        name="expert_first",
    )(rows_in, cot, gate, up)


def second_kernel(rows_ref, grad_ref, act_ref, slope_ref, up_ref, down_ref, made_ref, back_ref, up_grad_ref, turned, made_acc, back_acc):
    step = pl.program_id(0)
    @pl.when(step == 0)
    def _():
        turned[...] = rows_ref[...].T
    up = up_ref[0]
    down = down_ref[0]
    grads = dot_nt(grad_ref[...], down)
    low = (slope_ref[...].astype(jnp.float32) * grads).astype(jnp.bfloat16)
    up_grad_ref[...] = dot_nn(turned[...], low).astype(jnp.bfloat16)
    back = dot_nt(low, up)
    made = dot_nn(act_ref[...], down)
    last = pl.num_programs(0) - 1
    @pl.when(step == 0)
    def _():
        made_acc[...] = made
        back_acc[...] = back
    @pl.when((step > 0) & (step < last))
    def _():
        made_acc[...] += made
        back_acc[...] += back
    @pl.when(step == last)
    def _():
        made_ref[...] = (made_acc[...] + made).astype(jnp.bfloat16)
        back_ref[...] = (back_acc[...] + back).astype(jnp.bfloat16)

def expert_second(rows_in, grad, act, slope, up, down, which, tile=512):
    rows, width = rows_in.shape
    hidden = up.shape[2]
    fixed = pl.BlockSpec((rows, width), lambda i: (0, 0))
    column = pl.BlockSpec((rows, tile), lambda i: (0, i))
    return pl.pallas_call(
        second_kernel,
        grid=(hidden // tile,),
        in_specs=[fixed, fixed, column, column, pl.BlockSpec((1, width, tile), lambda i: (which, 0, i)), pl.BlockSpec((1, tile, width), lambda i: (which, i, 0))],
        out_specs=[fixed, fixed, pl.BlockSpec((width, tile), lambda i: (0, i))],
        out_shape=[jax.ShapeDtypeStruct((rows, width), jnp.bfloat16)] * 2 + [jax.ShapeDtypeStruct((width, hidden), jnp.bfloat16)],
        scratch_shapes=[pltpu.VMEM((width, rows), jnp.bfloat16), pltpu.VMEM((rows, width), jnp.float32), pltpu.VMEM((rows, width), jnp.float32)],
        compiler_params=pltpu.CompilerParams(vmem_limit_bytes=60 << 20),
        name="expert_second",
    )(rows_in, grad, act, slope, up, down)


def spread(row, block):
    return jnp.broadcast_to(row, (128, block)).T

def out_kernel(slots_ref, routes_ref, gates_ref, resid_ref, cot_ref, first_ref, second_ref, out_ref, logit_ref):
    block = out_ref.shape[0]
    half = first_ref.shape[0]
    lane = lax.broadcasted_iota(jnp.int32, (block, 128), 1)
    cot = cot_ref[...].astype(jnp.float32)
    result = resid_ref[...]
    gates, inner = [], []
    for c in range(2):
        slot = spread(slots_ref[c:c + 1, :], block)
        gate = spread(gates_ref[c:c + 1, :], block)[:, 0:1]
        hots = [jnp.where(slot == lane + k * 128, 1.0, 0.0).astype(jnp.bfloat16) for k in range(2 * half // 128)]
        count = half // 128
        picked = dot_nn(jnp.concatenate(hots[:count], axis=1), first_ref[...]) + dot_nn(jnp.concatenate(hots[count:], axis=1), second_ref[...])
        result = result + gate * picked
        gates.append(gate)
        inner.append(jnp.sum(cot * picked, axis=1, keepdims=True))
    out_ref[...] = result.astype(out_ref.dtype)
    middle = gates[0] * inner[0] + gates[1] * inner[1]
    logit = jnp.zeros((block, 128), jnp.float32)
    for c in range(2):
        route = spread(routes_ref[c:c + 1, :], block)
        logit = logit + jnp.where(route == lane, gates[c] * (inner[c] - middle), 0.0)
    logit_ref[...] = logit.astype(jnp.bfloat16)

def combine_out(slots, routes, gates, resid, cot, first, second, block=256):
    tokens, width = resid.shape
    small = pl.BlockSpec((2, block), lambda i: (0, i))
    rows = pl.BlockSpec((block, width), lambda i: (i, 0))
    fixed = pl.BlockSpec(first.shape, lambda i: (0, 0))
    return pl.pallas_call(
        out_kernel,
        grid=(tokens // block,),
        in_specs=[small, small, small, rows, rows, fixed, fixed],
        out_specs=[rows, pl.BlockSpec((block, 128), lambda i: (i, 0))],
        out_shape=[jax.ShapeDtypeStruct((tokens, width), jnp.bfloat16), jax.ShapeDtypeStruct((tokens, 128), jnp.bfloat16)],
        compiler_params=pltpu.CompilerParams(vmem_limit_bytes=48 << 20),
        name="combine_out",
    )(slots, routes, gates, resid, cot, first, second)


def back_kernel(slots_ref, logit_ref, router_ref, gain_ref, resid_ref, cot_ref, first_ref, second_ref, grad_ref, low_ref, gain_grad_ref, *, eps):
    block, width = grad_ref.shape
    half = first_ref.shape[0]
    lane = lax.broadcasted_iota(jnp.int32, (block, 128), 1)
    slots = [spread(slots_ref[c:c + 1, :], block) for c in range(2)]
    hots = [jnp.where((slots[0] == lane + k * 128) | (slots[1] == lane + k * 128), 1.0, 0.0).astype(jnp.bfloat16) for k in range(2 * half // 128)]
    count = half // 128
    grads = dot_nn(jnp.concatenate(hots[:count], axis=1), first_ref[...]) + dot_nn(jnp.concatenate(hots[count:], axis=1), second_ref[...])
    grads = grads + dot_nt(logit_ref[...], router_ref[...])
    resid = resid_ref[...]
    inverse = lax.rsqrt(jnp.mean(resid * resid, axis=1, keepdims=True) + eps)
    unit = resid * inverse
    @pl.when(pl.program_id(0) == 0)
    def _():
        gain_grad_ref[...] = jnp.zeros_like(gain_grad_ref)
    gain_grad_ref[...] += jnp.sum(grads * unit, axis=0, keepdims=True)
    scaled = grads * gain_ref[...]
    inner = jnp.mean(scaled * unit, axis=1, keepdims=True)
    total = cot_ref[...].astype(jnp.float32) + inverse * (scaled - unit * inner)
    grad_ref[...] = total
    low_ref[...] = total.astype(jnp.bfloat16)

def combine_back(slots, logit, router, gain, resid, cot, first, second, eps, block=256):
    tokens, width = resid.shape
    rows = pl.BlockSpec((block, width), lambda i: (i, 0))
    whole = lambda shape: pl.BlockSpec(shape, lambda i: (0, 0))
    return pl.pallas_call(
        partial(back_kernel, eps=eps),
        grid=(tokens // block,),
        in_specs=[pl.BlockSpec((2, block), lambda i: (0, i)), pl.BlockSpec((block, 128), lambda i: (i, 0)), whole(router.shape), whole(gain.shape), rows, rows, whole(first.shape), whole(second.shape)],
        out_specs=[rows, rows, whole((1, width))],
        out_shape=[jax.ShapeDtypeStruct((tokens, width), jnp.float32), jax.ShapeDtypeStruct((tokens, width), jnp.bfloat16), jax.ShapeDtypeStruct((1, width), jnp.float32)],
        compiler_params=pltpu.CompilerParams(vmem_limit_bytes=48 << 20),
        name="combine_back",
    )(slots, logit, router, gain, resid, cot, first, second)


def near_tiles(near_ref, head, block):
    spread = jnp.broadcast_to(near_ref[0, head:head + 1, :], (block, block))
    spread = pltpu.roll(spread, 0, 1, stride=1, stride_axis=0)
    key_at = lax.broadcasted_iota(jnp.int32, (block, block), 0)
    query_at = lax.broadcasted_iota(jnp.int32, (block, block), 1)
    return (jnp.where(query_at >= key_at, spread, masked_score), jnp.where(query_at < key_at, spread, 0.0), query_at < key_at)

def diagonal_sums(tile):
    block = tile.shape[1]
    total = tile[:8]
    for start in range(8, block, 8):
        total = total + pltpu.roll(tile[start:start + 8], block - start, 1)
    row = lax.broadcasted_iota(jnp.int32, total.shape, 0)
    for step in (1, 2, 4):
        total = jnp.where((row & step) != 0, pltpu.roll(total, block - step, 1), total)
    return jnp.sum(total, axis=0, keepdims=True)

def head_part(rows, head, size):
    lane = lax.broadcasted_iota(jnp.int32, rows.shape, 1)
    return jnp.where((lane >= head * size) & (lane < (head + 1) * size), rows, jnp.zeros_like(rows))

def attend_kernel(query_ref, key_ref, value_ref, near_ref, out_ref, total_ref, *, block, size, scale):
    length, lanes = query_ref.shape
    heads = lanes // size
    count = length // block
    flipped = value_ref[...].T
    tiles = [near_tiles(near_ref, head, block) for head in range(heads)]
    for i in range(count):
        rows = pl.ds(i * block, block)
        query_rows = query_ref[rows, :] * jnp.bfloat16(scale)
        parts = []
        for head in range(heads):
            query_part = head_part(query_rows, head, size)
            scores = []
            for j in range(i + 1):
                tile = dot_nt(key_ref[pl.ds(j * block, block), :], query_part)
                if j == i:
                    tile = tile + tiles[head][0]
                elif j == i - 1:
                    tile = tile + tiles[head][1]
                scores.append(tile)
            top = reduce(jnp.maximum, scores)
            top = jnp.max(top, axis=0, keepdims=True)
            mixed = None
            total = None
            for j in range(i + 1):
                weights = jnp.exp(scores[j] - top)
                sums = jnp.sum(weights, axis=0, keepdims=True)
                part = dot_nn(flipped[head * size:(head + 1) * size, j * block:(j + 1) * block], weights.astype(jnp.bfloat16))
                mixed = part if mixed is None else mixed + part
                total = sums if total is None else total + sums
            parts.append(mixed / total)
            total_ref[0, head:head + 1, rows] = top + jnp.log(total)
        out_ref[rows, :] = jnp.concatenate(parts, axis=0).T.astype(out_ref.dtype)

def attend(queries, keys, values, near, size, block):
    length, width = queries.shape
    lanes = 128
    heads = lanes // size
    groups = width // lanes
    column = pl.BlockSpec((length, lanes), lambda g: (0, g))
    head_rows = pl.BlockSpec((1, heads, block), lambda g: (g, 0, 0))
    return pl.pallas_call(
        partial(attend_kernel, block=block, size=size, scale=size ** -0.5),
        grid=(groups,),
        in_specs=[column, column, column, head_rows],
        out_specs=[column, pl.BlockSpec((1, heads, length), lambda g: (g, 0, 0))],
        out_shape=[jax.ShapeDtypeStruct((length, width), jnp.bfloat16), jax.ShapeDtypeStruct((groups, heads, length), jnp.float32)],
        compiler_params=pltpu.CompilerParams(vmem_limit_bytes=48 << 20),
        name="attend",
    )(queries, keys, values, near)

def attend_back_kernel(query_ref, key_ref, value_ref, grad_ref, out_ref, total_ref, near_ref, dq_ref, dk_ref, dv_ref, dist_ref, key_acc, value_acc, *, block, size, scale):
    length, lanes = query_ref.shape
    heads = lanes // size
    count = length // block
    flipped = key_ref[...].T
    tiles = [near_tiles(near_ref, head, block) for head in range(heads)]
    near_acc = [None] * heads
    far_acc = [None] * heads
    for i in range(count):
        rows = pl.ds(i * block, block)
        query_rows = query_ref[rows, :] * jnp.bfloat16(scale)
        grad_rows = grad_ref[rows, :]
        products = (grad_rows.astype(jnp.float32) * out_ref[rows, :].astype(jnp.float32)).T
        query_parts = [head_part(query_rows, head, size) for head in range(heads)]
        grad_parts = [head_part(grad_rows, head, size) for head in range(heads)]
        inner = [jnp.sum(products[head * size:(head + 1) * size], axis=0, keepdims=True) for head in range(heads)]
        query_stack = jnp.concatenate(query_parts, axis=0)
        grad_stack = jnp.concatenate(grad_parts, axis=0)
        query_grads = [None] * heads
        for j in range(i + 1):
            cols = pl.ds(j * block, block)
            weight_list = []
            score_list = []
            for head in range(heads):
                tile = dot_nt(key_ref[cols, :], query_parts[head])
                if j == i:
                    tile = tile + tiles[head][0]
                elif j == i - 1:
                    tile = tile + tiles[head][1]
                weights = jnp.exp(tile - total_ref[0, head:head + 1, rows])
                grads = dot_nt(value_ref[cols, :], grad_parts[head])
                score_grads = weights * (grads - inner[head])
                low = score_grads.astype(jnp.bfloat16)
                weight_list.append(weights.astype(jnp.bfloat16))
                score_list.append(low)
                part = dot_nn(flipped[head * size:(head + 1) * size, j * block:(j + 1) * block], low)
                query_grads[head] = part if query_grads[head] is None else query_grads[head] + part
                if j == i:
                    near_acc[head] = score_grads if near_acc[head] is None else near_acc[head] + score_grads
                else:
                    far = score_grads
                    if j == i - 1:
                        close = jnp.where(tiles[head][2], score_grads, 0.0)
                        near_acc[head] = near_acc[head] + close
                        far = score_grads - close
                    far = jnp.sum(far, axis=0, keepdims=True)
                    far_acc[head] = far if far_acc[head] is None else far_acc[head] + far
            value_part = dot_nn(jnp.concatenate(weight_list, axis=1), grad_stack)
            key_part = dot_nn(jnp.concatenate(score_list, axis=1), query_stack)
            if j == i:
                value_acc[cols, :] = value_part
                key_acc[cols, :] = key_part
            else:
                value_acc[cols, :] += value_part
                key_acc[cols, :] += key_part
        dq_ref[rows, :] = (jnp.concatenate(query_grads, axis=0) * scale).T.astype(dq_ref.dtype)
    dk_ref[...] = key_acc[...].astype(dk_ref.dtype)
    dv_ref[...] = value_acc[...].astype(dv_ref.dtype)
    for head in range(heads):
        dist_ref[0, head:head + 1, :] = diagonal_sums(near_acc[head])
        dist_ref[0, heads + head:heads + head + 1, :] = far_acc[head]

def attend_back(queries, keys, values, grads, outs, totals, near, size, block):
    length, width = queries.shape
    lanes = 128
    heads = lanes // size
    groups = width // lanes
    column = pl.BlockSpec((length, lanes), lambda g: (0, g))
    head_rows = pl.BlockSpec((1, heads, block), lambda g: (g, 0, 0))
    return pl.pallas_call(
        partial(attend_back_kernel, block=block, size=size, scale=size ** -0.5),
        grid=(groups,),
        in_specs=[column] * 5 + [pl.BlockSpec((1, heads, length), lambda g: (g, 0, 0)), head_rows],
        out_specs=[column, column, column, pl.BlockSpec((1, 2 * heads, block), lambda g: (g, 0, 0))],
        out_shape=[jax.ShapeDtypeStruct((length, width), jnp.bfloat16)] * 3 + [jax.ShapeDtypeStruct((groups, 2 * heads, block), jnp.float32)],
        scratch_shapes=[pltpu.VMEM((length, lanes), jnp.float32)] * 2,
        compiler_params=pltpu.CompilerParams(vmem_limit_bytes=56 << 20),
        name="attend_back",
    )(queries, keys, values, grads, outs, totals, near)


def project_kernel(inputs_ref, gain_ref, query_ref, key_ref, value_ref, low_ref, *out_refs, eps):
    rows = inputs_ref[...].astype(jnp.float32)
    inverse = lax.rsqrt(jnp.mean(rows * rows, axis=1, keepdims=True) + eps)
    low = (rows * inverse * gain_ref[...]).astype(jnp.bfloat16)
    low_ref[...] = low
    for weight_ref, out_ref in zip((query_ref, key_ref, value_ref), out_refs):
        out_ref[...] = dot_nn(low, weight_ref[...]).astype(jnp.bfloat16)

def project(inputs, gain, query, key, value, eps, block=256):
    tokens, width = inputs.shape
    rows = pl.BlockSpec((block, width), lambda i: (i, 0))
    whole = lambda shape: pl.BlockSpec(shape, lambda i: (0, 0))
    return pl.pallas_call(
        partial(project_kernel, eps=eps),
        grid=(tokens // block,),
        in_specs=[rows, whole(gain.shape)] + [whole(query.shape)] * 3,
        out_specs=[rows] * 4,
        out_shape=[jax.ShapeDtypeStruct((tokens, width), jnp.bfloat16)] * 4,
        compiler_params=pltpu.CompilerParams(vmem_limit_bytes=40 << 20),
        name="project",
    )(inputs, gain, query, key, value)


def settle_kernel(mixed_ref, merge_ref, inputs_ref, gain_ref, router_ref, routes_ref, resid_ref, low_ref, gates_ref, *, eps):
    block = mixed_ref.shape[0]
    resid = inputs_ref[...].astype(jnp.float32) + dot_nn(mixed_ref[...], merge_ref[...])
    resid_ref[...] = resid
    inverse = lax.rsqrt(jnp.mean(resid * resid, axis=1, keepdims=True) + eps)
    low = (resid * inverse * gain_ref[...]).astype(jnp.bfloat16)
    low_ref[...] = low
    logits = dot_nt(router_ref[...], low)
    expert = lax.broadcasted_iota(jnp.int32, logits.shape, 0)
    chosen = [jnp.sum(jnp.where(routes_ref[c:c + 1, :] == expert, logits, 0.0), axis=0, keepdims=True) for c in range(2)]
    top = jnp.maximum(chosen[0], chosen[1])
    powers = [jnp.exp(value - top) for value in chosen]
    total = powers[0] + powers[1]
    for c in range(2):
        gates_ref[c:c + 1, :] = powers[c] / total

def settle(mixed, merge, inputs, gain, router, routes, eps, block=256):
    tokens, width = inputs.shape
    rows = pl.BlockSpec((block, width), lambda i: (i, 0))
    whole = lambda shape: pl.BlockSpec(shape, lambda i: (0, 0))
    small = pl.BlockSpec((2, block), lambda i: (0, i))
    return pl.pallas_call(
        partial(settle_kernel, eps=eps),
        grid=(tokens // block,),
        in_specs=[rows, whole(merge.shape), rows, whole(gain.shape), whole(router.shape), small],
        out_specs=[rows, rows, small],
        out_shape=[jax.ShapeDtypeStruct((tokens, width), jnp.float32), jax.ShapeDtypeStruct((tokens, width), jnp.bfloat16), jax.ShapeDtypeStruct((2, tokens), jnp.float32)],
        compiler_params=pltpu.CompilerParams(vmem_limit_bytes=40 << 20),
        name="settle",
    )(mixed, merge, inputs, gain, router, routes)


def finish_kernel(dq_ref, dk_ref, dv_ref, query_ref, key_ref, value_ref, gain_ref, inputs_ref, resid_grad_ref, out_ref, gain_grad_ref, *, eps):
    grads = dot_nt(dq_ref[...], query_ref[...]) + dot_nt(dk_ref[...], key_ref[...]) + dot_nt(dv_ref[...], value_ref[...])
    rows = inputs_ref[...].astype(jnp.float32)
    inverse = lax.rsqrt(jnp.mean(rows * rows, axis=1, keepdims=True) + eps)
    unit = rows * inverse
    @pl.when(pl.program_id(0) == 0)
    def _():
        gain_grad_ref[...] = jnp.zeros_like(gain_grad_ref)
    gain_grad_ref[...] += jnp.sum(grads * unit, axis=0, keepdims=True)
    scaled = grads * gain_ref[...]
    inner = jnp.mean(scaled * unit, axis=1, keepdims=True)
    out_ref[...] = resid_grad_ref[...] + inverse * (scaled - unit * inner)

def finish(dq, dk, dv, query, key, value, gain, inputs, resid_grad, eps, block=256):
    tokens, width = inputs.shape
    rows = pl.BlockSpec((block, width), lambda i: (i, 0))
    whole = lambda shape: pl.BlockSpec(shape, lambda i: (0, 0))
    return pl.pallas_call(
        partial(finish_kernel, eps=eps),
        grid=(tokens // block,),
        in_specs=[rows] * 3 + [whole(query.shape)] * 3 + [whole(gain.shape), rows, rows],
        out_specs=[rows, whole((1, width))],
        out_shape=[jax.ShapeDtypeStruct((tokens, width), jnp.float32), jax.ShapeDtypeStruct((1, width), jnp.float32)],
        compiler_params=pltpu.CompilerParams(vmem_limit_bytes=40 << 20),
        name="finish",
    )(dq, dk, dv, query, key, value, gain, inputs, resid_grad)


def exchange(rows, bit):
    count = lax.axis_size("expert")
    return lax.ppermute(rows, "expert", [(i, i ^ bit) for i in range(count)])


def shift(rows, step):
    count = lax.axis_size("shard")
    return lax.ppermute(rows, "shard", [(i, (i + step) % count) for i in range(count)])


def gather_line(rows):
    count = lax.axis_size("shard")
    me = lax.axis_index("shard")
    out = jnp.zeros((count,) + rows.shape, rows.dtype)
    out = lax.dynamic_update_index_in_dim(out, rows, me, 0)
    for step in range(1, count):
        out = lax.dynamic_update_index_in_dim(out, shift(rows, step), (me - step) % count, 0)
    return out


def add_low(left, right):
    return (left.astype(jnp.float32) + right.astype(jnp.float32)).astype(jnp.bfloat16)


def reduce_stack(stack, bits):
    me = lax.axis_index("expert")
    for bit in bits:
        half = stack.shape[1] // 2
        side = (me // bit) % 2
        keep = lax.dynamic_slice_in_dim(stack, side * half, half, 1)
        send = lax.dynamic_slice_in_dim(stack, (1 - side) * half, half, 1)
        stack = add_low(keep, exchange(send, bit))
    count = lax.axis_size("shard")
    place = lax.axis_index("shard")
    total = lax.dynamic_index_in_dim(stack, place, 0, False).astype(jnp.float32)
    for step in range(1, count):
        send = lax.dynamic_index_in_dim(stack, (place + step) % count, 0, False)
        total = total + shift(send, step).astype(jnp.float32)
    piece = total.astype(jnp.bfloat16)
    for bit in reversed(bits):
        other = exchange(piece, bit)
        side = (me // bit) % 2
        piece = jnp.where(
            side == 0, jnp.concatenate([piece, other]), jnp.concatenate([other, piece])
        )
    return piece


def share_rows(rows, owners):
    count, width = rows.shape
    return lax.all_to_all(
        rows.reshape(owners, count // owners, width), "expert", 0, 0, tiled=True
    ).reshape(count, width)


def local(
    inputs,
    norm_gain,
    query_weight,
    key_weight,
    value_weight,
    merge_weight,
    bias_table,
    expert_gain,
    router_weight,
    up_weight,
    down_weight,
    routes,
    cotangent,
):
    f32, bf16 = jnp.float32, jnp.bfloat16
    tokens, width = inputs.shape
    owners = lax.axis_size("expert")
    shards = lax.axis_size("shard")
    me = lax.axis_index("expert")
    part = query_weight.shape[0]
    piece = part // owners
    local_heads = bias_table.shape[1]
    heads = local_heads * shards
    size = width // heads
    experts = router_weight.shape[1]
    local_count = up_weight.shape[0]
    capacity = (5 * tokens * routes.shape[1] + 4 * experts - 1) // (4 * experts)
    rows = owners * capacity

    small = jnp.concatenate(
        [norm_gain, expert_gain, router_weight.reshape(-1), bias_table.reshape(-1)]
    )
    small_rows = 8 * owners
    small = jnp.pad(small, (0, small_rows * width - small.shape[0])).reshape(small_rows, width)
    slices = [
        lax.dynamic_slice_in_dim(weight, me * piece, piece, 0)
        for weight in (query_weight, key_weight, value_weight)
    ] + [lax.dynamic_slice_in_dim(small, me * 8, 8, 0)]
    lined = gather_line(jnp.concatenate(slices))
    gathered = lax.all_gather(lined, "expert", axis=0, tiled=False)
    merge_full = lax.all_gather(merge_weight, "shard", axis=0, tiled=True)

    def whole_weight(index):
        block = gathered[:, :, index * piece : (index + 1) * piece]
        return block.transpose(1, 0, 2, 3).reshape(width, width)

    query_full, key_full, value_full = (whole_weight(index) for index in range(3))
    small_full = gathered[:, :, 3 * piece :].transpose(1, 0, 2, 3).reshape(shards, small_rows * width)
    gain_one = small_full[:, :part].reshape(1, width).astype(f32)
    gain_two = small_full[:, part : 2 * part].reshape(1, width).astype(f32)
    router_at = 2 * part + part * experts
    router_full = small_full[:, 2 * part : router_at].reshape(width, experts)
    table_full = small_full[:, router_at : router_at + BUCKETS * local_heads]
    table_full = table_full.reshape(shards, BUCKETS, local_heads).transpose(1, 0, 2)
    table_full = table_full.reshape(BUCKETS, heads).astype(f32)

    routes_line = routes.T
    base = (routes_line % local_count * owners + routes_line // local_count) * capacity
    slots = find_slots(routes_line, base, experts)
    cot_rows = [dispatch(slots, cotangent, index * rows, rows) for index in range(local_count)]

    low_one, queries, keys, values = project(
        inputs, gain_one, query_full, key_full, value_full, epsilon
    )
    block = 256
    hot = bucket_hot(tokens)
    assert hot[block:, -1].all()
    near_hot = jnp.asarray(hot[:block] - hot[-1:], dtype=f32)
    group = 128 // size
    near = jnp.dot(near_hot, table_full, precision=lax.Precision.HIGHEST).T
    near = near.reshape(heads // group, group, block)
    attended, totals = attend(queries, keys, values, near, size, block)
    resid, low_two, gates = settle(
        attended, merge_full, inputs, gain_two, router_full.T, routes_line, epsilon
    )

    made, back, up_grads, down_grads = [], [], [], []
    for index in range(local_count):
        rows_out, gate_out = dispatch(slots, low_two, index * rows, rows, gates)
        rows_in = share_rows(rows_out, owners)
        gate_in = lax.all_to_all(
            gate_out.reshape(owners, 1, capacity), "expert", 0, 0, tiled=True
        ).reshape(1, rows)
        cot_in = share_rows(cot_rows[index], owners)
        act, slope, down_grad, grad_in = expert_first(rows_in, cot_in, gate_in, up_weight, index)
        down_grads.append(lax.psum_scatter(down_grad, "shard", scatter_dimension=0, tiled=True))
        made_rows, back_rows, up_grad = expert_second(
            rows_in, grad_in, act, slope, up_weight, down_weight, index
        )
        up_grads.append(lax.psum_scatter(up_grad, "shard", scatter_dimension=1, tiled=True))
        made.append(share_rows(made_rows, owners))
        back.append(share_rows(back_rows, owners))
    output, logit_grad = combine_out(slots, routes_line, gates, resid, cotangent, *made)
    router_wide = jnp.pad(router_full, ((0, 0), (0, 128 - experts)))
    resid_grad, branch, gain_grad = combine_back(
        slots, logit_grad, router_wide, gain_two, resid, cotangent, *back, epsilon
    )

    def weight_grad(left, right):
        return jnp.einsum("ti,to->io", left, right, preferred_element_type=f32).astype(bf16)

    router_grad = weight_grad(low_two, logit_grad[:, :experts])
    merge_grad = weight_grad(attended, branch)
    mixed_grad = jnp.einsum(
        "to,io->ti", branch, merge_full, preferred_element_type=f32
    ).astype(bf16)
    grad_queries, grad_keys, grad_values, distances = attend_back(
        queries, keys, values, mixed_grad, attended, totals, near, size, block
    )
    close_sums = distances[:, :group].reshape(heads, block)
    far_sums = jnp.sum(distances[:, group:].reshape(heads, block), axis=1)
    table_grad = jnp.einsum(
        "nb,hn->bh", jnp.asarray(hot[:block]), close_sums, precision=lax.Precision.HIGHEST
    )
    table_grad = table_grad + jnp.asarray(hot[-1:]).T * far_sums[None, :]
    input_gradient, norm_grad = finish(
        grad_queries, grad_keys, grad_values, query_full, key_full, value_full,
        gain_one, inputs, resid_grad, epsilon,
    )

    def by_shard(grad):
        return grad.reshape(shards, part, width)

    small_grad = jnp.concatenate(
        [
            norm_grad.reshape(shards, part).astype(bf16),
            gain_grad.reshape(shards, part).astype(bf16),
            router_grad.reshape(shards, part * experts),
            table_grad.reshape(BUCKETS, shards, local_heads)
            .transpose(1, 0, 2)
            .reshape(shards, BUCKETS * local_heads)
            .astype(bf16),
        ],
        axis=1,
    )
    used = small_grad.shape[1]
    small_grad = jnp.pad(small_grad, ((0, 0), (0, small_rows * width - used)))
    small_grad = small_grad.reshape(shards, small_rows, width)
    bits = [1 << level for level in range(owners.bit_length() - 1)]
    first_stack = jnp.concatenate(
        [by_shard(weight_grad(low_one, grad)) for grad in (grad_queries, grad_keys)], axis=1
    )
    second_stack = jnp.concatenate(
        [by_shard(weight_grad(low_one, grad_values)), by_shard(merge_grad), small_grad], axis=1
    )
    first_sum = reduce_stack(first_stack, bits).astype(f32)
    second_sum = reduce_stack(second_stack, bits[:1] + bits[:0:-1]).astype(f32)
    small_sum = second_sum[2 * part :].reshape(-1)
    return (
        output,
        input_gradient,
        small_sum[:part],
        first_sum[:part],
        first_sum[part:],
        second_sum[:part],
        second_sum[part : 2 * part],
        small_sum[router_at : router_at + BUCKETS * local_heads].reshape(BUCKETS, local_heads),
        small_sum[part : 2 * part],
        small_sum[2 * part : router_at].reshape(part, experts),
        jnp.stack([grad.astype(f32) for grad in up_grads]),
        jnp.stack([grad.astype(f32) for grad in down_grads]),
    )


def solution(mesh):
    in_specs = (
        P(("expert", "shard"), None),
        P("shard"),
        P("shard", None),
        P("shard", None),
        P("shard", None),
        P("shard", None),
        P(None, "shard"),
        P("shard"),
        P("shard", None),
        P("expert", None, None),
        P("expert", None, None),
        P(("expert", "shard"), None),
        P(("expert", "shard"), None),
    )
    out_specs = (
        P(("expert", "shard"), None),
        P(("expert", "shard"), None),
        P("shard"),
        P("shard", None),
        P("shard", None),
        P("shard", None),
        P("shard", None),
        P(None, "shard"),
        P("shard"),
        P("shard", None),
        P("expert", None, "shard"),
        P("expert", "shard", None),
    )
    return jax.shard_map(local, mesh=mesh, in_specs=in_specs, out_specs=out_specs, check_vma=False)
```

time: 982 us -> 632 us (0.64)
  waiting for transfers between devices: 456 us -> 160 us
  matrix products: 225 us -> 12.5 us
  Pallas kernels: 58.3 us -> 232 us
  starting transfers between devices: 20 us -> 47.1 us
  local copies, waits for them, and re-layouts: 90.1 us -> 65 us
  other arithmetic: 42.1 us -> 19.6 us
    reduce_scatter x6 -> x4, waiting for transfers between devices: 398 us -> 0.01 us  [the longest x2 0.01 us: local(): lax.psum_scatter(down_grad, 'shard', scatter_dimension=0, tiled=True)]
    dot_general x27 -> x7, matrix products: 225 us -> 12.3 us  [the longest x5 8.22 us: weight_grad(): jnp.einsum('ti,to->io', left, right, preferred_element_type=f32)]
    pallas_call x0 -> x14, Pallas kernels: none -> 174 us  [the longest x2 73.4 us: expert_second(): pl.pallas_call(second_kernel, grid=(hidden // tile,), in_specs=[fixed, fi...]
    all_to_all x4 -> x6, waiting for transfers between devices: 0.01 us -> 74.9 us  [share_rows(): lax.all_to_all(rows.reshape(owners, count // owners, width), 'expert', 0,...]
    all_to_all x0 -> x4, blocking collectives: none -> 72.1 us  [the longest x2 57.8 us: share_rows(): lax.all_to_all(rows.reshape(owners, count // owners, width), 'expert', 0,...]
    ppermute x0 -> x21, waiting for transfers between devices: none -> 45.8 us  [the longest x12 28.2 us: exchange(): return lax.ppermute(rows, 'expert', [(i, i ^ bit) for i in range(count)])]
    eq x1 -> x0, local copies, waits for them, and re-layouts: 30.4 us -> none  [local(): pair_hot = (slot_ids[:, None] == slot_index[None, :]).astype(jnp.bfloat16)]
    all_gather x2 -> x0, blocking collectives: 25.9 us -> none  [the longest x1 13.1 us: local(): lax.all_gather(router_weight, 'shard', axis=0, tiled=True)]
  transfers between devices with their start and end apart: 16 -> 33, of which waited for: 9 -> 18; matrix products, arithmetic and copies ran while one was open for 32% -> 9% of each run, Pallas kernels for 2% -> 34%
where the time goes in v1:
time: 632 us; the launch traced here: 624 us
  Pallas kernels  232 us (37%)
  waiting for transfers between devices  160 us (25%)
  blocking collectives  72.1 us (11%)
  local copies, waits for them, and re-layouts  65 us (10%)
  starting transfers between devices  47.1 us (7%)
  other arithmetic  19.6 us (3%)
  between operations  15.2 us (2%)
  matrix products  12.5 us (2%)
    all_to_all x6, waiting for transfers between devices, share_rows(): lax.all_to_all(rows.reshape(owners, count // owners, width), 'expert', 0,...  74.9 us
    pallas_call x2, Pallas kernels, expert_second(): pl.pallas_call(second_kernel, grid=(hidden // tile,), in_specs=[fixed, fi...  73.4 us
    all_to_all x2, blocking collectives, share_rows(): lax.all_to_all(rows.reshape(owners, count // owners, width), 'expert', 0,...  57.8 us
    unnamed x131, local copies, waits for them, and re-layouts  39.9 us
    pallas_call x2, Pallas kernels, expert_first(): pl.pallas_call(partial(first_kernel, chunk=chunk), grid=(hidden // tile,)...  39.5 us
    all_gather x1, waiting for transfers between devices, local(): gathered = lax.all_gather(lined, 'expert', axis=0, tiled=False)  38 us
    pallas_call x1, Pallas kernels, attend_back(): pl.pallas_call(partial(attend_back_kernel, block=block, size=size, scale=...  35.8 us
    ppermute x12, waiting for transfers between devices, exchange(): return lax.ppermute(rows, 'expert', [(i, i ^ bit) for i in range(count)])  28.2 us
  transfers between devices with their start and end apart: 33, of which 18 were waited for; matrix products, arithmetic and copies ran while one was open for 9% of the time, Pallas kernels for 34%

profile of v1, /device:TPU:0, one launch (start us, length us, event | category | flops | bytes accessed | tf_op | source)
XLA Modules:
  0.0 623.5 jit_solution(13990688163748720021)
XLA Ops:
  20.9 4.4 collective-permute-done.1
  29.2 5.5 dispatch.5
  34.7 4.3 all-to-all-start.1
  39.1 38.0 %all-gather.3.cloned.1.call-done = bf16[8,4,80,768]{3,2,0,1:T(8,128)(2,1)} async-done(((bf16[1,4,80,768]{3,2,0,1:T(8,128)(2,1)}), bf16[8,4,80,768]{3,2,0,1:T(8,128)(2,1)}) %all-gather.3.cloned.1.call-update) | async-done | bytes 3932176 | tf_op jit(solution)/shard_map/all_gather | solution.py:588
  82.0 4.7 project.1
  89.1 22.2 %attend.1 = (bf16[1024,768]{1,0:T(8,128)(2,1)S(1)}, f32[6,2,1024]{2,1,0:T(2,128)S(1)}) custom-call(bf16[1024,768]{1,0:T(8,128)(2,1)S(1)} %get-tuple-element.50.query_ref, bf16[1024,768]{1,0:T(8,128)(2,1)S(1)} %get-tuple-element.51.key_ref, bf16[1024,768]{1,0:T(8,128)(2,1)} %copy-done.20, f32[6,2,256]{2,1,0:T(2,128)S(1)} %copy.59.near_ref), custom_call_target="tpu_custom_call" | custom-call | tf_op jit(solution)/shard_map/attend/pallas_call | solution.py:319
  123.3 5.7 dispatch.4
  129.8 7.3 %all_to_all.50 = f32[8,1,160]{2,1,0:T(1,128)S(1)} all-to-all(f32[8,1,160]{2,1,0:T(1,128)S(1)} %reshape.248), channel_id=1, replica_groups=mesh['expert'=8,'shard'=4] {'expert'}, dimensions={0} | all-to-all | bytes 10240 | tf_op jit(solution)/shard_map/all_to_all | solution.py:629
  142.0 23.9 %all-to-all-done = bf16[8,160,768]{2,1,0:T(8,128)(2,1)S(1)} async-done(((bf16[8,160,768]{2,1,0:T(8,128)(2,1)}), bf16[8,160,768]{2,1,0:T(8,128)(2,1)S(1)}, u32[]{:S(2)}, u32[]{:S(2)}) %all-to-all-start) | async-done | bytes 1966112 | tf_op jit(solution)/shard_map/all_to_all | solution.py:543
  167.1 19.7 %expert_first.2 = (bf16[1280,3072]{1,0:T(8,128)(2,1)}, bf16[1280,3072]{1,0:T(8,128)(2,1)}, bf16[3072,768]{1,0:T(8,128)(2,1)}, bf16[1280,768]{1,0:T(8,128)(2,1)}) custom-call(bf16[1280,768]{1,0:T(8,128)(2,1)} %bitcast.114, bf16[1280,768]{1,0:T(8,128)(2,1)} %bitcast.23.cot_ref, f32[1,1280]{1,0:T(1,128)} %reshape.220.gate_ref, bf16[2,768,3072]{2,1,0:T(8,128)(2,1)} %up_ref.7), custom_call_target="tpu_custom_call" | custom-call | tf_op jit(solution)/shard_map/expert_first/pallas_call | solution.py:123
  186.9 5.6 dispatch.7
  196.1 5.7 dispatch.6
  202.6 18.6 %all-to-all-done.5 = bf16[8,160,768]{2,1,0:T(8,128)(2,1)S(1)} async-done(((bf16[8,160,768]{2,1,0:T(8,128)(2,1)}), bf16[8,160,768]{2,1,0:T(8,128)(2,1)S(1)}, u32[]{:S(2)}, u32[]{:S(2)}) %all-to-all-start.5) | async-done | bytes 1966112 | tf_op jit(solution)/shard_map/all_to_all | solution.py:543
  221.2 7.1 %all_to_all.51 = f32[8,1,160]{2,1,0:T(1,128)S(1)} all-to-all(f32[8,1,160]{2,1,0:T(1,128)S(1)} %reshape.249), channel_id=1, replica_groups=mesh['expert'=8,'shard'=4] {'expert'}, dimensions={0} | all-to-all | bytes 10240 | tf_op jit(solution)/shard_map/all_to_all | solution.py:629
  232.7 24.4 %all-to-all-done.4 = bf16[8,160,768]{2,1,0:T(8,128)(2,1)S(1)} async-done(((bf16[8,160,768]{2,1,0:T(8,128)(2,1)}), bf16[8,160,768]{2,1,0:T(8,128)(2,1)S(1)}, u32[]{:S(2)}, u32[]{:S(2)}) %all-to-all-start.4) | async-done | bytes 1966112 | tf_op jit(solution)/shard_map/all_to_all | solution.py:543
  258.3 19.8 %expert_first.3 = (bf16[1280,3072]{1,0:T(8,128)(2,1)}, bf16[1280,3072]{1,0:T(8,128)(2,1)}, bf16[3072,768]{1,0:T(8,128)(2,1)}, bf16[1280,768]{1,0:T(8,128)(2,1)}) custom-call(bf16[1280,768]{1,0:T(8,128)(2,1)} %bitcast.116, bf16[1280,768]{1,0:T(8,128)(2,1)} %bitcast.118, f32[1,1280]{1,0:T(1,128)} %reshape.228.gate_ref, bf16[2,768,3072]{2,1,0:T(8,128)(2,1)} %up_ref.7), custom_call_target="tpu_custom_call" | custom-call | tf_op jit(solution)/shard_map/expert_first/pallas_call | solution.py:123
  278.4 36.7 %expert_second.2 = (bf16[1280,768]{1,0:T(8,128)(2,1)}, bf16[1280,768]{1,0:T(8,128)(2,1)}, bf16[768,3072]{1,0:T(8,128)(2,1)}) custom-call(bf16[1280,768]{1,0:T(8,128)(2,1)} %bitcast.115, bf16[1280,768]{1,0:T(8,128)(2,1)} %get-tuple-element.59.grad_ref, bf16[1280,3072]{1,0:T(8,128)(2,1)} %get-tuple-element.60.act_ref, ...), custom_call_target="tpu_custom_call" | custom-call | tf_op jit(solution)/shard_map/expert_second/pallas_call | solution.py:165
  316.6 28.3 %all_to_all.52 = bf16[8,160,768]{2,1,0:T(8,128)(2,1)} all-to-all(bf16[8,160,768]{2,1,0:T(8,128)(2,1)S(1)} %bitcast.129), channel_id=1, replica_groups=mesh['expert'=8,'shard'=4] {'expert'}, dimensions={0} | all-to-all | bytes 3932160 | tf_op jit(solution)/shard_map/all_to_all | solution.py:543
  348.5 36.7 %expert_second.3 = (bf16[1280,768]{1,0:T(8,128)(2,1)}, bf16[1280,768]{1,0:T(8,128)(2,1)}, bf16[768,3072]{1,0:T(8,128)(2,1)}) custom-call(bf16[1280,768]{1,0:T(8,128)(2,1)} %bitcast.117, bf16[1280,768]{1,0:T(8,128)(2,1)} %get-tuple-element.65.grad_ref, bf16[1280,3072]{1,0:T(8,128)(2,1)} %get-tuple-element.66.act_ref, ...), custom_call_target="tpu_custom_call" | custom-call | tf_op jit(solution)/shard_map/expert_second/pallas_call | solution.py:165
  385.3 29.5 %all_to_all.53 = bf16[8,160,768]{2,1,0:T(8,128)(2,1)} all-to-all(bf16[8,160,768]{2,1,0:T(8,128)(2,1)} %bitcast.130), channel_id=1, replica_groups=mesh['expert'=8,'shard'=4] {'expert'}, dimensions={0} | all-to-all | bytes 3932160 | tf_op jit(solution)/shard_map/all_to_all | solution.py:543
  414.8 4.3 all-to-all-start.9
  423.8 11.8 %combine_out.1 = (bf16[1024,768]{1,0:T(8,128)(2,1)}, bf16[1024,128]{1,0:T(8,128)(2,1)S(1)}) custom-call(s32[2,1024]{1,0:T(2,128)S(1)} %copy-done.33, s32[2,1024]{1,0:T(2,128)S(1)} %bitcast.112, f32[2,1024]{1,0:T(2,128)S(1)} %copy-done.38, f32[1024,768]{1,0:T(8,128)} %copy-done.7, bf16[1024,768]{1,0:T(8,128)(2,1)S(1)} %copy-done.2, ...), custom_call_target="tpu_custom_call" | custom-call | tf_op jit(solution)/shard_map/combine_out/pallas_call | solution.py:209
  436.3 8.1 %all-to-all-done.9 = bf16[8,160,768]{2,1,0:T(8,128)(2,1)} async-done(((bf16[8,160,768]{2,1,0:T(8,128)(2,1)}), bf16[8,160,768]{2,1,0:T(8,128)(2,1)}, u32[]{:S(2)}, u32[]{:S(2)}) %all-to-all-start.9) | async-done | bytes 1966112 | tf_op jit(solution)/shard_map/all_to_all | solution.py:543
  448.5 9.7 %combine_back.1 = (f32[1024,768]{1,0:T(8,128)}, bf16[1024,768]{1,0:T(8,128)(2,1)S(1)}, f32[1,768]{1,0:T(1,128)S(1)}) custom-call(s32[2,1024]{1,0:T(2,128)S(1)} %copy-done.33, bf16[1024,128]{1,0:T(8,128)(2,1)S(1)} %copy-done.30, bf16[768,128]{1,0:T(8,128)(2,1)S(1)} %copy-done.32, f32[1,768]{1,0:T(1,128)S(1)} %copy-done.41, f32[1024,768]{1,0:T(8,128)} %copy-done.7, ...), custom_call_target="tpu_custom_call" | custom-call | tf_op jit(solution)/shard_map/combine_back/pallas_call | solution.py:246
  465.0 35.8 %attend_back.1 = (bf16[1024,768]{1,0:T(8,128)(2,1)}, bf16[1024,768]{1,0:T(8,128)(2,1)}, bf16[1024,768]{1,0:T(8,128)(2,1)}, f32[6,4,256]{2,1,0:T(4,128)}) custom-call(bf16[1024,768]{1,0:T(8,128)(2,1)} %copy-done.18, bf16[1024,768]{1,0:T(8,128)(2,1)} %copy-done.19, bf16[1024,768]{1,0:T(8,128)(2,1)} %copy-done.20, ...), custom_call_target="tpu_custom_call" | custom-call | tf_op jit(solution)/shard_map/attend_back/pallas_call | solution.py:398
  510.6 7.1 %finish.1 = (f32[1024,768]{1,0:T(8,128)}, f32[1,768]{1,0:T(1,128)S(1)}) custom-call(bf16[1024,768]{1,0:T(8,128)(2,1)S(1)} %copy-done.26, bf16[1024,768]{1,0:T(8,128)(2,1)S(1)} %copy-done.24, bf16[1024,768]{1,0:T(8,128)(2,1)S(1)} %copy-done.22, bf16[768,768]{1,0:T(8,128)(2,1)S(1)} %bitcast.106, bf16[768,768]{1,0:T(8,128)(2,1)S(1)} %bitcast.104, ...), custom_call_target="tpu_custom_call" | custom-call | tf_op jit(solution)/shard_map/finish/pallas_call | solution.py:482
  537.6 11.4 %collective-permute-done.13 = bf16[4,96,768]{2,1,0:T(8,128)(2,1)} collective-permute-done((bf16[4,96,768]{2,1,0:T(8,128)(2,1)S(1)}, bf16[4,96,768]{2,1,0:T(8,128)(2,1)}, u32[]{:S(2)}, u32[]{:S(2)}) %collective-permute-start.13) | collective-permute-done | bytes 589856 | tf_op jit(solution)/shard_map/ppermute | solution.py:495
  550.9 4.5 collective-permute-done.4
  556.7 4.2 collective-permute-done.14
  595.1 9.4 %slice.83 = f32[16384,3]{1,0:T(8,128)} reshape(f32[64,768]{1,0:T(8,128)S(1)} %slice.96) | data formatting | bytes 393216 | tf_op jit(solution)/shard_map/slice | solution.py:705
  608.2 4.1 maximum_convert_fusion.1
  612.3 4.2 maximum_convert_fusion
  (284 shorter events, 145.6 us)
Async XLA Ops:
  7.2 69.9 %all-gather.3.cloned.1.call-start = ((), (), s32[]{:S(2)}) async-start(), calls=%async_computation.14 | async-start | bytes 4423680 | tf_op jit(solution)/shard_map/all_gather | solution.py:588
  11.5 9.4 %collective-permute-start = (bf16[80,768]{1,0:T(8,128)(2,1)S(1)}, bf16[80,768]{1,0:T(8,128)(2,1)S(1)}, u32[]{:S(2)}, u32[]{:S(2)}) collective-permute-start(bf16[80,768]{1,0:T(8,128)(2,1)S(1)} %pad_maximum_fusion.1), channel_id=1, source_target_pairs={{0,1},{1,2},{2,3},{3,0},{4,5},{5,6},{6,7},{7,4},{8,9},{9,10},{10,1... | collective-permute-start | bytes 368648 | tf_op jit(solution)/shard_map/ppermute | solution.py:500
  14.6 10.7 %collective-permute-start.1 = (bf16[80,768]{1,0:T(8,128)(2,1)S(1)}, bf16[80,768]{1,0:T(8,128)(2,1)S(1)}, u32[]{:S(2)}, u32[]{:S(2)}) collective-permute-start(bf16[80,768]{1,0:T(8,128)(2,1)S(1)} %pad_maximum_fusion.1), channel_id=1, source_target_pairs={{0,2},{1,3},{2,0},{3,1},{4,6},{5,7},{6,4},{7,5},{8,10},{9,11},{10,... | collective-permute-start | bytes 368648 | tf_op jit(solution)/shard_map/ppermute | solution.py:500
  17.2 8.1 %collective-permute-start.2 = (bf16[80,768]{1,0:T(8,128)(2,1)S(1)}, bf16[80,768]{1,0:T(8,128)(2,1)S(1)}, u32[]{:S(2)}, u32[]{:S(2)}) collective-permute-start(bf16[80,768]{1,0:T(8,128)(2,1)S(1)} %pad_maximum_fusion.1), channel_id=1, source_target_pairs={{0,3},{1,0},{2,1},{3,2},{4,7},{5,4},{6,5},{7,6},{8,11},{9,8},{10,9... | collective-permute-start | bytes 368648 | tf_op jit(solution)/shard_map/ppermute | solution.py:500
  26.2 88.1 %all-gather.5.cloned.1.call-start = ((), (), s32[]{:S(2)}) async-start(), calls=%async_computation.15 | async-start | bytes 1474560 | tf_op jit(solution)/shard_map/all_gather | solution.py:589
  34.7 95.1 %all-to-all-start.1 = ((bf16[8,160,768]{2,1,0:T(8,128)(2,1)}), bf16[8,160,768]{2,1,0:T(8,128)(2,1)}, u32[]{:S(2)}, u32[]{:S(2)}) async-start(bf16[8,160,768]{2,1,0:T(8,128)(2,1)} %bitcast.119), calls=%async_computation.1 | async-start | bytes 3932160 | tf_op jit(solution)/shard_map/all_to_all | solution.py:543
  137.1 28.8 %all-to-all-start = ((bf16[8,160,768]{2,1,0:T(8,128)(2,1)}), bf16[8,160,768]{2,1,0:T(8,128)(2,1)S(1)}, u32[]{:S(2)}, u32[]{:S(2)}) async-start(bf16[8,160,768]{2,1,0:T(8,128)(2,1)} %bitcast.128), calls=%async_computation | async-start | bytes 3932160 | tf_op jit(solution)/shard_map/all_to_all | solution.py:543
  140.7 467.5 %reduce-scatter.9.cloned.1.call-start = ((), (), s32[]{:S(2)}) async-start(), calls=%async_computation.18 | async-start | bytes 5898240 | tf_op jit(solution)/shard_map/reduce_scatter | solution.py:634
  192.5 28.7 %all-to-all-start.5 = ((bf16[8,160,768]{2,1,0:T(8,128)(2,1)}), bf16[8,160,768]{2,1,0:T(8,128)(2,1)S(1)}, u32[]{:S(2)}, u32[]{:S(2)}) async-start(bf16[8,160,768]{2,1,0:T(8,128)(2,1)} %bitcast.120), calls=%async_computation.5 | async-start | bytes 3932160 | tf_op jit(solution)/shard_map/all_to_all | solution.py:543
  228.3 28.8 %all-to-all-start.4 = ((bf16[8,160,768]{2,1,0:T(8,128)(2,1)}), bf16[8,160,768]{2,1,0:T(8,128)(2,1)S(1)}, u32[]{:S(2)}, u32[]{:S(2)}) async-start(bf16[8,160,768]{2,1,0:T(8,128)(2,1)} %bitcast.127), calls=%async_computation.4 | async-start | bytes 3932160 | tf_op jit(solution)/shard_map/all_to_all | solution.py:543
  231.9 376.3 %reduce-scatter.11.cloned.1.call-start = ((), (), s32[]{:S(2)}) async-start(), calls=%async_computation.19 | async-start | bytes 5898240 | tf_op jit(solution)/shard_map/reduce_scatter | solution.py:634
  278.1 334.2 %reduce-scatter.5.cloned.1.call-start = ((), (), s32[]{:S(2)}) async-start(), calls=%async_computation.16 | async-start | bytes 5898240 | tf_op jit(solution)/shard_map/reduce_scatter | solution.py:638
  344.9 40.3 %all-to-all-start.3 = ((bf16[8,160,768]{2,1,0:T(8,128)(2,1)}), bf16[8,160,768]{2,1,0:T(8,128)(2,1)S(1)}, u32[]{:S(2)}, u32[]{:S(2)}) async-start(bf16[8,160,768]{2,1,0:T(8,128)(2,1)} %bitcast.126), calls=%async_computation.3 | async-start | bytes 3932160 | tf_op jit(solution)/shard_map/all_to_all | solution.py:543
  414.8 29.6 %all-to-all-start.9 = ((bf16[8,160,768]{2,1,0:T(8,128)(2,1)}), bf16[8,160,768]{2,1,0:T(8,128)(2,1)}, u32[]{:S(2)}, u32[]{:S(2)}) async-start(bf16[8,160,768]{2,1,0:T(8,128)(2,1)} %bitcast.125), calls=%async_computation.9 | async-start | bytes 3932160 | tf_op jit(solution)/shard_map/all_to_all | solution.py:543
  419.1 193.2 %reduce-scatter.7.cloned.1.call-start = ((), (), s32[]{:S(2)}) async-start(), calls=%async_computation.17 | async-start | bytes 5898240 | tf_op jit(solution)/shard_map/reduce_scatter | solution.py:638
  525.4 5.3 collective-permute-start.12
  530.7 3.5 collective-permute-start.3
  533.0 15.9 %collective-permute-start.13 = (bf16[4,96,768]{2,1,0:T(8,128)(2,1)S(1)}, bf16[4,96,768]{2,1,0:T(8,128)(2,1)}, u32[]{:S(2)}, u32[]{:S(2)}) collective-permute-start(bf16[4,96,768]{2,1,0:T(8,128)(2,1)S(1)} %constant_dynamic-slice_fusion.1), channel_id=1, source_target_pairs={{0,8},{4,12},{8,0},{12,4},{16,24},{20,28},{24,16},{28,20},{1,9},{5... | collective-permute-start | bytes 1769480 | tf_op jit(solution)/shard_map/ppermute | solution.py:495
  537.0 18.4 %collective-permute-start.4 = (bf16[4,112,768]{2,1,0:T(8,128)(2,1)S(1)}, bf16[4,112,768]{2,1,0:T(8,128)(2,1)S(1)}, u32[]{:S(2)}, u32[]{:S(2)}) collective-permute-start(bf16[4,112,768]{2,1,0:T(8,128)(2,1)S(1)} %constant_dynamic-slice_fusion.3), channel_id=1, source_target_pairs={{0,16},{4,20},{8,24},{12,28},{16,0},{20,4},{24,8},{28,12},{1,17},{... | collective-permute-start | bytes 2064392 | tf_op jit(solution)/shard_map/ppermute | solution.py:495
  550.4 10.5 %collective-permute-start.14 = (bf16[4,48,768]{2,1,0:T(8,128)(2,1)S(1)}, bf16[4,48,768]{2,1,0:T(8,128)(2,1)S(1)}, u32[]{:S(2)}, u32[]{:S(2)}) collective-permute-start(bf16[4,48,768]{2,1,0:T(8,128)(2,1)S(1)} %constant_dynamic-slice_fusion), channel_id=1, source_target_pairs={{0,16},{4,20},{8,24},{12,28},{16,0},{20,4},{24,8},{28,12},{1,17},{... | collective-permute-start | bytes 884744 | tf_op jit(solution)/shard_map/ppermute | solution.py:495
  555.6 16.4 %collective-permute-start.5 = (bf16[4,56,768]{2,1,0:T(8,128)(2,1)S(1)}, bf16[4,56,768]{2,1,0:T(8,128)(2,1)S(1)}, u32[]{:S(2)}, u32[]{:S(2)}) collective-permute-start(bf16[4,56,768]{2,1,0:T(8,128)(2,1)S(1)} %constant_dynamic-slice_fusion.2), channel_id=1, source_target_pairs={{0,8},{4,12},{8,0},{12,4},{16,24},{20,28},{24,16},{28,20},{1,9},{5... | collective-permute-start | bytes 1032200 | tf_op jit(solution)/shard_map/ppermute | solution.py:495
  561.0 7.1 %collective-permute-start.15 = (bf16[48,768]{1,0:T(8,128)(2,1)S(1)}, bf16[48,768]{1,0:T(8,128)(2,1)S(1)}, u32[]{:S(2)}, u32[]{:S(2)}) collective-permute-start(bf16[48,768]{1,0:T(8,128)(2,1)S(1)} %get-tuple-element.124), channel_id=1, source_target_pairs={{0,1},{1,2},{2,3},{3,0},{4,5},{5,6},{6,7},{7,4},{8,9},{9,10},{10,1... | collective-permute-start | bytes 221192 | tf_op jit(solution)/shard_map/ppermute | solution.py:500
  562.5 5.6 collective-permute-start.17
  564.9 6.5 %collective-permute-start.16 = (bf16[48,768]{1,0:T(8,128)(2,1)S(1)}, bf16[48,768]{1,0:T(8,128)(2,1)S(1)}, u32[]{:S(2)}, u32[]{:S(2)}) collective-permute-start(bf16[48,768]{1,0:T(8,128)(2,1)S(1)} %get-tuple-element.126), channel_id=1, source_target_pairs={{0,2},{1,3},{2,0},{3,1},{4,6},{5,7},{6,4},{7,5},{8,10},{9,11},{10,... | collective-permute-start | bytes 221192 | tf_op jit(solution)/shard_map/ppermute | solution.py:500
  571.4 4.7 collective-permute-start.18
  572.1 7.3 %collective-permute-start.6 = (bf16[56,768]{1,0:T(8,128)(2,1)S(1)}, bf16[56,768]{1,0:T(8,128)(2,1)S(1)}, u32[]{:S(2)}, u32[]{:S(2)}) collective-permute-start(bf16[56,768]{1,0:T(8,128)(2,1)S(1)} %get-tuple-element.121), channel_id=1, source_target_pairs={{0,1},{1,2},{2,3},{3,0},{4,5},{5,6},{6,7},{7,4},{8,9},{9,10},{10,1... | collective-permute-start | bytes 258056 | tf_op jit(solution)/shard_map/ppermute | solution.py:500
  572.2 7.2 %collective-permute-start.8 = (bf16[56,768]{1,0:T(8,128)(2,1)S(1)}, bf16[56,768]{1,0:T(8,128)(2,1)S(1)}, u32[]{:S(2)}, u32[]{:S(2)}) collective-permute-start(bf16[56,768]{1,0:T(8,128)(2,1)S(1)} %get-tuple-element.122), channel_id=1, source_target_pairs={{0,3},{1,0},{2,1},{3,2},{4,7},{5,4},{6,5},{7,6},{8,11},{9,8},{10,9... | collective-permute-start | bytes 258056 | tf_op jit(solution)/shard_map/ppermute | solution.py:500
  576.1 6.3 %collective-permute-start.7 = (bf16[56,768]{1,0:T(8,128)(2,1)S(1)}, bf16[56,768]{1,0:T(8,128)(2,1)S(1)}, u32[]{:S(2)}, u32[]{:S(2)}) collective-permute-start(bf16[56,768]{1,0:T(8,128)(2,1)S(1)} %get-tuple-element.123), channel_id=1, source_target_pairs={{0,2},{1,3},{2,0},{3,1},{4,6},{5,7},{6,4},{7,5},{8,10},{9,11},{10,... | collective-permute-start | bytes 258056 | tf_op jit(solution)/shard_map/ppermute | solution.py:500
  576.2 7.5 %collective-permute-start.19 = (bf16[96,768]{1,0:T(8,128)(2,1)S(1)}, bf16[96,768]{1,0:T(8,128)(2,1)S(1)}, u32[]{:S(2)}, u32[]{:S(2)}) collective-permute-start(bf16[96,768]{1,0:T(8,128)(2,1)S(1)} %maximum_select_fusion.5), channel_id=1, source_target_pairs={{0,8},{4,12},{8,0},{12,4},{16,24},{20,28},{24,16},{28,20},{1,9},{5... | collective-permute-start | bytes 442376 | tf_op jit(solution)/shard_map/ppermute | solution.py:495
  582.5 4.6 collective-permute-start.9
  583.7 9.0 %collective-permute-start.20 = (bf16[192,768]{1,0:T(8,128)(2,1)S(1)}, bf16[192,768]{1,0:T(8,128)(2,1)S(1)}, u32[]{:S(2)}, u32[]{:S(2)}) collective-permute-start(bf16[192,768]{1,0:T(8,128)(2,1)S(1)} %maximum_select_fusion.3), channel_id=1, source_target_pairs={{0,4},{4,0},{8,12},{12,8},{16,20},{20,16},{24,28},{28,24},{1,5},{5... | collective-permute-start | bytes 884744 | tf_op jit(solution)/shard_map/ppermute | solution.py:495
  587.1 5.5 collective-permute-start.10
  (63 other events, 397.2 us)
Sparse Core Ops, SparseCore 0:
  26.3 50.7 all-gather.2
  78.7 30.2 all-gather.4
  187.0 84.3 reduce-scatter.8
  278.3 84.3 reduce-scatter.10
  365.4 85.7 reduce-scatter.4
  453.4 85.7 reduce-scatter.6

commit v2 on v1

--- a/solution.py
+++ b/solution.py
@@ -7,6 +7,7 @@
 from jax.experimental import pallas as pl
 from jax.experimental.pallas import tpu as pltpu
 from jax.sharding import PartitionSpec as P
+
 
 BUCKETS = 32
 MAX_DIST = 128
@@ -29,8 +30,10 @@
 def dot_nt(a, b):
     return lax.dot_general(a, b, (((1,), (1,)), ((), ())), preferred_element_type=jnp.float32)
 
+
 def dot_nn(a, b):
     return lax.dot_general(a, b, (((1,), (0,)), ((), ())), preferred_element_type=jnp.float32)
+
 
 def dot_tn(a, b):
     return lax.dot_general(a, b, (((0,), (0,)), ((), ())), preferred_element_type=jnp.float32)
@@ -49,6 +52,7 @@
         position = jnp.sum(jnp.where(hits[c], counts, 0.0), axis=0, keepdims=True)
         slots_ref[c:c + 1, :] = base_ref[c:c + 1, :] + position.astype(jnp.int32)
 
+
 def find_slots(routes, base, experts):
     return pl.pallas_call(
         partial(slot_kernel, experts=experts),
@@ -57,36 +61,53 @@
     )(routes, base)
 
 
-def dispatch_kernel(slots_ref, rows_ref, *refs, start, gated):
-    out_ref = refs[-2] if gated else refs[-1]
+def dispatch_kernel(slots_ref, rows_ref, *refs, start):
+    out_ref = refs[-1]
     block, tokens = out_ref.shape[0], rows_ref.shape[0]
     slot = lax.broadcasted_iota(jnp.int32, (block, tokens), 0) + (pl.program_id(0) * block + start)
+    hot = jnp.where((slot == slots_ref[0:1, :]) | (slot == slots_ref[1:2, :]), 1.0, 0.0)
+    out_ref[...] = dot_nn(hot.astype(jnp.bfloat16), rows_ref[...]).astype(out_ref.dtype)
+
+
+def dispatch(slots, rows, start, count, after=(), block=256):
+    _, width = rows.shape
+    whole = lambda shape: pl.BlockSpec(shape, lambda i: (0, 0))
+    return pl.pallas_call(
+        partial(dispatch_kernel, start=start),
+        grid=(count // block,),
+        in_specs=[whole(slots.shape), whole(rows.shape)] + [pl.BlockSpec(memory_space=pl.ANY)] * len(after),
+        out_specs=pl.BlockSpec((block, width), lambda i: (i, 0)),
+        out_shape=jax.ShapeDtypeStruct((count, width), rows.dtype),
+        name="dispatch",
+    )(slots, rows, *after)
+
+
+def dispatch_all_kernel(slots_ref, routes_ref, rows_ref, out_ref, other_ref, *, owners, capacity):
+    block, tokens = out_ref.shape[1], rows_ref.shape[0]
+    row = lax.broadcasted_iota(jnp.int32, (block, tokens), 0)
+    slot = row + pl.program_id(0) * capacity
+    for index in range(1, block // capacity):
+        slot = slot + jnp.where(row >= index * capacity, (owners - 1) * capacity, 0)
     hits = [slot == slots_ref[c:c + 1, :] for c in range(2)]
     hot = jnp.where(hits[0] | hits[1], 1.0, 0.0).astype(jnp.bfloat16)
-    out_ref[...] = dot_nn(hot, rows_ref[...]).astype(out_ref.dtype)
-    if gated:
-        gates_ref, gate_ref = refs[0], refs[-1]
-        gate = jnp.where(hits[0], gates_ref[0:1, :], jnp.where(hits[1], gates_ref[1:2, :], 0.0))
-        column = jnp.sum(gate, axis=1, keepdims=True)
-        gate_ref[...] = jnp.broadcast_to(column, (block, 128)).T[0:1, :]
-
-def dispatch(slots, rows, start, count, gates=None, block=256):
-    tokens, width = rows.shape
-    gated = gates is not None
+    out_ref[0] = dot_nn(hot, rows_ref[...]).astype(out_ref.dtype)
+    other = jnp.where(hits[0], routes_ref[1:2, :], jnp.where(hits[1], routes_ref[0:1, :], 0.0))
+    column = jnp.sum(other, axis=1, keepdims=True)
+    other_ref[0] = jnp.broadcast_to(column, (block, 128)).T[0:1, :]
+
+
+def dispatch_all(slots, routes, rows, owners, capacity, local_count):
+    _, width = rows.shape
+    block = local_count * capacity
     whole = lambda shape: pl.BlockSpec(shape, lambda i: (0, 0))
-    out_shape = jax.ShapeDtypeStruct((count, width), rows.dtype)
-    out_spec = pl.BlockSpec((block, width), lambda i: (i, 0))
-    if gated:
-        out_shape = [out_shape, jax.ShapeDtypeStruct((1, count), jnp.float32)]
-        out_spec = [out_spec, pl.BlockSpec((1, block), lambda i: (0, i))]
-    return pl.pallas_call(
-        partial(dispatch_kernel, start=start, gated=gated),
-        grid=(count // block,),
-        in_specs=[whole(slots.shape), whole(rows.shape)] + ([whole(gates.shape)] if gated else []),
-        out_specs=out_spec,
-        out_shape=out_shape,
-        name="dispatch",
-    )(slots, rows, *([gates] if gated else []))
+    return pl.pallas_call(
+        partial(dispatch_all_kernel, owners=owners, capacity=capacity),
+        grid=(owners,),
+        in_specs=[whole(slots.shape), whole(routes.shape), whole(rows.shape)],
+        out_specs=[pl.BlockSpec((1, block, width), lambda i: (i, 0, 0)), pl.BlockSpec((1, 1, block), lambda i: (i, 0, 0))],
+        out_shape=[jax.ShapeDtypeStruct((owners, block, width), rows.dtype), jax.ShapeDtypeStruct((owners, 1, block), jnp.float32)],
+        name="dispatch_all",
+    )(slots, routes, rows)
 
 
 def gelu_pair(v):
@@ -99,13 +120,23 @@
     return value, slope
 
 
-def first_kernel(rows_ref, cot_ref, gate_ref, up_ref, act_ref, slope_ref, down_grad_ref, grad_ref, *, chunk):
+def first_kernel(owner_ref, rows_ref, cot_ref, other_ref, router_ref, up_ref, *refs, chunk, index, local_count):
+    act_ref, slope_ref, down_grad_ref, grad_ref = refs[-4:]
     rows, width = rows_ref.shape
     @pl.when(pl.program_id(0) == 0)
     def _():
-        column = jnp.broadcast_to(gate_ref[...], (128, rows)).T
+        logits = dot_nt(router_ref[...], rows_ref[...])
+        expert = lax.broadcasted_iota(jnp.int32, logits.shape, 0)
+        mine = owner_ref[0] * local_count + index
+        own = jnp.sum(jnp.where(expert == mine, logits, 0.0), axis=0, keepdims=True)
+        other = other_ref[...].astype(jnp.int32)
+        other = jnp.sum(jnp.where(expert == other, logits, 0.0), axis=0, keepdims=True)
+        top = jnp.maximum(own, other)
+        own = jnp.exp(own - top)
+        gate = own / (own + jnp.exp(other - top))
+        column = jnp.broadcast_to(gate, (128, rows)).T
         for start in range(0, width, 128):
-            part = cot_ref[:, start:start + 128].astype(jnp.float32) * column
+            part = cot_ref[:, :, start:start + 128].reshape(rows, 128).astype(jnp.float32) * column
             grad_ref[:, start:start + 128] = part.astype(jnp.bfloat16)
     up = up_ref[0]
     for start in range(0, rows, chunk):
@@ -113,26 +144,49 @@
         value, slope = gelu_pair(pre)
         act_ref[start:start + chunk, :] = value.astype(jnp.bfloat16)
         slope_ref[start:start + chunk, :] = slope.astype(jnp.bfloat16)
-    down_grad_ref[...] = dot_tn(act_ref[...], grad_ref[...]).astype(jnp.bfloat16)
-
-def expert_first(rows_in, cot, gate, up, which, tile=512, chunk=256):
+    down_grad_ref[0] = dot_tn(act_ref[...], grad_ref[...]).astype(jnp.bfloat16)
+
+
+def expert_first(owner, rows_in, cot, other, router, up, index, local_count, shards, into=None, after=(), chunk=640):
     rows, width = rows_in.shape
     hidden = up.shape[2]
+    tile = hidden // shards
+    owners, _, capacity, _ = cot.shape
     fixed = pl.BlockSpec((rows, width), lambda i: (0, 0))
     column = pl.BlockSpec((rows, tile), lambda i: (0, i))
-    return pl.pallas_call(
-        partial(first_kernel, chunk=chunk),
-        grid=(hidden // tile,),
-        in_specs=[fixed, fixed, pl.BlockSpec((1, rows), lambda i: (0, 0)), pl.BlockSpec((1, width, tile), lambda i: (which, 0, i))],
-        out_specs=[column, column, pl.BlockSpec((tile, width), lambda i: (i, 0)), fixed],
-        out_shape=[jax.ShapeDtypeStruct((rows, hidden), jnp.bfloat16)] * 2 + [jax.ShapeDtypeStruct((hidden, width), jnp.bfloat16), jax.ShapeDtypeStruct((rows, width), jnp.bfloat16)],
-        compiler_params=pltpu.CompilerParams(vmem_limit_bytes=56 << 20),
+    chunk = chunk if rows % chunk == 0 else rows // 2
+    operands = [owner, rows_in, cot, other, router, up]
+    place, aliases = 0, {}
+    grad_shape = jax.ShapeDtypeStruct((shards, tile, width), jnp.bfloat16)
+    if into is not None:
+        aliases = {len(operands): 2}
+        operands.append(into)
+        place, grad_shape = 1, jax.ShapeDtypeStruct(into.shape, into.dtype)
+    operands += list(after)
+    return pl.pallas_call(
+        partial(first_kernel, chunk=chunk, index=index, local_count=local_count),
+        grid=(shards,),
+        in_specs=[
+            pl.BlockSpec(memory_space=pltpu.SMEM),
+            fixed,
+            pl.BlockSpec((owners, None, capacity, width), lambda i: (0, index, 0, 0)),
+            pl.BlockSpec((1, rows), lambda i: (0, 0)),
+            pl.BlockSpec(router.shape, lambda i: (0, 0)),
+            pl.BlockSpec((1, width, tile), lambda i: (index, 0, i)),
+        ]
+        + [pl.BlockSpec(memory_space=pl.ANY)] * (len(operands) - 6),
+        out_specs=[column, column, pl.BlockSpec((1, tile, width), lambda i: (i, place, 0)), fixed],
+        out_shape=[jax.ShapeDtypeStruct((rows, hidden), jnp.bfloat16)] * 2 + [grad_shape, jax.ShapeDtypeStruct((rows, width), jnp.bfloat16)],
+        input_output_aliases=aliases,
+        compiler_params=pltpu.CompilerParams(vmem_limit_bytes=60 << 20),
         name="expert_first",
-    )(rows_in, cot, gate, up)
-
-
-def second_kernel(rows_ref, grad_ref, act_ref, slope_ref, up_ref, down_ref, made_ref, back_ref, up_grad_ref, turned, made_acc, back_acc):
+    )(*operands)
+
+
+def second_kernel(rows_ref, grad_ref, act_ref, slope_ref, up_ref, down_ref, *refs):
+    made_ref, up_grad_ref, turned, made_acc, back_acc = refs[-5:]
     step = pl.program_id(0)
+    owners, _, capacity, width = made_ref.shape
     @pl.when(step == 0)
     def _():
         turned[...] = rows_ref[...].T
@@ -140,7 +194,7 @@
     down = down_ref[0]
     grads = dot_nt(grad_ref[...], down)
     low = (slope_ref[...].astype(jnp.float32) * grads).astype(jnp.bfloat16)
-    up_grad_ref[...] = dot_nn(turned[...], low).astype(jnp.bfloat16)
+    up_grad_ref[0] = dot_nn(turned[...], low).astype(jnp.bfloat16)
     back = dot_nt(low, up)
     made = dot_nn(act_ref[...], down)
     last = pl.num_programs(0) - 1
@@ -154,32 +208,51 @@
         back_acc[...] += back
     @pl.when(step == last)
     def _():
-        made_ref[...] = (made_acc[...] + made).astype(jnp.bfloat16)
-        back_ref[...] = (back_acc[...] + back).astype(jnp.bfloat16)
-
-def expert_second(rows_in, grad, act, slope, up, down, which, tile=512):
+        made_ref[:, 0] = (made_acc[...] + made).astype(jnp.bfloat16).reshape(owners, capacity, width)
+        made_ref[:, 1] = (back_acc[...] + back).astype(jnp.bfloat16).reshape(owners, capacity, width)
+
+
+def expert_second(rows_in, grad, act, slope, up, down, index, owners, shards, wide, after=()):
     rows, width = rows_in.shape
     hidden = up.shape[2]
+    tile = hidden // shards
     fixed = pl.BlockSpec((rows, width), lambda i: (0, 0))
     column = pl.BlockSpec((rows, tile), lambda i: (0, i))
+    made_shape = (owners, 2, rows // owners, width)
     return pl.pallas_call(
         second_kernel,
-        grid=(hidden // tile,),
-        in_specs=[fixed, fixed, column, column, pl.BlockSpec((1, width, tile), lambda i: (which, 0, i)), pl.BlockSpec((1, tile, width), lambda i: (which, i, 0))],
-        out_specs=[fixed, fixed, pl.BlockSpec((width, tile), lambda i: (0, i))],
-        out_shape=[jax.ShapeDtypeStruct((rows, width), jnp.bfloat16)] * 2 + [jax.ShapeDtypeStruct((width, hidden), jnp.bfloat16)],
+        grid=(shards,),
+        in_specs=[fixed, fixed, column, column, pl.BlockSpec((1, width, tile), lambda i: (index, 0, i)), pl.BlockSpec((1, tile, width), lambda i: (index, i, 0))]
+        + [pl.BlockSpec(memory_space=pl.ANY)] * len(after),
+        out_specs=[pl.BlockSpec(made_shape, lambda i: (0, 0, 0, 0)), pl.BlockSpec((1, width, tile), lambda i: (i, 0, 0))],
+        out_shape=[jax.ShapeDtypeStruct(made_shape, jnp.bfloat16), jax.ShapeDtypeStruct((shards, wide, tile), jnp.bfloat16)],
         scratch_shapes=[pltpu.VMEM((width, rows), jnp.bfloat16), pltpu.VMEM((rows, width), jnp.float32), pltpu.VMEM((rows, width), jnp.float32)],
-        compiler_params=pltpu.CompilerParams(vmem_limit_bytes=60 << 20),
+        compiler_params=pltpu.CompilerParams(vmem_limit_bytes=62 << 20),
         name="expert_second",
-    )(rows_in, grad, act, slope, up, down)
+    )(rows_in, grad, act, slope, up, down, *after)
 
 
 def spread(row, block):
     return jnp.broadcast_to(row, (128, block)).T
 
-def out_kernel(slots_ref, routes_ref, gates_ref, resid_ref, cot_ref, first_ref, second_ref, out_ref, logit_ref):
+
+def pick(slots, lane, back_refs):
+    picked = None
+    for index, back_ref in enumerate(back_refs):
+        owners, capacity, width = back_ref.shape
+        half = owners * capacity
+        hots = []
+        for start in range(index * half, (index + 1) * half, 128):
+            hit = reduce(jnp.logical_or, [slot == lane + start for slot in slots])
+            hots.append(jnp.where(hit, 1.0, 0.0).astype(jnp.bfloat16))
+        part = dot_nn(jnp.concatenate(hots, axis=1), back_ref[...].reshape(half, width))
+        picked = part if picked is None else picked + part
+    return picked
+
+
+def out_kernel(slots_ref, routes_ref, gates_ref, resid_ref, cot_ref, *refs):
+    back_refs, (out_ref, logit_ref) = refs[:-2], refs[-2:]
     block = out_ref.shape[0]
-    half = first_ref.shape[0]
     lane = lax.broadcasted_iota(jnp.int32, (block, 128), 1)
     cot = cot_ref[...].astype(jnp.float32)
     result = resid_ref[...]
@@ -187,9 +260,7 @@
     for c in range(2):
         slot = spread(slots_ref[c:c + 1, :], block)
         gate = spread(gates_ref[c:c + 1, :], block)[:, 0:1]
-        hots = [jnp.where(slot == lane + k * 128, 1.0, 0.0).astype(jnp.bfloat16) for k in range(2 * half // 128)]
-        count = half // 128
-        picked = dot_nn(jnp.concatenate(hots[:count], axis=1), first_ref[...]) + dot_nn(jnp.concatenate(hots[count:], axis=1), second_ref[...])
+        picked = pick([slot], lane, back_refs)
         result = result + gate * picked
         gates.append(gate)
         inner.append(jnp.sum(cot * picked, axis=1, keepdims=True))
@@ -201,31 +272,33 @@
         logit = logit + jnp.where(route == lane, gates[c] * (inner[c] - middle), 0.0)
     logit_ref[...] = logit.astype(jnp.bfloat16)
 
-def combine_out(slots, routes, gates, resid, cot, first, second, block=256):
+
+def returned_spec(returned, which):
+    owners, _, capacity, width = returned.shape
+    return pl.BlockSpec((owners, None, capacity, width), lambda i: (0, which, 0, 0))
+
+
+def combine_out(slots, routes, gates, resid, cot, returned, block=256):
     tokens, width = resid.shape
     small = pl.BlockSpec((2, block), lambda i: (0, i))
     rows = pl.BlockSpec((block, width), lambda i: (i, 0))
-    fixed = pl.BlockSpec(first.shape, lambda i: (0, 0))
     return pl.pallas_call(
         out_kernel,
         grid=(tokens // block,),
-        in_specs=[small, small, small, rows, rows, fixed, fixed],
+        in_specs=[small, small, small, rows, rows] + [returned_spec(part, 0) for part in returned],
         out_specs=[rows, pl.BlockSpec((block, 128), lambda i: (i, 0))],
         out_shape=[jax.ShapeDtypeStruct((tokens, width), jnp.bfloat16), jax.ShapeDtypeStruct((tokens, 128), jnp.bfloat16)],
         compiler_params=pltpu.CompilerParams(vmem_limit_bytes=48 << 20),
         name="combine_out",
-    )(slots, routes, gates, resid, cot, first, second)
-
-
-def back_kernel(slots_ref, logit_ref, router_ref, gain_ref, resid_ref, cot_ref, first_ref, second_ref, grad_ref, low_ref, gain_grad_ref, *, eps):
-    block, width = grad_ref.shape
-    half = first_ref.shape[0]
+    )(slots, routes, gates, resid, cot, *returned)
+
+
+def back_kernel(slots_ref, logit_ref, router_ref, gain_ref, resid_ref, cot_ref, merge_ref, *refs, eps):
+    back_refs, (grad_ref, low_ref, mixed_ref, gain_grad_ref) = refs[:-4], refs[-4:]
+    block, _ = grad_ref.shape
     lane = lax.broadcasted_iota(jnp.int32, (block, 128), 1)
-    slots = [spread(slots_ref[c:c + 1, :], block) for c in range(2)]
-    hots = [jnp.where((slots[0] == lane + k * 128) | (slots[1] == lane + k * 128), 1.0, 0.0).astype(jnp.bfloat16) for k in range(2 * half // 128)]
-    count = half // 128
-    grads = dot_nn(jnp.concatenate(hots[:count], axis=1), first_ref[...]) + dot_nn(jnp.concatenate(hots[count:], axis=1), second_ref[...])
-    grads = grads + dot_nt(logit_ref[...], router_ref[...])
+    grads = pick([spread(slots_ref[c:c + 1, :], block) for c in range(2)], lane, back_refs)
+    grads = grads + dot_nn(logit_ref[...], router_ref[...])
     resid = resid_ref[...]
     inverse = lax.rsqrt(jnp.mean(resid * resid, axis=1, keepdims=True) + eps)
     unit = resid * inverse
@@ -237,21 +310,26 @@
     inner = jnp.mean(scaled * unit, axis=1, keepdims=True)
     total = cot_ref[...].astype(jnp.float32) + inverse * (scaled - unit * inner)
     grad_ref[...] = total
-    low_ref[...] = total.astype(jnp.bfloat16)
-
-def combine_back(slots, logit, router, gain, resid, cot, first, second, eps, block=256):
+    low = total.astype(jnp.bfloat16)
+    low_ref[...] = low
+    mixed_ref[...] = dot_nt(low, merge_ref[...]).astype(jnp.bfloat16)
+
+
+def combine_back(slots, logit, router, gain, resid, cot, merge, returned, eps, block=256):
     tokens, width = resid.shape
     rows = pl.BlockSpec((block, width), lambda i: (i, 0))
     whole = lambda shape: pl.BlockSpec(shape, lambda i: (0, 0))
+    low = jax.ShapeDtypeStruct((tokens, width), jnp.bfloat16)
     return pl.pallas_call(
         partial(back_kernel, eps=eps),
         grid=(tokens // block,),
-        in_specs=[pl.BlockSpec((2, block), lambda i: (0, i)), pl.BlockSpec((block, 128), lambda i: (i, 0)), whole(router.shape), whole(gain.shape), rows, rows, whole(first.shape), whole(second.shape)],
-        out_specs=[rows, rows, whole((1, width))],
-        out_shape=[jax.ShapeDtypeStruct((tokens, width), jnp.float32), jax.ShapeDtypeStruct((tokens, width), jnp.bfloat16), jax.ShapeDtypeStruct((1, width), jnp.float32)],
+        in_specs=[pl.BlockSpec((2, block), lambda i: (0, i)), pl.BlockSpec((block, 128), lambda i: (i, 0)), whole(router.shape), whole(gain.shape), rows, rows, whole(merge.shape)]
+        + [returned_spec(part, 1) for part in returned],
+        out_specs=[rows, rows, rows, whole((1, width))],
+        out_shape=[jax.ShapeDtypeStruct((tokens, width), jnp.float32), low, low, jax.ShapeDtypeStruct((1, width), jnp.float32)],
         compiler_params=pltpu.CompilerParams(vmem_limit_bytes=48 << 20),
         name="combine_back",
-    )(slots, logit, router, gain, resid, cot, first, second)
+    )(slots, logit, router, gain, resid, cot, merge, *returned)
 
 
 def near_tiles(near_ref, head, block):
@@ -260,6 +338,7 @@
     key_at = lax.broadcasted_iota(jnp.int32, (block, block), 0)
     query_at = lax.broadcasted_iota(jnp.int32, (block, block), 1)
     return (jnp.where(query_at >= key_at, spread, masked_score), jnp.where(query_at < key_at, spread, 0.0), query_at < key_at)
+
 
 def diagonal_sums(tile):
     block = tile.shape[1]
@@ -271,9 +350,11 @@
         total = jnp.where((row & step) != 0, pltpu.roll(total, block - step, 1), total)
     return jnp.sum(total, axis=0, keepdims=True)
 
+
 def head_part(rows, head, size):
     lane = lax.broadcasted_iota(jnp.int32, rows.shape, 1)
     return jnp.where((lane >= head * size) & (lane < (head + 1) * size), rows, jnp.zeros_like(rows))
+
 
 def attend_kernel(query_ref, key_ref, value_ref, near_ref, out_ref, total_ref, *, block, size, scale):
     length, lanes = query_ref.shape
@@ -309,6 +390,7 @@
             total_ref[0, head:head + 1, rows] = top + jnp.log(total)
         out_ref[rows, :] = jnp.concatenate(parts, axis=0).T.astype(out_ref.dtype)
 
+
 def attend(queries, keys, values, near, size, block):
     length, width = queries.shape
     lanes = 128
@@ -326,7 +408,8 @@
         name="attend",
     )(queries, keys, values, near)
 
-def attend_back_kernel(query_ref, key_ref, value_ref, grad_ref, out_ref, total_ref, near_ref, dq_ref, dk_ref, dv_ref, dist_ref, key_acc, value_acc, *, block, size, scale):
+
+def attend_back_kernel(query_ref, key_ref, value_ref, grad_ref, out_ref, total_ref, near_ref, grads_ref, dist_ref, key_acc, value_acc, *, block, size, scale):
     length, lanes = query_ref.shape
     heads = lanes // size
     count = length // block
@@ -381,12 +464,13 @@
             else:
                 value_acc[cols, :] += value_part
                 key_acc[cols, :] += key_part
-        dq_ref[rows, :] = (jnp.concatenate(query_grads, axis=0) * scale).T.astype(dq_ref.dtype)
-    dk_ref[...] = key_acc[...].astype(dk_ref.dtype)
-    dv_ref[...] = value_acc[...].astype(dv_ref.dtype)
+        grads_ref[0, rows, :] = (jnp.concatenate(query_grads, axis=0) * scale).T.astype(grads_ref.dtype)
+    grads_ref[1] = key_acc[...].astype(grads_ref.dtype)
+    grads_ref[2] = value_acc[...].astype(grads_ref.dtype)
     for head in range(heads):
         dist_ref[0, head:head + 1, :] = diagonal_sums(near_acc[head])
         dist_ref[0, heads + head:heads + head + 1, :] = far_acc[head]
+
 
 def attend_back(queries, keys, values, grads, outs, totals, near, size, block):
     length, width = queries.shape
@@ -399,8 +483,8 @@
         partial(attend_back_kernel, block=block, size=size, scale=size ** -0.5),
         grid=(groups,),
         in_specs=[column] * 5 + [pl.BlockSpec((1, heads, length), lambda g: (g, 0, 0)), head_rows],
-        out_specs=[column, column, column, pl.BlockSpec((1, 2 * heads, block), lambda g: (g, 0, 0))],
-        out_shape=[jax.ShapeDtypeStruct((length, width), jnp.bfloat16)] * 3 + [jax.ShapeDtypeStruct((groups, 2 * heads, block), jnp.float32)],
+        out_specs=[pl.BlockSpec((3, length, lanes), lambda g: (0, 0, g)), pl.BlockSpec((1, 2 * heads, block), lambda g: (g, 0, 0))],
+        out_shape=[jax.ShapeDtypeStruct((3, length, width), jnp.bfloat16), jax.ShapeDtypeStruct((groups, 2 * heads, block), jnp.float32)],
         scratch_shapes=[pltpu.VMEM((length, lanes), jnp.float32)] * 2,
         compiler_params=pltpu.CompilerParams(vmem_limit_bytes=56 << 20),
         name="attend_back",
@@ -414,6 +498,7 @@
     low_ref[...] = low
     for weight_ref, out_ref in zip((query_ref, key_ref, value_ref), out_refs):
         out_ref[...] = dot_nn(low, weight_ref[...]).astype(jnp.bfloat16)
+
 
 def project(inputs, gain, query, key, value, eps, block=256):
     tokens, width = inputs.shape
@@ -431,7 +516,6 @@
 
 
 def settle_kernel(mixed_ref, merge_ref, inputs_ref, gain_ref, router_ref, routes_ref, resid_ref, low_ref, gates_ref, *, eps):
-    block = mixed_ref.shape[0]
     resid = inputs_ref[...].astype(jnp.float32) + dot_nn(mixed_ref[...], merge_ref[...])
     resid_ref[...] = resid
     inverse = lax.rsqrt(jnp.mean(resid * resid, axis=1, keepdims=True) + eps)
@@ -446,6 +530,7 @@
     for c in range(2):
         gates_ref[c:c + 1, :] = powers[c] / total
 
+
 def settle(mixed, merge, inputs, gain, router, routes, eps, block=256):
     tokens, width = inputs.shape
     rows = pl.BlockSpec((block, width), lambda i: (i, 0))
@@ -462,8 +547,8 @@
     )(mixed, merge, inputs, gain, router, routes)
 
 
-def finish_kernel(dq_ref, dk_ref, dv_ref, query_ref, key_ref, value_ref, gain_ref, inputs_ref, resid_grad_ref, out_ref, gain_grad_ref, *, eps):
-    grads = dot_nt(dq_ref[...], query_ref[...]) + dot_nt(dk_ref[...], key_ref[...]) + dot_nt(dv_ref[...], value_ref[...])
+def finish_kernel(heads_ref, query_ref, key_ref, value_ref, gain_ref, inputs_ref, resid_grad_ref, out_ref, gain_grad_ref, *, eps):
+    grads = dot_nt(heads_ref[0], query_ref[...]) + dot_nt(heads_ref[1], key_ref[...]) + dot_nt(heads_ref[2], value_ref[...])
     rows = inputs_ref[...].astype(jnp.float32)
     inverse = lax.rsqrt(jnp.mean(rows * rows, axis=1, keepdims=True) + eps)
     unit = rows * inverse
@@ -475,19 +560,46 @@
     inner = jnp.mean(scaled * unit, axis=1, keepdims=True)
     out_ref[...] = resid_grad_ref[...] + inverse * (scaled - unit * inner)
 
-def finish(dq, dk, dv, query, key, value, gain, inputs, resid_grad, eps, block=256):
+
+def finish(head_grads, query, key, value, gain, inputs, resid_grad, eps, block=256):
     tokens, width = inputs.shape
     rows = pl.BlockSpec((block, width), lambda i: (i, 0))
     whole = lambda shape: pl.BlockSpec(shape, lambda i: (0, 0))
     return pl.pallas_call(
         partial(finish_kernel, eps=eps),
         grid=(tokens // block,),
-        in_specs=[rows] * 3 + [whole(query.shape)] * 3 + [whole(gain.shape), rows, rows],
+        in_specs=[pl.BlockSpec((3, block, width), lambda i: (0, i, 0))] + [whole(query.shape)] * 3 + [whole(gain.shape), rows, rows],
         out_specs=[rows, whole((1, width))],
         out_shape=[jax.ShapeDtypeStruct((tokens, width), jnp.float32), jax.ShapeDtypeStruct((1, width), jnp.float32)],
         compiler_params=pltpu.CompilerParams(vmem_limit_bytes=40 << 20),
         name="finish",
-    )(dq, dk, dv, query, key, value, gain, inputs, resid_grad)
+    )(head_grads, query, key, value, gain, inputs, resid_grad)
+
+
+def weight_kernel(left_ref, right_ref, out_ref, turned):
+    shards, part, _ = out_ref.shape
+    @pl.when(pl.program_id(0) == 0)
+    def _():
+        turned[...] = left_ref[...].T
+    right = right_ref[...]
+    for shard in range(shards):
+        grad = dot_nn(turned[shard * part:(shard + 1) * part, :], right)
+        out_ref[shard] = grad.astype(jnp.bfloat16)
+
+
+def weight_grads(left, right, shards):
+    count, tokens, width = right.shape
+    part = width // shards
+    return pl.pallas_call(
+        weight_kernel,
+        grid=(count,),
+        in_specs=[pl.BlockSpec((tokens, width), lambda i: (0, 0)), pl.BlockSpec((None, tokens, width), lambda i: (i, 0, 0))],
+        out_specs=pl.BlockSpec((shards, part, width), lambda i: (0, i, 0)),
+        out_shape=jax.ShapeDtypeStruct((shards, count * part, width), jnp.bfloat16),
+        scratch_shapes=[pltpu.VMEM((width, tokens), jnp.bfloat16)],
+        compiler_params=pltpu.CompilerParams(vmem_limit_bytes=40 << 20),
+        name="weight_grads",
+    )(left, right)
 
 
 def exchange(rows, bit):
@@ -521,7 +633,8 @@
         side = (me // bit) % 2
         keep = lax.dynamic_slice_in_dim(stack, side * half, half, 1)
         send = lax.dynamic_slice_in_dim(stack, (1 - side) * half, half, 1)
-        stack = add_low(keep, exchange(send, bit))
+        got = exchange(send, bit)
+        stack = add_low(keep, got)
     count = lax.axis_size("shard")
     place = lax.axis_index("shard")
     total = lax.dynamic_index_in_dim(stack, place, 0, False).astype(jnp.float32)
@@ -538,11 +651,14 @@
     return piece
 
 
-def share_rows(rows, owners):
-    count, width = rows.shape
-    return lax.all_to_all(
-        rows.reshape(owners, count // owners, width), "expert", 0, 0, tiled=True
-    ).reshape(count, width)
+def scatter_sum(grads):
+    shards, rows, width = grads.shape
+    grads = grads.reshape(shards * rows, width)
+    return lax.psum_scatter(grads, "shard", scatter_dimension=0, tiled=True)
+
+
+def share_rows(rows):
+    return lax.all_to_all(rows, "expert", 0, 0, tiled=True)
 
 
 def local(
@@ -571,15 +687,25 @@
     heads = local_heads * shards
     size = width // heads
     experts = router_weight.shape[1]
-    local_count = up_weight.shape[0]
+    local_count, _, hidden = up_weight.shape
     capacity = (5 * tokens * routes.shape[1] + 4 * experts - 1) // (4 * experts)
+    capacity = -(-capacity // 16) * 16
     rows = owners * capacity
-
-    small = jnp.concatenate(
-        [norm_gain, expert_gain, router_weight.reshape(-1), bias_table.reshape(-1)]
-    )
+    assert local_count == 2 and hidden // shards == width
+
     small_rows = 8 * owners
-    small = jnp.pad(small, (0, small_rows * width - small.shape[0])).reshape(small_rows, width)
+    router_at = 2 + local_heads + (-(2 + local_heads)) % 8
+
+    def widen(block):
+        return jnp.pad(block, ((0, 0), (0, width - block.shape[1])))
+
+    def pack(gain_one, gain_two, table, router):
+        head = jnp.concatenate([gain_one, gain_two], axis=0)
+        gap = jnp.zeros((router_at - 2 - local_heads, width), bf16)
+        rest = jnp.zeros((small_rows - router_at - experts, width), bf16)
+        return jnp.concatenate([widen(head), widen(table), gap, widen(router), rest], axis=0)
+
+    small = pack(norm_gain[None], expert_gain[None], bias_table.T, router_weight.T)
     slices = [
         lax.dynamic_slice_in_dim(weight, me * piece, piece, 0)
         for weight in (query_weight, key_weight, value_weight)
@@ -593,120 +719,106 @@
         return block.transpose(1, 0, 2, 3).reshape(width, width)
 
     query_full, key_full, value_full = (whole_weight(index) for index in range(3))
-    small_full = gathered[:, :, 3 * piece :].transpose(1, 0, 2, 3).reshape(shards, small_rows * width)
-    gain_one = small_full[:, :part].reshape(1, width).astype(f32)
-    gain_two = small_full[:, part : 2 * part].reshape(1, width).astype(f32)
-    router_at = 2 * part + part * experts
-    router_full = small_full[:, 2 * part : router_at].reshape(width, experts)
-    table_full = small_full[:, router_at : router_at + BUCKETS * local_heads]
-    table_full = table_full.reshape(shards, BUCKETS, local_heads).transpose(1, 0, 2)
-    table_full = table_full.reshape(BUCKETS, heads).astype(f32)
+    small_full = gathered[:, :, 3 * piece :].transpose(1, 0, 2, 3).reshape(shards, small_rows, width)
+    gain_one = small_full[:, 0, :part].reshape(1, width).astype(f32)
+    gain_two = small_full[:, 1, :part].reshape(1, width).astype(f32)
+    table_full = small_full[:, 2 : 2 + local_heads, :BUCKETS].reshape(heads, BUCKETS).astype(f32)
+    router_full = small_full[:, router_at : router_at + experts, :part]
+    router_full = router_full.transpose(1, 0, 2).reshape(experts, width)
 
     routes_line = routes.T
     base = (routes_line % local_count * owners + routes_line // local_count) * capacity
     slots = find_slots(routes_line, base, experts)
-    cot_rows = [dispatch(slots, cotangent, index * rows, rows) for index in range(local_count)]
+    cot_rows, other = dispatch_all(
+        slots, routes_line.astype(f32), cotangent, owners, capacity, local_count
+    )
+    other = share_rows(other).reshape(owners, local_count, capacity)
 
     low_one, queries, keys, values = project(
         inputs, gain_one, query_full, key_full, value_full, epsilon
     )
+    cot_in = share_rows(cot_rows).reshape(owners, local_count, capacity, width)
     block = 256
     hot = bucket_hot(tokens)
     assert hot[block:, -1].all()
-    near_hot = jnp.asarray(hot[:block] - hot[-1:], dtype=f32)
+    near_hot = jnp.asarray((hot[:block] - hot[-1:]).T, dtype=f32)
     group = 128 // size
-    near = jnp.dot(near_hot, table_full, precision=lax.Precision.HIGHEST).T
+    near = jnp.dot(table_full, near_hot, precision=lax.Precision.HIGHEST)
     near = near.reshape(heads // group, group, block)
     attended, totals = attend(queries, keys, values, near, size, block)
     resid, low_two, gates = settle(
-        attended, merge_full, inputs, gain_two, router_full.T, routes_line, epsilon
-    )
-
-    made, back, up_grads, down_grads = [], [], [], []
+        attended, merge_full, inputs, gain_two, router_full, routes_line, epsilon
+    )
+
+    owner = me.astype(jnp.int32).reshape(1)
+    sends, rows_in = [], []
     for index in range(local_count):
-        rows_out, gate_out = dispatch(slots, low_two, index * rows, rows, gates)
-        rows_in = share_rows(rows_out, owners)
-        gate_in = lax.all_to_all(
-            gate_out.reshape(owners, 1, capacity), "expert", 0, 0, tiled=True
-        ).reshape(1, rows)
-        cot_in = share_rows(cot_rows[index], owners)
-        act, slope, down_grad, grad_in = expert_first(rows_in, cot_in, gate_in, up_weight, index)
-        down_grads.append(lax.psum_scatter(down_grad, "shard", scatter_dimension=0, tiled=True))
-        made_rows, back_rows, up_grad = expert_second(
-            rows_in, grad_in, act, slope, up_weight, down_weight, index
-        )
-        up_grads.append(lax.psum_scatter(up_grad, "shard", scatter_dimension=1, tiled=True))
-        made.append(share_rows(made_rows, owners))
-        back.append(share_rows(back_rows, owners))
-    output, logit_grad = combine_out(slots, routes_line, gates, resid, cotangent, *made)
-    router_wide = jnp.pad(router_full, ((0, 0), (0, 128 - experts)))
-    resid_grad, branch, gain_grad = combine_back(
-        slots, logit_grad, router_wide, gain_two, resid, cotangent, *back, epsilon
-    )
-
-    def weight_grad(left, right):
-        return jnp.einsum("ti,to->io", left, right, preferred_element_type=f32).astype(bf16)
-
-    router_grad = weight_grad(low_two, logit_grad[:, :experts])
-    merge_grad = weight_grad(attended, branch)
-    mixed_grad = jnp.einsum(
-        "to,io->ti", branch, merge_full, preferred_element_type=f32
-    ).astype(bf16)
-    grad_queries, grad_keys, grad_values, distances = attend_back(
+        sends.append(dispatch(slots, low_two, index * rows, rows))
+        send = share_rows(sends[index].reshape(owners, capacity, width))
+        rows_in.append(send.reshape(rows, width))
+    others = [other[:, index].reshape(1, rows) for index in range(local_count)]
+    act, slope, first_down, grad_in = expert_first(
+        owner, rows_in[0], cot_in, others[0], router_full, up_weight, 0, local_count, shards,
+        after=(sends[1],),
+    )
+    first_sum = scatter_sum(first_down)
+    first_made, pair = expert_second(
+        rows_in[0], grad_in, act, slope, up_weight, down_weight, 0, owners, shards, 2 * width
+    )
+    act, slope, pair, grad_in = expert_first(
+        owner, rows_in[1], cot_in, others[1], router_full, up_weight, 1, local_count, shards,
+        into=pair,
+    )
+    pair_sum = scatter_sum(pair)
+    second_made, last_up = expert_second(
+        rows_in[1], grad_in, act, slope, up_weight, down_weight, 1, owners, shards, width
+    )
+    last_sum = scatter_sum(last_up)
+    returned = []
+    for made in (first_made, second_made):
+        returned.append(share_rows(made))
+    output, logit_grad = combine_out(slots, routes_line, gates, resid, cotangent, returned)
+    router_wide = jnp.pad(router_full, ((0, 128 - experts), (0, 0)))
+    resid_grad, branch, mixed_grad, gain_grad = combine_back(
+        slots, logit_grad, router_wide, gain_two, resid, cotangent, merge_full, returned, epsilon
+    )
+    router_grad = jnp.einsum("te,ti->ei", logit_grad, low_two, preferred_element_type=f32)
+    merge_grad = weight_grads(attended, branch[None], shards)
+    head_grads, distances = attend_back(
         queries, keys, values, mixed_grad, attended, totals, near, size, block
     )
     close_sums = distances[:, :group].reshape(heads, block)
     far_sums = jnp.sum(distances[:, group:].reshape(heads, block), axis=1)
-    table_grad = jnp.einsum(
-        "nb,hn->bh", jnp.asarray(hot[:block]), close_sums, precision=lax.Precision.HIGHEST
-    )
-    table_grad = table_grad + jnp.asarray(hot[-1:]).T * far_sums[None, :]
+    table_grad = jnp.dot(close_sums, jnp.asarray(hot[:block]), precision=lax.Precision.HIGHEST)
+    table_grad = table_grad + far_sums[:, None] * jnp.asarray(hot[-1:])
+    head_sums = weight_grads(low_one, head_grads, shards)
     input_gradient, norm_grad = finish(
-        grad_queries, grad_keys, grad_values, query_full, key_full, value_full,
-        gain_one, inputs, resid_grad, epsilon,
-    )
-
-    def by_shard(grad):
-        return grad.reshape(shards, part, width)
-
-    small_grad = jnp.concatenate(
-        [
-            norm_grad.reshape(shards, part).astype(bf16),
-            gain_grad.reshape(shards, part).astype(bf16),
-            router_grad.reshape(shards, part * experts),
-            table_grad.reshape(BUCKETS, shards, local_heads)
-            .transpose(1, 0, 2)
-            .reshape(shards, BUCKETS * local_heads)
-            .astype(bf16),
-        ],
-        axis=1,
-    )
-    used = small_grad.shape[1]
-    small_grad = jnp.pad(small_grad, ((0, 0), (0, small_rows * width - used)))
-    small_grad = small_grad.reshape(shards, small_rows, width)
+        head_grads, query_full, key_full, value_full, gain_one, inputs, resid_grad, epsilon
+    )
+    small_grad = jax.vmap(pack)(
+        norm_grad.reshape(shards, 1, part).astype(bf16),
+        gain_grad.reshape(shards, 1, part).astype(bf16),
+        table_grad.reshape(shards, local_heads, BUCKETS).astype(bf16),
+        router_grad[:experts].reshape(experts, shards, part).transpose(1, 0, 2).astype(bf16),
+    )
     bits = [1 << level for level in range(owners.bit_length() - 1)]
-    first_stack = jnp.concatenate(
-        [by_shard(weight_grad(low_one, grad)) for grad in (grad_queries, grad_keys)], axis=1
-    )
-    second_stack = jnp.concatenate(
-        [by_shard(weight_grad(low_one, grad_values)), by_shard(merge_grad), small_grad], axis=1
-    )
-    first_sum = reduce_stack(first_stack, bits).astype(f32)
-    second_sum = reduce_stack(second_stack, bits[:1] + bits[:0:-1]).astype(f32)
-    small_sum = second_sum[2 * part :].reshape(-1)
+    head_sums = reduce_stack(head_sums, bits).astype(f32)
+    rest_sums = jnp.concatenate([merge_grad, small_grad], axis=1)
+    rest_sums = reduce_stack(rest_sums, bits[:1] + bits[:0:-1]).astype(f32)
+    small_sum = rest_sums[part:]
     return (
         output,
         input_gradient,
-        small_sum[:part],
-        first_sum[:part],
-        first_sum[part:],
-        second_sum[:part],
-        second_sum[part : 2 * part],
-        small_sum[router_at : router_at + BUCKETS * local_heads].reshape(BUCKETS, local_heads),
-        small_sum[part : 2 * part],
-        small_sum[2 * part : router_at].reshape(part, experts),
-        jnp.stack([grad.astype(f32) for grad in up_grads]),
-        jnp.stack([grad.astype(f32) for grad in down_grads]),
+        small_sum[0, :part],
+        head_sums[:part],
+        head_sums[part : 2 * part],
+        head_sums[2 * part :],
+        rest_sums[:part],
+        small_sum[2 : 2 + local_heads, :BUCKETS].T,
+        small_sum[1, :part],
+        small_sum[router_at : router_at + experts, :part].T,
+        jnp.stack([pair_sum[:width].astype(f32), last_sum.astype(f32)]),
+        jnp.stack([first_sum.astype(f32), pair_sum[width:].astype(f32)]),
     )
 
 

time: 632 us -> 614 us (0.972)
  blocking collectives: 72.1 us -> 8.45 us
  waiting for transfers between devices: 160 us -> 202 us
  Pallas kernels: 232 us -> 244 us
  matrix products: 12.5 us -> 2.26 us
    all_to_all x4 -> x1, blocking collectives: 72.1 us -> 8.45 us  [share_rows(): return lax.all_to_all(rows, 'expert', 0, 0, tiled=True)]
    reduce_scatter x4 -> x3, waiting for transfers between devices: 0.01 us -> 32.4 us  [scatter_sum(): return lax.psum_scatter(grads, 'shard', scatter_dimension=0, tiled=True)]
    all_gather x1, waiting for transfers between devices: 38 us -> 17.9 us  [local(): gathered = lax.all_gather(lined, 'expert', axis=0, tiled=False)]
    unnamed x131 -> x98, local copies, waits for them, and re-layouts: 39.9 us -> 25.5 us
    ppermute x9, waiting for transfers between devices: 17.6 us -> 31.9 us  [shift(): lax.ppermute(rows, 'shard', [(i, (i + step) % count) for i in range(count)])]
    ppermute x12, waiting for transfers between devices: 28.2 us -> 38.7 us  [exchange(): return lax.ppermute(rows, 'expert', [(i, i ^ bit) for i in range(count)])]
    concatenate x2, local copies, waits for them, and re-layouts: 1.52 us -> 11.8 us  [the longest x1 11.8 us: local(): rest_sums = jnp.concatenate([merge_grad, small_grad], axis=1)]
    dot_general x8 -> x3, matrix products: 12.5 us -> 2.26 us  [the longest x1 1.7 us: local(): jnp.dot(close_sums, jnp.asarray(hot[:block]), precision=lax.Precision.HIG...]
  transfers between devices with their start and end apart: 33 -> 31, of which waited for: 18 -> 21; matrix products, arithmetic and copies ran while one was open for 9% -> 9% of each run, Pallas kernels for 34% -> 37%
where the time goes in v2:
time: 614 us; the launch traced here: 604 us
  Pallas kernels  244 us (40%)
  waiting for transfers between devices  202 us (33%)
  local copies, waits for them, and re-layouts  67.3 us (11%)
  starting transfers between devices  48.6 us (8%)
  other arithmetic  16.9 us (3%)
  between operations  14.8 us (2%)
  blocking collectives  8.45 us (1%)
    all_to_all x5, waiting for transfers between devices, share_rows(): return lax.all_to_all(rows, 'expert', 0, 0, tiled=True)  73.9 us
    pallas_call x2, Pallas kernels, expert_second(): pl.pallas_call(second_kernel, grid=(shards,), in_specs=[fixed, fixed, col...  73.1 us
    pallas_call x2, Pallas kernels, expert_first(): pl.pallas_call(partial(first_kernel, chunk=chunk, index=index, local_coun...  41.7 us
    ppermute x12, waiting for transfers between devices, exchange(): return lax.ppermute(rows, 'expert', [(i, i ^ bit) for i in range(count)])  38.7 us
    pallas_call x1, Pallas kernels, attend_back(): pl.pallas_call(partial(attend_back_kernel, block=block, size=size, scale=...  35.9 us
    reduce_scatter x3, waiting for transfers between devices, scatter_sum(): return lax.psum_scatter(grads, 'shard', scatter_dimension=0, tiled=True)  32.4 us
    ppermute x9, waiting for transfers between devices, shift(): lax.ppermute(rows, 'shard', [(i, (i + step) % count) for i in range(count)])  31.9 us
    all_to_all x5, starting transfers between devices, share_rows(): return lax.all_to_all(rows, 'expert', 0, 0, tiled=True)  26.6 us
  transfers between devices with their start and end apart: 31, of which 21 were waited for; matrix products, arithmetic and copies ran while one was open for 9% of the time, Pallas kernels for 37%

profile of v2, /device:TPU:0, one launch (start us, length us, event | category | flops | bytes accessed | tf_op | source)
XLA Modules:
  0.0 604.0 jit_solution(11804275994341966499)
XLA Ops:
  28.5 9.7 %dispatch_all.1 = (bf16[8,320,768]{2,1,0:T(8,128)(2,1)}, f32[8,1,320]{2,1,0:T(1,128)}) custom-call(s32[2,1024]{1,0:T(2,128)} %find_slots.1.slots_ref, f32[2,1024]{1,0:T(2,128)} %bitcast_convert_fusion.routes_ref, bf16[1024,768]{1,0:T(8,128)(2,1)} %cot_ref.3), custom_call_target="tpu_custom_call" | custom-call | tf_op jit(solution)/shard_map/dispatch_all/pallas_call | solution.py:103
  38.2 8.4 %all_to_all.30 = f32[8,1,320]{2,1,0:T(1,128)S(1)} all-to-all(f32[8,1,320]{2,1,0:T(1,128)} %get-tuple-element.53), channel_id=1, replica_groups=mesh['expert'=8,'shard'=4] {'expert'}, dimensions={0} | all-to-all | bytes 20480 | tf_op jit(solution)/shard_map/all_to_all | solution.py:661
  46.7 4.7 all-to-all-start.1
  52.1 17.9 %all-gather.3.cloned.1.call-done = bf16[8,4,80,768]{3,2,0,1:T(8,128)(2,1)} async-done(((bf16[1,4,80,768]{3,2,0,1:T(8,128)(2,1)}), bf16[8,4,80,768]{3,2,0,1:T(8,128)(2,1)}) %all-gather.3.cloned.1.call-update) | async-done | bytes 3932176 | tf_op jit(solution)/shard_map/all_gather | solution.py:714
  74.1 4.7 project.1
  81.3 22.2 %attend.1 = (bf16[1024,768]{1,0:T(8,128)(2,1)S(1)}, f32[6,2,1024]{2,1,0:T(2,128)S(1)}) custom-call(bf16[1024,768]{1,0:T(8,128)(2,1)S(1)} %get-tuple-element.45.query_ref, bf16[1024,768]{1,0:T(8,128)(2,1)S(1)} %get-tuple-element.46.key_ref, bf16[1024,768]{1,0:T(8,128)(2,1)} %copy-done.22, f32[6,2,256]{2,1,0:T(2,128)S(1)} %copy.43.near_ref), custom_call_target="tpu_custom_call" | custom-call | tf_op jit(solution)/shard_map/attend/pallas_call | solution.py:401
  106.5 5.5 all-gather.5.cloned.1.call-done.merge_ref
  121.2 5.5 dispatch.2
  126.8 8.5 %all-to-all-start = ((bf16[8,160,768]{2,1,0:T(8,128)(2,1)}), bf16[8,160,768]{2,1,0:T(8,128)(2,1)S(1)}, u32[]{:S(2)}, u32[]{:S(2)}) async-start(bf16[8,160,768]{2,1,0:T(8,128)(2,1)} %bitcast.99), calls=%async_computation | async-start | bytes 3932160 | tf_op jit(solution)/shard_map/all_to_all | solution.py:661
  135.2 5.6 dispatch.3.refs_0_
  140.9 19.6 %all-to-all-done = bf16[8,160,768]{2,1,0:T(8,128)(2,1)S(1)} async-done(((bf16[8,160,768]{2,1,0:T(8,128)(2,1)}), bf16[8,160,768]{2,1,0:T(8,128)(2,1)S(1)}, u32[]{:S(2)}, u32[]{:S(2)}) %all-to-all-start) | async-done | bytes 1966112 | tf_op jit(solution)/shard_map/all_to_all | solution.py:661
  167.8 20.7 %expert_first.2 = (bf16[1280,3072]{1,0:T(8,128)(2,1)}, bf16[1280,3072]{1,0:T(8,128)(2,1)}, bf16[4,768,768]{2,1,0:T(8,128)(2,1)}, bf16[1280,768]{1,0:T(8,128)(2,1)}) custom-call(s32[1]{0:T(128)} %bitcast.24.owner_ref, bf16[1280,768]{1,0:T(8,128)(2,1)} %bitcast.96, bf16[8,2,160,768]{3,2,1,0:T(8,128)(2,1)} %bitcast.25.cot_ref, ...), custom_call_target="tpu_custom_call" | custom-call | tf_op jit(solution)/shard_map/expert_first/pallas_call | solution.py:166
  188.5 36.1 %expert_second.2 = (bf16[8,2,160,768]{3,2,1,0:T(8,128)(2,1)}, bf16[4,1536,768]{2,1,0:T(8,128)(2,1)}) custom-call(bf16[1280,768]{1,0:T(8,128)(2,1)} %bitcast.97, bf16[1280,768]{1,0:T(8,128)(2,1)} %get-tuple-element.54.grad_ref, bf16[1280,3072]{1,0:T(8,128)(2,1)} %get-tuple-element.55.act_ref, bf16[1280,3072]{1,0:T(8,128)(2,1)} %get-tuple-element.56.slope_ref, ...), custom_call_target="tpu_custom_call" | custom-call | tf_op jit(solution)/shard_map/expert_second/pallas_call | solution.py:222
  224.7 21.0 %expert_first.3 = (bf16[1280,3072]{1,0:T(8,128)(2,1)}, bf16[1280,3072]{1,0:T(8,128)(2,1)}, bf16[4,1536,768]{2,1,0:T(8,128)(2,1)}, bf16[1280,768]{1,0:T(8,128)(2,1)}) custom-call(s32[1]{0:T(128)} %bitcast.24.owner_ref, bf16[1280,768]{1,0:T(8,128)(2,1)} %bitcast.27.rows_ref, ...), custom_call_target="tpu_custom_call", output_to_operand_aliasing={{2}: (6, {})} | custom-call | tf_op jit(solution)/shard_map/expert_first/pallas_call | solution.py:166
  246.3 4.5 all-to-all-start.3
  250.8 37.0 %expert_second.3 = (bf16[8,2,160,768]{3,2,1,0:T(8,128)(2,1)}, bf16[4,768,768]{2,1,0:T(8,128)(2,1)}) custom-call(bf16[1280,768]{1,0:T(8,128)(2,1)} %bitcast.27.rows_ref, bf16[1280,768]{1,0:T(8,128)(2,1)} %get-tuple-element.59.grad_ref, bf16[1280,3072]{1,0:T(8,128)(2,1)} %get-tuple-element.60.act_ref, bf16[1280,3072]{1,0:T(8,128)(2,1)} %get-tuple-element.61.slope_ref, ...), custom_call_target="tpu_custom_call" | custom-call | tf_op jit(solution)/shard_map/expert_second/pallas_call | solution.py:222
  287.8 9.3 %all-to-all-done.3.refs_0_ = bf16[8,2,160,768]{3,2,1,0:T(8,128)(2,1)} async-done(((bf16[8,2,160,768]{3,2,1,0:T(8,128)(2,1)}), bf16[8,2,160,768]{3,2,1,0:T(8,128)(2,1)}, u32[]{:S(2)}, u32[]{:S(2)}) %all-to-all-start.3) | async-done | bytes 3932192 | tf_op jit(solution)/shard_map/all_to_all | solution.py:661
  297.1 4.5 all-to-all-start.5
  302.8 45.1 %all-to-all-done.5.refs_1_ = bf16[8,2,160,768]{3,2,1,0:T(8,128)(2,1)} async-done(((bf16[8,2,160,768]{3,2,1,0:T(8,128)(2,1)}), bf16[8,2,160,768]{3,2,1,0:T(8,128)(2,1)}, u32[]{:S(2)}, u32[]{:S(2)}) %all-to-all-start.5) | async-done | bytes 3932192 | tf_op jit(solution)/shard_map/all_to_all | solution.py:661
  349.8 12.7 %combine_out.1 = (bf16[1024,768]{1,0:T(8,128)(2,1)}, bf16[1024,128]{1,0:T(8,128)(2,1)S(1)}) custom-call(s32[2,1024]{1,0:T(2,128)S(1)} %copy-done.36, s32[2,1024]{1,0:T(2,128)S(1)} %bitcast.94, f32[2,1024]{1,0:T(2,128)S(1)} %get-tuple-element.49.gates_ref, f32[1024,768]{1,0:T(8,128)S(1)} %copy-done.13, bf16[1024,768]{1,0:T(8,128)(2,1)S(1)} %copy-done.8, ...), custom_call_target="tpu_custom_call" | custom-call | tf_op jit(solution)/shard_map/combine_out/pallas_call | solution.py:285
  362.5 13.7 %combine_back.1 = (f32[1024,768]{1,0:T(8,128)}, bf16[1024,768]{1,0:T(8,128)(2,1)S(1)}, bf16[1024,768]{1,0:T(8,128)(2,1)S(1)}, f32[1,768]{1,0:T(1,128)S(1)}) custom-call(s32[2,1024]{1,0:T(2,128)S(1)} %copy-done.36, bf16[1024,128]{1,0:T(8,128)(2,1)S(1)} %get-tuple-element.64.logit_ref, bf16[128,768]{1,0:T(8,128)(2,1)S(1)} %pad.31.router_ref, ...), custom_call_target="tpu_custom_call" | custom-call | tf_op jit(solution)/shard_map/combine_back/pallas_call | solution.py:323
  378.6 35.9 %attend_back.1 = (bf16[3,1024,768]{2,1,0:T(8,128)(2,1)}, f32[6,4,256]{2,1,0:T(4,128)}) custom-call(bf16[1024,768]{1,0:T(8,128)(2,1)} %copy-done.20, bf16[1024,768]{1,0:T(8,128)(2,1)} %copy-done.21, bf16[1024,768]{1,0:T(8,128)(2,1)} %copy-done.22, bf16[1024,768]{1,0:T(8,128)(2,1)} %copy-done.31, bf16[1024,768]{1,0:T(8,128)(2,1)} %copy-done.6, ...), custom_call_target="tpu_custom_call" | custom-call | tf_op jit(solution)/shard_map/attend_back/pallas_call | solution.py:482
  419.4 7.0 %finish.1 = (f32[1024,768]{1,0:T(8,128)}, f32[1,768]{1,0:T(1,128)S(1)}) custom-call(bf16[3,1024,768]{2,1,0:T(8,128)(2,1)S(1)} %copy-done.2, bf16[768,768]{1,0:T(8,128)(2,1)S(1)} %bitcast.90, bf16[768,768]{1,0:T(8,128)(2,1)S(1)} %bitcast.88, bf16[768,768]{1,0:T(8,128)(2,1)S(1)} %bitcast.86, f32[1,768]{1,0:T(1,128)S(1)} %reshape.172.gain_ref, ...), custom_call_target="tpu_custom_call" | custom-call | tf_op jit(solution)/shard_map/finish/pallas_call | solution.py:568
  426.4 5.3 weight_grads.3
  449.5 11.8 %concatenate.55 = bf16[4,256,768]{2,1,0:T(8,128)(2,1)} concatenate(bf16[4,192,768]{2,1,0:T(8,128)(2,1)} %copy-done.25, bf16[4,2,768]{2,1,0:T(2,128)(2,1)S(1)} %fusion.11, bf16[4,3,768]{2,1,0:T(4,128)(2,1)} %pad.33, bf16[4,3,768]{2,1,0:T(4,128)(2,1)} %broadcast_in_dim.33, bf16[4,16,768]{2,1,0:T(8,128)(2,1)} %pad.34, bf16[4,40,768]{2,1,0:T(8,128)(2,1)} %broadcast_in_dim.34), dimensions={1} | concatenate | bytes 3145728 | tf_op jit(solution)/shard_map/concatenate | solution.py:806
  473.0 6.9 %collective-permute-done.4 = bf16[4,64,768]{2,1,0:T(8,128)(2,1)} collective-permute-done((bf16[4,64,768]{2,1,0:T(8,128)(2,1)}, bf16[4,64,768]{2,1,0:T(8,128)(2,1)}, u32[]{:S(2)}, u32[]{:S(2)}) %collective-permute-start.4) | collective-permute-done | bytes 393248 | tf_op jit(solution)/shard_map/ppermute | solution.py:607
  481.2 17.7 %collective-permute-done.5 = bf16[4,32,768]{2,1,0:T(8,128)(2,1)S(1)} collective-permute-done((bf16[4,32,768]{2,1,0:T(8,128)(2,1)S(1)}, bf16[4,32,768]{2,1,0:T(8,128)(2,1)S(1)}, u32[]{:S(2)}, u32[]{:S(2)}) %collective-permute-start.5) | collective-permute-done | bytes 196640 | tf_op jit(solution)/shard_map/ppermute | solution.py:607
  508.6 6.1 %collective-permute-done.7 = bf16[32,768]{1,0:T(8,128)(2,1)S(1)} collective-permute-done((bf16[32,768]{1,0:T(8,128)(2,1)S(1)}, bf16[32,768]{1,0:T(8,128)(2,1)S(1)}, u32[]{:S(2)}, u32[]{:S(2)}) %collective-permute-start.7) | collective-permute-done | bytes 49184 | tf_op jit(solution)/shard_map/ppermute | solution.py:612
  523.9 5.9 collective-permute-done.15
  532.2 9.0 %collective-permute-done.16 = bf16[72,768]{1,0:T(8,128)(2,1)S(1)} collective-permute-done((bf16[72,768]{1,0:T(8,128)(2,1)S(1)}, bf16[72,768]{1,0:T(8,128)(2,1)S(1)}, u32[]{:S(2)}, u32[]{:S(2)}) %collective-permute-start.16) | collective-permute-done | bytes 110624 | tf_op jit(solution)/shard_map/ppermute | solution.py:612
  547.0 5.1 collective-permute-done.19
  561.1 32.4 %reduce-scatter.6.cloned.1.call-done = bf16[768,768]{1,0:T(8,128)(2,1)} async-done(((bf16[3072,768]{1,0:T(8,128)(2,1)}), bf16[768,768]{1,0:T(8,128)(2,1)}) %reduce-scatter.6.cloned.1.call-update) | async-done | bytes 1179664 | tf_op jit(solution)/shard_map/reduce_scatter | solution.py:657
  (237 shorter events, 129.0 us)
Async XLA Ops:
  7.2 62.8 %all-gather.3.cloned.1.call-start = ((), (), s32[]{:S(2)}) async-start(), calls=%async_computation.9 | async-start | bytes 4423680 | tf_op jit(solution)/shard_map/all_gather | solution.py:714
  10.9 9.4 %collective-permute-start = (bf16[80,768]{1,0:T(8,128)(2,1)S(1)}, bf16[80,768]{1,0:T(8,128)(2,1)S(1)}, u32[]{:S(2)}, u32[]{:S(2)}) collective-permute-start(bf16[80,768]{1,0:T(8,128)(2,1)S(1)} %pad_maximum_fusion), channel_id=1, source_target_pairs={{0,1},{1,2},{2,3},{3,0},{4,5},{5,6},{6,7},{7,4},{8,9},{9,10},{10,1... | collective-permute-start | bytes 368648 | tf_op jit(solution)/shard_map/ppermute | solution.py:612
  14.1 10.7 %collective-permute-start.1 = (bf16[80,768]{1,0:T(8,128)(2,1)S(1)}, bf16[80,768]{1,0:T(8,128)(2,1)S(1)}, u32[]{:S(2)}, u32[]{:S(2)}) collective-permute-start(bf16[80,768]{1,0:T(8,128)(2,1)S(1)} %pad_maximum_fusion), channel_id=1, source_target_pairs={{0,2},{1,3},{2,0},{3,1},{4,6},{5,7},{6,4},{7,5},{8,10},{9,11},{10,... | collective-permute-start | bytes 368648 | tf_op jit(solution)/shard_map/ppermute | solution.py:612
  16.6 8.1 %collective-permute-start.2 = (bf16[80,768]{1,0:T(8,128)(2,1)S(1)}, bf16[80,768]{1,0:T(8,128)(2,1)S(1)}, u32[]{:S(2)}, u32[]{:S(2)}) collective-permute-start(bf16[80,768]{1,0:T(8,128)(2,1)S(1)} %pad_maximum_fusion), channel_id=1, source_target_pairs={{0,3},{1,0},{2,1},{3,2},{4,7},{5,4},{6,5},{7,6},{8,11},{9,8},{10,9... | collective-permute-start | bytes 368648 | tf_op jit(solution)/shard_map/ppermute | solution.py:612
  46.7 80.1 %all-to-all-start.1 = ((bf16[8,320,768]{2,1,0:T(8,128)(2,1)}), bf16[8,320,768]{2,1,0:T(8,128)(2,1)}, u32[]{:S(2)}, u32[]{:S(2)}) async-start(bf16[8,320,768]{2,1,0:T(8,128)(2,1)} %get-tuple-element.52), calls=%async_computation.1 | async-start | bytes 7864320 | tf_op jit(solution)/shard_map/all_to_all | solution.py:661
  51.4 60.6 %all-gather.5.cloned.1.call-start = ((), (), s32[]{:S(2)}) async-start(), calls=%async_computation.10 | async-start | bytes 1474560 | tf_op jit(solution)/shard_map/all_gather | solution.py:715
  126.8 33.7 %all-to-all-start = ((bf16[8,160,768]{2,1,0:T(8,128)(2,1)}), bf16[8,160,768]{2,1,0:T(8,128)(2,1)S(1)}, u32[]{:S(2)}, u32[]{:S(2)}) async-start(bf16[8,160,768]{2,1,0:T(8,128)(2,1)} %bitcast.99), calls=%async_computation | async-start | bytes 3932160 | tf_op jit(solution)/shard_map/all_to_all | solution.py:661
  161.7 62.9 %all-to-all-start.4 = ((bf16[8,160,768]{2,1,0:T(8,128)(2,1)}), bf16[8,160,768]{2,1,0:T(8,128)(2,1)}, u32[]{:S(2)}, u32[]{:S(2)}) async-start(bf16[8,160,768]{2,1,0:T(8,128)(2,1)} %bitcast.98), calls=%async_computation.4 | async-start | bytes 3932160 | tf_op jit(solution)/shard_map/all_to_all | solution.py:661
  166.1 389.4 %reduce-scatter.4.cloned.1.call-start = ((), (), s32[]{:S(2)}) async-start(), calls=%async_computation.11 | async-start | bytes 11796480 | tf_op jit(solution)/shard_map/reduce_scatter | solution.py:657
  245.7 311.6 %reduce-scatter.8.cloned.1.call-start = ((), (), s32[]{:S(2)}) async-start(), calls=%async_computation.13 | async-start | bytes 5898240 | tf_op jit(solution)/shard_map/reduce_scatter | solution.py:657
  246.3 50.8 %all-to-all-start.3 = ((bf16[8,2,160,768]{3,2,1,0:T(8,128)(2,1)}), bf16[8,2,160,768]{3,2,1,0:T(8,128)(2,1)}, u32[]{:S(2)}, u32[]{:S(2)}) async-start(bf16[8,2,160,768]{3,2,1,0:T(8,128)(2,1)} %get-tuple-element.57), calls=%async_computation.3 | async-start | bytes 7864320 | tf_op jit(solution)/shard_map/all_to_all | solution.py:661
  297.1 50.8 %all-to-all-start.5 = ((bf16[8,2,160,768]{3,2,1,0:T(8,128)(2,1)}), bf16[8,2,160,768]{3,2,1,0:T(8,128)(2,1)}, u32[]{:S(2)}, u32[]{:S(2)}) async-start(bf16[8,2,160,768]{3,2,1,0:T(8,128)(2,1)} %get-tuple-element.62), calls=%async_computation.5 | async-start | bytes 7864320 | tf_op jit(solution)/shard_map/all_to_all | solution.py:661
  301.6 291.9 %reduce-scatter.6.cloned.1.call-start = ((), (), s32[]{:S(2)}) async-start(), calls=%async_computation.12 | async-start | bytes 5898240 | tf_op jit(solution)/shard_map/reduce_scatter | solution.py:657
  302.1 45.8 %copy-start.8 = (bf16[1024,768]{1,0:T(8,128)(2,1)S(1)}, bf16[1024,768]{1,0:T(8,128)(2,1)}, u32[]{:S(2)}) copy-start(bf16[1024,768]{1,0:T(8,128)(2,1)} %cot_ref.3) | copy-start | bytes 4718596
  433.1 35.5 %collective-permute-start.12 = (bf16[4,288,768]{2,1,0:T(8,128)(2,1)}, bf16[4,288,768]{2,1,0:T(8,128)(2,1)}, u32[]{:S(2)}, u32[]{:S(2)}) collective-permute-start(bf16[4,288,768]{2,1,0:T(8,128)(2,1)} %constant_dynamic-slice_fusion.2), channel_id=1, source_target_pairs={{0,4},{4,0},{8,12},{12,8},{16,20},{20,16},{24,28},{28,24},{1,5},{5... | collective-permute-start | bytes 5308424 | tf_op jit(solution)/shard_map/ppermute | solution.py:607
  463.4 2.6 collective-permute-start.3
  468.4 11.5 %collective-permute-start.4 = (bf16[4,64,768]{2,1,0:T(8,128)(2,1)}, bf16[4,64,768]{2,1,0:T(8,128)(2,1)}, u32[]{:S(2)}, u32[]{:S(2)}) collective-permute-start(bf16[4,64,768]{2,1,0:T(8,128)(2,1)} %constant_dynamic-slice_fusion.4), channel_id=1, source_target_pairs={{0,16},{4,20},{8,24},{12,28},{16,0},{20,4},{24,8},{28,12},{1,17},{... | collective-permute-start | bytes 1179656 | tf_op jit(solution)/shard_map/ppermute | solution.py:607
  472.8 26.2 %collective-permute-start.13 = (bf16[4,144,768]{2,1,0:T(8,128)(2,1)}, bf16[4,144,768]{2,1,0:T(8,128)(2,1)}, u32[]{:S(2)}, u32[]{:S(2)}) collective-permute-start(bf16[4,144,768]{2,1,0:T(8,128)(2,1)} %constant_dynamic-slice_fusion.1), channel_id=1, source_target_pairs={{0,8},{4,12},{8,0},{12,4},{16,24},{20,28},{24,16},{28,20},{1,9},{5... | collective-permute-start | bytes 2654216 | tf_op jit(solution)/shard_map/ppermute | solution.py:607
  481.0 17.9 %collective-permute-start.5 = (bf16[4,32,768]{2,1,0:T(8,128)(2,1)S(1)}, bf16[4,32,768]{2,1,0:T(8,128)(2,1)S(1)}, u32[]{:S(2)}, u32[]{:S(2)}) collective-permute-start(bf16[4,32,768]{2,1,0:T(8,128)(2,1)S(1)} %constant_dynamic-slice_fusion.3), channel_id=1, source_target_pairs={{0,8},{4,12},{8,0},{12,4},{16,24},{20,28},{24,16},{28,20},{1,9},{5... | collective-permute-start | bytes 589832 | tf_op jit(solution)/shard_map/ppermute | solution.py:607
  500.5 19.3 %collective-permute-start.14 = (bf16[4,72,768]{2,1,0:T(8,128)(2,1)S(1)}, bf16[4,72,768]{2,1,0:T(8,128)(2,1)S(1)}, u32[]{:S(2)}, u32[]{:S(2)}) collective-permute-start(bf16[4,72,768]{2,1,0:T(8,128)(2,1)S(1)} %constant_dynamic-slice_fusion), channel_id=1, source_target_pairs={{0,16},{4,20},{8,24},{12,28},{16,0},{20,4},{24,8},{28,12},{1,17},{... | collective-permute-start | bytes 1327112 | tf_op jit(solution)/shard_map/ppermute | solution.py:607
  502.1 6.0 collective-permute-start.6
  502.1 6.4 %collective-permute-start.8 = (bf16[32,768]{1,0:T(8,128)(2,1)S(1)}, bf16[32,768]{1,0:T(8,128)(2,1)S(1)}, u32[]{:S(2)}, u32[]{:S(2)}) collective-permute-start(bf16[32,768]{1,0:T(8,128)(2,1)S(1)} %get-tuple-element.96), channel_id=1, source_target_pairs={{0,3},{1,0},{2,1},{3,2},{4,7},{5,4},{6,5},{7,6},{8,11},{9,8},{10,9... | collective-permute-start | bytes 147464 | tf_op jit(solution)/shard_map/ppermute | solution.py:612
  505.9 8.8 %collective-permute-start.7 = (bf16[32,768]{1,0:T(8,128)(2,1)S(1)}, bf16[32,768]{1,0:T(8,128)(2,1)S(1)}, u32[]{:S(2)}, u32[]{:S(2)}) collective-permute-start(bf16[32,768]{1,0:T(8,128)(2,1)S(1)} %get-tuple-element.97), channel_id=1, source_target_pairs={{0,2},{1,3},{2,0},{3,1},{4,6},{5,7},{6,4},{7,5},{8,10},{9,11},{10,... | collective-permute-start | bytes 147464 | tf_op jit(solution)/shard_map/ppermute | solution.py:612
  514.8 4.2 collective-permute-start.9
  518.9 4.8 collective-permute-start.10
  519.9 9.9 %collective-permute-start.15 = (bf16[72,768]{1,0:T(8,128)(2,1)S(1)}, bf16[72,768]{1,0:T(8,128)(2,1)S(1)}, u32[]{:S(2)}, u32[]{:S(2)}) collective-permute-start(bf16[72,768]{1,0:T(8,128)(2,1)S(1)} %get-tuple-element.92), channel_id=1, source_target_pairs={{0,1},{1,2},{2,3},{3,0},{4,5},{5,6},{6,7},{7,4},{8,9},{9,10},{10,1... | collective-permute-start | bytes 331784 | tf_op jit(solution)/shard_map/ppermute | solution.py:612
  519.9 12.3 %collective-permute-start.17 = (bf16[72,768]{1,0:T(8,128)(2,1)S(1)}, bf16[72,768]{1,0:T(8,128)(2,1)S(1)}, u32[]{:S(2)}, u32[]{:S(2)}) collective-permute-start(bf16[72,768]{1,0:T(8,128)(2,1)S(1)} %get-tuple-element.93), channel_id=1, source_target_pairs={{0,3},{1,0},{2,1},{3,2},{4,7},{5,4},{6,5},{7,6},{8,11},{9,8},{10,9... | collective-permute-start | bytes 331784 | tf_op jit(solution)/shard_map/ppermute | solution.py:612
  523.7 17.5 %collective-permute-start.16 = (bf16[72,768]{1,0:T(8,128)(2,1)S(1)}, bf16[72,768]{1,0:T(8,128)(2,1)S(1)}, u32[]{:S(2)}, u32[]{:S(2)}) collective-permute-start(bf16[72,768]{1,0:T(8,128)(2,1)S(1)} %get-tuple-element.94), channel_id=1, source_target_pairs={{0,2},{1,3},{2,0},{3,1},{4,6},{5,7},{6,4},{7,5},{8,10},{9,11},{10,... | collective-permute-start | bytes 331784 | tf_op jit(solution)/shard_map/ppermute | solution.py:612
  523.8 19.0 %collective-permute-start.11 = (bf16[128,768]{1,0:T(8,128)(2,1)S(1)}, bf16[128,768]{1,0:T(8,128)(2,1)S(1)}, u32[]{:S(2)}, u32[]{:S(2)}) collective-permute-start(bf16[128,768]{1,0:T(8,128)(2,1)S(1)} %maximum_select_fusion.4), channel_id=1, source_target_pairs={{0,4},{4,0},{8,12},{12,8},{16,20},{20,16},{24,28},{28,24},{1,5},{5... | collective-permute-start | bytes 589832 | tf_op jit(solution)/shard_map/ppermute | solution.py:607
  541.3 4.8 collective-permute-start.18
  546.2 6.0 collective-permute-start.19
  552.3 1.9 collective-permute-start.20
  (48 other events, 450.7 us)
Sparse Core Ops, SparseCore 0:
  25.7 44.2 all-gather.2
  71.6 40.2 all-gather.4
  245.8 161.8 reduce-scatter.3
  410.5 86.2 reduce-scatter.7
  499.4 94.0 reduce-scatter.5

commit v3 on v2

--- a/solution.py
+++ b/solution.py
@@ -82,15 +82,18 @@
     )(slots, rows, *after)
 
 
-def dispatch_all_kernel(slots_ref, routes_ref, rows_ref, out_ref, other_ref, *, owners, capacity):
-    block, tokens = out_ref.shape[1], rows_ref.shape[0]
+def dispatch_all_kernel(slots_ref, routes_ref, rows_ref, *refs, owners, capacity):
+    out_refs, other_ref = refs[:-1], refs[-1]
+    block, tokens = len(out_refs) * capacity, rows_ref.shape[0]
     row = lax.broadcasted_iota(jnp.int32, (block, tokens), 0)
     slot = row + pl.program_id(0) * capacity
     for index in range(1, block // capacity):
         slot = slot + jnp.where(row >= index * capacity, (owners - 1) * capacity, 0)
     hits = [slot == slots_ref[c:c + 1, :] for c in range(2)]
     hot = jnp.where(hits[0] | hits[1], 1.0, 0.0).astype(jnp.bfloat16)
-    out_ref[0] = dot_nn(hot, rows_ref[...]).astype(out_ref.dtype)
+    picked = dot_nn(hot, rows_ref[...]).astype(rows_ref.dtype)
+    for index, out_ref in enumerate(out_refs):
+        out_ref[0] = picked[index * capacity:(index + 1) * capacity]
     other = jnp.where(hits[0], routes_ref[1:2, :], jnp.where(hits[1], routes_ref[0:1, :], 0.0))
     column = jnp.sum(other, axis=1, keepdims=True)
     other_ref[0] = jnp.broadcast_to(column, (block, 128)).T[0:1, :]
@@ -104,8 +107,8 @@
         partial(dispatch_all_kernel, owners=owners, capacity=capacity),
         grid=(owners,),
         in_specs=[whole(slots.shape), whole(routes.shape), whole(rows.shape)],
-        out_specs=[pl.BlockSpec((1, block, width), lambda i: (i, 0, 0)), pl.BlockSpec((1, 1, block), lambda i: (i, 0, 0))],
-        out_shape=[jax.ShapeDtypeStruct((owners, block, width), rows.dtype), jax.ShapeDtypeStruct((owners, 1, block), jnp.float32)],
+        out_specs=[pl.BlockSpec((1, capacity, width), lambda i: (i, 0, 0))] * local_count + [pl.BlockSpec((1, 1, block), lambda i: (i, 0, 0))],
+        out_shape=[jax.ShapeDtypeStruct((owners, capacity, width), rows.dtype)] * local_count + [jax.ShapeDtypeStruct((owners, 1, block), jnp.float32)],
         name="dispatch_all",
     )(slots, routes, rows)
 
@@ -136,7 +139,7 @@
         gate = own / (own + jnp.exp(other - top))
         column = jnp.broadcast_to(gate, (128, rows)).T
         for start in range(0, width, 128):
-            part = cot_ref[:, :, start:start + 128].reshape(rows, 128).astype(jnp.float32) * column
+            part = cot_ref[:, start:start + 128].astype(jnp.float32) * column
             grad_ref[:, start:start + 128] = part.astype(jnp.bfloat16)
     up = up_ref[0]
     for start in range(0, rows, chunk):
@@ -151,7 +154,6 @@
     rows, width = rows_in.shape
     hidden = up.shape[2]
     tile = hidden // shards
-    owners, _, capacity, _ = cot.shape
     fixed = pl.BlockSpec((rows, width), lambda i: (0, 0))
     column = pl.BlockSpec((rows, tile), lambda i: (0, i))
     chunk = chunk if rows % chunk == 0 else rows // 2
@@ -169,7 +171,7 @@
         in_specs=[
             pl.BlockSpec(memory_space=pltpu.SMEM),
             fixed,
-            pl.BlockSpec((owners, None, capacity, width), lambda i: (0, index, 0, 0)),
+            fixed,
             pl.BlockSpec((1, rows), lambda i: (0, 0)),
             pl.BlockSpec(router.shape, lambda i: (0, 0)),
             pl.BlockSpec((1, width, tile), lambda i: (index, 0, i)),
@@ -178,7 +180,7 @@
         out_specs=[column, column, pl.BlockSpec((1, tile, width), lambda i: (i, place, 0)), fixed],
         out_shape=[jax.ShapeDtypeStruct((rows, hidden), jnp.bfloat16)] * 2 + [grad_shape, jax.ShapeDtypeStruct((rows, width), jnp.bfloat16)],
         input_output_aliases=aliases,
-        compiler_params=pltpu.CompilerParams(vmem_limit_bytes=60 << 20),
+        compiler_params=pltpu.CompilerParams(vmem_limit_bytes=62 << 20),
         name="expert_first",
     )(*operands)
 
@@ -288,7 +290,7 @@
         in_specs=[small, small, small, rows, rows] + [returned_spec(part, 0) for part in returned],
         out_specs=[rows, pl.BlockSpec((block, 128), lambda i: (i, 0))],
         out_shape=[jax.ShapeDtypeStruct((tokens, width), jnp.bfloat16), jax.ShapeDtypeStruct((tokens, 128), jnp.bfloat16)],
-        compiler_params=pltpu.CompilerParams(vmem_limit_bytes=48 << 20),
+        compiler_params=pltpu.CompilerParams(vmem_limit_bytes=62 << 20),
         name="combine_out",
     )(slots, routes, gates, resid, cot, *returned)
 
@@ -327,7 +329,7 @@
         + [returned_spec(part, 1) for part in returned],
         out_specs=[rows, rows, rows, whole((1, width))],
         out_shape=[jax.ShapeDtypeStruct((tokens, width), jnp.float32), low, low, jax.ShapeDtypeStruct((1, width), jnp.float32)],
-        compiler_params=pltpu.CompilerParams(vmem_limit_bytes=48 << 20),
+        compiler_params=pltpu.CompilerParams(vmem_limit_bytes=62 << 20),
         name="combine_back",
     )(slots, logit, router, gain, resid, cot, merge, *returned)
 
@@ -404,7 +406,7 @@
         in_specs=[column, column, column, head_rows],
         out_specs=[column, pl.BlockSpec((1, heads, length), lambda g: (g, 0, 0))],
         out_shape=[jax.ShapeDtypeStruct((length, width), jnp.bfloat16), jax.ShapeDtypeStruct((groups, heads, length), jnp.float32)],
-        compiler_params=pltpu.CompilerParams(vmem_limit_bytes=48 << 20),
+        compiler_params=pltpu.CompilerParams(vmem_limit_bytes=62 << 20),
         name="attend",
     )(queries, keys, values, near)
 
@@ -486,33 +488,60 @@
         out_specs=[pl.BlockSpec((3, length, lanes), lambda g: (0, 0, g)), pl.BlockSpec((1, 2 * heads, block), lambda g: (g, 0, 0))],
         out_shape=[jax.ShapeDtypeStruct((3, length, width), jnp.bfloat16), jax.ShapeDtypeStruct((groups, 2 * heads, block), jnp.float32)],
         scratch_shapes=[pltpu.VMEM((length, lanes), jnp.float32)] * 2,
-        compiler_params=pltpu.CompilerParams(vmem_limit_bytes=56 << 20),
+        compiler_params=pltpu.CompilerParams(vmem_limit_bytes=62 << 20),
         name="attend_back",
     )(queries, keys, values, grads, outs, totals, near)
 
 
-def project_kernel(inputs_ref, gain_ref, query_ref, key_ref, value_ref, low_ref, *out_refs, eps):
+def reverse_bits(value, count):
+    out = value * 0
+    for level in range(count):
+        out = out * 2 + (value >> level) % 2
+    return out
+
+
+def project_kernel(owner_ref, inputs_ref, gain_ref, *refs, eps):
+    piece_refs, weight_refs, low_ref, out_refs = refs[:4], refs[4:7], refs[7], refs[8:]
+    count, half, three, _ = piece_refs[0].shape
+    piece = three // 3
+    owners = 2 * count
+    part = owners * piece
+    @pl.when(pl.program_id(0) == 0)
+    def _():
+        me = owner_ref[0]
+        for source in range(owners):
+            apart = jnp.bitwise_xor(me, source)
+            near = apart % 2 == 0
+            place = apart // 2
+            places = (place, reverse_bits(place, owners.bit_length() - 2))
+            for group in range(2):
+                for line in range(half):
+                    block = jnp.where(near, piece_refs[2 * group][places[group], line], piece_refs[2 * group + 1][places[group], line])
+                    start = (group * half + line) * part + source * piece
+                    for index in range(3):
+                        weight_refs[index][start:start + piece, :] = block[index * piece:(index + 1) * piece]
     rows = inputs_ref[...].astype(jnp.float32)
     inverse = lax.rsqrt(jnp.mean(rows * rows, axis=1, keepdims=True) + eps)
     low = (rows * inverse * gain_ref[...]).astype(jnp.bfloat16)
     low_ref[...] = low
-    for weight_ref, out_ref in zip((query_ref, key_ref, value_ref), out_refs):
+    for weight_ref, out_ref in zip(weight_refs, out_refs):
         out_ref[...] = dot_nn(low, weight_ref[...]).astype(jnp.bfloat16)
 
 
-def project(inputs, gain, query, key, value, eps, block=256):
+def project(owner, inputs, gain, pieces, eps, block=256):
     tokens, width = inputs.shape
     rows = pl.BlockSpec((block, width), lambda i: (i, 0))
-    whole = lambda shape: pl.BlockSpec(shape, lambda i: (0, 0))
+    whole = lambda shape: pl.BlockSpec(shape, lambda i: (0,) * len(shape))
+    weight = jax.ShapeDtypeStruct((width, width), jnp.bfloat16)
     return pl.pallas_call(
         partial(project_kernel, eps=eps),
         grid=(tokens // block,),
-        in_specs=[rows, whole(gain.shape)] + [whole(query.shape)] * 3,
-        out_specs=[rows] * 4,
-        out_shape=[jax.ShapeDtypeStruct((tokens, width), jnp.bfloat16)] * 4,
-        compiler_params=pltpu.CompilerParams(vmem_limit_bytes=40 << 20),
+        in_specs=[pl.BlockSpec(memory_space=pltpu.SMEM), rows, whole(gain.shape)] + [whole(piece.shape) for piece in pieces],
+        out_specs=[whole(weight.shape)] * 3 + [rows] * 4,
+        out_shape=[weight] * 3 + [jax.ShapeDtypeStruct((tokens, width), jnp.bfloat16)] * 4,
+        compiler_params=pltpu.CompilerParams(vmem_limit_bytes=62 << 20),
         name="project",
-    )(inputs, gain, query, key, value)
+    )(owner, inputs, gain, *pieces)
 
 
 def settle_kernel(mixed_ref, merge_ref, inputs_ref, gain_ref, router_ref, routes_ref, resid_ref, low_ref, gates_ref, *, eps):
@@ -542,7 +571,7 @@
         in_specs=[rows, whole(merge.shape), rows, whole(gain.shape), whole(router.shape), small],
         out_specs=[rows, rows, small],
         out_shape=[jax.ShapeDtypeStruct((tokens, width), jnp.float32), jax.ShapeDtypeStruct((tokens, width), jnp.bfloat16), jax.ShapeDtypeStruct((2, tokens), jnp.float32)],
-        compiler_params=pltpu.CompilerParams(vmem_limit_bytes=40 << 20),
+        compiler_params=pltpu.CompilerParams(vmem_limit_bytes=62 << 20),
         name="settle",
     )(mixed, merge, inputs, gain, router, routes)
 
@@ -571,7 +600,7 @@
         in_specs=[pl.BlockSpec((3, block, width), lambda i: (0, i, 0))] + [whole(query.shape)] * 3 + [whole(gain.shape), rows, rows],
         out_specs=[rows, whole((1, width))],
         out_shape=[jax.ShapeDtypeStruct((tokens, width), jnp.float32), jax.ShapeDtypeStruct((1, width), jnp.float32)],
-        compiler_params=pltpu.CompilerParams(vmem_limit_bytes=40 << 20),
+        compiler_params=pltpu.CompilerParams(vmem_limit_bytes=62 << 20),
         name="finish",
     )(head_grads, query, key, value, gain, inputs, resid_grad)
 
@@ -597,7 +626,7 @@
         out_specs=pl.BlockSpec((shards, part, width), lambda i: (0, i, 0)),
         out_shape=jax.ShapeDtypeStruct((shards, count * part, width), jnp.bfloat16),
         scratch_shapes=[pltpu.VMEM((width, tokens), jnp.bfloat16)],
-        compiler_params=pltpu.CompilerParams(vmem_limit_bytes=40 << 20),
+        compiler_params=pltpu.CompilerParams(vmem_limit_bytes=62 << 20),
         name="weight_grads",
     )(left, right)
 
@@ -618,7 +647,8 @@
     out = jnp.zeros((count,) + rows.shape, rows.dtype)
     out = lax.dynamic_update_index_in_dim(out, rows, me, 0)
     for step in range(1, count):
-        out = lax.dynamic_update_index_in_dim(out, shift(rows, step), (me - step) % count, 0)
+        got = shift(rows, step)
+        out = lax.dynamic_update_index_in_dim(out, got, (me - step) % count, 0)
     return out
 
 
@@ -693,7 +723,6 @@
     rows = owners * capacity
     assert local_count == 2 and hidden // shards == width
 
-    small_rows = 8 * owners
     router_at = 2 + local_heads + (-(2 + local_heads)) % 8
 
     def widen(block):
@@ -702,24 +731,25 @@
     def pack(gain_one, gain_two, table, router):
         head = jnp.concatenate([gain_one, gain_two], axis=0)
         gap = jnp.zeros((router_at - 2 - local_heads, width), bf16)
-        rest = jnp.zeros((small_rows - router_at - experts, width), bf16)
-        return jnp.concatenate([widen(head), widen(table), gap, widen(router), rest], axis=0)
+        return jnp.concatenate([widen(head), widen(table), gap, widen(router)], axis=0)
 
     small = pack(norm_gain[None], expert_gain[None], bias_table.T, router_weight.T)
     slices = [
         lax.dynamic_slice_in_dim(weight, me * piece, piece, 0)
         for weight in (query_weight, key_weight, value_weight)
-    ] + [lax.dynamic_slice_in_dim(small, me * 8, 8, 0)]
-    lined = gather_line(jnp.concatenate(slices))
-    gathered = lax.all_gather(lined, "expert", axis=0, tiled=False)
+    ]
+    lined = gather_line(jnp.concatenate(slices + [small]))
+    small_full = lined[:, 3 * piece :]
+    bits = [1 << level for level in range(owners.bit_length() - 1)]
+    pieces = []
+    for index, order in enumerate((bits[1:], bits[:0:-1])):
+        held = lined[index * shards // 2 : (index + 1) * shards // 2, : 3 * piece][None]
+        for bit in order:
+            got = exchange(held, bit)
+            held = jnp.concatenate([held, got])
+        pieces += [held, exchange(held, bits[0])]
     merge_full = lax.all_gather(merge_weight, "shard", axis=0, tiled=True)
 
-    def whole_weight(index):
-        block = gathered[:, :, index * piece : (index + 1) * piece]
-        return block.transpose(1, 0, 2, 3).reshape(width, width)
-
-    query_full, key_full, value_full = (whole_weight(index) for index in range(3))
-    small_full = gathered[:, :, 3 * piece :].transpose(1, 0, 2, 3).reshape(shards, small_rows, width)
     gain_one = small_full[:, 0, :part].reshape(1, width).astype(f32)
     gain_two = small_full[:, 1, :part].reshape(1, width).astype(f32)
     table_full = small_full[:, 2 : 2 + local_heads, :BUCKETS].reshape(heads, BUCKETS).astype(f32)
@@ -729,15 +759,16 @@
     routes_line = routes.T
     base = (routes_line % local_count * owners + routes_line // local_count) * capacity
     slots = find_slots(routes_line, base, experts)
-    cot_rows, other = dispatch_all(
+    *cot_rows, other = dispatch_all(
         slots, routes_line.astype(f32), cotangent, owners, capacity, local_count
     )
     other = share_rows(other).reshape(owners, local_count, capacity)
 
-    low_one, queries, keys, values = project(
-        inputs, gain_one, query_full, key_full, value_full, epsilon
-    )
-    cot_in = share_rows(cot_rows).reshape(owners, local_count, capacity, width)
+    owner = me.astype(jnp.int32).reshape(1)
+    query_full, key_full, value_full, low_one, queries, keys, values = project(owner, inputs, gain_one, pieces, epsilon)
+    cot_in = []
+    for index in range(local_count):
+        cot_in.append(share_rows(cot_rows[index]).reshape(rows, width))
     block = 256
     hot = bucket_hot(tokens)
     assert hot[block:, -1].all()
@@ -750,7 +781,6 @@
         attended, merge_full, inputs, gain_two, router_full, routes_line, epsilon
     )
 
-    owner = me.astype(jnp.int32).reshape(1)
     sends, rows_in = [], []
     for index in range(local_count):
         sends.append(dispatch(slots, low_two, index * rows, rows))
@@ -758,7 +788,7 @@
         rows_in.append(send.reshape(rows, width))
     others = [other[:, index].reshape(1, rows) for index in range(local_count)]
     act, slope, first_down, grad_in = expert_first(
-        owner, rows_in[0], cot_in, others[0], router_full, up_weight, 0, local_count, shards,
+        owner, rows_in[0], cot_in[0], others[0], router_full, up_weight, 0, local_count, shards,
         after=(sends[1],),
     )
     first_sum = scatter_sum(first_down)
@@ -766,7 +796,7 @@
         rows_in[0], grad_in, act, slope, up_weight, down_weight, 0, owners, shards, 2 * width
     )
     act, slope, pair, grad_in = expert_first(
-        owner, rows_in[1], cot_in, others[1], router_full, up_weight, 1, local_count, shards,
+        owner, rows_in[1], cot_in[1], others[1], router_full, up_weight, 1, local_count, shards,
         into=pair,
     )
     pair_sum = scatter_sum(pair)
@@ -801,8 +831,9 @@
         table_grad.reshape(shards, local_heads, BUCKETS).astype(bf16),
         router_grad[:experts].reshape(experts, shards, part).transpose(1, 0, 2).astype(bf16),
     )
-    bits = [1 << level for level in range(owners.bit_length() - 1)]
     head_sums = reduce_stack(head_sums, bits).astype(f32)
+    spare = -small_grad.shape[1] % (8 * owners)
+    small_grad = jnp.pad(small_grad, ((0, 0), (0, spare), (0, 0)))
     rest_sums = jnp.concatenate([merge_grad, small_grad], axis=1)
     rest_sums = reduce_stack(rest_sums, bits[:1] + bits[:0:-1]).astype(f32)
     small_sum = rest_sums[part:]

time: 614 us -> 632 us (1.029)
  local copies, waits for them, and re-layouts: 67.3 us -> 29.9 us
  waiting for transfers between devices: 202 us -> 229 us
  Pallas kernels: 244 us -> 261 us
  starting transfers between devices: 48.6 us -> 63.8 us
  blocking collectives: 8.45 us -> 0 us
    ppermute x12 -> x18, waiting for transfers between devices: 38.7 us -> 66.5 us  [exchange(): return lax.ppermute(rows, 'expert', [(i, i ^ bit) for i in range(count)])]
    unnamed x98 -> x46, local copies, waits for them, and re-layouts: 25.5 us -> 6.55 us
    all_gather x1 -> x0, waiting for transfers between devices: 17.9 us -> none  [local(): gathered = lax.all_gather(lined, 'expert', axis=0, tiled=False)]
    ppermute x12 -> x18, starting transfers between devices: 5.48 us -> 20.4 us  [exchange(): return lax.ppermute(rows, 'expert', [(i, i ^ bit) for i in range(count)])]
    reduce_scatter x3, waiting for transfers between devices: 32.4 us -> 46.6 us  [scatter_sum(): return lax.psum_scatter(grads, 'shard', scatter_dimension=0, tiled=True)]
    concatenate x2, local copies, waits for them, and re-layouts: 11.8 us -> 0.11 us  [the longest x1 0.08 us: pack(): jnp.concatenate([widen(head), widen(table), gap, widen(router)], axis=0)]
    all_to_all x1 -> x0, blocking collectives: 8.45 us -> none  [share_rows(): return lax.all_to_all(rows, 'expert', 0, 0, tiled=True)]
    all_to_all x5 -> x7, waiting for transfers between devices: 73.9 us -> 80.1 us  [share_rows(): return lax.all_to_all(rows, 'expert', 0, 0, tiled=True)]
  transfers between devices with their start and end apart: 31 -> 38, of which waited for: 21 -> 21; matrix products, arithmetic and copies ran while one was open for 9% -> 7% of each run, Pallas kernels for 37% -> 37%
where the time goes in v3:
time: 632 us; the launch traced here: 623 us
  Pallas kernels  261 us (41%)
  waiting for transfers between devices  229 us (36%)
  starting transfers between devices  63.8 us (10%)
  local copies, waits for them, and re-layouts  29.9 us (5%)
  other arithmetic  22.9 us (4%)
  between operations  14.5 us (2%)
    all_to_all x7, waiting for transfers between devices, share_rows(): return lax.all_to_all(rows, 'expert', 0, 0, tiled=True)  80.1 us
    pallas_call x2, Pallas kernels, expert_second(): pl.pallas_call(second_kernel, grid=(shards,), in_specs=[fixed, fixed, col...  73.1 us
    ppermute x18, waiting for transfers between devices, exchange(): return lax.ppermute(rows, 'expert', [(i, i ^ bit) for i in range(count)])  66.5 us
    reduce_scatter x3, waiting for transfers between devices, scatter_sum(): return lax.psum_scatter(grads, 'shard', scatter_dimension=0, tiled=True)  46.6 us
    pallas_call x2, Pallas kernels, expert_first(): pl.pallas_call(partial(first_kernel, chunk=chunk, index=index, local_coun...  41.8 us
    pallas_call x1, Pallas kernels, attend_back(): pl.pallas_call(partial(attend_back_kernel, block=block, size=size, scale=...  35.8 us
    ppermute x9, waiting for transfers between devices, shift(): lax.ppermute(rows, 'shard', [(i, (i + step) % count) for i in range(count)])  35.4 us
    all_to_all x7, starting transfers between devices, share_rows(): return lax.all_to_all(rows, 'expert', 0, 0, tiled=True)  29.4 us
  transfers between devices with their start and end apart: 38, of which 21 were waited for; matrix products, arithmetic and copies ran while one was open for 7% of the time, Pallas kernels for 37%

profile of v3, /device:TPU:0, one launch (start us, length us, event | category | flops | bytes accessed | tf_op | source)
XLA Modules:
  0.0 622.8 jit_solution(11707977518591023097)
XLA Ops:
  11.5 9.7 %dispatch_all.1 = (bf16[8,160,768]{2,1,0:T(8,128)(2,1)}, bf16[8,160,768]{2,1,0:T(8,128)(2,1)}, f32[8,1,320]{2,1,0:T(1,128)}) custom-call(s32[2,1024]{1,0:T(2,128)} %find_slots.1.slots_ref, f32[2,1024]{1,0:T(2,128)} %bitcast_convert_fusion.routes_ref, bf16[1024,768]{1,0:T(8,128)(2,1)} %cot_ref.3), custom_call_target="tpu_custom_call" | custom-call | tf_op jit(solution)/shard_map/dispatch_all/pallas_call | solution.py:106
  21.2 5.2 all-to-all-start.2
  31.1 4.3 all-to-all-start.1
  41.2 9.8 %collective-permute-done = bf16[96,768]{1,0:T(8,128)(2,1)S(1)} collective-permute-done((bf16[96,768]{1,0:T(8,128)(2,1)S(1)}, bf16[96,768]{1,0:T(8,128)(2,1)S(1)}, u32[]{:S(2)}, u32[]{:S(2)}) %collective-permute-start) | collective-permute-done | bytes 147488 | tf_op jit(solution)/shard_map/ppermute | solution.py:641
  56.4 4.9 all-to-all-done.1
  68.6 30.0 %collective-permute-done.4 = bf16[2,2,72,768]{3,2,1,0:T(8,128)(2,1)S(1)} collective-permute-done((bf16[2,2,72,768]{3,2,1,0:T(8,128)(2,1)S(1)}, bf16[2,2,72,768]{3,2,1,0:T(8,128)(2,1)S(1)}, u32[]{:S(2)}, u32[]{:S(2)}) %collective-permute-start.4) | collective-permute-done | bytes 442400 | tf_op jit(solution)/shard_map/ppermute | solution.py:636
  107.3 8.5 %project.1 = (bf16[768,768]{1,0:T(8,128)(2,1)}, bf16[768,768]{1,0:T(8,128)(2,1)}, bf16[768,768]{1,0:T(8,128)(2,1)}, bf16[1024,768]{1,0:T(8,128)(2,1)}, bf16[1024...) custom-call(s32[1]{0:T(128)} %bitcast.1.owner_ref, bf16[1024,768]{1,0:T(8,128)(2,1)} %inputs_ref.5, ...), custom_call_target="tpu_custom_call" | custom-call | tf_op jit(solution)/shard_map/project/pallas_call | solution.py:536
  115.7 22.6 %attend.1 = (bf16[1024,768]{1,0:T(8,128)(2,1)}, f32[6,2,1024]{2,1,0:T(2,128)}) custom-call(bf16[1024,768]{1,0:T(8,128)(2,1)} %get-tuple-element.49.query_ref, bf16[1024,768]{1,0:T(8,128)(2,1)} %get-tuple-element.50.key_ref, bf16[1024,768]{1,0:T(8,128)(2,1)} %get-tuple-element.51.value_ref, f32[6,2,256]{2,1,0:T(2,128)} %copy.36.near_ref), custom_call_target="tpu_custom_call" | custom-call | tf_op jit(solution)/shard_map/attend/pallas_call | solution.py:403
  138.3 6.3 %settle.1 = (f32[1024,768]{1,0:T(8,128)}, bf16[1024,768]{1,0:T(8,128)(2,1)}, f32[2,1024]{1,0:T(2,128)}) custom-call(bf16[1024,768]{1,0:T(8,128)(2,1)} %get-tuple-element.52.mixed_ref.out_ref.left_ref, bf16[768,768]{1,0:T(8,128)(2,1)} %all-gather.2.cloned.1.call-done.merge_ref, bf16[1024,768]{1,0:T(8,128)(2,1)} %inputs_ref.5, f32[1,768]{1,0:T(1,128)} %reshape.149.gain_ref, ...), custom_call_target="tpu_custom_call" | custom-call | tf_op jit(solution)/shard_map/settle/pallas_call | solution.py:568
  144.7 5.6 dispatch.2
  155.1 5.6 dispatch.3.refs_0_
  160.7 19.5 %all-to-all-done = bf16[8,160,768]{2,1,0:T(8,128)(2,1)S(1)} async-done(((bf16[8,160,768]{2,1,0:T(8,128)(2,1)}), bf16[8,160,768]{2,1,0:T(8,128)(2,1)S(1)}, u32[]{:S(2)}, u32[]{:S(2)}) %all-to-all-start) | async-done | bytes 1966112 | tf_op jit(solution)/shard_map/all_to_all | solution.py:691
  186.9 20.7 %expert_first.2 = (bf16[1280,3072]{1,0:T(8,128)(2,1)}, bf16[1280,3072]{1,0:T(8,128)(2,1)}, bf16[4,768,768]{2,1,0:T(8,128)(2,1)}, bf16[1280,768]{1,0:T(8,128)(2,1)}) custom-call(s32[1]{0:T(128)} %bitcast.1.owner_ref, bf16[1280,768]{1,0:T(8,128)(2,1)} %bitcast.72, bf16[1280,768]{1,0:T(8,128)(2,1)} %bitcast.14.cot_ref, f32[1,1280]{1,0:T(1,128)} %reshape_squeeze.8.other_ref, ...), custom_call_target="tpu_custom_call" | custom-call | tf_op jit(solution)/shard_map/expert_first/pallas_call | solution.py:168
  207.6 36.1 %expert_second.2 = (bf16[8,2,160,768]{3,2,1,0:T(8,128)(2,1)}, bf16[4,1536,768]{2,1,0:T(8,128)(2,1)}) custom-call(bf16[1280,768]{1,0:T(8,128)(2,1)} %bitcast.73, bf16[1280,768]{1,0:T(8,128)(2,1)} %get-tuple-element.58.grad_ref, bf16[1280,3072]{1,0:T(8,128)(2,1)} %get-tuple-element.59.act_ref, bf16[1280,3072]{1,0:T(8,128)(2,1)} %get-tuple-element.60.slope_ref, ...), custom_call_target="tpu_custom_call" | custom-call | tf_op jit(solution)/shard_map/expert_second/pallas_call | solution.py:224
  245.0 21.0 %expert_first.3 = (bf16[1280,3072]{1,0:T(8,128)(2,1)}, bf16[1280,3072]{1,0:T(8,128)(2,1)}, bf16[4,1536,768]{2,1,0:T(8,128)(2,1)}, bf16[1280,768]{1,0:T(8,128)(2,1)}) custom-call(s32[1]{0:T(128)} %bitcast.1.owner_ref, bf16[1280,768]{1,0:T(8,128)(2,1)} %bitcast.70, bf16[1280,768]{1,0:T(8,128)(2,1)} %bitcast.76, ...), custom_call_target="tpu_custom_call", output_to_operand_aliasing={{2}: (6, {})} | custom-call | tf_op jit(solution)/shard_map/expert_first/pallas_call | solution.py:168
  266.8 4.5 all-to-all-start.3
  271.3 37.0 %expert_second.3 = (bf16[8,2,160,768]{3,2,1,0:T(8,128)(2,1)}, bf16[4,768,768]{2,1,0:T(8,128)(2,1)}) custom-call(bf16[1280,768]{1,0:T(8,128)(2,1)} %bitcast.71, bf16[1280,768]{1,0:T(8,128)(2,1)} %get-tuple-element.64.grad_ref, bf16[1280,3072]{1,0:T(8,128)(2,1)} %get-tuple-element.65.act_ref, bf16[1280,3072]{1,0:T(8,128)(2,1)} %get-tuple-element.66.slope_ref, ...), custom_call_target="tpu_custom_call" | custom-call | tf_op jit(solution)/shard_map/expert_second/pallas_call | solution.py:224
  308.3 9.3 %all-to-all-done.3.refs_0_ = bf16[8,2,160,768]{3,2,1,0:T(8,128)(2,1)} async-done(((bf16[8,2,160,768]{3,2,1,0:T(8,128)(2,1)}), bf16[8,2,160,768]{3,2,1,0:T(8,128)(2,1)}, u32[]{:S(2)}, u32[]{:S(2)}) %all-to-all-start.3) | async-done | bytes 3932192 | tf_op jit(solution)/shard_map/all_to_all | solution.py:691
  317.6 4.5 all-to-all-start.6
  324.1 44.4 %all-to-all-done.6.refs_1_ = bf16[8,2,160,768]{3,2,1,0:T(8,128)(2,1)} async-done(((bf16[8,2,160,768]{3,2,1,0:T(8,128)(2,1)}), bf16[8,2,160,768]{3,2,1,0:T(8,128)(2,1)}, u32[]{:S(2)}, u32[]{:S(2)}) %all-to-all-start.6) | async-done | bytes 3932192 | tf_op jit(solution)/shard_map/all_to_all | solution.py:691
  368.5 13.2 %combine_out.1 = (bf16[1024,768]{1,0:T(8,128)(2,1)}, bf16[1024,128]{1,0:T(8,128)(2,1)}) custom-call(s32[2,1024]{1,0:T(2,128)} %find_slots.1.slots_ref, s32[2,1024]{1,0:T(2,128)} %bitcast.84, f32[2,1024]{1,0:T(2,128)} %get-tuple-element.53.gates_ref, f32[1024,768]{1,0:T(8,128)} %get-tuple-element.54.resid_ref, bf16[1024,768]{1,0:T(8,128)(2,1)} %cot_ref.3, ...), custom_call_target="tpu_custom_call" | custom-call | tf_op jit(solution)/shard_map/combine_out/pallas_call | solution.py:287
  383.0 14.2 %combine_back.1 = (f32[1024,768]{1,0:T(8,128)}, bf16[1024,768]{1,0:T(8,128)(2,1)}, bf16[1024,768]{1,0:T(8,128)(2,1)}, f32[1,768]{1,0:T(1,128)}) custom-call(s32[2,1024]{1,0:T(2,128)} %find_slots.1.slots_ref, bf16[1024,128]{1,0:T(8,128)(2,1)} %get-tuple-element.69.logit_ref, bf16[128,768]{1,0:T(8,128)(2,1)} %pad.35.router_ref, f32[1,768]{1,0:T(1,128)} %reshape.149.gain_ref, ...), custom_call_target="tpu_custom_call" | custom-call | tf_op jit(solution)/shard_map/combine_back/pallas_call | solution.py:325
  401.5 35.8 %attend_back.1 = (bf16[3,1024,768]{2,1,0:T(8,128)(2,1)}, f32[6,4,256]{2,1,0:T(4,128)}) custom-call(bf16[1024,768]{1,0:T(8,128)(2,1)} %get-tuple-element.49.query_ref, bf16[1024,768]{1,0:T(8,128)(2,1)} %get-tuple-element.50.key_ref, bf16[1024,768]{1,0:T(8,128)(2,1)} %get-tuple-element.51.value_ref, bf16[1024,768]{1,0:T(8,128)(2,1)} %get-tuple-element.70.grad_ref, ...), custom_call_target="tpu_custom_call" | custom-call | tf_op jit(solution)/shard_map/attend_back/pallas_call | solution.py:484
  438.3 10.4 %finish.1 = (f32[1024,768]{1,0:T(8,128)}, f32[1,768]{1,0:T(1,128)}) custom-call(bf16[3,1024,768]{2,1,0:T(8,128)(2,1)} %get-tuple-element.72.heads_ref.right_ref, bf16[768,768]{1,0:T(8,128)(2,1)} %get-tuple-element.73.query_ref, bf16[768,768]{1,0:T(8,128)(2,1)} %get-tuple-element.74.key_ref, bf16[768,768]{1,0:T(8,128)(2,1)} %get-tuple-element.75.value_ref, ...), custom_call_target="tpu_custom_call" | custom-call | tf_op jit(solution)/shard_map/finish/pallas_call | solution.py:597
  450.0 8.1 %weight_grads.3 = bf16[4,576,768]{2,1,0:T(8,128)(2,1)} custom-call(bf16[1024,768]{1,0:T(8,128)(2,1)} %get-tuple-element.82.left_ref, bf16[3,1024,768]{2,1,0:T(8,128)(2,1)} %get-tuple-element.72.heads_ref.right_ref), custom_call_target="tpu_custom_call" | custom-call | tf_op jit(solution)/shard_map/weight_grads/pallas_call | solution.py:622
  475.2 6.4 %collective-permute-done.10 = bf16[4,64,768]{2,1,0:T(8,128)(2,1)} collective-permute-done((bf16[4,64,768]{2,1,0:T(8,128)(2,1)}, bf16[4,64,768]{2,1,0:T(8,128)(2,1)}, u32[]{:S(2)}, u32[]{:S(2)}) %collective-permute-start.10) | collective-permute-done | bytes 393248 | tf_op jit(solution)/shard_map/ppermute | solution.py:636
  483.7 17.4 %collective-permute-done.11 = bf16[4,32,768]{2,1,0:T(8,128)(2,1)S(1)} collective-permute-done((bf16[4,32,768]{2,1,0:T(8,128)(2,1)S(1)}, bf16[4,32,768]{2,1,0:T(8,128)(2,1)S(1)}, u32[]{:S(2)}, u32[]{:S(2)}) %collective-permute-start.11) | collective-permute-done | bytes 196640 | tf_op jit(solution)/shard_map/ppermute | solution.py:636
  512.9 6.2 collective-permute-done.13
  532.8 9.0 %collective-permute-done.22 = bf16[72,768]{1,0:T(8,128)(2,1)S(1)} collective-permute-done((bf16[72,768]{1,0:T(8,128)(2,1)S(1)}, bf16[72,768]{1,0:T(8,128)(2,1)S(1)}, u32[]{:S(2)}, u32[]{:S(2)}) %collective-permute-start.22) | collective-permute-done | bytes 110624 | tf_op jit(solution)/shard_map/ppermute | solution.py:641
  541.9 6.1 collective-permute-start.24
  551.5 5.3 collective-permute-done.25
  565.8 46.5 %reduce-scatter.6.cloned.1.call-done = bf16[768,768]{1,0:T(8,128)(2,1)} async-done(((bf16[3072,768]{1,0:T(8,128)(2,1)}), bf16[768,768]{1,0:T(8,128)(2,1)}) %reduce-scatter.6.cloned.1.call-update) | async-done | bytes 1179664 | tf_op jit(solution)/shard_map/reduce_scatter | solution.py:687
  (197 shorter events, 120.0 us)
Async XLA Ops:
  21.2 9.9 %all-to-all-start.2 = ((f32[8,1,320]{2,1,0:T(1,128)}), f32[8,1,320]{2,1,0:T(1,128)S(1)}, u32[]{:S(2)}, u32[]{:S(2)}) async-start(f32[8,1,320]{2,1,0:T(1,128)} %get-tuple-element.57), calls=%async_computation.2 | async-start | bytes 24576 | tf_op jit(solution)/shard_map/all_to_all | solution.py:691
  31.1 30.2 %all-to-all-start.1 = ((bf16[8,160,768]{2,1,0:T(8,128)(2,1)}), bf16[8,160,768]{2,1,0:T(8,128)(2,1)}, u32[]{:S(2)}, u32[]{:S(2)}) async-start(bf16[8,160,768]{2,1,0:T(8,128)(2,1)} %get-tuple-element.56), calls=%async_computation.1 | async-start | bytes 3932160 | tf_op jit(solution)/shard_map/all_to_all | solution.py:691
  35.5 102.8 %all-gather.2.cloned.1.call-start = ((), (), s32[]{:S(2)}) async-start(), calls=%async_computation.10 | async-start | bytes 1474560 | tf_op jit(solution)/shard_map/all_gather | solution.py:751
  36.4 16.7 %collective-permute-start.2 = (bf16[96,768]{1,0:T(8,128)(2,1)S(1)}, bf16[96,768]{1,0:T(8,128)(2,1)S(1)}, u32[]{:S(2)}, u32[]{:S(2)}) collective-permute-start(bf16[96,768]{1,0:T(8,128)(2,1)S(1)} %concatenate.66), channel_id=1, source_target_pairs={{0,3},{1,0},{2,1},{3,2},{4,7},{5,4},{6,5},{7,6},{8,11},{9,8},{10,9... | collective-permute-start | bytes 442376 | tf_op jit(solution)/shard_map/ppermute | solution.py:641
  40.1 13.0 %collective-permute-start.1 = (bf16[96,768]{1,0:T(8,128)(2,1)S(1)}, bf16[96,768]{1,0:T(8,128)(2,1)S(1)}, u32[]{:S(2)}, u32[]{:S(2)}) collective-permute-start(bf16[96,768]{1,0:T(8,128)(2,1)S(1)} %concatenate.66), channel_id=1, source_target_pairs={{0,2},{1,3},{2,0},{3,1},{4,6},{5,7},{6,4},{7,5},{8,10},{9,11},{10,... | collective-permute-start | bytes 442376 | tf_op jit(solution)/shard_map/ppermute | solution.py:641
  40.1 10.9 %collective-permute-start = (bf16[96,768]{1,0:T(8,128)(2,1)S(1)}, bf16[96,768]{1,0:T(8,128)(2,1)S(1)}, u32[]{:S(2)}, u32[]{:S(2)}) collective-permute-start(bf16[96,768]{1,0:T(8,128)(2,1)S(1)} %concatenate.66), channel_id=1, source_target_pairs={{0,1},{1,2},{2,3},{3,0},{4,5},{5,6},{6,7},{7,4},{8,9},{9,10},{10,1... | collective-permute-start | bytes 442376 | tf_op jit(solution)/shard_map/ppermute | solution.py:641
  53.2 11.7 %collective-permute-start.3 = (bf16[1,2,72,768]{3,2,1,0:T(8,128)(2,1)S(1)}, bf16[1,2,72,768]{3,2,1,0:T(8,128)(2,1)S(1)}, u32[]{:S(2)}, u32[]{:S(2)}) collective-permute-start(bf16[1,2,72,768]{3,2,1,0:T(8,128)(2,1)S(1)} %get-tuple-element.98), channel_id=1, source_target_pairs={{0,8},{4,12},{8,0},{12,4},{16,24},{20,28},{24,16},{28,20},{1,9},{5... | collective-permute-start | bytes 663560 | tf_op jit(solution)/shard_map/ppermute | solution.py:636
  54.9 12.1 %collective-permute-start.6 = (bf16[1,2,72,768]{3,2,1,0:T(8,128)(2,1)S(1)}, bf16[1,2,72,768]{3,2,1,0:T(8,128)(2,1)S(1)}, u32[]{:S(2)}, u32[]{:S(2)}) collective-permute-start(bf16[1,2,72,768]{3,2,1,0:T(8,128)(2,1)S(1)} %get-tuple-element.97), channel_id=1, source_target_pairs={{0,16},{4,20},{8,24},{12,28},{16,0},{20,4},{24,8},{28,12},{1,17},{... | collective-permute-start | bytes 663560 | tf_op jit(solution)/shard_map/ppermute | solution.py:636
  61.3 88.9 %all-to-all-start.5 = ((bf16[8,160,768]{2,1,0:T(8,128)(2,1)}), bf16[8,160,768]{2,1,0:T(8,128)(2,1)S(1)}, u32[]{:S(2)}, u32[]{:S(2)}) async-start(bf16[8,160,768]{2,1,0:T(8,128)(2,1)} %get-tuple-element.62), calls=%async_computation.5 | async-start | bytes 3932160 | tf_op jit(solution)/shard_map/all_to_all | solution.py:691
  65.0 33.6 %collective-permute-start.4 = (bf16[2,2,72,768]{3,2,1,0:T(8,128)(2,1)S(1)}, bf16[2,2,72,768]{3,2,1,0:T(8,128)(2,1)S(1)}, u32[]{:S(2)}, u32[]{:S(2)}) collective-permute-start(bf16[2,2,72,768]{3,2,1,0:T(8,128)(2,1)S(1)} %pad_maximum_fusion.2), channel_id=1, source_target_pairs={{0,16},{4,20},{8,24},{12,28},{16,0},{20,4},{24,8},{28,12},{1,17},{... | collective-permute-start | bytes 1327112 | tf_op jit(solution)/shard_map/ppermute | solution.py:636
  67.1 33.5 %collective-permute-start.7 = (bf16[2,2,72,768]{3,2,1,0:T(8,128)(2,1)S(1)}, bf16[2,2,72,768]{3,2,1,0:T(8,128)(2,1)S(1)}, u32[]{:S(2)}, u32[]{:S(2)}) collective-permute-start(bf16[2,2,72,768]{3,2,1,0:T(8,128)(2,1)S(1)} %pad_maximum_fusion.3), channel_id=1, source_target_pairs={{0,8},{4,12},{8,0},{12,4},{16,24},{20,28},{24,16},{28,20},{1,9},{5... | collective-permute-start | bytes 1327112 | tf_op jit(solution)/shard_map/ppermute | solution.py:636
  100.6 6.7 %collective-permute-start.5 = (bf16[4,2,72,768]{3,2,1,0:T(8,128)(2,1)S(1)}, bf16[4,2,72,768]{3,2,1,0:T(8,128)(2,1)}, u32[]{:S(2)}, u32[]{:S(2)}) collective-permute-start(bf16[4,2,72,768]{3,2,1,0:T(8,128)(2,1)S(1)} %pad_maximum_fusion.refs_0_), channel_id=1, source_target_pairs={{0,4},{4,0},{8,12},{12,8},{16,20},{20,16},{24,28},{28,24},{1,5},{5... | collective-permute-start | bytes 2654216 | tf_op jit(solution)/shard_map/ppermute | solution.py:636
  151.5 28.8 %all-to-all-start = ((bf16[8,160,768]{2,1,0:T(8,128)(2,1)}), bf16[8,160,768]{2,1,0:T(8,128)(2,1)S(1)}, u32[]{:S(2)}, u32[]{:S(2)}) async-start(bf16[8,160,768]{2,1,0:T(8,128)(2,1)} %bitcast.75), calls=%async_computation | async-start | bytes 3932160 | tf_op jit(solution)/shard_map/all_to_all | solution.py:691
  181.5 62.1 %all-to-all-start.4 = ((bf16[8,160,768]{2,1,0:T(8,128)(2,1)}), bf16[8,160,768]{2,1,0:T(8,128)(2,1)S(1)}, u32[]{:S(2)}, u32[]{:S(2)}) async-start(bf16[8,160,768]{2,1,0:T(8,128)(2,1)} %bitcast.74), calls=%async_computation.4 | async-start | bytes 3932160 | tf_op jit(solution)/shard_map/all_to_all | solution.py:691
  185.1 375.1 %reduce-scatter.4.cloned.1.call-start = ((), (), s32[]{:S(2)}) async-start(), calls=%async_computation.11 | async-start | bytes 11796480 | tf_op jit(solution)/shard_map/reduce_scatter | solution.py:687
  266.1 295.9 %reduce-scatter.8.cloned.1.call-start = ((), (), s32[]{:S(2)}) async-start(), calls=%async_computation.13 | async-start | bytes 5898240 | tf_op jit(solution)/shard_map/reduce_scatter | solution.py:687
  266.8 50.8 %all-to-all-start.3 = ((bf16[8,2,160,768]{3,2,1,0:T(8,128)(2,1)}), bf16[8,2,160,768]{3,2,1,0:T(8,128)(2,1)}, u32[]{:S(2)}, u32[]{:S(2)}) async-start(bf16[8,2,160,768]{3,2,1,0:T(8,128)(2,1)} %get-tuple-element.61), calls=%async_computation.3 | async-start | bytes 7864320 | tf_op jit(solution)/shard_map/all_to_all | solution.py:691
  317.6 50.8 %all-to-all-start.6 = ((bf16[8,2,160,768]{3,2,1,0:T(8,128)(2,1)}), bf16[8,2,160,768]{3,2,1,0:T(8,128)(2,1)}, u32[]{:S(2)}, u32[]{:S(2)}) async-start(bf16[8,2,160,768]{3,2,1,0:T(8,128)(2,1)} %get-tuple-element.67), calls=%async_computation.6 | async-start | bytes 7864320 | tf_op jit(solution)/shard_map/all_to_all | solution.py:691
  322.2 290.1 %reduce-scatter.6.cloned.1.call-start = ((), (), s32[]{:S(2)}) async-start(), calls=%async_computation.12 | async-start | bytes 5898240 | tf_op jit(solution)/shard_map/reduce_scatter | solution.py:687
  461.1 9.7 %collective-permute-start.18 = (bf16[4,288,768]{2,1,0:T(8,128)(2,1)}, bf16[4,288,768]{2,1,0:T(8,128)(2,1)}, u32[]{:S(2)}, u32[]{:S(2)}) collective-permute-start(bf16[4,288,768]{2,1,0:T(8,128)(2,1)} %constant_dynamic-slice_fusion.2), channel_id=1, source_target_pairs={{0,4},{4,0},{8,12},{12,8},{16,20},{20,16},{24,28},{28,24},{1,5},{5... | collective-permute-start | bytes 5308424 | tf_op jit(solution)/shard_map/ppermute | solution.py:636
  469.9 11.7 %collective-permute-start.10 = (bf16[4,64,768]{2,1,0:T(8,128)(2,1)}, bf16[4,64,768]{2,1,0:T(8,128)(2,1)}, u32[]{:S(2)}, u32[]{:S(2)}) collective-permute-start(bf16[4,64,768]{2,1,0:T(8,128)(2,1)} %constant_dynamic-slice_fusion.4), channel_id=1, source_target_pairs={{0,16},{4,20},{8,24},{12,28},{16,0},{20,4},{24,8},{28,12},{1,17},{... | collective-permute-start | bytes 1179656 | tf_op jit(solution)/shard_map/ppermute | solution.py:636
  475.0 26.1 %collective-permute-start.19 = (bf16[4,144,768]{2,1,0:T(8,128)(2,1)}, bf16[4,144,768]{2,1,0:T(8,128)(2,1)}, u32[]{:S(2)}, u32[]{:S(2)}) collective-permute-start(bf16[4,144,768]{2,1,0:T(8,128)(2,1)} %constant_dynamic-slice_fusion.1), channel_id=1, source_target_pairs={{0,8},{4,12},{8,0},{12,4},{16,24},{20,28},{24,16},{28,20},{1,9},{5... | collective-permute-start | bytes 2654216 | tf_op jit(solution)/shard_map/ppermute | solution.py:636
  482.7 18.3 %collective-permute-start.11 = (bf16[4,32,768]{2,1,0:T(8,128)(2,1)S(1)}, bf16[4,32,768]{2,1,0:T(8,128)(2,1)S(1)}, u32[]{:S(2)}, u32[]{:S(2)}) collective-permute-start(bf16[4,32,768]{2,1,0:T(8,128)(2,1)S(1)} %constant_dynamic-slice_fusion.3), channel_id=1, source_target_pairs={{0,8},{4,12},{8,0},{12,4},{16,24},{20,28},{24,16},{28,20},{1,9},{5... | collective-permute-start | bytes 589832 | tf_op jit(solution)/shard_map/ppermute | solution.py:636
  502.5 22.2 %collective-permute-start.20 = (bf16[4,72,768]{2,1,0:T(8,128)(2,1)S(1)}, bf16[4,72,768]{2,1,0:T(8,128)(2,1)S(1)}, u32[]{:S(2)}, u32[]{:S(2)}) collective-permute-start(bf16[4,72,768]{2,1,0:T(8,128)(2,1)S(1)} %constant_dynamic-slice_fusion), channel_id=1, source_target_pairs={{0,16},{4,20},{8,24},{12,28},{16,0},{20,4},{24,8},{28,12},{1,17},{... | collective-permute-start | bytes 1327112 | tf_op jit(solution)/shard_map/ppermute | solution.py:636
  503.7 7.5 %collective-permute-start.12 = (bf16[32,768]{1,0:T(8,128)(2,1)S(1)}, bf16[32,768]{1,0:T(8,128)(2,1)S(1)}, u32[]{:S(2)}, u32[]{:S(2)}) collective-permute-start(bf16[32,768]{1,0:T(8,128)(2,1)S(1)} %get-tuple-element.102), channel_id=1, source_target_pairs={{0,1},{1,2},{2,3},{3,0},{4,5},{5,6},{6,7},{7,4},{8,9},{9,10},{10,1... | collective-permute-start | bytes 147464 | tf_op jit(solution)/shard_map/ppermute | solution.py:641
  505.5 7.4 %collective-permute-start.14 = (bf16[32,768]{1,0:T(8,128)(2,1)S(1)}, bf16[32,768]{1,0:T(8,128)(2,1)S(1)}, u32[]{:S(2)}, u32[]{:S(2)}) collective-permute-start(bf16[32,768]{1,0:T(8,128)(2,1)S(1)} %get-tuple-element.103), channel_id=1, source_target_pairs={{0,3},{1,0},{2,1},{3,2},{4,7},{5,4},{6,5},{7,6},{8,11},{9,8},{10,9... | collective-permute-start | bytes 147464 | tf_op jit(solution)/shard_map/ppermute | solution.py:641
  507.6 11.4 %collective-permute-start.13 = (bf16[32,768]{1,0:T(8,128)(2,1)S(1)}, bf16[32,768]{1,0:T(8,128)(2,1)S(1)}, u32[]{:S(2)}, u32[]{:S(2)}) collective-permute-start(bf16[32,768]{1,0:T(8,128)(2,1)S(1)} %get-tuple-element.104), channel_id=1, source_target_pairs={{0,2},{1,3},{2,0},{3,1},{4,6},{5,7},{6,4},{7,5},{8,10},{9,11},{10,... | collective-permute-start | bytes 147464 | tf_op jit(solution)/shard_map/ppermute | solution.py:641
  524.9 7.9 %collective-permute-start.21 = (bf16[72,768]{1,0:T(8,128)(2,1)S(1)}, bf16[72,768]{1,0:T(8,128)(2,1)S(1)}, u32[]{:S(2)}, u32[]{:S(2)}) collective-permute-start(bf16[72,768]{1,0:T(8,128)(2,1)S(1)} %get-tuple-element.99), channel_id=1, source_target_pairs={{0,1},{1,2},{2,3},{3,0},{4,5},{5,6},{6,7},{7,4},{8,9},{9,10},{10,1... | collective-permute-start | bytes 331784 | tf_op jit(solution)/shard_map/ppermute | solution.py:641
  525.0 7.8 %collective-permute-start.23 = (bf16[72,768]{1,0:T(8,128)(2,1)S(1)}, bf16[72,768]{1,0:T(8,128)(2,1)S(1)}, u32[]{:S(2)}, u32[]{:S(2)}) collective-permute-start(bf16[72,768]{1,0:T(8,128)(2,1)S(1)} %get-tuple-element.100), channel_id=1, source_target_pairs={{0,3},{1,0},{2,1},{3,2},{4,7},{5,4},{6,5},{7,6},{8,11},{9,8},{10,9... | collective-permute-start | bytes 331784 | tf_op jit(solution)/shard_map/ppermute | solution.py:641
  528.8 13.0 %collective-permute-start.22 = (bf16[72,768]{1,0:T(8,128)(2,1)S(1)}, bf16[72,768]{1,0:T(8,128)(2,1)S(1)}, u32[]{:S(2)}, u32[]{:S(2)}) collective-permute-start(bf16[72,768]{1,0:T(8,128)(2,1)S(1)} %get-tuple-element.101), channel_id=1, source_target_pairs={{0,2},{1,3},{2,0},{3,1},{4,6},{5,7},{6,4},{7,5},{8,10},{9,11},{10,... | collective-permute-start | bytes 331784 | tf_op jit(solution)/shard_map/ppermute | solution.py:641
  528.9 19.2 %collective-permute-start.17 = (bf16[128,768]{1,0:T(8,128)(2,1)S(1)}, bf16[128,768]{1,0:T(8,128)(2,1)S(1)}, u32[]{:S(2)}, u32[]{:S(2)}) collective-permute-start(bf16[128,768]{1,0:T(8,128)(2,1)S(1)} %maximum_select_fusion.4), channel_id=1, source_target_pairs={{0,4},{4,0},{8,12},{12,8},{16,20},{20,16},{24,28},{28,24},{1,5},{5... | collective-permute-start | bytes 589832 | tf_op jit(solution)/shard_map/ppermute | solution.py:636
  541.9 8.9 %collective-permute-start.24 = (bf16[72,768]{1,0:T(8,128)(2,1)S(1)}, bf16[72,768]{1,0:T(8,128)(2,1)S(1)}, u32[]{:S(2)}, u32[]{:S(2)}) collective-permute-start(bf16[72,768]{1,0:T(8,128)(2,1)S(1)} %fusion.10), channel_id=1, source_target_pairs={{0,16},{4,20},{8,24},{12,28},{16,0},{20,4},{24,8},{28,12},{1,17},{... | collective-permute-start | bytes 331784 | tf_op jit(solution)/shard_map/ppermute | solution.py:636
  (30 other events, 231.9 us)
Sparse Core Ops, SparseCore 0:
  56.6 28.9 all-gather.1
  266.2 162.7 reduce-scatter.3
  431.9 89.4 reduce-scatter.7
  524.1 88.1 reduce-scatter.5

commit v4 on v3

--- a/solution.py
+++ b/solution.py
@@ -57,7 +57,6 @@
     return pl.pallas_call(
         partial(slot_kernel, experts=experts),
         out_shape=jax.ShapeDtypeStruct(routes.shape, jnp.int32),
-        name="find_slots",
     )(routes, base)
 
 
@@ -78,8 +77,29 @@
         in_specs=[whole(slots.shape), whole(rows.shape)] + [pl.BlockSpec(memory_space=pl.ANY)] * len(after),
         out_specs=pl.BlockSpec((block, width), lambda i: (i, 0)),
         out_shape=jax.ShapeDtypeStruct((count, width), rows.dtype),
-        name="dispatch",
     )(slots, rows, *after)
+
+
+def dispatch_into_kernel(slots_ref, rows_ref, into_ref, out_ref, *, start):
+    del into_ref
+    _, _, block, _ = out_ref.shape
+    tokens = rows_ref.shape[0]
+    slot = lax.broadcasted_iota(jnp.int32, (block, tokens), 0) + (pl.program_id(0) * block + start)
+    hot = jnp.where((slot == slots_ref[0:1, :]) | (slot == slots_ref[1:2, :]), 1.0, 0.0)
+    out_ref[0, 0] = dot_nn(hot.astype(jnp.bfloat16), rows_ref[...]).astype(out_ref.dtype)
+
+
+def dispatch_into(slots, rows, start, into):
+    owners, _, capacity, width = into.shape
+    whole = lambda shape: pl.BlockSpec(shape, lambda i: (0, 0))
+    return pl.pallas_call(
+        partial(dispatch_into_kernel, start=start),
+        grid=(owners,),
+        in_specs=[whole(slots.shape), whole(rows.shape), pl.BlockSpec(memory_space=pl.ANY)],
+        out_specs=pl.BlockSpec((1, 1, capacity, width), lambda i: (i, 0, 0, 0)),
+        out_shape=jax.ShapeDtypeStruct(into.shape, into.dtype),
+        input_output_aliases={2: 0},
+    )(slots, rows, into)
 
 
 def dispatch_all_kernel(slots_ref, routes_ref, rows_ref, *refs, owners, capacity):
@@ -92,8 +112,8 @@
     hits = [slot == slots_ref[c:c + 1, :] for c in range(2)]
     hot = jnp.where(hits[0] | hits[1], 1.0, 0.0).astype(jnp.bfloat16)
     picked = dot_nn(hot, rows_ref[...]).astype(rows_ref.dtype)
-    for index, out_ref in enumerate(out_refs):
-        out_ref[0] = picked[index * capacity:(index + 1) * capacity]
+    out_refs[0][0] = picked[:capacity]
+    out_refs[1][0, 0] = picked[capacity:]
     other = jnp.where(hits[0], routes_ref[1:2, :], jnp.where(hits[1], routes_ref[0:1, :], 0.0))
     column = jnp.sum(other, axis=1, keepdims=True)
     other_ref[0] = jnp.broadcast_to(column, (block, 128)).T[0:1, :]
@@ -107,9 +127,8 @@
         partial(dispatch_all_kernel, owners=owners, capacity=capacity),
         grid=(owners,),
         in_specs=[whole(slots.shape), whole(routes.shape), whole(rows.shape)],
-        out_specs=[pl.BlockSpec((1, capacity, width), lambda i: (i, 0, 0))] * local_count + [pl.BlockSpec((1, 1, block), lambda i: (i, 0, 0))],
-        out_shape=[jax.ShapeDtypeStruct((owners, capacity, width), rows.dtype)] * local_count + [jax.ShapeDtypeStruct((owners, 1, block), jnp.float32)],
-        name="dispatch_all",
+        out_specs=[pl.BlockSpec((1, capacity, width), lambda i: (i, 0, 0)), pl.BlockSpec((1, 1, capacity, width), lambda i: (i, 1, 0, 0)), pl.BlockSpec((1, 1, block), lambda i: (i, 0, 0))],
+        out_shape=[jax.ShapeDtypeStruct((owners, capacity, width), rows.dtype), jax.ShapeDtypeStruct((owners, 2, capacity, width), rows.dtype), jax.ShapeDtypeStruct((owners, 1, block), jnp.float32)],
     )(slots, routes, rows)
 
 
@@ -125,10 +144,11 @@
 
 def first_kernel(owner_ref, rows_ref, cot_ref, other_ref, router_ref, up_ref, *refs, chunk, index, local_count):
     act_ref, slope_ref, down_grad_ref, grad_ref = refs[-4:]
-    rows, width = rows_ref.shape
+    owners, capacity, width = rows_ref.shape
+    rows = owners * capacity
     @pl.when(pl.program_id(0) == 0)
     def _():
-        logits = dot_nt(router_ref[...], rows_ref[...])
+        logits = dot_nt(router_ref[...], rows_ref[...].reshape(rows, width))
         expert = lax.broadcasted_iota(jnp.int32, logits.shape, 0)
         mine = owner_ref[0] * local_count + index
         own = jnp.sum(jnp.where(expert == mine, logits, 0.0), axis=0, keepdims=True)
@@ -139,24 +159,33 @@
         gate = own / (own + jnp.exp(other - top))
         column = jnp.broadcast_to(gate, (128, rows)).T
         for start in range(0, width, 128):
-            part = cot_ref[:, start:start + 128].astype(jnp.float32) * column
+            part = cot_ref[:, :, start:start + 128].reshape(rows, 128).astype(jnp.float32) * column
             grad_ref[:, start:start + 128] = part.astype(jnp.bfloat16)
     up = up_ref[0]
     for start in range(0, rows, chunk):
-        pre = dot_nn(rows_ref[start:start + chunk, :], up)
+        part = rows_ref[start // capacity:(start + chunk) // capacity].reshape(chunk, width)
+        pre = dot_nn(part, up)
         value, slope = gelu_pair(pre)
         act_ref[start:start + chunk, :] = value.astype(jnp.bfloat16)
         slope_ref[start:start + chunk, :] = slope.astype(jnp.bfloat16)
     down_grad_ref[0] = dot_tn(act_ref[...], grad_ref[...]).astype(jnp.bfloat16)
 
 
-def expert_first(owner, rows_in, cot, other, router, up, index, local_count, shards, into=None, after=(), chunk=640):
-    rows, width = rows_in.shape
+def arrived_spec(arrived, which):
+    if arrived.ndim == 3:
+        return pl.BlockSpec(arrived.shape, lambda i: (0, 0, 0))
+    owners, _, capacity, width = arrived.shape
+    return pl.BlockSpec((owners, None, capacity, width), lambda i: (0, which, 0, 0))
+
+
+def expert_first(owner, rows_in, cot, other, router, up, index, local_count, shards, into=None, after=()):
+    owners, capacity, width = rows_in.shape[0], *rows_in.shape[-2:]
+    rows = owners * capacity
     hidden = up.shape[2]
     tile = hidden // shards
+    chunk = rows // 2
     fixed = pl.BlockSpec((rows, width), lambda i: (0, 0))
     column = pl.BlockSpec((rows, tile), lambda i: (0, i))
-    chunk = chunk if rows % chunk == 0 else rows // 2
     operands = [owner, rows_in, cot, other, router, up]
     place, aliases = 0, {}
     grad_shape = jax.ShapeDtypeStruct((shards, tile, width), jnp.bfloat16)
@@ -170,8 +199,8 @@
         grid=(shards,),
         in_specs=[
             pl.BlockSpec(memory_space=pltpu.SMEM),
-            fixed,
-            fixed,
+            arrived_spec(rows_in, 0),
+            arrived_spec(cot, 1),
             pl.BlockSpec((1, rows), lambda i: (0, 0)),
             pl.BlockSpec(router.shape, lambda i: (0, 0)),
             pl.BlockSpec((1, width, tile), lambda i: (index, 0, i)),
@@ -181,7 +210,6 @@
         out_shape=[jax.ShapeDtypeStruct((rows, hidden), jnp.bfloat16)] * 2 + [grad_shape, jax.ShapeDtypeStruct((rows, width), jnp.bfloat16)],
         input_output_aliases=aliases,
         compiler_params=pltpu.CompilerParams(vmem_limit_bytes=62 << 20),
-        name="expert_first",
     )(*operands)
 
 
@@ -191,7 +219,7 @@
     owners, _, capacity, width = made_ref.shape
     @pl.when(step == 0)
     def _():
-        turned[...] = rows_ref[...].T
+        turned[...] = rows_ref[...].reshape(grad_ref.shape).T
     up = up_ref[0]
     down = down_ref[0]
     grads = dot_nt(grad_ref[...], down)
@@ -215,7 +243,7 @@
 
 
 def expert_second(rows_in, grad, act, slope, up, down, index, owners, shards, wide, after=()):
-    rows, width = rows_in.shape
+    rows, width = grad.shape
     hidden = up.shape[2]
     tile = hidden // shards
     fixed = pl.BlockSpec((rows, width), lambda i: (0, 0))
@@ -224,13 +252,12 @@
     return pl.pallas_call(
         second_kernel,
         grid=(shards,),
-        in_specs=[fixed, fixed, column, column, pl.BlockSpec((1, width, tile), lambda i: (index, 0, i)), pl.BlockSpec((1, tile, width), lambda i: (index, i, 0))]
+        in_specs=[arrived_spec(rows_in, 0), fixed, column, column, pl.BlockSpec((1, width, tile), lambda i: (index, 0, i)), pl.BlockSpec((1, tile, width), lambda i: (index, i, 0))]
         + [pl.BlockSpec(memory_space=pl.ANY)] * len(after),
         out_specs=[pl.BlockSpec(made_shape, lambda i: (0, 0, 0, 0)), pl.BlockSpec((1, width, tile), lambda i: (i, 0, 0))],
         out_shape=[jax.ShapeDtypeStruct(made_shape, jnp.bfloat16), jax.ShapeDtypeStruct((shards, wide, tile), jnp.bfloat16)],
         scratch_shapes=[pltpu.VMEM((width, rows), jnp.bfloat16), pltpu.VMEM((rows, width), jnp.float32), pltpu.VMEM((rows, width), jnp.float32)],
         compiler_params=pltpu.CompilerParams(vmem_limit_bytes=62 << 20),
-        name="expert_second",
     )(rows_in, grad, act, slope, up, down, *after)
 
 
@@ -238,9 +265,9 @@
     return jnp.broadcast_to(row, (128, block)).T
 
 
-def pick(slots, lane, back_refs):
+def pick(slots, lane, back_refs, first=0):
     picked = None
-    for index, back_ref in enumerate(back_refs):
+    for index, back_ref in enumerate(back_refs, first):
         owners, capacity, width = back_ref.shape
         half = owners * capacity
         hots = []
@@ -252,20 +279,50 @@
     return picked
 
 
-def out_kernel(slots_ref, routes_ref, gates_ref, resid_ref, cot_ref, *refs):
-    back_refs, (out_ref, logit_ref) = refs[:-2], refs[-2:]
+def part_kernel(slots_ref, gates_ref, resid_ref, cot_ref, made_ref, back_ref, result_ref, inner_ref, grads_ref):
+    block = result_ref.shape[0]
+    lane = lax.broadcasted_iota(jnp.int32, (block, 128), 1)
+    cot = cot_ref[...].astype(jnp.float32)
+    result = resid_ref[...]
+    inner = jnp.zeros((block, 128), jnp.float32)
+    slots = [spread(slots_ref[c:c + 1, :], block) for c in range(2)]
+    for c in range(2):
+        picked = pick([slots[c]], lane, [made_ref])
+        result = result + spread(gates_ref[c:c + 1, :], block)[:, 0:1] * picked
+        inner = inner + jnp.where(lane == c, jnp.sum(cot * picked, axis=1, keepdims=True), 0.0)
+    result_ref[...] = result
+    inner_ref[...] = inner
+    grads_ref[...] = pick(slots, lane, [back_ref])
+
+
+def combine_part(slots, gates, resid, cot, returned, block=256):
+    tokens, width = resid.shape
+    small = pl.BlockSpec((2, block), lambda i: (0, i))
+    rows = pl.BlockSpec((block, width), lambda i: (i, 0))
+    wide = jax.ShapeDtypeStruct((tokens, width), jnp.float32)
+    return pl.pallas_call(
+        part_kernel,
+        grid=(tokens // block,),
+        in_specs=[small, small, rows, rows, returned_spec(returned, 0), returned_spec(returned, 1)],
+        out_specs=[rows, pl.BlockSpec((block, 128), lambda i: (i, 0)), rows],
+        out_shape=[wide, jax.ShapeDtypeStruct((tokens, 128), jnp.float32), wide],
+        compiler_params=pltpu.CompilerParams(vmem_limit_bytes=62 << 20),
+    )(slots, gates, resid, cot, returned, returned)
+
+
+def out_kernel(slots_ref, routes_ref, gates_ref, result_ref, inner_ref, cot_ref, made_ref, out_ref, logit_ref):
     block = out_ref.shape[0]
     lane = lax.broadcasted_iota(jnp.int32, (block, 128), 1)
     cot = cot_ref[...].astype(jnp.float32)
-    result = resid_ref[...]
+    result = result_ref[...]
     gates, inner = [], []
     for c in range(2):
         slot = spread(slots_ref[c:c + 1, :], block)
         gate = spread(gates_ref[c:c + 1, :], block)[:, 0:1]
-        picked = pick([slot], lane, back_refs)
+        picked = pick([slot], lane, [made_ref], 1)
         result = result + gate * picked
         gates.append(gate)
-        inner.append(jnp.sum(cot * picked, axis=1, keepdims=True))
+        inner.append(inner_ref[:, c:c + 1] + jnp.sum(cot * picked, axis=1, keepdims=True))
     out_ref[...] = result.astype(out_ref.dtype)
     middle = gates[0] * inner[0] + gates[1] * inner[1]
     logit = jnp.zeros((block, 128), jnp.float32)
@@ -280,26 +337,24 @@
     return pl.BlockSpec((owners, None, capacity, width), lambda i: (0, which, 0, 0))
 
 
-def combine_out(slots, routes, gates, resid, cot, returned, block=256):
-    tokens, width = resid.shape
+def combine_out(slots, routes, gates, result, inner, cot, returned, block=256):
+    tokens, width = result.shape
     small = pl.BlockSpec((2, block), lambda i: (0, i))
     rows = pl.BlockSpec((block, width), lambda i: (i, 0))
     return pl.pallas_call(
         out_kernel,
         grid=(tokens // block,),
-        in_specs=[small, small, small, rows, rows] + [returned_spec(part, 0) for part in returned],
+        in_specs=[small, small, small, rows, pl.BlockSpec((block, 128), lambda i: (i, 0)), rows, returned_spec(returned, 0)],
         out_specs=[rows, pl.BlockSpec((block, 128), lambda i: (i, 0))],
         out_shape=[jax.ShapeDtypeStruct((tokens, width), jnp.bfloat16), jax.ShapeDtypeStruct((tokens, 128), jnp.bfloat16)],
         compiler_params=pltpu.CompilerParams(vmem_limit_bytes=62 << 20),
-        name="combine_out",
-    )(slots, routes, gates, resid, cot, *returned)
-
-
-def back_kernel(slots_ref, logit_ref, router_ref, gain_ref, resid_ref, cot_ref, merge_ref, *refs, eps):
-    back_refs, (grad_ref, low_ref, mixed_ref, gain_grad_ref) = refs[:-4], refs[-4:]
+    )(slots, routes, gates, result, inner, cot, returned)
+
+
+def back_kernel(slots_ref, logit_ref, router_ref, gain_ref, resid_ref, cot_ref, merge_ref, part_ref, back_ref, grad_ref, low_ref, mixed_ref, gain_grad_ref, *, eps):
     block, _ = grad_ref.shape
     lane = lax.broadcasted_iota(jnp.int32, (block, 128), 1)
-    grads = pick([spread(slots_ref[c:c + 1, :], block) for c in range(2)], lane, back_refs)
+    grads = part_ref[...] + pick([spread(slots_ref[c:c + 1, :], block) for c in range(2)], lane, [back_ref], 1)
     grads = grads + dot_nn(logit_ref[...], router_ref[...])
     resid = resid_ref[...]
     inverse = lax.rsqrt(jnp.mean(resid * resid, axis=1, keepdims=True) + eps)
@@ -317,7 +372,7 @@
     mixed_ref[...] = dot_nt(low, merge_ref[...]).astype(jnp.bfloat16)
 
 
-def combine_back(slots, logit, router, gain, resid, cot, merge, returned, eps, block=256):
+def combine_back(slots, logit, router, gain, resid, cot, merge, part, returned, eps, block=256):
     tokens, width = resid.shape
     rows = pl.BlockSpec((block, width), lambda i: (i, 0))
     whole = lambda shape: pl.BlockSpec(shape, lambda i: (0, 0))
@@ -325,13 +380,11 @@
     return pl.pallas_call(
         partial(back_kernel, eps=eps),
         grid=(tokens // block,),
-        in_specs=[pl.BlockSpec((2, block), lambda i: (0, i)), pl.BlockSpec((block, 128), lambda i: (i, 0)), whole(router.shape), whole(gain.shape), rows, rows, whole(merge.shape)]
-        + [returned_spec(part, 1) for part in returned],
+        in_specs=[pl.BlockSpec((2, block), lambda i: (0, i)), pl.BlockSpec((block, 128), lambda i: (i, 0)), whole(router.shape), whole(gain.shape), rows, rows, whole(merge.shape), rows, returned_spec(returned, 1)],
         out_specs=[rows, rows, rows, whole((1, width))],
         out_shape=[jax.ShapeDtypeStruct((tokens, width), jnp.float32), low, low, jax.ShapeDtypeStruct((1, width), jnp.float32)],
         compiler_params=pltpu.CompilerParams(vmem_limit_bytes=62 << 20),
-        name="combine_back",
-    )(slots, logit, router, gain, resid, cot, merge, *returned)
+    )(slots, logit, router, gain, resid, cot, merge, part, returned)
 
 
 def near_tiles(near_ref, head, block):
@@ -407,7 +460,6 @@
         out_specs=[column, pl.BlockSpec((1, heads, length), lambda g: (g, 0, 0))],
         out_shape=[jax.ShapeDtypeStruct((length, width), jnp.bfloat16), jax.ShapeDtypeStruct((groups, heads, length), jnp.float32)],
         compiler_params=pltpu.CompilerParams(vmem_limit_bytes=62 << 20),
-        name="attend",
     )(queries, keys, values, near)
 
 
@@ -489,7 +541,6 @@
         out_shape=[jax.ShapeDtypeStruct((3, length, width), jnp.bfloat16), jax.ShapeDtypeStruct((groups, 2 * heads, block), jnp.float32)],
         scratch_shapes=[pltpu.VMEM((length, lanes), jnp.float32)] * 2,
         compiler_params=pltpu.CompilerParams(vmem_limit_bytes=62 << 20),
-        name="attend_back",
     )(queries, keys, values, grads, outs, totals, near)
 
 
@@ -501,7 +552,7 @@
 
 
 def project_kernel(owner_ref, inputs_ref, gain_ref, *refs, eps):
-    piece_refs, weight_refs, low_ref, out_refs = refs[:4], refs[4:7], refs[7], refs[8:]
+    piece_refs, weight_refs, low_ref, out_refs = refs[:4], refs[-7:-4], refs[-4], refs[-3:]
     count, half, three, _ = piece_refs[0].shape
     piece = three // 3
     owners = 2 * count
@@ -528,7 +579,7 @@
         out_ref[...] = dot_nn(low, weight_ref[...]).astype(jnp.bfloat16)
 
 
-def project(owner, inputs, gain, pieces, eps, block=256):
+def project(owner, inputs, gain, pieces, eps, after=(), block=256):
     tokens, width = inputs.shape
     rows = pl.BlockSpec((block, width), lambda i: (i, 0))
     whole = lambda shape: pl.BlockSpec(shape, lambda i: (0,) * len(shape))
@@ -536,12 +587,11 @@
     return pl.pallas_call(
         partial(project_kernel, eps=eps),
         grid=(tokens // block,),
-        in_specs=[pl.BlockSpec(memory_space=pltpu.SMEM), rows, whole(gain.shape)] + [whole(piece.shape) for piece in pieces],
+        in_specs=[pl.BlockSpec(memory_space=pltpu.SMEM), rows, whole(gain.shape)] + [whole(piece.shape) for piece in pieces] + [pl.BlockSpec(memory_space=pl.ANY)] * len(after),
         out_specs=[whole(weight.shape)] * 3 + [rows] * 4,
         out_shape=[weight] * 3 + [jax.ShapeDtypeStruct((tokens, width), jnp.bfloat16)] * 4,
         compiler_params=pltpu.CompilerParams(vmem_limit_bytes=62 << 20),
-        name="project",
-    )(owner, inputs, gain, *pieces)
+    )(owner, inputs, gain, *pieces, *after)
 
 
 def settle_kernel(mixed_ref, merge_ref, inputs_ref, gain_ref, router_ref, routes_ref, resid_ref, low_ref, gates_ref, *, eps):
@@ -572,7 +622,6 @@
         out_specs=[rows, rows, small],
         out_shape=[jax.ShapeDtypeStruct((tokens, width), jnp.float32), jax.ShapeDtypeStruct((tokens, width), jnp.bfloat16), jax.ShapeDtypeStruct((2, tokens), jnp.float32)],
         compiler_params=pltpu.CompilerParams(vmem_limit_bytes=62 << 20),
-        name="settle",
     )(mixed, merge, inputs, gain, router, routes)
 
 
@@ -601,7 +650,6 @@
         out_specs=[rows, whole((1, width))],
         out_shape=[jax.ShapeDtypeStruct((tokens, width), jnp.float32), jax.ShapeDtypeStruct((1, width), jnp.float32)],
         compiler_params=pltpu.CompilerParams(vmem_limit_bytes=62 << 20),
-        name="finish",
     )(head_grads, query, key, value, gain, inputs, resid_grad)
 
 
@@ -627,23 +675,26 @@
         out_shape=jax.ShapeDtypeStruct((shards, count * part, width), jnp.bfloat16),
         scratch_shapes=[pltpu.VMEM((width, tokens), jnp.bfloat16)],
         compiler_params=pltpu.CompilerParams(vmem_limit_bytes=62 << 20),
-        name="weight_grads",
     )(left, right)
 
 
+OWNER = "expert"
+LINE = "shard"
+
+
 def exchange(rows, bit):
-    count = lax.axis_size("expert")
-    return lax.ppermute(rows, "expert", [(i, i ^ bit) for i in range(count)])
+    count = lax.axis_size(OWNER)
+    return lax.ppermute(rows, OWNER, [(i, i ^ bit) for i in range(count)])
 
 
 def shift(rows, step):
-    count = lax.axis_size("shard")
-    return lax.ppermute(rows, "shard", [(i, (i + step) % count) for i in range(count)])
+    count = lax.axis_size(LINE)
+    return lax.ppermute(rows, LINE, [(i, (i + step) % count) for i in range(count)])
 
 
 def gather_line(rows):
-    count = lax.axis_size("shard")
-    me = lax.axis_index("shard")
+    count = lax.axis_size(LINE)
+    me = lax.axis_index(LINE)
     out = jnp.zeros((count,) + rows.shape, rows.dtype)
     out = lax.dynamic_update_index_in_dim(out, rows, me, 0)
     for step in range(1, count):
@@ -656,39 +707,62 @@
     return (left.astype(jnp.float32) + right.astype(jnp.float32)).astype(jnp.bfloat16)
 
 
-def reduce_stack(stack, bits):
-    me = lax.axis_index("expert")
-    for bit in bits:
-        half = stack.shape[1] // 2
-        side = (me // bit) % 2
-        keep = lax.dynamic_slice_in_dim(stack, side * half, half, 1)
-        send = lax.dynamic_slice_in_dim(stack, (1 - side) * half, half, 1)
-        got = exchange(send, bit)
-        stack = add_low(keep, got)
-    count = lax.axis_size("shard")
-    place = lax.axis_index("shard")
+def side(bit):
+    return (lax.axis_index(OWNER) // bit) % 2
+
+
+def halve(stack, bit):
+    half = stack.shape[1] // 2
+    keep = lax.dynamic_slice_in_dim(stack, side(bit) * half, half, 1)
+    send = lax.dynamic_slice_in_dim(stack, (1 - side(bit)) * half, half, 1)
+    got = exchange(send, bit)
+    return add_low(keep, got)
+
+
+def line_sum(stack):
+    count = lax.axis_size(LINE)
+    place = lax.axis_index(LINE)
     total = lax.dynamic_index_in_dim(stack, place, 0, False).astype(jnp.float32)
     for step in range(1, count):
         send = lax.dynamic_index_in_dim(stack, (place + step) % count, 0, False)
         total = total + shift(send, step).astype(jnp.float32)
-    piece = total.astype(jnp.bfloat16)
-    for bit in reversed(bits):
-        other = exchange(piece, bit)
-        side = (me // bit) % 2
-        piece = jnp.where(
-            side == 0, jnp.concatenate([piece, other]), jnp.concatenate([other, piece])
-        )
-    return piece
+    return total.astype(jnp.bfloat16)
+
+
+def grow(piece, bit):
+    other = exchange(piece, bit)
+    return jnp.where(
+        side(bit) == 0, jnp.concatenate([piece, other]), jnp.concatenate([other, piece])
+    )
+
+
+def reduce_stack(stack, bits, cuts):
+    stack = halve(stack, bits[0])
+    cuts = [0] + cuts + [stack.shape[1]]
+    parts = [stack[:, low:high] for low, high in zip(cuts, cuts[1:])]
+    orders = [bits[1:], bits[:0:-1]]
+    for level in range(len(bits) - 1):
+        parts = [halve(part, order[level]) for part, order in zip(parts, orders)]
+    sizes = [part.shape[1] for part in parts]
+    piece = line_sum(jnp.concatenate(parts, axis=1))
+    parts = [piece[: sizes[0]], piece[sizes[0] :]][: len(parts)]
+    for level in reversed(range(len(bits) - 1)):
+        parts = [grow(part, order[level]) for part, order in zip(parts, orders)]
+    return grow(jnp.concatenate(parts), bits[0])
 
 
 def scatter_sum(grads):
     shards, rows, width = grads.shape
     grads = grads.reshape(shards * rows, width)
-    return lax.psum_scatter(grads, "shard", scatter_dimension=0, tiled=True)
+    return lax.psum_scatter(grads, LINE, scatter_dimension=0, tiled=True)
 
 
 def share_rows(rows):
-    return lax.all_to_all(rows, "expert", 0, 0, tiled=True)
+    return lax.all_to_all(rows, OWNER, 0, 0, tiled=True)
+
+
+def share_large(rows):
+    return pltpu.with_memory_space_constraint(share_rows(rows), pltpu.HBM)
 
 
 def local(
@@ -708,9 +782,9 @@
 ):
     f32, bf16 = jnp.float32, jnp.bfloat16
     tokens, width = inputs.shape
-    owners = lax.axis_size("expert")
-    shards = lax.axis_size("shard")
-    me = lax.axis_index("expert")
+    owners = lax.axis_size(OWNER)
+    shards = lax.axis_size(LINE)
+    me = lax.axis_index(OWNER)
     part = query_weight.shape[0]
     piece = part // owners
     local_heads = bias_table.shape[1]
@@ -748,7 +822,7 @@
             got = exchange(held, bit)
             held = jnp.concatenate([held, got])
         pieces += [held, exchange(held, bits[0])]
-    merge_full = lax.all_gather(merge_weight, "shard", axis=0, tiled=True)
+    merge_full = lax.all_gather(merge_weight, LINE, axis=0, tiled=True)
 
     gain_one = small_full[:, 0, :part].reshape(1, width).astype(f32)
     gain_two = small_full[:, 1, :part].reshape(1, width).astype(f32)
@@ -759,16 +833,12 @@
     routes_line = routes.T
     base = (routes_line % local_count * owners + routes_line // local_count) * capacity
     slots = find_slots(routes_line, base, experts)
-    *cot_rows, other = dispatch_all(
+    cot_rows, joint, other = dispatch_all(
         slots, routes_line.astype(f32), cotangent, owners, capacity, local_count
     )
     other = share_rows(other).reshape(owners, local_count, capacity)
 
     owner = me.astype(jnp.int32).reshape(1)
-    query_full, key_full, value_full, low_one, queries, keys, values = project(owner, inputs, gain_one, pieces, epsilon)
-    cot_in = []
-    for index in range(local_count):
-        cot_in.append(share_rows(cot_rows[index]).reshape(rows, width))
     block = 256
     hot = bucket_hot(tokens)
     assert hot[block:, -1].all()
@@ -776,41 +846,44 @@
     group = 128 // size
     near = jnp.dot(table_full, near_hot, precision=lax.Precision.HIGHEST)
     near = near.reshape(heads // group, group, block)
+    query_full, key_full, value_full, low_one, queries, keys, values = project(
+        owner, inputs, gain_one, pieces, epsilon, after=(near, router_full)
+    )
+    cot_in = share_large(cot_rows)
     attended, totals = attend(queries, keys, values, near, size, block)
     resid, low_two, gates = settle(
         attended, merge_full, inputs, gain_two, router_full, routes_line, epsilon
     )
 
-    sends, rows_in = [], []
-    for index in range(local_count):
-        sends.append(dispatch(slots, low_two, index * rows, rows))
-        send = share_rows(sends[index].reshape(owners, capacity, width))
-        rows_in.append(send.reshape(rows, width))
+    send = dispatch(slots, low_two, 0, rows).reshape(owners, capacity, width)
+    rows_in = share_large(send)
+    joint = dispatch_into(slots, low_two, rows, joint)
+    joint_in = share_large(joint)
     others = [other[:, index].reshape(1, rows) for index in range(local_count)]
     act, slope, first_down, grad_in = expert_first(
-        owner, rows_in[0], cot_in[0], others[0], router_full, up_weight, 0, local_count, shards,
-        after=(sends[1],),
+    owner, rows_in, cot_in, others[0], router_full, up_weight, 0, local_count, shards,
     )
     first_sum = scatter_sum(first_down)
-    first_made, pair = expert_second(
-        rows_in[0], grad_in, act, slope, up_weight, down_weight, 0, owners, shards, 2 * width
-    )
+    first_made, pair = expert_second(rows_in, grad_in, act, slope, up_weight, down_weight, 0, owners, shards, 2 * width)
     act, slope, pair, grad_in = expert_first(
-        owner, rows_in[1], cot_in[1], others[1], router_full, up_weight, 1, local_count, shards,
+        owner, joint_in, joint_in, others[1], router_full, up_weight, 1, local_count, shards,
         into=pair,
     )
     pair_sum = scatter_sum(pair)
     second_made, last_up = expert_second(
-        rows_in[1], grad_in, act, slope, up_weight, down_weight, 1, owners, shards, width
+        joint_in, grad_in, act, slope, up_weight, down_weight, 1, owners, shards, width
     )
     last_sum = scatter_sum(last_up)
-    returned = []
-    for made in (first_made, second_made):
-        returned.append(share_rows(made))
-    output, logit_grad = combine_out(slots, routes_line, gates, resid, cotangent, returned)
+    returned = share_rows(first_made)
+    result, inner, part_grads = combine_part(slots, gates, resid, cotangent, returned)
+    returned = share_rows(second_made)
+    output, logit_grad = combine_out(
+        slots, routes_line, gates, result, inner, cotangent, returned
+    )
     router_wide = jnp.pad(router_full, ((0, 128 - experts), (0, 0)))
     resid_grad, branch, mixed_grad, gain_grad = combine_back(
-        slots, logit_grad, router_wide, gain_two, resid, cotangent, merge_full, returned, epsilon
+        slots, logit_grad, router_wide, gain_two, resid, cotangent, merge_full,
+        part_grads, returned, epsilon
     )
     router_grad = jnp.einsum("te,ti->ei", logit_grad, low_two, preferred_element_type=f32)
     merge_grad = weight_grads(attended, branch[None], shards)
@@ -831,11 +904,11 @@
         table_grad.reshape(shards, local_heads, BUCKETS).astype(bf16),
         router_grad[:experts].reshape(experts, shards, part).transpose(1, 0, 2).astype(bf16),
     )
-    head_sums = reduce_stack(head_sums, bits).astype(f32)
+    head_sums = reduce_stack(head_sums, bits, [5 * part // 6]).astype(f32)
     spare = -small_grad.shape[1] % (8 * owners)
     small_grad = jnp.pad(small_grad, ((0, 0), (0, spare), (0, 0)))
     rest_sums = jnp.concatenate([merge_grad, small_grad], axis=1)
-    rest_sums = reduce_stack(rest_sums, bits[:1] + bits[:0:-1]).astype(f32)
+    rest_sums = reduce_stack(rest_sums, bits[:1] + bits[:0:-1], []).astype(f32)
     small_sum = rest_sums[part:]
     return (
         output,
@@ -855,32 +928,33 @@
 
 def solution(mesh):
     in_specs = (
-        P(("expert", "shard"), None),
-        P("shard"),
-        P("shard", None),
-        P("shard", None),
-        P("shard", None),
-        P("shard", None),
-        P(None, "shard"),
-        P("shard"),
-        P("shard", None),
-        P("expert", None, None),
-        P("expert", None, None),
-        P(("expert", "shard"), None),
-        P(("expert", "shard"), None),
+        P((OWNER, LINE), None),
+        P(LINE),
+        P(LINE, None),
+        P(LINE, None),
+        P(LINE, None),
+        P(LINE, None),
+        P(None, LINE),
+        P(LINE),
+        P(LINE, None),
+        P(OWNER, None, None),
+        P(OWNER, None, None),
+        P((OWNER, LINE), None),
+        P((OWNER, LINE), None),
     )
     out_specs = (
-        P(("expert", "shard"), None),
-        P(("expert", "shard"), None),
-        P("shard"),
-        P("shard", None),
-        P("shard", None),
-        P("shard", None),
-        P("shard", None),
-        P(None, "shard"),
-        P("shard"),
-        P("shard", None),
-        P("expert", None, "shard"),
-        P("expert", "shard", None),
-    )
+        P((OWNER, LINE), None),
+        P((OWNER, LINE), None),
+        P(LINE),
+        P(LINE, None),
+        P(LINE, None),
+        P(LINE, None),
+        P(LINE, None),
+        P(None, LINE),
+        P(LINE),
+        P(LINE, None),
+        P(OWNER, None, LINE),
+        P(OWNER, LINE, None),
+    )
+
     return jax.shard_map(local, mesh=mesh, in_specs=in_specs, out_specs=out_specs, check_vma=False)

time: 632 us -> 630 us (level)
  local copies, waits for them, and re-layouts: 29.9 us -> 20.7 us
  blocking collectives: 0 us -> 7.97 us
    reduce_scatter x3, waiting for transfers between devices: 46.6 us -> 78.5 us  [scatter_sum(): return lax.psum_scatter(grads, LINE, scatter_dimension=0, tiled=True)]
    all_to_all x7 -> x5, waiting for transfers between devices: 80.1 us -> 63.1 us  [share_rows(): return lax.all_to_all(rows, OWNER, 0, 0, tiled=True)]
    pallas_call x2 -> x4, Pallas kernels: 73.1 us -> 88.8 us  [the longest x2 71.2 us: expert_second(): pl.pallas_call(second_kernel, grid=(shards,), in_specs=[arrived_spec(rows...]
    ppermute x27 -> x31, waiting for transfers between devices: 102 us -> 89.4 us  [the longest x22 57.4 us: exchange(): return lax.ppermute(rows, OWNER, [(i, i ^ bit) for i in range(count)])]
    all_to_all x0 -> x1, blocking collectives: none -> 7.97 us  [share_rows(): return lax.all_to_all(rows, OWNER, 0, 0, tiled=True)]
    all_to_all x7 -> x5, starting transfers between devices: 29.4 us -> 21.6 us  [share_rows(): return lax.all_to_all(rows, OWNER, 0, 0, tiled=True)]
    ppermute x27 -> x31, starting transfers between devices: 33.6 us -> 41.3 us  [the longest x9 23.3 us: shift(): lax.ppermute(rows, LINE, [(i, (i + step) % count) for i in range(count)])]
  transfers between devices with their start and end apart: 38 -> 40, of which waited for: 21 -> 23; matrix products, arithmetic and copies ran while one was open for 7% -> 5% of each run, Pallas kernels for 37% -> 39%
where the time goes in v4:
time: 630 us; the launch traced here: 621 us
  Pallas kernels  263 us (42%)
  waiting for transfers between devices  232 us (37%)
  starting transfers between devices  63.6 us (10%)
  local copies, waits for them, and re-layouts  20.7 us (3%)
  other arithmetic  17.3 us (3%)
  between operations  14.8 us (2%)
  blocking collectives  7.97 us (1%)
    reduce_scatter x3, waiting for transfers between devices, scatter_sum(): return lax.psum_scatter(grads, LINE, scatter_dimension=0, tiled=True)  78.5 us
    pallas_call x2, Pallas kernels, expert_second(): pl.pallas_call(second_kernel, grid=(shards,), in_specs=[arrived_spec(rows...  71.2 us
    all_to_all x5, waiting for transfers between devices, share_rows(): return lax.all_to_all(rows, OWNER, 0, 0, tiled=True)  63.1 us
    ppermute x22, waiting for transfers between devices, exchange(): return lax.ppermute(rows, OWNER, [(i, i ^ bit) for i in range(count)])  57.4 us
    pallas_call x2, Pallas kernels, expert_first(): pl.pallas_call(partial(first_kernel, chunk=chunk, index=index, local_coun...  41.7 us
    pallas_call x1, Pallas kernels, attend_back(): pl.pallas_call(partial(attend_back_kernel, block=block, size=size, scale=...  35.7 us
    ppermute x9, waiting for transfers between devices, shift(): lax.ppermute(rows, LINE, [(i, (i + step) % count) for i in range(count)])  32 us
    ppermute x9, starting transfers between devices, shift(): lax.ppermute(rows, LINE, [(i, (i + step) % count) for i in range(count)])  23.3 us
  transfers between devices with their start and end apart: 40, of which 23 were waited for; matrix products, arithmetic and copies ran while one was open for 5% of the time, Pallas kernels for 39%

profile of v4, /device:TPU:0, one launch (start us, length us, event | category | flops | bytes accessed | tf_op | source)
XLA Modules:
  0.0 621.3 jit_solution(15751667475666518995)
XLA Ops:
  10.9 5.1 collective-permute-start.2
  17.8 8.6 %collective-permute-done = bf16[96,768]{1,0:T(8,128)(2,1)S(1)} collective-permute-done((bf16[96,768]{1,0:T(8,128)(2,1)S(1)}, bf16[96,768]{1,0:T(8,128)(2,1)S(1)}, u32[]{:S(2)}, u32[]{:S(2)}) %collective-permute-start) | collective-permute-done | bytes 147488 | tf_op jit(solution)/shard_map/ppermute | solution.py:692
  34.0 9.7 %shard_map.252 = (bf16[8,160,768]{2,1,0:T(8,128)(2,1)}, bf16[8,2,160,768]{3,2,1,0:T(8,128)(2,1)}, f32[8,1,320]{2,1,0:T(1,128)}) custom-call(s32[2,1024]{1,0:T(2,128)} %shard_map.247.slots_ref, f32[2,1024]{1,0:T(2,128)} %bitcast_convert_fusion.routes_ref, bf16[1024,768]{1,0:T(8,128)(2,1)} %cot_ref.5), custom_call_target="tpu_custom_call" | custom-call | tf_op jit(solution)/shard_map/pallas_call | solution.py:126
  43.7 8.0 %all_to_all.30 = f32[8,1,320]{2,1,0:T(1,128)S(1)} all-to-all(f32[8,1,320]{2,1,0:T(1,128)} %get-tuple-element.60), channel_id=1, replica_groups=mesh['expert'=8,'shard'=4] {'expert'}, dimensions={0} | all-to-all | bytes 20480 | tf_op jit(solution)/shard_map/all_to_all | solution.py:761
  59.6 30.0 %collective-permute-done.4 = bf16[2,2,72,768]{3,2,1,0:T(8,128)(2,1)S(1)} collective-permute-done((bf16[2,2,72,768]{3,2,1,0:T(8,128)(2,1)S(1)}, bf16[2,2,72,768]{3,2,1,0:T(8,128)(2,1)S(1)}, u32[]{:S(2)}, u32[]{:S(2)}) %collective-permute-start.4) | collective-permute-done | bytes 442400 | tf_op jit(solution)/shard_map/ppermute | solution.py:687
  93.6 8.4 %shard_map.248 = (bf16[768,768]{1,0:T(8,128)(2,1)}, bf16[768,768]{1,0:T(8,128)(2,1)}, bf16[768,768]{1,0:T(8,128)(2,1)}, bf16[1024,768]{1,0:T(8,128)(2,1)}, bf16[...) custom-call(s32[1]{0:T(128)} %bitcast.1.owner_ref, bf16[1024,768]{1,0:T(8,128)(2,1)} %inputs_ref.5, ...), custom_call_target="tpu_custom_call" | custom-call | tf_op jit(solution)/shard_map/pallas_call | solution.py:587
  102.0 22.6 %shard_map.249 = (bf16[1024,768]{1,0:T(8,128)(2,1)}, f32[6,2,1024]{2,1,0:T(2,128)}) custom-call(bf16[1024,768]{1,0:T(8,128)(2,1)} %get-tuple-element.52.query_ref, bf16[1024,768]{1,0:T(8,128)(2,1)} %get-tuple-element.53.key_ref, bf16[1024,768]{1,0:T(8,128)(2,1)} %get-tuple-element.54.value_ref, f32[6,2,256]{2,1,0:T(2,128)} %copy.39.refs_4_.near_ref), custom_call_target="tpu_custom_call" | custom-call | tf_op jit(solution)/shard_map/pallas_call | solution.py:456
  124.6 6.3 %shard_map.250 = (f32[1024,768]{1,0:T(8,128)}, bf16[1024,768]{1,0:T(8,128)(2,1)}, f32[2,1024]{1,0:T(2,128)}) custom-call(bf16[1024,768]{1,0:T(8,128)(2,1)} %get-tuple-element.55.mixed_ref.out_ref.left_ref, bf16[768,768]{1,0:T(8,128)(2,1)} %all-gather.2.cloned.1.call-done.merge_ref, bf16[1024,768]{1,0:T(8,128)(2,1)} %inputs_ref.5, ...), custom_call_target="tpu_custom_call" | custom-call | tf_op jit(solution)/shard_map/pallas_call | solution.py:618
  131.0 5.6 shard_map.251
  140.2 6.5 %shard_map.256 = bf16[8,2,160,768]{3,2,1,0:T(8,128)(2,1)} custom-call(s32[2,1024]{1,0:T(2,128)} %shard_map.247.slots_ref, bf16[1024,768]{1,0:T(8,128)(2,1)} %get-tuple-element.58.rows_ref, bf16[8,2,160,768]{3,2,1,0:T(8,128)(2,1)} %get-tuple-element.67.into_ref), custom_call_target="tpu_custom_call", output_to_operand_aliasing={{}: (2, {})} | custom-call | tf_op jit(solution)/shard_map/pallas_call | solution.py:95
  146.7 18.6 %all-to-all-done.rows_ref = bf16[8,160,768]{2,1,0:T(8,128)(2,1)S(1)} async-done(((bf16[8,160,768]{2,1,0:T(8,128)(2,1)}), bf16[8,160,768]{2,1,0:T(8,128)(2,1)S(1)}, u32[]{:S(2)}, u32[]{:S(2)}) %all-to-all-start) | async-done | bytes 1966112 | tf_op jit(solution)/shard_map/all_to_all | solution.py:761
  172.9 20.7 %shard_map.253 = (bf16[1280,3072]{1,0:T(8,128)(2,1)}, bf16[1280,3072]{1,0:T(8,128)(2,1)}, bf16[4,768,768]{2,1,0:T(8,128)(2,1)}, bf16[1280,768]{1,0:T(8,128)(2,1)}) custom-call(s32[1]{0:T(128)} %bitcast.1.owner_ref, bf16[8,160,768]{2,1,0:T(8,128)(2,1)} %copy-done.2, bf16[8,160,768]{2,1,0:T(8,128)(2,1)} %all-to-all-done.1.cot_ref, ...), custom_call_target="tpu_custom_call" | custom-call | tf_op jit(solution)/shard_map/pallas_call | solution.py:197
  193.6 36.1 %shard_map.254 = (bf16[8,2,160,768]{3,2,1,0:T(8,128)(2,1)}, bf16[4,1536,768]{2,1,0:T(8,128)(2,1)}) custom-call(bf16[8,160,768]{2,1,0:T(8,128)(2,1)} %copy-done.2, bf16[1280,768]{1,0:T(8,128)(2,1)} %get-tuple-element.61.grad_ref, bf16[1280,3072]{1,0:T(8,128)(2,1)} %get-tuple-element.62.act_ref, bf16[1280,3072]{1,0:T(8,128)(2,1)} %get-tuple-element.63.slope_ref, ...), custom_call_target="tpu_custom_call" | custom-call | tf_op jit(solution)/shard_map/pallas_call | solution.py:252
  229.7 21.0 %shard_map.257 = (bf16[1280,3072]{1,0:T(8,128)(2,1)}, bf16[1280,3072]{1,0:T(8,128)(2,1)}, bf16[4,1536,768]{2,1,0:T(8,128)(2,1)}, bf16[1280,768]{1,0:T(8,128)(2,1)}) custom-call(s32[1]{0:T(128)} %bitcast.1.owner_ref, bf16[8,2,160,768]{3,2,1,0:T(8,128)(2,1)} %all-to-all-done.4.rows_ref.cot_ref, ...), custom_call_target="tpu_custom_call", output_to_operand_aliasing={{2}: (6, {})} | custom-call | tf_op jit(solution)/shard_map/pallas_call | solution.py:197
  255.9 35.1 %shard_map.258 = (bf16[8,2,160,768]{3,2,1,0:T(8,128)(2,1)}, bf16[4,768,768]{2,1,0:T(8,128)(2,1)}) custom-call(bf16[8,2,160,768]{3,2,1,0:T(8,128)(2,1)} %all-to-all-done.4.rows_ref.cot_ref, bf16[1280,768]{1,0:T(8,128)(2,1)} %get-tuple-element.69.grad_ref, bf16[1280,3072]{1,0:T(8,128)(2,1)} %get-tuple-element.70.act_ref, ...), custom_call_target="tpu_custom_call" | custom-call | tf_op jit(solution)/shard_map/pallas_call | solution.py:252
  291.0 11.2 %all-to-all-done.3.made_ref.back_ref = bf16[8,2,160,768]{3,2,1,0:T(8,128)(2,1)} async-done(((bf16[8,2,160,768]{3,2,1,0:T(8,128)(2,1)}), bf16[8,2,160,768]{3,2,1,0:T(8,128)(2,1)}, u32[]{:S(2)}, u32[]{:S(2)}) %all-to-all-start.3) | async-done | bytes 3932192 | tf_op jit(solution)/shard_map/all_to_all | solution.py:761
  302.2 4.6 all-to-all-start.5
  308.7 11.2 %shard_map.255 = (f32[1024,768]{1,0:T(8,128)}, f32[1024,128]{1,0:T(8,128)}, f32[1024,768]{1,0:T(8,128)}) custom-call(s32[2,1024]{1,0:T(2,128)} %shard_map.247.slots_ref, f32[2,1024]{1,0:T(2,128)} %get-tuple-element.56.gates_ref, f32[1024,768]{1,0:T(8,128)} %get-tuple-element.57.resid_ref, bf16[1024,768]{1,0:T(8,128)(2,1)} %cot_ref.5, ...), custom_call_target="tpu_custom_call" | custom-call | tf_op jit(solution)/shard_map/pallas_call | solution.py:303
  319.9 33.2 %all-to-all-done.5.made_ref.back_ref = bf16[8,2,160,768]{3,2,1,0:T(8,128)(2,1)} async-done(((bf16[8,2,160,768]{3,2,1,0:T(8,128)(2,1)}), bf16[8,2,160,768]{3,2,1,0:T(8,128)(2,1)}, u32[]{:S(2)}, u32[]{:S(2)}) %all-to-all-start.5) | async-done | bytes 3932192 | tf_op jit(solution)/shard_map/all_to_all | solution.py:761
  353.1 9.5 %shard_map.259 = (bf16[1024,768]{1,0:T(8,128)(2,1)}, bf16[1024,128]{1,0:T(8,128)(2,1)}) custom-call(s32[2,1024]{1,0:T(2,128)} %shard_map.247.slots_ref, s32[2,1024]{1,0:T(2,128)} %bitcast.75, f32[2,1024]{1,0:T(2,128)} %get-tuple-element.56.gates_ref, f32[1024,768]{1,0:T(8,128)} %get-tuple-element.65.result_ref, f32[1024,128]{1,0:T(8,128)} %get-tuple-element.66.inner_ref, ...), custom_call_target="tpu_custom_call" | custom-call | tf_op jit(solution)/shard_map/pallas_call | solution.py:344
  364.0 10.6 %shard_map.260 = (f32[1024,768]{1,0:T(8,128)}, bf16[1024,768]{1,0:T(8,128)(2,1)}, bf16[1024,768]{1,0:T(8,128)(2,1)}, f32[1,768]{1,0:T(1,128)}) custom-call(s32[2,1024]{1,0:T(2,128)} %shard_map.247.slots_ref, bf16[1024,128]{1,0:T(8,128)(2,1)} %get-tuple-element.74.logit_ref, bf16[128,768]{1,0:T(8,128)(2,1)} %pad.35.router_ref, f32[1,768]{1,0:T(1,128)} %reshape.129.gain_ref, ...), custom_call_target="tpu_custom_call" | custom-call | tf_op jit(solution)/shard_map/pallas_call | solution.py:380
  378.9 35.7 %shard_map.261 = (bf16[3,1024,768]{2,1,0:T(8,128)(2,1)}, f32[6,4,256]{2,1,0:T(4,128)}) custom-call(bf16[1024,768]{1,0:T(8,128)(2,1)} %get-tuple-element.52.query_ref, bf16[1024,768]{1,0:T(8,128)(2,1)} %get-tuple-element.53.key_ref, bf16[1024,768]{1,0:T(8,128)(2,1)} %get-tuple-element.54.value_ref, bf16[1024,768]{1,0:T(8,128)(2,1)} %get-tuple-element.76.grad_ref, ...), custom_call_target="tpu_custom_call" | custom-call | tf_op jit(solution)/shard_map/pallas_call | solution.py:536
  415.6 9.9 %shard_map.262 = (f32[1024,768]{1,0:T(8,128)}, f32[1,768]{1,0:T(1,128)}) custom-call(bf16[3,1024,768]{2,1,0:T(8,128)(2,1)} %get-tuple-element.78.heads_ref.right_ref, bf16[768,768]{1,0:T(8,128)(2,1)} %get-tuple-element.79.query_ref, bf16[768,768]{1,0:T(8,128)(2,1)} %get-tuple-element.80.key_ref, bf16[768,768]{1,0:T(8,128)(2,1)} %get-tuple-element.81.value_ref, ...), custom_call_target="tpu_custom_call" | custom-call | tf_op jit(solution)/shard_map/pallas_call | solution.py:646
  429.3 8.6 %shard_map.264 = bf16[4,576,768]{2,1,0:T(8,128)(2,1)} custom-call(bf16[1024,768]{1,0:T(8,128)(2,1)} %get-tuple-element.88.left_ref, bf16[3,1024,768]{2,1,0:T(8,128)(2,1)} %get-tuple-element.78.heads_ref.right_ref), custom_call_target="tpu_custom_call" | custom-call | tf_op jit(solution)/shard_map/pallas_call | solution.py:670
  443.0 11.0 %collective-permute-done.10 = bf16[4,64,768]{2,1,0:T(8,128)(2,1)S(1)} collective-permute-done((bf16[4,64,768]{2,1,0:T(8,128)(2,1)S(1)}, bf16[4,64,768]{2,1,0:T(8,128)(2,1)S(1)}, u32[]{:S(2)}, u32[]{:S(2)}) %collective-permute-start.10) | collective-permute-done | bytes 393248 | tf_op jit(solution)/shard_map/ppermute | solution.py:687
  454.2 6.0 collective-permute-done.11
  463.4 7.4 %collective-permute-start.12 = (bf16[32,768]{1,0:T(8,128)(2,1)S(1)}, bf16[32,768]{1,0:T(8,128)(2,1)S(1)}, u32[]{:S(2)}, u32[]{:S(2)}) collective-permute-start(bf16[32,768]{1,0:T(8,128)(2,1)S(1)} %get-tuple-element.108), channel_id=1, source_target_pairs={{0,1},{1,2},{2,3},{3,0},{4,5},{5,6},{6,7},{7,4},{8,9},{9,10},{10,1... | collective-permute-start | bytes 147464 | tf_op jit(solution)/shard_map/ppermute | solution.py:692
  470.8 5.5 collective-permute-start.13
  479.3 6.6 %collective-permute-done.13 = bf16[32,768]{1,0:T(8,128)(2,1)S(1)} collective-permute-done((bf16[32,768]{1,0:T(8,128)(2,1)S(1)}, bf16[32,768]{1,0:T(8,128)(2,1)S(1)}, u32[]{:S(2)}, u32[]{:S(2)}) %collective-permute-start.13) | collective-permute-done | bytes 49184 | tf_op jit(solution)/shard_map/ppermute | solution.py:692
  499.9 5.7 collective-permute-done.23
  505.6 6.3 %collective-permute-done.24 = bf16[72,768]{1,0:T(8,128)(2,1)S(1)} collective-permute-done((bf16[72,768]{1,0:T(8,128)(2,1)S(1)}, bf16[72,768]{1,0:T(8,128)(2,1)S(1)}, u32[]{:S(2)}, u32[]{:S(2)}) %collective-permute-start.24) | collective-permute-done | bytes 110624 | tf_op jit(solution)/shard_map/ppermute | solution.py:692
  532.3 78.5 %reduce-scatter.6.cloned.1.call-done = bf16[768,768]{1,0:T(8,128)(2,1)} async-done(((bf16[3072,768]{1,0:T(8,128)(2,1)}), bf16[768,768]{1,0:T(8,128)(2,1)}) %reduce-scatter.6.cloned.1.call-update) | async-done | bytes 1179664 | tf_op jit(solution)/shard_map/reduce_scatter | solution.py:757
  (194 shorter events, 102.8 us)
Async XLA Ops:
  7.2 117.4 %all-gather.2.cloned.1.call-start = ((), (), s32[]{:S(2)}) async-start(), calls=%async_computation.9 | async-start | bytes 1474560 | tf_op jit(solution)/shard_map/all_gather | solution.py:825
  10.9 17.7 %collective-permute-start.2 = (bf16[96,768]{1,0:T(8,128)(2,1)S(1)}, bf16[96,768]{1,0:T(8,128)(2,1)S(1)}, u32[]{:S(2)}, u32[]{:S(2)}) collective-permute-start(bf16[96,768]{1,0:T(8,128)(2,1)S(1)} %concatenate.86), channel_id=1, source_target_pairs={{0,3},{1,0},{2,1},{3,2},{4,7},{5,4},{6,5},{7,6},{8,11},{9,8},{10,9... | collective-permute-start | bytes 442376 | tf_op jit(solution)/shard_map/ppermute | solution.py:692
  16.0 12.5 %collective-permute-start.1 = (bf16[96,768]{1,0:T(8,128)(2,1)S(1)}, bf16[96,768]{1,0:T(8,128)(2,1)S(1)}, u32[]{:S(2)}, u32[]{:S(2)}) collective-permute-start(bf16[96,768]{1,0:T(8,128)(2,1)S(1)} %concatenate.86), channel_id=1, source_target_pairs={{0,2},{1,3},{2,0},{3,1},{4,6},{5,7},{6,4},{7,5},{8,10},{9,11},{10,... | collective-permute-start | bytes 442376 | tf_op jit(solution)/shard_map/ppermute | solution.py:692
  16.0 10.4 %collective-permute-start = (bf16[96,768]{1,0:T(8,128)(2,1)S(1)}, bf16[96,768]{1,0:T(8,128)(2,1)S(1)}, u32[]{:S(2)}, u32[]{:S(2)}) collective-permute-start(bf16[96,768]{1,0:T(8,128)(2,1)S(1)} %concatenate.86), channel_id=1, source_target_pairs={{0,1},{1,2},{2,3},{3,0},{4,5},{5,6},{6,7},{7,4},{8,9},{9,10},{10,1... | collective-permute-start | bytes 442376 | tf_op jit(solution)/shard_map/ppermute | solution.py:692
  28.7 29.4 %collective-permute-start.6 = (bf16[1,2,72,768]{3,2,1,0:T(8,128)(2,1)S(1)}, bf16[1,2,72,768]{3,2,1,0:T(8,128)(2,1)S(1)}, u32[]{:S(2)}, u32[]{:S(2)}) collective-permute-start(bf16[1,2,72,768]{3,2,1,0:T(8,128)(2,1)S(1)} %get-tuple-element.103), channel_id=1, source_target_pairs={{0,16},{4,20},{8,24},{12,28},{16,0},{20,4},{24,8},{28,12},{1,17},{... | collective-permute-start | bytes 663560 | tf_op jit(solution)/shard_map/ppermute | solution.py:687
  30.2 25.8 %collective-permute-start.3 = (bf16[1,2,72,768]{3,2,1,0:T(8,128)(2,1)S(1)}, bf16[1,2,72,768]{3,2,1,0:T(8,128)(2,1)S(1)}, u32[]{:S(2)}, u32[]{:S(2)}) collective-permute-start(bf16[1,2,72,768]{3,2,1,0:T(8,128)(2,1)S(1)} %get-tuple-element.104), channel_id=1, source_target_pairs={{0,8},{4,12},{8,0},{12,4},{16,24},{20,28},{24,16},{28,20},{1,9},{5... | collective-permute-start | bytes 663560 | tf_op jit(solution)/shard_map/ppermute | solution.py:687
  51.7 84.9 %all-to-all-start.1 = ((bf16[8,160,768]{2,1,0:T(8,128)(2,1)}), bf16[8,160,768]{2,1,0:T(8,128)(2,1)}, u32[]{:S(2)}, u32[]{:S(2)}) async-start(bf16[8,160,768]{2,1,0:T(8,128)(2,1)} %get-tuple-element.59), calls=%async_computation.1 | async-start | bytes 3932160 | tf_op jit(solution)/shard_map/all_to_all | solution.py:761
  56.1 33.6 %collective-permute-start.4 = (bf16[2,2,72,768]{3,2,1,0:T(8,128)(2,1)S(1)}, bf16[2,2,72,768]{3,2,1,0:T(8,128)(2,1)S(1)}, u32[]{:S(2)}, u32[]{:S(2)}) collective-permute-start(bf16[2,2,72,768]{3,2,1,0:T(8,128)(2,1)S(1)} %pad_maximum_fusion.2), channel_id=1, source_target_pairs={{0,16},{4,20},{8,24},{12,28},{16,0},{20,4},{24,8},{28,12},{1,17},{... | collective-permute-start | bytes 1327112 | tf_op jit(solution)/shard_map/ppermute | solution.py:687
  58.1 31.7 %collective-permute-start.7 = (bf16[2,2,72,768]{3,2,1,0:T(8,128)(2,1)S(1)}, bf16[2,2,72,768]{3,2,1,0:T(8,128)(2,1)S(1)}, u32[]{:S(2)}, u32[]{:S(2)}) collective-permute-start(bf16[2,2,72,768]{3,2,1,0:T(8,128)(2,1)S(1)} %pad_maximum_fusion.3), channel_id=1, source_target_pairs={{0,8},{4,12},{8,0},{12,4},{16,24},{20,28},{24,16},{28,20},{1,9},{5... | collective-permute-start | bytes 1327112 | tf_op jit(solution)/shard_map/ppermute | solution.py:687
  136.6 28.8 %all-to-all-start = ((bf16[8,160,768]{2,1,0:T(8,128)(2,1)}), bf16[8,160,768]{2,1,0:T(8,128)(2,1)S(1)}, u32[]{:S(2)}, u32[]{:S(2)}) async-start(bf16[8,160,768]{2,1,0:T(8,128)(2,1)} %bitcast.67), calls=%async_computation | async-start | bytes 3932160 | tf_op jit(solution)/shard_map/all_to_all | solution.py:761
  166.6 63.1 %all-to-all-start.4 = ((bf16[8,2,160,768]{3,2,1,0:T(8,128)(2,1)}), bf16[8,2,160,768]{3,2,1,0:T(8,128)(2,1)}, u32[]{:S(2)}, u32[]{:S(2)}) async-start(bf16[8,2,160,768]{3,2,1,0:T(8,128)(2,1)} %shard_map.256), calls=%async_computation.4 | async-start | bytes 7864320 | tf_op jit(solution)/shard_map/all_to_all | solution.py:761
  171.1 355.4 %reduce-scatter.4.cloned.1.call-start = ((), (), s32[]{:S(2)}) async-start(), calls=%async_computation.10 | async-start | bytes 11796480 | tf_op jit(solution)/shard_map/reduce_scatter | solution.py:757
  250.7 277.6 %reduce-scatter.8.cloned.1.call-start = ((), (), s32[]{:S(2)}) async-start(), calls=%async_computation.12 | async-start | bytes 5898240 | tf_op jit(solution)/shard_map/reduce_scatter | solution.py:757
  251.4 50.8 %all-to-all-start.3 = ((bf16[8,2,160,768]{3,2,1,0:T(8,128)(2,1)}), bf16[8,2,160,768]{3,2,1,0:T(8,128)(2,1)}, u32[]{:S(2)}, u32[]{:S(2)}) async-start(bf16[8,2,160,768]{3,2,1,0:T(8,128)(2,1)} %get-tuple-element.64), calls=%async_computation.3 | async-start | bytes 7864320 | tf_op jit(solution)/shard_map/all_to_all | solution.py:761
  302.2 50.9 %all-to-all-start.5 = ((bf16[8,2,160,768]{3,2,1,0:T(8,128)(2,1)}), bf16[8,2,160,768]{3,2,1,0:T(8,128)(2,1)}, u32[]{:S(2)}, u32[]{:S(2)}) async-start(bf16[8,2,160,768]{3,2,1,0:T(8,128)(2,1)} %get-tuple-element.72), calls=%async_computation.5 | async-start | bytes 7864320 | tf_op jit(solution)/shard_map/all_to_all | solution.py:761
  306.8 304.0 %reduce-scatter.6.cloned.1.call-start = ((), (), s32[]{:S(2)}) async-start(), calls=%async_computation.11 | async-start | bytes 5898240 | tf_op jit(solution)/shard_map/reduce_scatter | solution.py:757
  429.3 12.2 %collective-permute-start.9 = (bf16[4,128,768]{2,1,0:T(8,128)(2,1)}, bf16[4,128,768]{2,1,0:T(8,128)(2,1)}, u32[]{:S(2)}, u32[]{:S(2)}) collective-permute-start(bf16[4,128,768]{2,1,0:T(8,128)(2,1)} %constant_dynamic-slice_fusion.7), channel_id=1, source_target_pairs={{0,4},{4,0},{8,12},{12,8},{16,20},{20,16},{24,28},{28,24},{1,5},{5... | collective-permute-start | bytes 2359304 | tf_op jit(solution)/shard_map/ppermute | solution.py:687
  440.8 19.5 %collective-permute-start.18 = (bf16[4,288,768]{2,1,0:T(8,128)(2,1)}, bf16[4,288,768]{2,1,0:T(8,128)(2,1)}, u32[]{:S(2)}, u32[]{:S(2)}) collective-permute-start(bf16[4,288,768]{2,1,0:T(8,128)(2,1)} %constant_dynamic-slice_fusion.4), channel_id=1, source_target_pairs={{0,4},{4,0},{8,12},{12,8},{16,20},{20,16},{24,28},{28,24},{1,5},{5... | collective-permute-start | bytes 5308424 | tf_op jit(solution)/shard_map/ppermute | solution.py:687
  442.8 11.1 %collective-permute-start.10 = (bf16[4,64,768]{2,1,0:T(8,128)(2,1)S(1)}, bf16[4,64,768]{2,1,0:T(8,128)(2,1)S(1)}, u32[]{:S(2)}, u32[]{:S(2)}) collective-permute-start(bf16[4,64,768]{2,1,0:T(8,128)(2,1)S(1)} %constant_dynamic-slice_fusion.6), channel_id=1, source_target_pairs={{0,16},{4,20},{8,24},{12,28},{16,0},{20,4},{24,8},{28,12},{1,17},{... | collective-permute-start | bytes 1179656 | tf_op jit(solution)/shard_map/ppermute | solution.py:687
  454.1 6.1 collective-permute-start.11
  462.8 24.5 %collective-permute-start.21 = (bf16[4,64,768]{2,1,0:T(8,128)(2,1)S(1)}, bf16[4,64,768]{2,1,0:T(8,128)(2,1)S(1)}, u32[]{:S(2)}, u32[]{:S(2)}) collective-permute-start(bf16[4,64,768]{2,1,0:T(8,128)(2,1)S(1)} %constant_dynamic-slice_fusion.1), channel_id=1, source_target_pairs={{0,16},{4,20},{8,24},{12,28},{16,0},{20,4},{24,8},{28,12},{1,17},{... | collective-permute-start | bytes 1179656 | tf_op jit(solution)/shard_map/ppermute | solution.py:687
  463.4 13.3 %collective-permute-start.12 = (bf16[32,768]{1,0:T(8,128)(2,1)S(1)}, bf16[32,768]{1,0:T(8,128)(2,1)S(1)}, u32[]{:S(2)}, u32[]{:S(2)}) collective-permute-start(bf16[32,768]{1,0:T(8,128)(2,1)S(1)} %get-tuple-element.108), channel_id=1, source_target_pairs={{0,1},{1,2},{2,3},{3,0},{4,5},{5,6},{6,7},{7,4},{8,9},{9,10},{10,1... | collective-permute-start | bytes 147464 | tf_op jit(solution)/shard_map/ppermute | solution.py:692
  470.8 8.5 %collective-permute-start.14 = (bf16[32,768]{1,0:T(8,128)(2,1)S(1)}, bf16[32,768]{1,0:T(8,128)(2,1)S(1)}, u32[]{:S(2)}, u32[]{:S(2)}) collective-permute-start(bf16[32,768]{1,0:T(8,128)(2,1)S(1)} %get-tuple-element.109), channel_id=1, source_target_pairs={{0,3},{1,0},{2,1},{3,2},{4,7},{5,4},{6,5},{7,6},{8,11},{9,8},{10,9... | collective-permute-start | bytes 147464 | tf_op jit(solution)/shard_map/ppermute | solution.py:692
  470.8 15.1 %collective-permute-start.13 = (bf16[32,768]{1,0:T(8,128)(2,1)S(1)}, bf16[32,768]{1,0:T(8,128)(2,1)S(1)}, u32[]{:S(2)}, u32[]{:S(2)}) collective-permute-start(bf16[32,768]{1,0:T(8,128)(2,1)S(1)} %get-tuple-element.110), channel_id=1, source_target_pairs={{0,2},{1,3},{2,0},{3,1},{4,6},{5,7},{6,4},{7,5},{8,10},{9,11},{10,... | collective-permute-start | bytes 147464 | tf_op jit(solution)/shard_map/ppermute | solution.py:692
  476.4 12.4 %collective-permute-start.19 = (bf16[4,80,768]{2,1,0:T(8,128)(2,1)S(1)}, bf16[4,80,768]{2,1,0:T(8,128)(2,1)S(1)}, u32[]{:S(2)}, u32[]{:S(2)}) collective-permute-start(bf16[4,80,768]{2,1,0:T(8,128)(2,1)S(1)} %constant_dynamic-slice_fusion.3), channel_id=1, source_target_pairs={{0,8},{4,12},{8,0},{12,4},{16,24},{20,28},{24,16},{28,20},{1,9},{5... | collective-permute-start | bytes 1474568 | tf_op jit(solution)/shard_map/ppermute | solution.py:687
  487.5 5.7 collective-permute-start.22
  489.0 6.3 %collective-permute-start.20 = (bf16[4,40,768]{2,1,0:T(8,128)(2,1)S(1)}, bf16[4,40,768]{2,1,0:T(8,128)(2,1)S(1)}, u32[]{:S(2)}, u32[]{:S(2)}) collective-permute-start(bf16[4,40,768]{2,1,0:T(8,128)(2,1)S(1)} %constant_dynamic-slice_fusion.2), channel_id=1, source_target_pairs={{0,16},{4,20},{8,24},{12,28},{16,0},{20,4},{24,8},{28,12},{1,17},{... | collective-permute-start | bytes 737288 | tf_op jit(solution)/shard_map/ppermute | solution.py:687
  490.5 9.3 %collective-permute-start.16 = (bf16[64,768]{1,0:T(8,128)(2,1)S(1)}, bf16[64,768]{1,0:T(8,128)(2,1)S(1)}, u32[]{:S(2)}, u32[]{:S(2)}) collective-permute-start(bf16[64,768]{1,0:T(8,128)(2,1)S(1)} %maximum_select_fusion.6), channel_id=1, source_target_pairs={{0,16},{4,20},{8,24},{12,28},{16,0},{20,4},{24,8},{28,12},{1,17},{... | collective-permute-start | bytes 294920 | tf_op jit(solution)/shard_map/ppermute | solution.py:687
  495.4 10.2 %collective-permute-start.23 = (bf16[72,768]{1,0:T(8,128)(2,1)S(1)}, bf16[72,768]{1,0:T(8,128)(2,1)S(1)}, u32[]{:S(2)}, u32[]{:S(2)}) collective-permute-start(bf16[72,768]{1,0:T(8,128)(2,1)S(1)} %get-tuple-element.105), channel_id=1, source_target_pairs={{0,1},{1,2},{2,3},{3,0},{4,5},{5,6},{6,7},{7,4},{8,9},{9,10},{10,1... | collective-permute-start | bytes 331784 | tf_op jit(solution)/shard_map/ppermute | solution.py:692
  496.8 15.1 %collective-permute-start.24 = (bf16[72,768]{1,0:T(8,128)(2,1)S(1)}, bf16[72,768]{1,0:T(8,128)(2,1)S(1)}, u32[]{:S(2)}, u32[]{:S(2)}) collective-permute-start(bf16[72,768]{1,0:T(8,128)(2,1)S(1)} %get-tuple-element.106), channel_id=1, source_target_pairs={{0,2},{1,3},{2,0},{3,1},{4,6},{5,7},{6,4},{7,5},{8,10},{9,11},{10,... | collective-permute-start | bytes 331784 | tf_op jit(solution)/shard_map/ppermute | solution.py:692
  499.0 13.1 %collective-permute-start.25 = (bf16[72,768]{1,0:T(8,128)(2,1)S(1)}, bf16[72,768]{1,0:T(8,128)(2,1)S(1)}, u32[]{:S(2)}, u32[]{:S(2)}) collective-permute-start(bf16[72,768]{1,0:T(8,128)(2,1)S(1)} %get-tuple-element.107), channel_id=1, source_target_pairs={{0,3},{1,0},{2,1},{3,2},{4,7},{5,4},{6,5},{7,6},{8,11},{9,8},{10,9... | collective-permute-start | bytes 331784 | tf_op jit(solution)/shard_map/ppermute | solution.py:692
  499.8 13.0 %collective-permute-start.17 = (bf16[128,768]{1,0:T(8,128)(2,1)S(1)}, bf16[128,768]{1,0:T(8,128)(2,1)S(1)}, u32[]{:S(2)}, u32[]{:S(2)}) collective-permute-start(bf16[128,768]{1,0:T(8,128)(2,1)S(1)} %maximum_select_fusion.3), channel_id=1, source_target_pairs={{0,4},{4,0},{8,12},{12,8},{16,20},{20,16},{24,28},{28,24},{1,5},{5... | collective-permute-start | bytes 589832 | tf_op jit(solution)/shard_map/ppermute | solution.py:687
  (22 other events, 156.8 us)
Sparse Core Ops, SparseCore 0:
  17.2 30.5 all-gather.1
  250.8 169.9 reduce-scatter.3
  423.7 96.5 reduce-scatter.7
  523.0 87.7 reduce-scatter.5

commit v5 on v4

--- a/solution.py
+++ b/solution.py
@@ -80,55 +80,49 @@
     )(slots, rows, *after)
 
 
-def dispatch_into_kernel(slots_ref, rows_ref, into_ref, out_ref, *, start):
-    del into_ref
-    _, _, block, _ = out_ref.shape
-    tokens = rows_ref.shape[0]
+def dispatch_both_kernel(slots_ref, rows_ref, cot_ref, out_ref, *, start):
+    block, tokens = out_ref.shape[2], rows_ref.shape[0]
     slot = lax.broadcasted_iota(jnp.int32, (block, tokens), 0) + (pl.program_id(0) * block + start)
     hot = jnp.where((slot == slots_ref[0:1, :]) | (slot == slots_ref[1:2, :]), 1.0, 0.0)
-    out_ref[0, 0] = dot_nn(hot.astype(jnp.bfloat16), rows_ref[...]).astype(out_ref.dtype)
-
-
-def dispatch_into(slots, rows, start, into):
-    owners, _, capacity, width = into.shape
+    hot = hot.astype(jnp.bfloat16)
+    out_ref[0, 0] = dot_nn(hot, rows_ref[...]).astype(out_ref.dtype)
+    out_ref[0, 1] = dot_nn(hot, cot_ref[...]).astype(out_ref.dtype)
+
+
+def dispatch_both(slots, rows, cot, start, owners, capacity):
+    width = rows.shape[1]
     whole = lambda shape: pl.BlockSpec(shape, lambda i: (0, 0))
     return pl.pallas_call(
-        partial(dispatch_into_kernel, start=start),
+        partial(dispatch_both_kernel, start=start),
         grid=(owners,),
-        in_specs=[whole(slots.shape), whole(rows.shape), pl.BlockSpec(memory_space=pl.ANY)],
-        out_specs=pl.BlockSpec((1, 1, capacity, width), lambda i: (i, 0, 0, 0)),
-        out_shape=jax.ShapeDtypeStruct(into.shape, into.dtype),
-        input_output_aliases={2: 0},
-    )(slots, rows, into)
-
-
-def dispatch_all_kernel(slots_ref, routes_ref, rows_ref, *refs, owners, capacity):
-    out_refs, other_ref = refs[:-1], refs[-1]
-    block, tokens = len(out_refs) * capacity, rows_ref.shape[0]
+        in_specs=[whole(slots.shape), whole(rows.shape), whole(cot.shape)],
+        out_specs=pl.BlockSpec((1, 2, capacity, width), lambda i: (i, 0, 0, 0)),
+        out_shape=jax.ShapeDtypeStruct((owners, 2, capacity, width), rows.dtype),
+    )(slots, rows, cot)
+
+
+def dispatch_first_kernel(slots_ref, routes_ref, rows_ref, out_ref, other_ref, *, owners, capacity):
+    block, tokens = other_ref.shape[2], rows_ref.shape[0]
     row = lax.broadcasted_iota(jnp.int32, (block, tokens), 0)
     slot = row + pl.program_id(0) * capacity
-    for index in range(1, block // capacity):
-        slot = slot + jnp.where(row >= index * capacity, (owners - 1) * capacity, 0)
+    slot = slot + jnp.where(row >= capacity, (owners - 1) * capacity, 0)
     hits = [slot == slots_ref[c:c + 1, :] for c in range(2)]
-    hot = jnp.where(hits[0] | hits[1], 1.0, 0.0).astype(jnp.bfloat16)
-    picked = dot_nn(hot, rows_ref[...]).astype(rows_ref.dtype)
-    out_refs[0][0] = picked[:capacity]
-    out_refs[1][0, 0] = picked[capacity:]
+    hot = jnp.where(hits[0] | hits[1], 1.0, 0.0)[:capacity]
+    out_ref[0] = dot_nn(hot.astype(jnp.bfloat16), rows_ref[...]).astype(out_ref.dtype)
     other = jnp.where(hits[0], routes_ref[1:2, :], jnp.where(hits[1], routes_ref[0:1, :], 0.0))
     column = jnp.sum(other, axis=1, keepdims=True)
     other_ref[0] = jnp.broadcast_to(column, (block, 128)).T[0:1, :]
 
 
-def dispatch_all(slots, routes, rows, owners, capacity, local_count):
-    _, width = rows.shape
-    block = local_count * capacity
+def dispatch_first(slots, routes, rows, owners, capacity):
+    width = rows.shape[1]
     whole = lambda shape: pl.BlockSpec(shape, lambda i: (0, 0))
     return pl.pallas_call(
-        partial(dispatch_all_kernel, owners=owners, capacity=capacity),
+        partial(dispatch_first_kernel, owners=owners, capacity=capacity),
         grid=(owners,),
         in_specs=[whole(slots.shape), whole(routes.shape), whole(rows.shape)],
-        out_specs=[pl.BlockSpec((1, capacity, width), lambda i: (i, 0, 0)), pl.BlockSpec((1, 1, capacity, width), lambda i: (i, 1, 0, 0)), pl.BlockSpec((1, 1, block), lambda i: (i, 0, 0))],
-        out_shape=[jax.ShapeDtypeStruct((owners, capacity, width), rows.dtype), jax.ShapeDtypeStruct((owners, 2, capacity, width), rows.dtype), jax.ShapeDtypeStruct((owners, 1, block), jnp.float32)],
+        out_specs=[pl.BlockSpec((1, capacity, width), lambda i: (i, 0, 0)), pl.BlockSpec((1, 1, 2 * capacity), lambda i: (i, 0, 0))],
+        out_shape=[jax.ShapeDtypeStruct((owners, capacity, width), rows.dtype), jax.ShapeDtypeStruct((owners, 1, 2 * capacity), jnp.float32)],
     )(slots, routes, rows)
 
 
@@ -192,7 +186,7 @@
     if into is not None:
         aliases = {len(operands): 2}
         operands.append(into)
-        place, grad_shape = 1, jax.ShapeDtypeStruct(into.shape, into.dtype)
+        place, grad_shape = 2, jax.ShapeDtypeStruct(into.shape, into.dtype)
     operands += list(after)
     return pl.pallas_call(
         partial(first_kernel, chunk=chunk, index=index, local_count=local_count),
@@ -259,6 +253,72 @@
         scratch_shapes=[pltpu.VMEM((width, rows), jnp.bfloat16), pltpu.VMEM((rows, width), jnp.float32), pltpu.VMEM((rows, width), jnp.float32)],
         compiler_params=pltpu.CompilerParams(vmem_limit_bytes=62 << 20),
     )(rows_in, grad, act, slope, up, down, *after)
+
+
+def slope_kernel(rows_ref, grad_ref, slope_ref, down_ref, into_ref, low_ref, up_grad_ref, turned):
+    del into_ref
+    @pl.when(pl.program_id(0) == 0)
+    def _():
+        turned[...] = rows_ref[...].reshape(grad_ref.shape).T
+    grads = dot_nt(grad_ref[...], down_ref[0])
+    low = (slope_ref[...].astype(jnp.float32) * grads).astype(jnp.bfloat16)
+    low_ref[...] = low
+    up_grad_ref[0] = dot_nn(turned[...], low).astype(jnp.bfloat16)
+
+
+def expert_slope(rows_in, grad, slope, down, index, shards, into, place):
+    rows, width = grad.shape
+    hidden = slope.shape[1]
+    tile = hidden // shards
+    fixed = pl.BlockSpec((rows, width), lambda i: (0, 0))
+    column = pl.BlockSpec((rows, tile), lambda i: (0, i))
+    return pl.pallas_call(
+        slope_kernel,
+        grid=(shards,),
+        in_specs=[arrived_spec(rows_in, 0), fixed, column, pl.BlockSpec((1, tile, width), lambda i: (index, i, 0)), pl.BlockSpec(memory_space=pl.ANY)],
+        out_specs=[column, pl.BlockSpec((1, width, tile), lambda i: (i, place, 0))],
+        out_shape=[jax.ShapeDtypeStruct((rows, hidden), jnp.bfloat16), jax.ShapeDtypeStruct(into.shape, into.dtype)],
+        input_output_aliases={4: 1},
+        scratch_shapes=[pltpu.VMEM((width, rows), jnp.bfloat16)],
+        compiler_params=pltpu.CompilerParams(vmem_limit_bytes=62 << 20),
+    )(rows_in, grad, slope, down, into)
+
+
+def last_kernel(act_ref, low_ref, up_ref, down_ref, made_ref, made_acc, back_acc):
+    step = pl.program_id(0)
+    owners, _, capacity, width = made_ref.shape
+    back = dot_nt(low_ref[...], up_ref[0])
+    made = dot_nn(act_ref[...], down_ref[0])
+    last = pl.num_programs(0) - 1
+    @pl.when(step == 0)
+    def _():
+        made_acc[...] = made
+        back_acc[...] = back
+    @pl.when((step > 0) & (step < last))
+    def _():
+        made_acc[...] += made
+        back_acc[...] += back
+    @pl.when(step == last)
+    def _():
+        made_ref[:, 0] = (made_acc[...] + made).astype(jnp.bfloat16).reshape(owners, capacity, width)
+        made_ref[:, 1] = (back_acc[...] + back).astype(jnp.bfloat16).reshape(owners, capacity, width)
+
+
+def expert_last(act, low, up, down, index, owners, shards):
+    rows, hidden = act.shape
+    width = up.shape[1]
+    tile = hidden // shards
+    column = pl.BlockSpec((rows, tile), lambda i: (0, i))
+    made_shape = (owners, 2, rows // owners, width)
+    return pl.pallas_call(
+        last_kernel,
+        grid=(shards,),
+        in_specs=[column, column, pl.BlockSpec((1, width, tile), lambda i: (index, 0, i)), pl.BlockSpec((1, tile, width), lambda i: (index, i, 0))],
+        out_specs=pl.BlockSpec(made_shape, lambda i: (0, 0, 0, 0)),
+        out_shape=jax.ShapeDtypeStruct(made_shape, jnp.bfloat16),
+        scratch_shapes=[pltpu.VMEM((rows, width), jnp.float32), pltpu.VMEM((rows, width), jnp.float32)],
+        compiler_params=pltpu.CompilerParams(vmem_limit_bytes=62 << 20),
+    )(act, low, up, down)
 
 
 def spread(row, block):
@@ -653,29 +713,82 @@
     )(head_grads, query, key, value, gain, inputs, resid_grad)
 
 
-def weight_kernel(left_ref, right_ref, out_ref, turned):
+def weight_kernel(left_ref, mixed_ref, heads_ref, branch_ref, out_ref, turned, right):
     shards, part, _ = out_ref.shape
-    @pl.when(pl.program_id(0) == 0)
+    step = pl.program_id(0)
+    last = pl.num_programs(0) - 1
+    @pl.when(step == 0)
     def _():
         turned[...] = left_ref[...].T
-    right = right_ref[...]
+    @pl.when(step < last)
+    def _():
+        right[...] = heads_ref[...]
+    @pl.when(step == last)
+    def _():
+        turned[...] = mixed_ref[...].T
+        right[...] = branch_ref[...]
     for shard in range(shards):
-        grad = dot_nn(turned[shard * part:(shard + 1) * part, :], right)
+        grad = dot_nn(turned[shard * part:(shard + 1) * part, :], right[...])
         out_ref[shard] = grad.astype(jnp.bfloat16)
 
 
-def weight_grads(left, right, shards):
-    count, tokens, width = right.shape
+def weight_grads(left, mixed, head_grads, branch, shards):
+    count, tokens, width = head_grads.shape
     part = width // shards
+    fixed = pl.BlockSpec((tokens, width), lambda i: (0, 0))
     return pl.pallas_call(
         weight_kernel,
-        grid=(count,),
-        in_specs=[pl.BlockSpec((tokens, width), lambda i: (0, 0)), pl.BlockSpec((None, tokens, width), lambda i: (i, 0, 0))],
+        grid=(count + 1,),
+        in_specs=[fixed, fixed, pl.BlockSpec((None, tokens, width), lambda i: (jnp.minimum(i, count - 1), 0, 0)), fixed],
         out_specs=pl.BlockSpec((shards, part, width), lambda i: (0, i, 0)),
-        out_shape=jax.ShapeDtypeStruct((shards, count * part, width), jnp.bfloat16),
-        scratch_shapes=[pltpu.VMEM((width, tokens), jnp.bfloat16)],
-        compiler_params=pltpu.CompilerParams(vmem_limit_bytes=62 << 20),
-    )(left, right)
+        out_shape=jax.ShapeDtypeStruct((shards, (count + 1) * part, width), jnp.bfloat16),
+        scratch_shapes=[pltpu.VMEM((width, tokens), jnp.bfloat16), pltpu.VMEM((tokens, width), jnp.bfloat16)],
+        compiler_params=pltpu.CompilerParams(vmem_limit_bytes=62 << 20),
+    )(left, mixed, head_grads, branch)
+
+
+def widen_first_kernel(rows_ref, out_ref):
+    out_ref[...] = rows_ref[...].astype(jnp.float32)
+
+
+def widen_first(rows):
+    count, width = rows.shape
+    half = pl.BlockSpec((count // 2, width), lambda i: (i, 0))
+    return pl.pallas_call(
+        widen_first_kernel,
+        grid=(2,),
+        in_specs=[half],
+        out_specs=half,
+        out_shape=jax.ShapeDtypeStruct((2 * count, width), jnp.float32),
+        compiler_params=pltpu.CompilerParams(vmem_limit_bytes=62 << 20),
+    )(rows)
+
+
+def widen_rest_kernel(rows_ref, into_ref, up_ref, down_ref):
+    del into_ref
+    wide = rows_ref[...].astype(jnp.float32)
+    step = pl.program_id(0)
+    @pl.when(step < 4)
+    def _():
+        up_ref[...] = wide
+    @pl.when(step >= 4)
+    def _():
+        down_ref[...] = wide
+
+
+def widen_rest(rows, into):
+    count, width = rows.shape[0] // 3, rows.shape[1]
+    half = lambda place: pl.BlockSpec((count // 2, width), lambda i: (place(i), 0))
+    wide = jax.ShapeDtypeStruct((2 * count, width), jnp.float32)
+    return pl.pallas_call(
+        widen_rest_kernel,
+        grid=(6,),
+        in_specs=[half(lambda i: i), pl.BlockSpec(memory_space=pl.ANY)],
+        out_specs=[half(lambda i: jnp.minimum(i, 3)), half(lambda i: jnp.maximum(i - 4, 0) + 2)],
+        out_shape=[wide, wide],
+        input_output_aliases={1: 1},
+        compiler_params=pltpu.CompilerParams(vmem_limit_bytes=62 << 20),
+    )(rows, into)
 
 
 OWNER = "expert"
@@ -736,16 +849,16 @@
     )
 
 
-def reduce_stack(stack, bits, cuts):
-    stack = halve(stack, bits[0])
-    cuts = [0] + cuts + [stack.shape[1]]
-    parts = [stack[:, low:high] for low, high in zip(cuts, cuts[1:])]
+def reduce_rows(stack, bits):
+    unit = 8 << (len(bits) - 1)
+    cut = -(-stack.shape[1] // (2 * unit)) * unit
+    parts = [stack[:, :cut], stack[:, cut:]]
     orders = [bits[1:], bits[:0:-1]]
     for level in range(len(bits) - 1):
         parts = [halve(part, order[level]) for part, order in zip(parts, orders)]
-    sizes = [part.shape[1] for part in parts]
+    low = parts[0].shape[1]
     piece = line_sum(jnp.concatenate(parts, axis=1))
-    parts = [piece[: sizes[0]], piece[sizes[0] :]][: len(parts)]
+    parts = [piece[:low], piece[low:]]
     for level in reversed(range(len(bits) - 1)):
         parts = [grow(part, order[level]) for part, order in zip(parts, orders)]
     return grow(jnp.concatenate(parts), bits[0])
@@ -833,8 +946,8 @@
     routes_line = routes.T
     base = (routes_line % local_count * owners + routes_line // local_count) * capacity
     slots = find_slots(routes_line, base, experts)
-    cot_rows, joint, other = dispatch_all(
-        slots, routes_line.astype(f32), cotangent, owners, capacity, local_count
+    cot_rows, other = dispatch_first(
+        slots, routes_line.astype(f32), cotangent, owners, capacity
     )
     other = share_rows(other).reshape(owners, local_count, capacity)
 
@@ -857,23 +970,21 @@
 
     send = dispatch(slots, low_two, 0, rows).reshape(owners, capacity, width)
     rows_in = share_large(send)
-    joint = dispatch_into(slots, low_two, rows, joint)
+    joint = dispatch_both(slots, low_two, cotangent, rows, owners, capacity)
     joint_in = share_large(joint)
     others = [other[:, index].reshape(1, rows) for index in range(local_count)]
     act, slope, first_down, grad_in = expert_first(
     owner, rows_in, cot_in, others[0], router_full, up_weight, 0, local_count, shards,
     )
     first_sum = scatter_sum(first_down)
-    first_made, pair = expert_second(rows_in, grad_in, act, slope, up_weight, down_weight, 0, owners, shards, 2 * width)
+    first_made, pair = expert_second(rows_in, grad_in, act, slope, up_weight, down_weight, 0, owners, shards, 3 * width)
     act, slope, pair, grad_in = expert_first(
         owner, joint_in, joint_in, others[1], router_full, up_weight, 1, local_count, shards,
         into=pair,
     )
+    low, pair = expert_slope(joint_in, grad_in, slope, down_weight, 1, shards, pair, 1)
     pair_sum = scatter_sum(pair)
-    second_made, last_up = expert_second(
-        joint_in, grad_in, act, slope, up_weight, down_weight, 1, owners, shards, width
-    )
-    last_sum = scatter_sum(last_up)
+    second_made = expert_last(act, low, up_weight, down_weight, 1, owners, shards)
     returned = share_rows(first_made)
     result, inner, part_grads = combine_part(slots, gates, resid, cotangent, returned)
     returned = share_rows(second_made)
@@ -886,7 +997,6 @@
         part_grads, returned, epsilon
     )
     router_grad = jnp.einsum("te,ti->ei", logit_grad, low_two, preferred_element_type=f32)
-    merge_grad = weight_grads(attended, branch[None], shards)
     head_grads, distances = attend_back(
         queries, keys, values, mixed_grad, attended, totals, near, size, block
     )
@@ -894,7 +1004,8 @@
     far_sums = jnp.sum(distances[:, group:].reshape(heads, block), axis=1)
     table_grad = jnp.dot(close_sums, jnp.asarray(hot[:block]), precision=lax.Precision.HIGHEST)
     table_grad = table_grad + far_sums[:, None] * jnp.asarray(hot[-1:])
-    head_sums = weight_grads(low_one, head_grads, shards)
+    sums = weight_grads(low_one, attended, head_grads, branch, shards)
+    sums = halve(sums, bits[0])
     input_gradient, norm_grad = finish(
         head_grads, query_full, key_full, value_full, gain_one, inputs, resid_grad, epsilon
     )
@@ -904,25 +1015,27 @@
         table_grad.reshape(shards, local_heads, BUCKETS).astype(bf16),
         router_grad[:experts].reshape(experts, shards, part).transpose(1, 0, 2).astype(bf16),
     )
-    head_sums = reduce_stack(head_sums, bits, [5 * part // 6]).astype(f32)
     spare = -small_grad.shape[1] % (8 * owners)
-    small_grad = jnp.pad(small_grad, ((0, 0), (0, spare), (0, 0)))
-    rest_sums = jnp.concatenate([merge_grad, small_grad], axis=1)
-    rest_sums = reduce_stack(rest_sums, bits[:1] + bits[:0:-1], []).astype(f32)
-    small_sum = rest_sums[part:]
+    small_grad = halve(jnp.pad(small_grad, ((0, 0), (0, spare), (0, 0))), bits[0])
+    kept = sums.shape[1]
+    sums = reduce_rows(jnp.concatenate([sums, small_grad], axis=1), bits)
+    half = sums.shape[0] // 2
+    weights = jnp.concatenate([sums[:kept], sums[half : half + kept]]).astype(f32)
+    small_sum = jnp.concatenate([sums[kept:half], sums[half + kept :]]).astype(f32)
+    up_sum, down_sum = widen_rest(pair_sum, widen_first(first_sum))
     return (
         output,
         input_gradient,
         small_sum[0, :part],
-        head_sums[:part],
-        head_sums[part : 2 * part],
-        head_sums[2 * part :],
-        rest_sums[:part],
+        weights[:part],
+        weights[part : 2 * part],
+        weights[2 * part : 3 * part],
+        weights[3 * part :],
         small_sum[2 : 2 + local_heads, :BUCKETS].T,
         small_sum[1, :part],
         small_sum[router_at : router_at + experts, :part].T,
-        jnp.stack([pair_sum[:width].astype(f32), last_sum.astype(f32)]),
-        jnp.stack([first_sum.astype(f32), pair_sum[width:].astype(f32)]),
+        up_sum.reshape(local_count, width, width),
+        down_sum.reshape(local_count, width, width),
     )
 
 

time: 630 us -> 576 us (0.914)
  the two profiles are of different devices: /device:TPU:0 before, /device:TPU:9 now
where the time goes in v5:
time: 576 us; the launch traced here: 569 us
  Pallas kernels  275 us (48%)
  waiting for transfers between devices  176 us (31%)
  starting transfers between devices  64 us (11%)
  local copies, waits for them, and re-layouts  16.2 us (3%)
  between operations  14.5 us (3%)
  other arithmetic  12.1 us (2%)
  blocking collectives  9.92 us (2%)
    all_to_all x5, waiting for transfers between devices, share_rows(): return lax.all_to_all(rows, OWNER, 0, 0, tiled=True)  78.5 us
    ppermute x17, waiting for transfers between devices, exchange(): return lax.ppermute(rows, OWNER, [(i, i ^ bit) for i in range(count)])  57.9 us
    pallas_call x2, Pallas kernels, expert_first(): pl.pallas_call(partial(first_kernel, chunk=chunk, index=index, local_coun...  41.5 us
    ppermute x6, waiting for transfers between devices, shift(): lax.ppermute(rows, LINE, [(i, (i + step) % count) for i in range(count)])  40 us
    pallas_call x1, Pallas kernels, expert_second(): pl.pallas_call(second_kernel, grid=(shards,), in_specs=[arrived_spec(rows...  36.2 us
    pallas_call x1, Pallas kernels, attend_back(): pl.pallas_call(partial(attend_back_kernel, block=block, size=size, scale=...  35.6 us
    all_to_all x5, starting transfers between devices, share_rows(): return lax.all_to_all(rows, OWNER, 0, 0, tiled=True)  33.9 us
    pallas_call x1, Pallas kernels, attend(): pl.pallas_call(partial(attend_kernel, block=block, size=size, scale=size...  22.6 us
  transfers between devices with their start and end apart: 31, of which 20 were waited for; matrix products, arithmetic and copies ran while one was open for 4% of the time, Pallas kernels for 44%

profile of v5, /device:TPU:9, one launch (start us, length us, event | category | flops | bytes accessed | tf_op | source)
XLA Modules:
  0.0 568.7 jit_solution(9992798015594108880)
XLA Ops:
  16.2 10.1 %collective-permute-done.1 = bf16[96,768]{1,0:T(8,128)(2,1)S(1)} collective-permute-done((bf16[96,768]{1,0:T(8,128)(2,1)S(1)}, bf16[96,768]{1,0:T(8,128)(2,1)S(1)}, u32[]{:S(2)}, u32[]{:S(2)}) %collective-permute-start.1) | collective-permute-done | bytes 147488 | tf_op jit(solution)/shard_map/ppermute | solution.py:805
  36.3 6.8 %shard_map.252 = (bf16[8,160,768]{2,1,0:T(8,128)(2,1)}, f32[8,1,320]{2,1,0:T(1,128)}) custom-call(s32[2,1024]{1,0:T(2,128)} %shard_map.247.slots_ref, f32[2,1024]{1,0:T(2,128)} %bitcast_convert_fusion.routes_ref, bf16[1024,768]{1,0:T(8,128)(2,1)} %cot_ref.7), custom_call_target="tpu_custom_call" | custom-call | tf_op jit(solution)/shard_map/pallas_call | solution.py:120
  43.1 9.9 %all_to_all.30 = f32[8,1,320]{2,1,0:T(1,128)S(1)} all-to-all(f32[8,1,320]{2,1,0:T(1,128)} %get-tuple-element.61), channel_id=1, replica_groups=mesh['expert'=8,'shard'=4] {'expert'}, dimensions={0} | all-to-all | bytes 20480 | tf_op jit(solution)/shard_map/all_to_all | solution.py:874
  53.1 4.9 all-to-all-start.1
  60.8 30.1 %collective-permute-done.7 = bf16[2,2,72,768]{3,2,1,0:T(8,128)(2,1)S(1)} collective-permute-done((bf16[2,2,72,768]{3,2,1,0:T(8,128)(2,1)S(1)}, bf16[2,2,72,768]{3,2,1,0:T(8,128)(2,1)S(1)}, u32[]{:S(2)}, u32[]{:S(2)}) %collective-permute-start.7) | collective-permute-done | bytes 442400 | tf_op jit(solution)/shard_map/ppermute | solution.py:800
  95.5 8.5 %shard_map.248 = (bf16[768,768]{1,0:T(8,128)(2,1)}, bf16[768,768]{1,0:T(8,128)(2,1)}, bf16[768,768]{1,0:T(8,128)(2,1)}, bf16[1024,768]{1,0:T(8,128)(2,1)}, bf16[...) custom-call(s32[1]{0:T(128)} %bitcast.1.owner_ref, bf16[1024,768]{1,0:T(8,128)(2,1)} %inputs_ref.5, ...), custom_call_target="tpu_custom_call" | custom-call | tf_op jit(solution)/shard_map/pallas_call | solution.py:647
  103.9 22.6 %shard_map.249 = (bf16[1024,768]{1,0:T(8,128)(2,1)}, f32[6,2,1024]{2,1,0:T(2,128)}) custom-call(bf16[1024,768]{1,0:T(8,128)(2,1)} %get-tuple-element.53.query_ref, bf16[1024,768]{1,0:T(8,128)(2,1)} %get-tuple-element.54.key_ref, bf16[1024,768]{1,0:T(8,128)(2,1)} %get-tuple-element.55.value_ref, f32[6,2,256]{2,1,0:T(2,128)} %copy.40.refs_4_.near_ref), custom_call_target="tpu_custom_call" | custom-call | tf_op jit(solution)/shard_map/pallas_call | solution.py:516
  126.5 6.3 %shard_map.250 = (f32[1024,768]{1,0:T(8,128)}, bf16[1024,768]{1,0:T(8,128)(2,1)}, f32[2,1024]{1,0:T(2,128)}) custom-call(bf16[1024,768]{1,0:T(8,128)(2,1)} %get-tuple-element.56.mixed_ref.out_ref, bf16[768,768]{1,0:T(8,128)(2,1)} %all-gather.2.cloned.1.call-done.merge_ref, bf16[1024,768]{1,0:T(8,128)(2,1)} %inputs_ref.5, f32[1,768]{1,0:T(1,128)} %reshape.131.gain_ref, ...), custom_call_target="tpu_custom_call" | custom-call | tf_op jit(solution)/shard_map/pallas_call | solution.py:678
  132.9 5.6 shard_map.251
  144.1 20.7 %all-to-all-done.rows_ref = bf16[8,160,768]{2,1,0:T(8,128)(2,1)} async-done(((bf16[8,160,768]{2,1,0:T(8,128)(2,1)}), bf16[8,160,768]{2,1,0:T(8,128)(2,1)}, u32[]{:S(2)}, u32[]{:S(2)}) %all-to-all-start) | async-done | bytes 1966112 | tf_op jit(solution)/shard_map/all_to_all | solution.py:874
  164.8 20.7 %shard_map.253 = (bf16[1280,3072]{1,0:T(8,128)(2,1)}, bf16[1280,3072]{1,0:T(8,128)(2,1)}, bf16[4,768,768]{2,1,0:T(8,128)(2,1)}, bf16[1280,768]{1,0:T(8,128)(2,1)}) custom-call(s32[1]{0:T(128)} %bitcast.1.owner_ref, bf16[8,160,768]{2,1,0:T(8,128)(2,1)} %all-to-all-done.rows_ref, bf16[8,160,768]{2,1,0:T(8,128)(2,1)} %all-to-all-done.1.cot_ref, ...), custom_call_target="tpu_custom_call" | custom-call | tf_op jit(solution)/shard_map/pallas_call | solution.py:191
  185.5 8.5 %shard_map.256 = bf16[8,2,160,768]{3,2,1,0:T(8,128)(2,1)} custom-call(s32[2,1024]{1,0:T(2,128)} %shard_map.247.slots_ref, bf16[1024,768]{1,0:T(8,128)(2,1)} %get-tuple-element.59.rows_ref, bf16[1024,768]{1,0:T(8,128)(2,1)} %cot_ref.7), custom_call_target="tpu_custom_call" | custom-call | tf_op jit(solution)/shard_map/pallas_call | solution.py:95
  194.0 8.0 %all-to-all-start.4 = ((bf16[8,2,160,768]{3,2,1,0:T(8,128)(2,1)}), bf16[8,2,160,768]{3,2,1,0:T(8,128)(2,1)}, u32[]{:S(2)}, u32[]{:S(2)}) async-start(bf16[8,2,160,768]{3,2,1,0:T(8,128)(2,1)} %shard_map.256), calls=%async_computation.4 | async-start | bytes 7864320 | tf_op jit(solution)/shard_map/all_to_all | solution.py:874
  202.8 36.2 %shard_map.254 = (bf16[8,2,160,768]{3,2,1,0:T(8,128)(2,1)}, bf16[4,2304,768]{2,1,0:T(8,128)(2,1)}) custom-call(bf16[8,160,768]{2,1,0:T(8,128)(2,1)} %all-to-all-done.rows_ref, bf16[1280,768]{1,0:T(8,128)(2,1)} %get-tuple-element.62.grad_ref, bf16[1280,3072]{1,0:T(8,128)(2,1)} %get-tuple-element.63.act_ref, bf16[1280,3072]{1,0:T(8,128)(2,1)} %get-tuple-element.64.slope_ref, ...), custom_call_target="tpu_custom_call" | custom-call | tf_op jit(solution)/shard_map/pallas_call | solution.py:246
  239.0 5.9 %all-to-all-done.4.rows_ref.cot_ref = bf16[8,2,160,768]{3,2,1,0:T(8,128)(2,1)} async-done(((bf16[8,2,160,768]{3,2,1,0:T(8,128)(2,1)}), bf16[8,2,160,768]{3,2,1,0:T(8,128)(2,1)}, u32[]{:S(2)}, u32[]{:S(2)}) %all-to-all-start.4) | async-done | bytes 3932192 | tf_op jit(solution)/shard_map/all_to_all | solution.py:874
  244.9 20.8 %shard_map.257 = (bf16[1280,3072]{1,0:T(8,128)(2,1)}, bf16[1280,3072]{1,0:T(8,128)(2,1)}, bf16[4,2304,768]{2,1,0:T(8,128)(2,1)}, bf16[1280,768]{1,0:T(8,128)(2,1)}) custom-call(s32[1]{0:T(128)} %bitcast.1.owner_ref, bf16[8,2,160,768]{3,2,1,0:T(8,128)(2,1)} %all-to-all-done.4.rows_ref.cot_ref, ...), custom_call_target="tpu_custom_call", output_to_operand_aliasing={{2}: (6, {})} | custom-call | tf_op jit(solution)/shard_map/pallas_call | solution.py:191
  265.7 18.2 %shard_map.258 = (bf16[1280,3072]{1,0:T(8,128)(2,1)}, bf16[4,2304,768]{2,1,0:T(8,128)(2,1)}) custom-call(bf16[8,2,160,768]{3,2,1,0:T(8,128)(2,1)} %all-to-all-done.4.rows_ref.cot_ref, bf16[1280,768]{1,0:T(8,128)(2,1)} %get-tuple-element.70.grad_ref, bf16[1280,3072]{1,0:T(8,128)(2,1)} %get-tuple-element.71.slope_ref, ...), custom_call_target="tpu_custom_call", output_to_operand_aliasing={{1}: (4, {})} | custom-call | tf_op jit(solution)/shard_map/pallas_call | solution.py:275
  283.9 7.8 %all-to-all-start.3 = ((bf16[8,2,160,768]{3,2,1,0:T(8,128)(2,1)}), bf16[8,2,160,768]{3,2,1,0:T(8,128)(2,1)}, u32[]{:S(2)}, u32[]{:S(2)}) async-start(bf16[8,2,160,768]{3,2,1,0:T(8,128)(2,1)} %get-tuple-element.65), calls=%async_computation.3 | async-start | bytes 7864320 | tf_op jit(solution)/shard_map/all_to_all | solution.py:874
  291.8 21.8 %shard_map.259 = bf16[8,2,160,768]{3,2,1,0:T(8,128)(2,1)} custom-call(bf16[1280,3072]{1,0:T(8,128)(2,1)} %get-tuple-element.69.act_ref, bf16[1280,3072]{1,0:T(8,128)(2,1)} %get-tuple-element.73.low_ref, bf16[2,768,3072]{2,1,0:T(8,128)(2,1)} %up_ref.7, bf16[2,3072,768]{2,1,0:T(8,128)(2,1)} %down_ref.5), custom_call_target="tpu_custom_call" | custom-call | tf_op jit(solution)/shard_map/pallas_call | solution.py:313
  313.5 21.0 %all-to-all-done.3.made_ref.back_ref = bf16[8,2,160,768]{3,2,1,0:T(8,128)(2,1)} async-done(((bf16[8,2,160,768]{3,2,1,0:T(8,128)(2,1)}), bf16[8,2,160,768]{3,2,1,0:T(8,128)(2,1)}, u32[]{:S(2)}, u32[]{:S(2)}) %all-to-all-start.3) | async-done | bytes 3932192 | tf_op jit(solution)/shard_map/all_to_all | solution.py:874
  334.6 8.5 %all-to-all-start.5 = ((bf16[8,2,160,768]{3,2,1,0:T(8,128)(2,1)}), bf16[8,2,160,768]{3,2,1,0:T(8,128)(2,1)}, u32[]{:S(2)}, u32[]{:S(2)}) async-start(bf16[8,2,160,768]{3,2,1,0:T(8,128)(2,1)} %shard_map.259), calls=%async_computation.5 | async-start | bytes 7864320 | tf_op jit(solution)/shard_map/all_to_all | solution.py:874
  343.8 11.2 %shard_map.255 = (f32[1024,768]{1,0:T(8,128)}, f32[1024,128]{1,0:T(8,128)}, f32[1024,768]{1,0:T(8,128)}) custom-call(s32[2,1024]{1,0:T(2,128)} %shard_map.247.slots_ref, f32[2,1024]{1,0:T(2,128)} %get-tuple-element.57.gates_ref, f32[1024,768]{1,0:T(8,128)} %get-tuple-element.58.resid_ref, bf16[1024,768]{1,0:T(8,128)(2,1)} %cot_ref.7, ...), custom_call_target="tpu_custom_call" | custom-call | tf_op jit(solution)/shard_map/pallas_call | solution.py:363
  355.0 30.8 %all-to-all-done.5.made_ref.back_ref = bf16[8,2,160,768]{3,2,1,0:T(8,128)(2,1)} async-done(((bf16[8,2,160,768]{3,2,1,0:T(8,128)(2,1)}), bf16[8,2,160,768]{3,2,1,0:T(8,128)(2,1)}, u32[]{:S(2)}, u32[]{:S(2)}) %all-to-all-start.5) | async-done | bytes 3932192 | tf_op jit(solution)/shard_map/all_to_all | solution.py:874
  385.8 9.4 %shard_map.260 = (bf16[1024,768]{1,0:T(8,128)(2,1)}, bf16[1024,128]{1,0:T(8,128)(2,1)}) custom-call(s32[2,1024]{1,0:T(2,128)} %shard_map.247.slots_ref, s32[2,1024]{1,0:T(2,128)} %bitcast.57, f32[2,1024]{1,0:T(2,128)} %get-tuple-element.57.gates_ref, f32[1024,768]{1,0:T(8,128)} %get-tuple-element.66.result_ref, f32[1024,128]{1,0:T(8,128)} %get-tuple-element.67.inner_ref, ...), custom_call_target="tpu_custom_call" | custom-call | tf_op jit(solution)/shard_map/pallas_call | solution.py:404
  395.2 10.6 %shard_map.261 = (f32[1024,768]{1,0:T(8,128)}, bf16[1024,768]{1,0:T(8,128)(2,1)}, bf16[1024,768]{1,0:T(8,128)(2,1)}, f32[1,768]{1,0:T(1,128)}) custom-call(s32[2,1024]{1,0:T(2,128)} %shard_map.247.slots_ref, bf16[1024,128]{1,0:T(8,128)(2,1)} %get-tuple-element.75.logit_ref, bf16[128,768]{1,0:T(8,128)(2,1)} %pad.35.router_ref, f32[1,768]{1,0:T(1,128)} %reshape.131.gain_ref, ...), custom_call_target="tpu_custom_call" | custom-call | tf_op jit(solution)/shard_map/pallas_call | solution.py:440
  405.8 35.6 %shard_map.262 = (bf16[3,1024,768]{2,1,0:T(8,128)(2,1)}, f32[6,4,256]{2,1,0:T(4,128)}) custom-call(bf16[1024,768]{1,0:T(8,128)(2,1)} %get-tuple-element.53.query_ref, bf16[1024,768]{1,0:T(8,128)(2,1)} %get-tuple-element.54.key_ref, bf16[1024,768]{1,0:T(8,128)(2,1)} %get-tuple-element.55.value_ref, bf16[1024,768]{1,0:T(8,128)(2,1)} %get-tuple-element.77.grad_ref, ...), custom_call_target="tpu_custom_call" | custom-call | tf_op jit(solution)/shard_map/pallas_call | solution.py:596
  441.5 11.4 %shard_map.264 = bf16[4,768,768]{2,1,0:T(8,128)(2,1)} custom-call(bf16[1024,768]{1,0:T(8,128)(2,1)} %get-tuple-element.85.left_ref, bf16[1024,768]{1,0:T(8,128)(2,1)} %get-tuple-element.56.mixed_ref.out_ref, bf16[3,1024,768]{2,1,0:T(8,128)(2,1)} %get-tuple-element.79.heads_ref, bf16[1024,768]{1,0:T(8,128)(2,1)} %get-tuple-element.86.branch_ref), custom_call_target="tpu_custom_call" | custom-call | tf_op jit(solution)/shard_map/pallas_call | solution.py:739
  459.7 9.9 %shard_map.263 = (f32[1024,768]{1,0:T(8,128)}, f32[1,768]{1,0:T(1,128)}) custom-call(bf16[3,1024,768]{2,1,0:T(8,128)(2,1)} %get-tuple-element.79.heads_ref, bf16[768,768]{1,0:T(8,128)(2,1)} %get-tuple-element.80.query_ref, bf16[768,768]{1,0:T(8,128)(2,1)} %get-tuple-element.81.key_ref, bf16[768,768]{1,0:T(8,128)(2,1)} %get-tuple-element.82.value_ref, ...), custom_call_target="tpu_custom_call" | custom-call | tf_op jit(solution)/shard_map/pallas_call | solution.py:706
  479.2 12.1 %collective-permute-done.13 = bf16[4,96,768]{2,1,0:T(8,128)(2,1)} collective-permute-done((bf16[4,96,768]{2,1,0:T(8,128)(2,1)S(1)}, bf16[4,96,768]{2,1,0:T(8,128)(2,1)}, u32[]{:S(2)}, u32[]{:S(2)}) %collective-permute-start.13) | collective-permute-done | bytes 589856 | tf_op jit(solution)/shard_map/ppermute | solution.py:800
  510.3 7.5 %collective-permute-done.15 = bf16[104,768]{1,0:T(8,128)(2,1)S(1)} collective-permute-done((bf16[104,768]{1,0:T(8,128)(2,1)S(1)}, bf16[104,768]{1,0:T(8,128)(2,1)S(1)}, u32[]{:S(2)}, u32[]{:S(2)}) %collective-permute-start.15) | collective-permute-done | bytes 159776 | tf_op jit(solution)/shard_map/ppermute | solution.py:805
  517.8 16.1 %collective-permute-done.16 = bf16[104,768]{1,0:T(8,128)(2,1)S(1)} collective-permute-done((bf16[104,768]{1,0:T(8,128)(2,1)S(1)}, bf16[104,768]{1,0:T(8,128)(2,1)S(1)}, u32[]{:S(2)}, u32[]{:S(2)}) %collective-permute-start.16) | collective-permute-done | bytes 159776 | tf_op jit(solution)/shard_map/ppermute | solution.py:805
  555.4 6.5 %shard_map.266 = (f32[1536,768]{1,0:T(8,128)}, f32[1536,768]{1,0:T(8,128)}) custom-call(bf16[2304,768]{1,0:T(8,128)(2,1)} %reduce-scatter.3.cloned.1.call-done.rows_ref, f32[1536,768]{1,0:T(8,128)} %shard_map.265.into_ref), custom_call_target="tpu_custom_call", output_to_operand_aliasing={{1}: (1, {})} | custom-call | tf_op jit(solution)/shard_map/pallas_call | solution.py:783
  (168 shorter events, 90.0 us)
Async XLA Ops:
  7.2 119.3 %all-gather.2.cloned.1.call-start = ((), (), s32[]{:S(2)}) async-start(), calls=%async_computation.8 | async-start | bytes 1474560 | tf_op jit(solution)/shard_map/all_gather | solution.py:938
  10.9 5.3 collective-permute-start
  12.2 14.1 %collective-permute-start.1 = (bf16[96,768]{1,0:T(8,128)(2,1)S(1)}, bf16[96,768]{1,0:T(8,128)(2,1)S(1)}, u32[]{:S(2)}, u32[]{:S(2)}) collective-permute-start(bf16[96,768]{1,0:T(8,128)(2,1)S(1)} %concatenate.74), channel_id=1, source_target_pairs={{0,2},{1,3},{2,0},{3,1},{4,6},{5,7},{6,4},{7,5},{8,10},{9,11},{10,... | collective-permute-start | bytes 442376 | tf_op jit(solution)/shard_map/ppermute | solution.py:805
  13.3 17.8 %collective-permute-start.2 = (bf16[96,768]{1,0:T(8,128)(2,1)S(1)}, bf16[96,768]{1,0:T(8,128)(2,1)S(1)}, u32[]{:S(2)}, u32[]{:S(2)}) collective-permute-start(bf16[96,768]{1,0:T(8,128)(2,1)S(1)} %concatenate.74), channel_id=1, source_target_pairs={{0,3},{1,0},{2,1},{3,2},{4,7},{5,4},{6,5},{7,6},{8,11},{9,8},{10,9... | collective-permute-start | bytes 442376 | tf_op jit(solution)/shard_map/ppermute | solution.py:805
  31.1 26.9 %collective-permute-start.6 = (bf16[1,2,72,768]{3,2,1,0:T(8,128)(2,1)S(1)}, bf16[1,2,72,768]{3,2,1,0:T(8,128)(2,1)S(1)}, u32[]{:S(2)}, u32[]{:S(2)}) collective-permute-start(bf16[1,2,72,768]{3,2,1,0:T(8,128)(2,1)S(1)} %get-tuple-element.109), channel_id=1, source_target_pairs={{0,16},{4,20},{8,24},{12,28},{16,0},{20,4},{24,8},{28,12},{1,17},{... | collective-permute-start | bytes 663560 | tf_op jit(solution)/shard_map/ppermute | solution.py:800
  32.6 26.9 %collective-permute-start.3 = (bf16[1,2,72,768]{3,2,1,0:T(8,128)(2,1)S(1)}, bf16[1,2,72,768]{3,2,1,0:T(8,128)(2,1)S(1)}, u32[]{:S(2)}, u32[]{:S(2)}) collective-permute-start(bf16[1,2,72,768]{3,2,1,0:T(8,128)(2,1)S(1)} %get-tuple-element.110), channel_id=1, source_target_pairs={{0,8},{4,12},{8,0},{12,4},{16,24},{20,28},{24,16},{28,20},{1,9},{5... | collective-permute-start | bytes 663560 | tf_op jit(solution)/shard_map/ppermute | solution.py:800
  53.1 85.4 %all-to-all-start.1 = ((bf16[8,160,768]{2,1,0:T(8,128)(2,1)}), bf16[8,160,768]{2,1,0:T(8,128)(2,1)}, u32[]{:S(2)}, u32[]{:S(2)}) async-start(bf16[8,160,768]{2,1,0:T(8,128)(2,1)} %get-tuple-element.60), calls=%async_computation.1 | async-start | bytes 3932160 | tf_op jit(solution)/shard_map/all_to_all | solution.py:874
  58.1 32.8 %collective-permute-start.7 = (bf16[2,2,72,768]{3,2,1,0:T(8,128)(2,1)S(1)}, bf16[2,2,72,768]{3,2,1,0:T(8,128)(2,1)S(1)}, u32[]{:S(2)}, u32[]{:S(2)}) collective-permute-start(bf16[2,2,72,768]{3,2,1,0:T(8,128)(2,1)S(1)} %pad_maximum_fusion.4), channel_id=1, source_target_pairs={{0,8},{4,12},{8,0},{12,4},{16,24},{20,28},{24,16},{28,20},{1,9},{5... | collective-permute-start | bytes 1327112 | tf_op jit(solution)/shard_map/ppermute | solution.py:800
  59.5 33.5 %copy-start.11 = (f32[32,256,1]{1,0,2:T(8,128)S(1)}, f32[32,256,1]{1,0,2:T(8,128)}, u32[]{:S(2)}) copy-start(f32[32,256,1]{1,0,2:T(8,128)} %constant.250) | copy-start | bytes 98308
  59.5 32.5 %collective-permute-start.4 = (bf16[2,2,72,768]{3,2,1,0:T(8,128)(2,1)S(1)}, bf16[2,2,72,768]{3,2,1,0:T(8,128)(2,1)S(1)}, u32[]{:S(2)}, u32[]{:S(2)}) collective-permute-start(bf16[2,2,72,768]{3,2,1,0:T(8,128)(2,1)S(1)} %pad_maximum_fusion.3), channel_id=1, source_target_pairs={{0,16},{4,20},{8,24},{12,28},{16,0},{20,4},{24,8},{28,12},{1,17},{... | collective-permute-start | bytes 1327112 | tf_op jit(solution)/shard_map/ppermute | solution.py:800
  91.0 4.2 collective-permute-start.8
  92.1 3.3 collective-permute-start.5
  138.4 26.3 %all-to-all-start = ((bf16[8,160,768]{2,1,0:T(8,128)(2,1)}), bf16[8,160,768]{2,1,0:T(8,128)(2,1)}, u32[]{:S(2)}, u32[]{:S(2)}) async-start(bf16[8,160,768]{2,1,0:T(8,128)(2,1)} %bitcast.53), calls=%async_computation | async-start | bytes 3932160 | tf_op jit(solution)/shard_map/all_to_all | solution.py:874
  143.0 405.8 %reduce-scatter.5.cloned.1.call-start = ((), (), s32[]{:S(2)}) async-start(), calls=%async_computation.10 | async-start | bytes 5898240 | tf_op jit(solution)/shard_map/reduce_scatter | solution.py:870
  194.0 50.8 %all-to-all-start.4 = ((bf16[8,2,160,768]{3,2,1,0:T(8,128)(2,1)}), bf16[8,2,160,768]{3,2,1,0:T(8,128)(2,1)}, u32[]{:S(2)}, u32[]{:S(2)}) async-start(bf16[8,2,160,768]{3,2,1,0:T(8,128)(2,1)} %shard_map.256), calls=%async_computation.4 | async-start | bytes 7864320 | tf_op jit(solution)/shard_map/all_to_all | solution.py:874
  202.1 353.3 %reduce-scatter.3.cloned.1.call-start = ((), (), s32[]{:S(2)}) async-start(), calls=%async_computation.9 | async-start | bytes 17694720 | tf_op jit(solution)/shard_map/reduce_scatter | solution.py:870
  283.9 50.6 %all-to-all-start.3 = ((bf16[8,2,160,768]{3,2,1,0:T(8,128)(2,1)}), bf16[8,2,160,768]{3,2,1,0:T(8,128)(2,1)}, u32[]{:S(2)}, u32[]{:S(2)}) async-start(bf16[8,2,160,768]{3,2,1,0:T(8,128)(2,1)} %get-tuple-element.65), calls=%async_computation.3 | async-start | bytes 7864320 | tf_op jit(solution)/shard_map/all_to_all | solution.py:874
  334.6 51.2 %all-to-all-start.5 = ((bf16[8,2,160,768]{3,2,1,0:T(8,128)(2,1)}), bf16[8,2,160,768]{3,2,1,0:T(8,128)(2,1)}, u32[]{:S(2)}, u32[]{:S(2)}) async-start(bf16[8,2,160,768]{3,2,1,0:T(8,128)(2,1)} %shard_map.259), calls=%async_computation.5 | async-start | bytes 7864320 | tf_op jit(solution)/shard_map/all_to_all | solution.py:874
  456.1 17.1 %collective-permute-start.9 = (bf16[4,384,768]{2,1,0:T(8,128)(2,1)}, bf16[4,384,768]{2,1,0:T(8,128)(2,1)}, u32[]{:S(2)}, u32[]{:S(2)}) collective-permute-start(bf16[4,384,768]{2,1,0:T(8,128)(2,1)} %constant_dynamic-slice_fusion.3), channel_id=1, source_target_pairs={{0,4},{4,0},{8,12},{12,8},{16,20},{20,16},{24,28},{28,24},{1,5},{5... | collective-permute-start | bytes 7077896 | tf_op jit(solution)/shard_map/ppermute | solution.py:800
  471.6 1.5 collective-permute-start.12
  476.4 14.9 %collective-permute-start.13 = (bf16[4,96,768]{2,1,0:T(8,128)(2,1)S(1)}, bf16[4,96,768]{2,1,0:T(8,128)(2,1)}, u32[]{:S(2)}, u32[]{:S(2)}) collective-permute-start(bf16[4,96,768]{2,1,0:T(8,128)(2,1)S(1)} %fusion.1), channel_id=1, source_target_pairs={{0,16},{4,20},{8,24},{12,28},{16,0},{20,4},{24,8},{28,12},{1,17},{... | collective-permute-start | bytes 1769480 | tf_op jit(solution)/shard_map/ppermute | solution.py:800
  478.9 17.0 %collective-permute-start.10 = (bf16[4,112,768]{2,1,0:T(8,128)(2,1)}, bf16[4,112,768]{2,1,0:T(8,128)(2,1)}, u32[]{:S(2)}, u32[]{:S(2)}) collective-permute-start(bf16[4,112,768]{2,1,0:T(8,128)(2,1)} %constant_dynamic-slice_fusion.2), channel_id=1, source_target_pairs={{0,8},{4,12},{8,0},{12,4},{16,24},{20,28},{24,16},{28,20},{1,9},{5... | collective-permute-start | bytes 2064392 | tf_op jit(solution)/shard_map/ppermute | solution.py:800
  492.8 9.5 %collective-permute-start.14 = (bf16[4,48,768]{2,1,0:T(8,128)(2,1)S(1)}, bf16[4,48,768]{2,1,0:T(8,128)(2,1)S(1)}, u32[]{:S(2)}, u32[]{:S(2)}) collective-permute-start(bf16[4,48,768]{2,1,0:T(8,128)(2,1)S(1)} %constant_dynamic-slice_fusion), channel_id=1, source_target_pairs={{0,8},{4,12},{8,0},{12,4},{16,24},{20,28},{24,16},{28,20},{1,9},{5... | collective-permute-start | bytes 884744 | tf_op jit(solution)/shard_map/ppermute | solution.py:800
  497.3 7.9 %collective-permute-start.11 = (bf16[4,56,768]{2,1,0:T(8,128)(2,1)S(1)}, bf16[4,56,768]{2,1,0:T(8,128)(2,1)S(1)}, u32[]{:S(2)}, u32[]{:S(2)}) collective-permute-start(bf16[4,56,768]{2,1,0:T(8,128)(2,1)S(1)} %constant_dynamic-slice_fusion.1), channel_id=1, source_target_pairs={{0,16},{4,20},{8,24},{12,28},{16,0},{20,4},{24,8},{28,12},{1,17},{... | collective-permute-start | bytes 1032200 | tf_op jit(solution)/shard_map/ppermute | solution.py:800
  505.3 12.5 %collective-permute-start.15 = (bf16[104,768]{1,0:T(8,128)(2,1)S(1)}, bf16[104,768]{1,0:T(8,128)(2,1)S(1)}, u32[]{:S(2)}, u32[]{:S(2)}) collective-permute-start(bf16[104,768]{1,0:T(8,128)(2,1)S(1)} %get-tuple-element.106), channel_id=1, source_target_pairs={{0,1},{1,2},{2,3},{3,0},{4,5},{5,6},{6,7},{7,4},{8,9},{9,10},{10,1... | collective-permute-start | bytes 479240 | tf_op jit(solution)/shard_map/ppermute | solution.py:805
  505.4 28.5 %collective-permute-start.16 = (bf16[104,768]{1,0:T(8,128)(2,1)S(1)}, bf16[104,768]{1,0:T(8,128)(2,1)S(1)}, u32[]{:S(2)}, u32[]{:S(2)}) collective-permute-start(bf16[104,768]{1,0:T(8,128)(2,1)S(1)} %get-tuple-element.107), channel_id=1, source_target_pairs={{0,2},{1,3},{2,0},{3,1},{4,6},{5,7},{6,4},{7,5},{8,10},{9,11},{10,... | collective-permute-start | bytes 479240 | tf_op jit(solution)/shard_map/ppermute | solution.py:805
  508.9 26.6 %collective-permute-start.17 = (bf16[104,768]{1,0:T(8,128)(2,1)S(1)}, bf16[104,768]{1,0:T(8,128)(2,1)S(1)}, u32[]{:S(2)}, u32[]{:S(2)}) collective-permute-start(bf16[104,768]{1,0:T(8,128)(2,1)S(1)} %get-tuple-element.108), channel_id=1, source_target_pairs={{0,3},{1,0},{2,1},{3,2},{4,7},{5,4},{6,5},{7,6},{8,11},{9,8},{10,9... | collective-permute-start | bytes 479240 | tf_op jit(solution)/shard_map/ppermute | solution.py:805
  535.6 3.3 collective-permute-start.20
  537.1 3.6 collective-permute-start.18
  538.9 4.6 collective-permute-start.21
  540.8 4.6 collective-permute-start.19
  545.5 5.9 %collective-permute-start.22 = (bf16[416,768]{1,0:T(8,128)(2,1)S(1)}, bf16[416,768]{1,0:T(8,128)(2,1)S(1)}, u32[]{:S(2)}, u32[]{:S(2)}) collective-permute-start(bf16[416,768]{1,0:T(8,128)(2,1)S(1)} %pad_maximum_fusion.2), channel_id=1, source_target_pairs={{0,4},{4,0},{8,12},{12,8},{16,20},{20,16},{24,28},{28,24},{1,5},{5... | collective-permute-start | bytes 1916936 | tf_op jit(solution)/shard_map/ppermute | solution.py:800
  (14 other events, 157.1 us)
Sparse Core Ops, SparseCore 0:
  14.8 29.7 all-gather.1
  185.6 88.2 reduce-scatter.4
  284.1 253.2 reduce-scatter.2

commit v6 on v5

--- a/solution.py
+++ b/solution.py
@@ -60,27 +60,8 @@
     )(routes, base)
 
 
-def dispatch_kernel(slots_ref, rows_ref, *refs, start):
+def dispatch_both_kernel(slots_ref, rows_ref, cot_ref, *refs, start):
     out_ref = refs[-1]
-    block, tokens = out_ref.shape[0], rows_ref.shape[0]
-    slot = lax.broadcasted_iota(jnp.int32, (block, tokens), 0) + (pl.program_id(0) * block + start)
-    hot = jnp.where((slot == slots_ref[0:1, :]) | (slot == slots_ref[1:2, :]), 1.0, 0.0)
-    out_ref[...] = dot_nn(hot.astype(jnp.bfloat16), rows_ref[...]).astype(out_ref.dtype)
-
-
-def dispatch(slots, rows, start, count, after=(), block=256):
-    _, width = rows.shape
-    whole = lambda shape: pl.BlockSpec(shape, lambda i: (0, 0))
-    return pl.pallas_call(
-        partial(dispatch_kernel, start=start),
-        grid=(count // block,),
-        in_specs=[whole(slots.shape), whole(rows.shape)] + [pl.BlockSpec(memory_space=pl.ANY)] * len(after),
-        out_specs=pl.BlockSpec((block, width), lambda i: (i, 0)),
-        out_shape=jax.ShapeDtypeStruct((count, width), rows.dtype),
-    )(slots, rows, *after)
-
-
-def dispatch_both_kernel(slots_ref, rows_ref, cot_ref, out_ref, *, start):
     block, tokens = out_ref.shape[2], rows_ref.shape[0]
     slot = lax.broadcasted_iota(jnp.int32, (block, tokens), 0) + (pl.program_id(0) * block + start)
     hot = jnp.where((slot == slots_ref[0:1, :]) | (slot == slots_ref[1:2, :]), 1.0, 0.0)
@@ -89,16 +70,17 @@
     out_ref[0, 1] = dot_nn(hot, cot_ref[...]).astype(out_ref.dtype)
 
 
-def dispatch_both(slots, rows, cot, start, owners, capacity):
+def dispatch_both(slots, rows, cot, start, owners, capacity, after=()):
     width = rows.shape[1]
     whole = lambda shape: pl.BlockSpec(shape, lambda i: (0, 0))
     return pl.pallas_call(
         partial(dispatch_both_kernel, start=start),
         grid=(owners,),
-        in_specs=[whole(slots.shape), whole(rows.shape), whole(cot.shape)],
+        in_specs=[whole(slots.shape), whole(rows.shape), whole(cot.shape)] + [pl.BlockSpec(memory_space=pl.ANY)] * len(after),
         out_specs=pl.BlockSpec((1, 2, capacity, width), lambda i: (i, 0, 0, 0)),
         out_shape=jax.ShapeDtypeStruct((owners, 2, capacity, width), rows.dtype),
-    )(slots, rows, cot)
+        compiler_params=pltpu.CompilerParams(vmem_limit_bytes=62 << 20),
+    )(slots, rows, cot, *after)
 
 
 def dispatch_first_kernel(slots_ref, routes_ref, rows_ref, out_ref, other_ref, *, owners, capacity):
@@ -471,39 +453,56 @@
     return jnp.where((lane >= head * size) & (lane < (head + 1) * size), rows, jnp.zeros_like(rows))
 
 
-def attend_kernel(query_ref, key_ref, value_ref, near_ref, out_ref, total_ref, *, block, size, scale):
+def attend_kernel(query_ref, key_ref, value_ref, near_ref, out_ref, total_ref, held, *, block, size, scale):
     length, lanes = query_ref.shape
     heads = lanes // size
     count = length // block
-    flipped = value_ref[...].T
+    turned = value_ref[...].T
+    ones = jnp.ones((16, length), jnp.bfloat16)
+    flipped = [jnp.concatenate([turned[head * size:(head + 1) * size], ones], axis=0) for head in range(heads)]
     tiles = [near_tiles(near_ref, head, block) for head in range(heads)]
-    for i in range(count):
+    units = [(i, head) for i in range(count) for head in range(heads)]
+    def fold(tile, op):
+        parts = [tile[k:k + 8] for k in range(0, tile.shape[0], 8)]
+        while len(parts) > 1:
+            parts = [op(parts[k], parts[k + 1]) for k in range(0, len(parts), 2)]
+        return parts[0]
+    def score_tile(unit, query_part, j, slot):
+        i, head = unit
+        tile = dot_nt(key_ref[pl.ds(j * block, block), :], query_part)
+        if j == i:
+            tile = tile + tiles[head][0]
+        elif j == i - 1:
+            tile = tile + tiles[head][1]
+        held[slot, pl.ds(j * block, block), :] = tile
+        return fold(tile, jnp.maximum)
+    def part_of(unit):
+        i, head = unit
+        return head_part(query_ref[pl.ds(i * block, block), :] * jnp.bfloat16(scale), head, size)
+    tops = {0: [score_tile(units[0], part_of(units[0]), 0, 0)]}
+    outs = []
+    for n, (i, head) in enumerate(units):
+        top = jnp.max(reduce(jnp.maximum, tops[n]), axis=0, keepdims=True)
+        following = units[n + 1] if n + 1 < len(units) else None
+        if following is not None:
+            query_part = part_of(following)
+            tops[n + 1] = []
+        mixed = None
+        total = None
+        steps = max(i + 1, following[0] + 1 if following else 0)
+        for j in range(steps):
+            if following is not None and j <= following[0]:
+                tops[n + 1].append(score_tile(following, query_part, j, (n + 1) % 2))
+            if j <= i:
+                weights = jnp.exp(held[n % 2, pl.ds(j * block, block), :] - top)
+                part = dot_nn(flipped[head][:, j * block:(j + 1) * block], weights.astype(jnp.bfloat16))
+                mixed = part if mixed is None else mixed + part
+        total = mixed[size:size + 1]
+        outs.append(mixed[:size] / total)
         rows = pl.ds(i * block, block)
-        query_rows = query_ref[rows, :] * jnp.bfloat16(scale)
-        parts = []
-        for head in range(heads):
-            query_part = head_part(query_rows, head, size)
-            scores = []
-            for j in range(i + 1):
-                tile = dot_nt(key_ref[pl.ds(j * block, block), :], query_part)
-                if j == i:
-                    tile = tile + tiles[head][0]
-                elif j == i - 1:
-                    tile = tile + tiles[head][1]
-                scores.append(tile)
-            top = reduce(jnp.maximum, scores)
-            top = jnp.max(top, axis=0, keepdims=True)
-            mixed = None
-            total = None
-            for j in range(i + 1):
-                weights = jnp.exp(scores[j] - top)
-                sums = jnp.sum(weights, axis=0, keepdims=True)
-                part = dot_nn(flipped[head * size:(head + 1) * size, j * block:(j + 1) * block], weights.astype(jnp.bfloat16))
-                mixed = part if mixed is None else mixed + part
-                total = sums if total is None else total + sums
-            parts.append(mixed / total)
-            total_ref[0, head:head + 1, rows] = top + jnp.log(total)
-        out_ref[rows, :] = jnp.concatenate(parts, axis=0).T.astype(out_ref.dtype)
+        total_ref[0, head:head + 1, rows] = top + jnp.log(total)
+        if head == heads - 1:
+            out_ref[rows, :] = jnp.concatenate(outs[-heads:], axis=0).T.astype(out_ref.dtype)
 
 
 def attend(queries, keys, values, near, size, block):
@@ -519,6 +518,7 @@
         in_specs=[column, column, column, head_rows],
         out_specs=[column, pl.BlockSpec((1, heads, length), lambda g: (g, 0, 0))],
         out_shape=[jax.ShapeDtypeStruct((length, width), jnp.bfloat16), jax.ShapeDtypeStruct((groups, heads, length), jnp.float32)],
+        scratch_shapes=[pltpu.VMEM((2, length, block), jnp.float32)],
         compiler_params=pltpu.CompilerParams(vmem_limit_bytes=62 << 20),
     )(queries, keys, values, near)
 
@@ -654,35 +654,49 @@
     )(owner, inputs, gain, *pieces, *after)
 
 
-def settle_kernel(mixed_ref, merge_ref, inputs_ref, gain_ref, router_ref, routes_ref, resid_ref, low_ref, gates_ref, *, eps):
-    resid = inputs_ref[...].astype(jnp.float32) + dot_nn(mixed_ref[...], merge_ref[...])
-    resid_ref[...] = resid
-    inverse = lax.rsqrt(jnp.mean(resid * resid, axis=1, keepdims=True) + eps)
-    low = (resid * inverse * gain_ref[...]).astype(jnp.bfloat16)
-    low_ref[...] = low
-    logits = dot_nt(router_ref[...], low)
-    expert = lax.broadcasted_iota(jnp.int32, logits.shape, 0)
-    chosen = [jnp.sum(jnp.where(routes_ref[c:c + 1, :] == expert, logits, 0.0), axis=0, keepdims=True) for c in range(2)]
-    top = jnp.maximum(chosen[0], chosen[1])
-    powers = [jnp.exp(value - top) for value in chosen]
-    total = powers[0] + powers[1]
-    for c in range(2):
-        gates_ref[c:c + 1, :] = powers[c] / total
-
-
-def settle(mixed, merge, inputs, gain, router, routes, eps, block=256):
+def settle_kernel(mixed_ref, merge_ref, inputs_ref, gain_ref, router_ref, routes_ref, slots_ref, resid_ref, low_ref, gates_ref, out_ref, held, *, eps, settling):
+    step = pl.program_id(0)
+    block = mixed_ref.shape[0]
+    @pl.when(step < settling)
+    def _():
+        resid = inputs_ref[...].astype(jnp.float32) + dot_nn(mixed_ref[...], merge_ref[...])
+        resid_ref[...] = resid
+        inverse = lax.rsqrt(jnp.mean(resid * resid, axis=1, keepdims=True) + eps)
+        low = (resid * inverse * gain_ref[...]).astype(jnp.bfloat16)
+        low_ref[...] = low
+        held[pl.ds(pl.multiple_of(step * block, block), block), :] = low
+        logits = dot_nt(router_ref[...], low)
+        expert = lax.broadcasted_iota(jnp.int32, logits.shape, 0)
+        chosen = [jnp.sum(jnp.where(routes_ref[c:c + 1, :] == expert, logits, 0.0), axis=0, keepdims=True) for c in range(2)]
+        top = jnp.maximum(chosen[0], chosen[1])
+        powers = [jnp.exp(value - top) for value in chosen]
+        total = powers[0] + powers[1]
+        for c in range(2):
+            gates_ref[c:c + 1, :] = powers[c] / total
+    @pl.when(step >= settling)
+    def _():
+        tokens = held.shape[0]
+        slot = lax.broadcasted_iota(jnp.int32, (block, tokens), 0) + (step - settling) * block
+        hot = jnp.where((slot == slots_ref[0:1, :]) | (slot == slots_ref[1:2, :]), 1.0, 0.0)
+        out_ref[...] = dot_nn(hot.astype(jnp.bfloat16), held[...]).astype(out_ref.dtype)
+
+
+def settle(mixed, merge, inputs, gain, router, routes, slots, count, eps, block=256):
     tokens, width = inputs.shape
-    rows = pl.BlockSpec((block, width), lambda i: (i, 0))
+    settling = tokens // block
+    early = lambda i: jnp.minimum(i, settling - 1)
+    rows = pl.BlockSpec((block, width), lambda i: (early(i), 0))
     whole = lambda shape: pl.BlockSpec(shape, lambda i: (0, 0))
-    small = pl.BlockSpec((2, block), lambda i: (0, i))
-    return pl.pallas_call(
-        partial(settle_kernel, eps=eps),
-        grid=(tokens // block,),
-        in_specs=[rows, whole(merge.shape), rows, whole(gain.shape), whole(router.shape), small],
-        out_specs=[rows, rows, small],
-        out_shape=[jax.ShapeDtypeStruct((tokens, width), jnp.float32), jax.ShapeDtypeStruct((tokens, width), jnp.bfloat16), jax.ShapeDtypeStruct((2, tokens), jnp.float32)],
-        compiler_params=pltpu.CompilerParams(vmem_limit_bytes=62 << 20),
-    )(mixed, merge, inputs, gain, router, routes)
+    small = pl.BlockSpec((2, block), lambda i: (0, early(i)))
+    return pl.pallas_call(
+        partial(settle_kernel, eps=eps, settling=settling),
+        grid=(settling + count // block,),
+        in_specs=[rows, whole(merge.shape), rows, whole(gain.shape), whole(router.shape), small, whole(slots.shape)],
+        out_specs=[rows, rows, small, pl.BlockSpec((block, width), lambda i: (jnp.maximum(i - settling, 0), 0))],
+        out_shape=[jax.ShapeDtypeStruct((tokens, width), jnp.float32), jax.ShapeDtypeStruct((tokens, width), jnp.bfloat16), jax.ShapeDtypeStruct((2, tokens), jnp.float32), jax.ShapeDtypeStruct((count, width), jnp.bfloat16)],
+        scratch_shapes=[pltpu.VMEM((tokens, width), jnp.bfloat16)],
+        compiler_params=pltpu.CompilerParams(vmem_limit_bytes=62 << 20),
+    )(mixed, merge, inputs, gain, router, routes, slots)
 
 
 def finish_kernel(heads_ref, query_ref, key_ref, value_ref, gain_ref, inputs_ref, resid_grad_ref, out_ref, gain_grad_ref, *, eps):
@@ -768,23 +782,23 @@
     del into_ref
     wide = rows_ref[...].astype(jnp.float32)
     step = pl.program_id(0)
-    @pl.when(step < 4)
+    @pl.when(step < 2)
     def _():
         up_ref[...] = wide
-    @pl.when(step >= 4)
+    @pl.when(step >= 2)
     def _():
         down_ref[...] = wide
 
 
 def widen_rest(rows, into):
     count, width = rows.shape[0] // 3, rows.shape[1]
-    half = lambda place: pl.BlockSpec((count // 2, width), lambda i: (place(i), 0))
+    half = lambda place: pl.BlockSpec((count, width), lambda i: (place(i), 0))
     wide = jax.ShapeDtypeStruct((2 * count, width), jnp.float32)
     return pl.pallas_call(
         widen_rest_kernel,
-        grid=(6,),
+        grid=(3,),
         in_specs=[half(lambda i: i), pl.BlockSpec(memory_space=pl.ANY)],
-        out_specs=[half(lambda i: jnp.minimum(i, 3)), half(lambda i: jnp.maximum(i - 4, 0) + 2)],
+        out_specs=[half(lambda i: jnp.minimum(i, 1)), half(lambda i: 1)],
         out_shape=[wide, wide],
         input_output_aliases={1: 1},
         compiler_params=pltpu.CompilerParams(vmem_limit_bytes=62 << 20),
@@ -964,15 +978,16 @@
     )
     cot_in = share_large(cot_rows)
     attended, totals = attend(queries, keys, values, near, size, block)
-    resid, low_two, gates = settle(
-        attended, merge_full, inputs, gain_two, router_full, routes_line, epsilon
-    )
-
-    send = dispatch(slots, low_two, 0, rows).reshape(owners, capacity, width)
-    rows_in = share_large(send)
-    joint = dispatch_both(slots, low_two, cotangent, rows, owners, capacity)
+    resid, low_two, gates, send = settle(
+        attended, merge_full, inputs, gain_two, router_full, routes_line, slots, rows, epsilon
+    )
+
+    others = [other[:, index].reshape(1, rows) for index in range(local_count)]
+    rows_in = share_large(send.reshape(owners, capacity, width))
+    joint = dispatch_both(
+        slots, low_two, cotangent, rows, owners, capacity, after=others
+    )
     joint_in = share_large(joint)
-    others = [other[:, index].reshape(1, rows) for index in range(local_count)]
     act, slope, first_down, grad_in = expert_first(
     owner, rows_in, cot_in, others[0], router_full, up_weight, 0, local_count, shards,
     )

time: 576 us -> 570 us (0.990)
  Pallas kernels: 275 us -> 268 us
    pallas_call x3 -> x2, Pallas kernels: 18.4 us -> 17 us  [the longest x1 10.9 us: settle(): pl.pallas_call(partial(settle_kernel, eps=eps, settling=settling), grid=(...]
  transfers between devices with their start and end apart: 31 -> 31, of which waited for: 20 -> 20; matrix products, arithmetic and copies ran while one was open for 4% -> 4% of each run, Pallas kernels for 44% -> 43%
where the time goes in v6:
time: 570 us; the launch traced here: 563 us
  Pallas kernels  268 us (47%)
  waiting for transfers between devices  177 us (31%)
  starting transfers between devices  64.6 us (11%)
  local copies, waits for them, and re-layouts  16.2 us (3%)
  between operations  14.5 us (3%)
  other arithmetic  12.1 us (2%)
  blocking collectives  9.92 us (2%)
    all_to_all x5, waiting for transfers between devices, share_rows(): return lax.all_to_all(rows, OWNER, 0, 0, tiled=True)  78.6 us
    ppermute x17, waiting for transfers between devices, exchange(): return lax.ppermute(rows, OWNER, [(i, i ^ bit) for i in range(count)])  57.9 us
    pallas_call x2, Pallas kernels, expert_first(): pl.pallas_call(partial(first_kernel, chunk=chunk, index=index, local_coun...  41.5 us
    ppermute x6, waiting for transfers between devices, shift(): lax.ppermute(rows, LINE, [(i, (i + step) % count) for i in range(count)])  40 us
    pallas_call x1, Pallas kernels, expert_second(): pl.pallas_call(second_kernel, grid=(shards,), in_specs=[arrived_spec(rows...  36.2 us
    pallas_call x1, Pallas kernels, attend_back(): pl.pallas_call(partial(attend_back_kernel, block=block, size=size, scale=...  35.6 us
    all_to_all x5, starting transfers between devices, share_rows(): return lax.all_to_all(rows, OWNER, 0, 0, tiled=True)  33.9 us
    pallas_call x1, Pallas kernels, expert_last(): pl.pallas_call(last_kernel, grid=(shards,), in_specs=[column, column, pl....  21.8 us
  transfers between devices with their start and end apart: 31, of which 20 were waited for; matrix products, arithmetic and copies ran while one was open for 4% of the time, Pallas kernels for 43%

profile of v6, /device:TPU:9, one launch (start us, length us, event | category | flops | bytes accessed | tf_op | source)
XLA Modules:
  0.0 562.6 jit_solution(6223202411708539459)
XLA Ops:
  16.2 10.1 %collective-permute-done.1 = bf16[96,768]{1,0:T(8,128)(2,1)S(1)} collective-permute-done((bf16[96,768]{1,0:T(8,128)(2,1)S(1)}, bf16[96,768]{1,0:T(8,128)(2,1)S(1)}, u32[]{:S(2)}, u32[]{:S(2)}) %collective-permute-start.1) | collective-permute-done | bytes 147488 | tf_op jit(solution)/shard_map/ppermute | solution.py:819
  26.3 4.8 collective-permute-done.2
  36.3 6.8 %shard_map.251 = (bf16[8,160,768]{2,1,0:T(8,128)(2,1)}, f32[8,1,320]{2,1,0:T(1,128)}) custom-call(s32[2,1024]{1,0:T(2,128)} %shard_map.247.slots_ref, f32[2,1024]{1,0:T(2,128)} %bitcast_convert_fusion.routes_ref, bf16[1024,768]{1,0:T(8,128)(2,1)} %cot_ref.7), custom_call_target="tpu_custom_call" | custom-call | tf_op jit(solution)/shard_map/pallas_call | solution.py:102
  43.1 9.9 %all_to_all.30 = f32[8,1,320]{2,1,0:T(1,128)S(1)} all-to-all(f32[8,1,320]{2,1,0:T(1,128)} %get-tuple-element.62), channel_id=1, replica_groups=mesh['expert'=8,'shard'=4] {'expert'}, dimensions={0} | all-to-all | bytes 20480 | tf_op jit(solution)/shard_map/all_to_all | solution.py:888
  53.1 4.9 all-to-all-start.1
  60.8 30.1 %collective-permute-done.7 = bf16[2,2,72,768]{3,2,1,0:T(8,128)(2,1)S(1)} collective-permute-done((bf16[2,2,72,768]{3,2,1,0:T(8,128)(2,1)S(1)}, bf16[2,2,72,768]{3,2,1,0:T(8,128)(2,1)S(1)}, u32[]{:S(2)}, u32[]{:S(2)}) %collective-permute-start.7) | collective-permute-done | bytes 442400 | tf_op jit(solution)/shard_map/ppermute | solution.py:814
  95.5 8.5 %shard_map.248 = (bf16[768,768]{1,0:T(8,128)(2,1)}, bf16[768,768]{1,0:T(8,128)(2,1)}, bf16[768,768]{1,0:T(8,128)(2,1)}, bf16[1024,768]{1,0:T(8,128)(2,1)}, bf16[...) custom-call(s32[1]{0:T(128)} %bitcast.1.owner_ref, bf16[1024,768]{1,0:T(8,128)(2,1)} %inputs_ref.5, ...), custom_call_target="tpu_custom_call" | custom-call | tf_op jit(solution)/shard_map/pallas_call | solution.py:647
  103.9 17.3 %shard_map.249 = (bf16[1024,768]{1,0:T(8,128)(2,1)}, f32[6,2,1024]{2,1,0:T(2,128)}) custom-call(bf16[1024,768]{1,0:T(8,128)(2,1)} %get-tuple-element.54.query_ref, bf16[1024,768]{1,0:T(8,128)(2,1)} %get-tuple-element.55.key_ref, bf16[1024,768]{1,0:T(8,128)(2,1)} %get-tuple-element.56.value_ref, f32[6,2,256]{2,1,0:T(2,128)} %copy.40.refs_4_.near_ref), custom_call_target="tpu_custom_call" | custom-call | tf_op jit(solution)/shard_map/pallas_call | solution.py:515
  121.2 10.9 %shard_map.250 = (f32[1024,768]{1,0:T(8,128)}, bf16[1024,768]{1,0:T(8,128)(2,1)}, f32[2,1024]{1,0:T(2,128)}, bf16[1280,768]{1,0:T(8,128)(2,1)}) custom-call(bf16[1024,768]{1,0:T(8,128)(2,1)} %get-tuple-element.57.mixed_ref.out_ref, bf16[768,768]{1,0:T(8,128)(2,1)} %all-gather.2.cloned.1.call-done.merge_ref, bf16[1024,768]{1,0:T(8,128)(2,1)} %inputs_ref.5, ...), custom_call_target="tpu_custom_call" | custom-call | tf_op jit(solution)/shard_map/pallas_call | solution.py:691
  138.1 20.4 %all-to-all-done.rows_ref = bf16[8,160,768]{2,1,0:T(8,128)(2,1)} async-done(((bf16[8,160,768]{2,1,0:T(8,128)(2,1)}), bf16[8,160,768]{2,1,0:T(8,128)(2,1)}, u32[]{:S(2)}, u32[]{:S(2)}) %all-to-all-start) | async-done | bytes 1966112 | tf_op jit(solution)/shard_map/all_to_all | solution.py:888
  158.4 20.7 %shard_map.252 = (bf16[1280,3072]{1,0:T(8,128)(2,1)}, bf16[1280,3072]{1,0:T(8,128)(2,1)}, bf16[4,768,768]{2,1,0:T(8,128)(2,1)}, bf16[1280,768]{1,0:T(8,128)(2,1)}) custom-call(s32[1]{0:T(128)} %bitcast.1.owner_ref, bf16[8,160,768]{2,1,0:T(8,128)(2,1)} %all-to-all-done.rows_ref, bf16[8,160,768]{2,1,0:T(8,128)(2,1)} %all-to-all-done.1.cot_ref, ...), custom_call_target="tpu_custom_call" | custom-call | tf_op jit(solution)/shard_map/pallas_call | solution.py:173
  179.9 8.5 %shard_map.255 = bf16[8,2,160,768]{3,2,1,0:T(8,128)(2,1)} custom-call(s32[2,1024]{1,0:T(2,128)} %shard_map.247.slots_ref, bf16[1024,768]{1,0:T(8,128)(2,1)} %get-tuple-element.69.rows_ref, bf16[1024,768]{1,0:T(8,128)(2,1)} %cot_ref.7, f32[1,1280]{1,0:T(1,128)} %reshape_squeeze.8.other_ref.refs_0_, f32[1,1280]{1,0:T(1,128)} %reshape_squeeze.9.refs_1_.other_ref), custom_call_target="tpu_custom_call" | custom-call | tf_op jit(solution)/shard_map/pallas_call | solution.py:76
  188.4 8.0 %all-to-all-start.4 = ((bf16[8,2,160,768]{3,2,1,0:T(8,128)(2,1)}), bf16[8,2,160,768]{3,2,1,0:T(8,128)(2,1)}, u32[]{:S(2)}, u32[]{:S(2)}) async-start(bf16[8,2,160,768]{3,2,1,0:T(8,128)(2,1)} %shard_map.255), calls=%async_computation.4 | async-start | bytes 7864320 | tf_op jit(solution)/shard_map/all_to_all | solution.py:888
  196.6 36.2 %shard_map.253 = (bf16[8,2,160,768]{3,2,1,0:T(8,128)(2,1)}, bf16[4,2304,768]{2,1,0:T(8,128)(2,1)}) custom-call(bf16[8,160,768]{2,1,0:T(8,128)(2,1)} %all-to-all-done.rows_ref, bf16[1280,768]{1,0:T(8,128)(2,1)} %get-tuple-element.63.grad_ref, bf16[1280,3072]{1,0:T(8,128)(2,1)} %get-tuple-element.64.act_ref, bf16[1280,3072]{1,0:T(8,128)(2,1)} %get-tuple-element.65.slope_ref, ...), custom_call_target="tpu_custom_call" | custom-call | tf_op jit(solution)/shard_map/pallas_call | solution.py:228
  232.8 6.4 %all-to-all-done.4.rows_ref.cot_ref = bf16[8,2,160,768]{3,2,1,0:T(8,128)(2,1)} async-done(((bf16[8,2,160,768]{3,2,1,0:T(8,128)(2,1)}), bf16[8,2,160,768]{3,2,1,0:T(8,128)(2,1)}, u32[]{:S(2)}, u32[]{:S(2)}) %all-to-all-start.4) | async-done | bytes 3932192 | tf_op jit(solution)/shard_map/all_to_all | solution.py:888
  239.2 20.7 %shard_map.256 = (bf16[1280,3072]{1,0:T(8,128)(2,1)}, bf16[1280,3072]{1,0:T(8,128)(2,1)}, bf16[4,2304,768]{2,1,0:T(8,128)(2,1)}, bf16[1280,768]{1,0:T(8,128)(2,1)}) custom-call(s32[1]{0:T(128)} %bitcast.1.owner_ref, bf16[8,2,160,768]{3,2,1,0:T(8,128)(2,1)} %all-to-all-done.4.rows_ref.cot_ref, ...), custom_call_target="tpu_custom_call", output_to_operand_aliasing={{2}: (6, {})} | custom-call | tf_op jit(solution)/shard_map/pallas_call | solution.py:173
  259.9 18.2 %shard_map.257 = (bf16[1280,3072]{1,0:T(8,128)(2,1)}, bf16[4,2304,768]{2,1,0:T(8,128)(2,1)}) custom-call(bf16[8,2,160,768]{3,2,1,0:T(8,128)(2,1)} %all-to-all-done.4.rows_ref.cot_ref, bf16[1280,768]{1,0:T(8,128)(2,1)} %get-tuple-element.72.grad_ref, bf16[1280,3072]{1,0:T(8,128)(2,1)} %get-tuple-element.73.slope_ref, ...), custom_call_target="tpu_custom_call", output_to_operand_aliasing={{1}: (4, {})} | custom-call | tf_op jit(solution)/shard_map/pallas_call | solution.py:257
  278.2 7.9 %all-to-all-start.3 = ((bf16[8,2,160,768]{3,2,1,0:T(8,128)(2,1)}), bf16[8,2,160,768]{3,2,1,0:T(8,128)(2,1)}, u32[]{:S(2)}, u32[]{:S(2)}) async-start(bf16[8,2,160,768]{3,2,1,0:T(8,128)(2,1)} %get-tuple-element.66), calls=%async_computation.3 | async-start | bytes 7864320 | tf_op jit(solution)/shard_map/all_to_all | solution.py:888
  286.1 21.8 %shard_map.258 = bf16[8,2,160,768]{3,2,1,0:T(8,128)(2,1)} custom-call(bf16[1280,3072]{1,0:T(8,128)(2,1)} %get-tuple-element.71.act_ref, bf16[1280,3072]{1,0:T(8,128)(2,1)} %get-tuple-element.75.low_ref, bf16[2,768,3072]{2,1,0:T(8,128)(2,1)} %up_ref.7, bf16[2,3072,768]{2,1,0:T(8,128)(2,1)} %down_ref.5), custom_call_target="tpu_custom_call" | custom-call | tf_op jit(solution)/shard_map/pallas_call | solution.py:295
  307.8 21.0 %all-to-all-done.3.made_ref.back_ref = bf16[8,2,160,768]{3,2,1,0:T(8,128)(2,1)} async-done(((bf16[8,2,160,768]{3,2,1,0:T(8,128)(2,1)}), bf16[8,2,160,768]{3,2,1,0:T(8,128)(2,1)}, u32[]{:S(2)}, u32[]{:S(2)}) %all-to-all-start.3) | async-done | bytes 3932192 | tf_op jit(solution)/shard_map/all_to_all | solution.py:888
  328.9 8.5 %all-to-all-start.5 = ((bf16[8,2,160,768]{3,2,1,0:T(8,128)(2,1)}), bf16[8,2,160,768]{3,2,1,0:T(8,128)(2,1)}, u32[]{:S(2)}, u32[]{:S(2)}) async-start(bf16[8,2,160,768]{3,2,1,0:T(8,128)(2,1)} %shard_map.258), calls=%async_computation.5 | async-start | bytes 7864320 | tf_op jit(solution)/shard_map/all_to_all | solution.py:888
  338.1 11.2 %shard_map.254 = (f32[1024,768]{1,0:T(8,128)}, f32[1024,128]{1,0:T(8,128)}, f32[1024,768]{1,0:T(8,128)}) custom-call(s32[2,1024]{1,0:T(2,128)} %shard_map.247.slots_ref, f32[2,1024]{1,0:T(2,128)} %get-tuple-element.58.gates_ref, f32[1024,768]{1,0:T(8,128)} %get-tuple-element.59.resid_ref, bf16[1024,768]{1,0:T(8,128)(2,1)} %cot_ref.7, ...), custom_call_target="tpu_custom_call" | custom-call | tf_op jit(solution)/shard_map/pallas_call | solution.py:345
  349.3 30.8 %all-to-all-done.5.made_ref.back_ref = bf16[8,2,160,768]{3,2,1,0:T(8,128)(2,1)} async-done(((bf16[8,2,160,768]{3,2,1,0:T(8,128)(2,1)}), bf16[8,2,160,768]{3,2,1,0:T(8,128)(2,1)}, u32[]{:S(2)}, u32[]{:S(2)}) %all-to-all-start.5) | async-done | bytes 3932192 | tf_op jit(solution)/shard_map/all_to_all | solution.py:888
  380.1 9.4 %shard_map.259 = (bf16[1024,768]{1,0:T(8,128)(2,1)}, bf16[1024,128]{1,0:T(8,128)(2,1)}) custom-call(s32[2,1024]{1,0:T(2,128)} %shard_map.247.slots_ref, s32[2,1024]{1,0:T(2,128)} %bitcast.57, f32[2,1024]{1,0:T(2,128)} %get-tuple-element.58.gates_ref, f32[1024,768]{1,0:T(8,128)} %get-tuple-element.67.result_ref, f32[1024,128]{1,0:T(8,128)} %get-tuple-element.68.inner_ref, ...), custom_call_target="tpu_custom_call" | custom-call | tf_op jit(solution)/shard_map/pallas_call | solution.py:386
  389.5 10.6 %shard_map.260 = (f32[1024,768]{1,0:T(8,128)}, bf16[1024,768]{1,0:T(8,128)(2,1)}, bf16[1024,768]{1,0:T(8,128)(2,1)}, f32[1,768]{1,0:T(1,128)}) custom-call(s32[2,1024]{1,0:T(2,128)} %shard_map.247.slots_ref, bf16[1024,128]{1,0:T(8,128)(2,1)} %get-tuple-element.77.logit_ref, bf16[128,768]{1,0:T(8,128)(2,1)} %pad.35.router_ref, f32[1,768]{1,0:T(1,128)} %reshape.131.gain_ref, ...), custom_call_target="tpu_custom_call" | custom-call | tf_op jit(solution)/shard_map/pallas_call | solution.py:422
  400.1 35.6 %shard_map.261 = (bf16[3,1024,768]{2,1,0:T(8,128)(2,1)}, f32[6,4,256]{2,1,0:T(4,128)}) custom-call(bf16[1024,768]{1,0:T(8,128)(2,1)} %get-tuple-element.54.query_ref, bf16[1024,768]{1,0:T(8,128)(2,1)} %get-tuple-element.55.key_ref, bf16[1024,768]{1,0:T(8,128)(2,1)} %get-tuple-element.56.value_ref, bf16[1024,768]{1,0:T(8,128)(2,1)} %get-tuple-element.79.grad_ref, ...), custom_call_target="tpu_custom_call" | custom-call | tf_op jit(solution)/shard_map/pallas_call | solution.py:596
  435.8 11.4 %shard_map.263 = bf16[4,768,768]{2,1,0:T(8,128)(2,1)} custom-call(bf16[1024,768]{1,0:T(8,128)(2,1)} %get-tuple-element.87.left_ref, bf16[1024,768]{1,0:T(8,128)(2,1)} %get-tuple-element.57.mixed_ref.out_ref, bf16[3,1024,768]{2,1,0:T(8,128)(2,1)} %get-tuple-element.81.heads_ref, bf16[1024,768]{1,0:T(8,128)(2,1)} %get-tuple-element.88.branch_ref), custom_call_target="tpu_custom_call" | custom-call | tf_op jit(solution)/shard_map/pallas_call | solution.py:753
  454.0 9.9 %shard_map.262 = (f32[1024,768]{1,0:T(8,128)}, f32[1,768]{1,0:T(1,128)}) custom-call(bf16[3,1024,768]{2,1,0:T(8,128)(2,1)} %get-tuple-element.81.heads_ref, bf16[768,768]{1,0:T(8,128)(2,1)} %get-tuple-element.82.query_ref, bf16[768,768]{1,0:T(8,128)(2,1)} %get-tuple-element.83.key_ref, bf16[768,768]{1,0:T(8,128)(2,1)} %get-tuple-element.84.value_ref, ...), custom_call_target="tpu_custom_call" | custom-call | tf_op jit(solution)/shard_map/pallas_call | solution.py:720
  473.6 12.1 %collective-permute-done.13 = bf16[4,96,768]{2,1,0:T(8,128)(2,1)} collective-permute-done((bf16[4,96,768]{2,1,0:T(8,128)(2,1)S(1)}, bf16[4,96,768]{2,1,0:T(8,128)(2,1)}, u32[]{:S(2)}, u32[]{:S(2)}) %collective-permute-start.13) | collective-permute-done | bytes 589856 | tf_op jit(solution)/shard_map/ppermute | solution.py:814
  504.6 7.4 %collective-permute-done.15 = bf16[104,768]{1,0:T(8,128)(2,1)S(1)} collective-permute-done((bf16[104,768]{1,0:T(8,128)(2,1)S(1)}, bf16[104,768]{1,0:T(8,128)(2,1)S(1)}, u32[]{:S(2)}, u32[]{:S(2)}) %collective-permute-start.15) | collective-permute-done | bytes 159776 | tf_op jit(solution)/shard_map/ppermute | solution.py:819
  512.1 16.1 %collective-permute-done.16 = bf16[104,768]{1,0:T(8,128)(2,1)S(1)} collective-permute-done((bf16[104,768]{1,0:T(8,128)(2,1)S(1)}, bf16[104,768]{1,0:T(8,128)(2,1)S(1)}, u32[]{:S(2)}, u32[]{:S(2)}) %collective-permute-start.16) | collective-permute-done | bytes 159776 | tf_op jit(solution)/shard_map/ppermute | solution.py:819
  549.8 6.1 %shard_map.265 = (f32[1536,768]{1,0:T(8,128)}, f32[1536,768]{1,0:T(8,128)}) custom-call(bf16[2304,768]{1,0:T(8,128)(2,1)} %reduce-scatter.3.cloned.1.call-done.rows_ref, f32[1536,768]{1,0:T(8,128)} %shard_map.264.into_ref), custom_call_target="tpu_custom_call", output_to_operand_aliasing={{1}: (1, {})} | custom-call | tf_op jit(solution)/shard_map/pallas_call | solution.py:797
  (167 shorter events, 85.8 us)
Async XLA Ops:
  7.2 114.0 %all-gather.2.cloned.1.call-start = ((), (), s32[]{:S(2)}) async-start(), calls=%async_computation.8 | async-start | bytes 1474560 | tf_op jit(solution)/shard_map/all_gather | solution.py:952
  10.9 5.3 collective-permute-start
  12.2 14.1 %collective-permute-start.1 = (bf16[96,768]{1,0:T(8,128)(2,1)S(1)}, bf16[96,768]{1,0:T(8,128)(2,1)S(1)}, u32[]{:S(2)}, u32[]{:S(2)}) collective-permute-start(bf16[96,768]{1,0:T(8,128)(2,1)S(1)} %concatenate.74), channel_id=1, source_target_pairs={{0,2},{1,3},{2,0},{3,1},{4,6},{5,7},{6,4},{7,5},{8,10},{9,11},{10,... | collective-permute-start | bytes 442376 | tf_op jit(solution)/shard_map/ppermute | solution.py:819
  13.3 17.8 %collective-permute-start.2 = (bf16[96,768]{1,0:T(8,128)(2,1)S(1)}, bf16[96,768]{1,0:T(8,128)(2,1)S(1)}, u32[]{:S(2)}, u32[]{:S(2)}) collective-permute-start(bf16[96,768]{1,0:T(8,128)(2,1)S(1)} %concatenate.74), channel_id=1, source_target_pairs={{0,3},{1,0},{2,1},{3,2},{4,7},{5,4},{6,5},{7,6},{8,11},{9,8},{10,9... | collective-permute-start | bytes 442376 | tf_op jit(solution)/shard_map/ppermute | solution.py:819
  31.1 26.9 %collective-permute-start.6 = (bf16[1,2,72,768]{3,2,1,0:T(8,128)(2,1)S(1)}, bf16[1,2,72,768]{3,2,1,0:T(8,128)(2,1)S(1)}, u32[]{:S(2)}, u32[]{:S(2)}) collective-permute-start(bf16[1,2,72,768]{3,2,1,0:T(8,128)(2,1)S(1)} %get-tuple-element.111), channel_id=1, source_target_pairs={{0,16},{4,20},{8,24},{12,28},{16,0},{20,4},{24,8},{28,12},{1,17},{... | collective-permute-start | bytes 663560 | tf_op jit(solution)/shard_map/ppermute | solution.py:814
  32.6 26.9 %collective-permute-start.3 = (bf16[1,2,72,768]{3,2,1,0:T(8,128)(2,1)S(1)}, bf16[1,2,72,768]{3,2,1,0:T(8,128)(2,1)S(1)}, u32[]{:S(2)}, u32[]{:S(2)}) collective-permute-start(bf16[1,2,72,768]{3,2,1,0:T(8,128)(2,1)S(1)} %get-tuple-element.112), channel_id=1, source_target_pairs={{0,8},{4,12},{8,0},{12,4},{16,24},{20,28},{24,16},{28,20},{1,9},{5... | collective-permute-start | bytes 663560 | tf_op jit(solution)/shard_map/ppermute | solution.py:814
  53.1 79.0 %all-to-all-start.1 = ((bf16[8,160,768]{2,1,0:T(8,128)(2,1)}), bf16[8,160,768]{2,1,0:T(8,128)(2,1)}, u32[]{:S(2)}, u32[]{:S(2)}) async-start(bf16[8,160,768]{2,1,0:T(8,128)(2,1)} %get-tuple-element.61), calls=%async_computation.1 | async-start | bytes 3932160 | tf_op jit(solution)/shard_map/all_to_all | solution.py:888
  58.1 32.8 %collective-permute-start.7 = (bf16[2,2,72,768]{3,2,1,0:T(8,128)(2,1)S(1)}, bf16[2,2,72,768]{3,2,1,0:T(8,128)(2,1)S(1)}, u32[]{:S(2)}, u32[]{:S(2)}) collective-permute-start(bf16[2,2,72,768]{3,2,1,0:T(8,128)(2,1)S(1)} %pad_maximum_fusion.4), channel_id=1, source_target_pairs={{0,8},{4,12},{8,0},{12,4},{16,24},{20,28},{24,16},{28,20},{1,9},{5... | collective-permute-start | bytes 1327112 | tf_op jit(solution)/shard_map/ppermute | solution.py:814
  59.5 33.5 %copy-start.11 = (f32[32,256,1]{1,0,2:T(8,128)S(1)}, f32[32,256,1]{1,0,2:T(8,128)}, u32[]{:S(2)}) copy-start(f32[32,256,1]{1,0,2:T(8,128)} %constant.250) | copy-start | bytes 98308
  59.5 32.5 %collective-permute-start.4 = (bf16[2,2,72,768]{3,2,1,0:T(8,128)(2,1)S(1)}, bf16[2,2,72,768]{3,2,1,0:T(8,128)(2,1)S(1)}, u32[]{:S(2)}, u32[]{:S(2)}) collective-permute-start(bf16[2,2,72,768]{3,2,1,0:T(8,128)(2,1)S(1)} %pad_maximum_fusion.3), channel_id=1, source_target_pairs={{0,16},{4,20},{8,24},{12,28},{16,0},{20,4},{24,8},{28,12},{1,17},{... | collective-permute-start | bytes 1327112 | tf_op jit(solution)/shard_map/ppermute | solution.py:814
  91.0 4.2 collective-permute-start.8
  92.1 3.3 collective-permute-start.5
  132.1 26.4 %all-to-all-start = ((bf16[8,160,768]{2,1,0:T(8,128)(2,1)}), bf16[8,160,768]{2,1,0:T(8,128)(2,1)}, u32[]{:S(2)}, u32[]{:S(2)}) async-start(bf16[8,160,768]{2,1,0:T(8,128)(2,1)} %bitcast.54), calls=%async_computation | async-start | bytes 3932160 | tf_op jit(solution)/shard_map/all_to_all | solution.py:888
  136.7 406.5 %reduce-scatter.5.cloned.1.call-start = ((), (), s32[]{:S(2)}) async-start(), calls=%async_computation.10 | async-start | bytes 5898240 | tf_op jit(solution)/shard_map/reduce_scatter | solution.py:884
  188.4 50.8 %all-to-all-start.4 = ((bf16[8,2,160,768]{3,2,1,0:T(8,128)(2,1)}), bf16[8,2,160,768]{3,2,1,0:T(8,128)(2,1)}, u32[]{:S(2)}, u32[]{:S(2)}) async-start(bf16[8,2,160,768]{3,2,1,0:T(8,128)(2,1)} %shard_map.255), calls=%async_computation.4 | async-start | bytes 7864320 | tf_op jit(solution)/shard_map/all_to_all | solution.py:888
  196.4 353.4 %reduce-scatter.3.cloned.1.call-start = ((), (), s32[]{:S(2)}) async-start(), calls=%async_computation.9 | async-start | bytes 17694720 | tf_op jit(solution)/shard_map/reduce_scatter | solution.py:884
  278.2 50.7 %all-to-all-start.3 = ((bf16[8,2,160,768]{3,2,1,0:T(8,128)(2,1)}), bf16[8,2,160,768]{3,2,1,0:T(8,128)(2,1)}, u32[]{:S(2)}, u32[]{:S(2)}) async-start(bf16[8,2,160,768]{3,2,1,0:T(8,128)(2,1)} %get-tuple-element.66), calls=%async_computation.3 | async-start | bytes 7864320 | tf_op jit(solution)/shard_map/all_to_all | solution.py:888
  328.9 51.2 %all-to-all-start.5 = ((bf16[8,2,160,768]{3,2,1,0:T(8,128)(2,1)}), bf16[8,2,160,768]{3,2,1,0:T(8,128)(2,1)}, u32[]{:S(2)}, u32[]{:S(2)}) async-start(bf16[8,2,160,768]{3,2,1,0:T(8,128)(2,1)} %shard_map.258), calls=%async_computation.5 | async-start | bytes 7864320 | tf_op jit(solution)/shard_map/all_to_all | solution.py:888
  450.4 17.1 %collective-permute-start.9 = (bf16[4,384,768]{2,1,0:T(8,128)(2,1)}, bf16[4,384,768]{2,1,0:T(8,128)(2,1)}, u32[]{:S(2)}, u32[]{:S(2)}) collective-permute-start(bf16[4,384,768]{2,1,0:T(8,128)(2,1)} %constant_dynamic-slice_fusion.3), channel_id=1, source_target_pairs={{0,4},{4,0},{8,12},{12,8},{16,20},{20,16},{24,28},{28,24},{1,5},{5... | collective-permute-start | bytes 7077896 | tf_op jit(solution)/shard_map/ppermute | solution.py:814
  465.9 1.5 collective-permute-start.12
  470.8 14.9 %collective-permute-start.13 = (bf16[4,96,768]{2,1,0:T(8,128)(2,1)S(1)}, bf16[4,96,768]{2,1,0:T(8,128)(2,1)}, u32[]{:S(2)}, u32[]{:S(2)}) collective-permute-start(bf16[4,96,768]{2,1,0:T(8,128)(2,1)S(1)} %fusion.1), channel_id=1, source_target_pairs={{0,16},{4,20},{8,24},{12,28},{16,0},{20,4},{24,8},{28,12},{1,17},{... | collective-permute-start | bytes 1769480 | tf_op jit(solution)/shard_map/ppermute | solution.py:814
  473.3 17.0 %collective-permute-start.10 = (bf16[4,112,768]{2,1,0:T(8,128)(2,1)}, bf16[4,112,768]{2,1,0:T(8,128)(2,1)}, u32[]{:S(2)}, u32[]{:S(2)}) collective-permute-start(bf16[4,112,768]{2,1,0:T(8,128)(2,1)} %constant_dynamic-slice_fusion.2), channel_id=1, source_target_pairs={{0,8},{4,12},{8,0},{12,4},{16,24},{20,28},{24,16},{28,20},{1,9},{5... | collective-permute-start | bytes 2064392 | tf_op jit(solution)/shard_map/ppermute | solution.py:814
  487.1 9.5 %collective-permute-start.14 = (bf16[4,48,768]{2,1,0:T(8,128)(2,1)S(1)}, bf16[4,48,768]{2,1,0:T(8,128)(2,1)S(1)}, u32[]{:S(2)}, u32[]{:S(2)}) collective-permute-start(bf16[4,48,768]{2,1,0:T(8,128)(2,1)S(1)} %constant_dynamic-slice_fusion), channel_id=1, source_target_pairs={{0,8},{4,12},{8,0},{12,4},{16,24},{20,28},{24,16},{28,20},{1,9},{5... | collective-permute-start | bytes 884744 | tf_op jit(solution)/shard_map/ppermute | solution.py:814
  491.6 7.9 %collective-permute-start.11 = (bf16[4,56,768]{2,1,0:T(8,128)(2,1)S(1)}, bf16[4,56,768]{2,1,0:T(8,128)(2,1)S(1)}, u32[]{:S(2)}, u32[]{:S(2)}) collective-permute-start(bf16[4,56,768]{2,1,0:T(8,128)(2,1)S(1)} %constant_dynamic-slice_fusion.1), channel_id=1, source_target_pairs={{0,16},{4,20},{8,24},{12,28},{16,0},{20,4},{24,8},{28,12},{1,17},{... | collective-permute-start | bytes 1032200 | tf_op jit(solution)/shard_map/ppermute | solution.py:814
  499.6 12.5 %collective-permute-start.15 = (bf16[104,768]{1,0:T(8,128)(2,1)S(1)}, bf16[104,768]{1,0:T(8,128)(2,1)S(1)}, u32[]{:S(2)}, u32[]{:S(2)}) collective-permute-start(bf16[104,768]{1,0:T(8,128)(2,1)S(1)} %get-tuple-element.108), channel_id=1, source_target_pairs={{0,1},{1,2},{2,3},{3,0},{4,5},{5,6},{6,7},{7,4},{8,9},{9,10},{10,1... | collective-permute-start | bytes 479240 | tf_op jit(solution)/shard_map/ppermute | solution.py:819
  499.7 28.5 %collective-permute-start.16 = (bf16[104,768]{1,0:T(8,128)(2,1)S(1)}, bf16[104,768]{1,0:T(8,128)(2,1)S(1)}, u32[]{:S(2)}, u32[]{:S(2)}) collective-permute-start(bf16[104,768]{1,0:T(8,128)(2,1)S(1)} %get-tuple-element.109), channel_id=1, source_target_pairs={{0,2},{1,3},{2,0},{3,1},{4,6},{5,7},{6,4},{7,5},{8,10},{9,11},{10,... | collective-permute-start | bytes 479240 | tf_op jit(solution)/shard_map/ppermute | solution.py:819
  503.2 26.6 %collective-permute-start.17 = (bf16[104,768]{1,0:T(8,128)(2,1)S(1)}, bf16[104,768]{1,0:T(8,128)(2,1)S(1)}, u32[]{:S(2)}, u32[]{:S(2)}) collective-permute-start(bf16[104,768]{1,0:T(8,128)(2,1)S(1)} %get-tuple-element.110), channel_id=1, source_target_pairs={{0,3},{1,0},{2,1},{3,2},{4,7},{5,4},{6,5},{7,6},{8,11},{9,8},{10,9... | collective-permute-start | bytes 479240 | tf_op jit(solution)/shard_map/ppermute | solution.py:819
  529.9 3.3 collective-permute-start.20
  531.5 3.6 collective-permute-start.18
  533.2 4.6 collective-permute-start.21
  535.1 4.6 collective-permute-start.19
  539.9 5.9 %collective-permute-start.22 = (bf16[416,768]{1,0:T(8,128)(2,1)S(1)}, bf16[416,768]{1,0:T(8,128)(2,1)S(1)}, u32[]{:S(2)}, u32[]{:S(2)}) collective-permute-start(bf16[416,768]{1,0:T(8,128)(2,1)S(1)} %pad_maximum_fusion.2), channel_id=1, source_target_pairs={{0,4},{4,0},{8,12},{12,8},{16,20},{20,16},{24,28},{28,24},{1,5},{5... | collective-permute-start | bytes 1916936 | tf_op jit(solution)/shard_map/ppermute | solution.py:814
  (14 other events, 156.7 us)
Sparse Core Ops, SparseCore 0:
  14.8 29.7 all-gather.1
  179.3 88.2 reduce-scatter.4
  278.3 253.2 reduce-scatter.2

commit v7 on v6

--- a/solution.py
+++ b/solution.py
@@ -39,7 +39,7 @@
     return lax.dot_general(a, b, (((0,), (0,)), ((), ())), preferred_element_type=jnp.float32)
 
 
-def slot_kernel(routes_ref, base_ref, slots_ref, *, experts):
+def slot_kernel(routes_ref, slots_ref, float_ref, *, experts, local_count, owners, capacity):
     tokens = routes_ref.shape[1]
     expert = lax.broadcasted_iota(jnp.int32, (experts, tokens), 0)
     hits = [routes_ref[c:c + 1, :] == expert for c in range(2)]
@@ -48,37 +48,42 @@
     later = lax.broadcasted_iota(jnp.int32, (tokens, tokens), 1)
     before = jnp.where(earlier < later, 1.0, 0.0).astype(jnp.bfloat16)
     counts = dot_nn(hot, before)
+    column = lax.broadcasted_iota(jnp.int32, (experts, 1), 0)
+    base = (column % local_count * owners + column // local_count) * capacity
+    counts = counts + base.astype(jnp.float32)
     for c in range(2):
-        position = jnp.sum(jnp.where(hits[c], counts, 0.0), axis=0, keepdims=True)
-        slots_ref[c:c + 1, :] = base_ref[c:c + 1, :] + position.astype(jnp.int32)
-
-
-def find_slots(routes, base, experts):
-    return pl.pallas_call(
-        partial(slot_kernel, experts=experts),
-        out_shape=jax.ShapeDtypeStruct(routes.shape, jnp.int32),
-    )(routes, base)
-
-
-def dispatch_both_kernel(slots_ref, rows_ref, cot_ref, *refs, start):
+        slot = jnp.sum(jnp.where(hits[c], counts, 0.0), axis=0, keepdims=True)
+        slots_ref[c:c + 1, :] = slot.astype(jnp.int32)
+    float_ref[...] = routes_ref[...].astype(jnp.float32)
+
+
+def find_slots(routes, experts, local_count, owners, capacity):
+    return pl.pallas_call(
+        partial(slot_kernel, experts=experts, local_count=local_count, owners=owners, capacity=capacity),
+        out_shape=[jax.ShapeDtypeStruct(routes.shape, jnp.int32), jax.ShapeDtypeStruct(routes.shape, jnp.float32)],
+    )(routes)
+
+
+def dispatch_both_kernel(slots_ref, rows_ref, cot_ref, *refs, start, capacity, early):
     out_ref = refs[-1]
-    block, tokens = out_ref.shape[2], rows_ref.shape[0]
+    block, tokens = capacity, rows_ref.shape[0]
     slot = lax.broadcasted_iota(jnp.int32, (block, tokens), 0) + (pl.program_id(0) * block + start)
     hot = jnp.where((slot == slots_ref[0:1, :]) | (slot == slots_ref[1:2, :]), 1.0, 0.0)
     hot = hot.astype(jnp.bfloat16)
-    out_ref[0, 0] = dot_nn(hot, rows_ref[...]).astype(out_ref.dtype)
-    out_ref[0, 1] = dot_nn(hot, cot_ref[...]).astype(out_ref.dtype)
-
-
-def dispatch_both(slots, rows, cot, start, owners, capacity, after=()):
+    out_ref[0, :capacity] = dot_nn(hot, rows_ref[...]).astype(out_ref.dtype)
+    out_ref[0, capacity:] = dot_nn(hot[early:], cot_ref[...]).astype(out_ref.dtype)
+
+
+def dispatch_both(slots, rows, cot, start, owners, capacity, early, after=()):
     width = rows.shape[1]
+    total = 2 * capacity - early
     whole = lambda shape: pl.BlockSpec(shape, lambda i: (0, 0))
     return pl.pallas_call(
-        partial(dispatch_both_kernel, start=start),
+        partial(dispatch_both_kernel, start=start, capacity=capacity, early=early),
         grid=(owners,),
         in_specs=[whole(slots.shape), whole(rows.shape), whole(cot.shape)] + [pl.BlockSpec(memory_space=pl.ANY)] * len(after),
-        out_specs=pl.BlockSpec((1, 2, capacity, width), lambda i: (i, 0, 0, 0)),
-        out_shape=jax.ShapeDtypeStruct((owners, 2, capacity, width), rows.dtype),
+        out_specs=pl.BlockSpec((1, total, width), lambda i: (i, 0, 0)),
+        out_shape=jax.ShapeDtypeStruct((owners, total, width), rows.dtype),
         compiler_params=pltpu.CompilerParams(vmem_limit_bytes=62 << 20),
     )(slots, rows, cot, *after)
 
@@ -89,42 +94,51 @@
     slot = row + pl.program_id(0) * capacity
     slot = slot + jnp.where(row >= capacity, (owners - 1) * capacity, 0)
     hits = [slot == slots_ref[c:c + 1, :] for c in range(2)]
-    hot = jnp.where(hits[0] | hits[1], 1.0, 0.0)[:capacity]
+    hot = jnp.where(hits[0] | hits[1], 1.0, 0.0)[:out_ref.shape[1]]
     out_ref[0] = dot_nn(hot.astype(jnp.bfloat16), rows_ref[...]).astype(out_ref.dtype)
     other = jnp.where(hits[0], routes_ref[1:2, :], jnp.where(hits[1], routes_ref[0:1, :], 0.0))
     column = jnp.sum(other, axis=1, keepdims=True)
     other_ref[0] = jnp.broadcast_to(column, (block, 128)).T[0:1, :]
 
 
-def dispatch_first(slots, routes, rows, owners, capacity):
+def dispatch_first(slots, routes, rows, owners, capacity, early):
     width = rows.shape[1]
+    total = capacity + early
     whole = lambda shape: pl.BlockSpec(shape, lambda i: (0, 0))
     return pl.pallas_call(
         partial(dispatch_first_kernel, owners=owners, capacity=capacity),
         grid=(owners,),
         in_specs=[whole(slots.shape), whole(routes.shape), whole(rows.shape)],
-        out_specs=[pl.BlockSpec((1, capacity, width), lambda i: (i, 0, 0)), pl.BlockSpec((1, 1, 2 * capacity), lambda i: (i, 0, 0))],
-        out_shape=[jax.ShapeDtypeStruct((owners, capacity, width), rows.dtype), jax.ShapeDtypeStruct((owners, 1, 2 * capacity), jnp.float32)],
+        out_specs=[pl.BlockSpec((1, total, width), lambda i: (i, 0, 0)), pl.BlockSpec((1, 1, 2 * capacity), lambda i: (i, 0, 0))],
+        out_shape=[jax.ShapeDtypeStruct((owners, total, width), rows.dtype), jax.ShapeDtypeStruct((owners, 1, 2 * capacity), jnp.float32)],
     )(slots, routes, rows)
 
 
-def gelu_pair(v):
+def gelu_half(v):
     c = np.float32(np.sqrt(2.0 / np.pi))
-    a = np.float32(0.044715)
     square = v * v
-    half = 0.5 * jnp.tanh(v * (c * a * square + c)) + 0.5
-    value = v * half
-    slope = half + value * (1.0 - half) * (6.0 * c * a * square + 2.0 * c)
-    return value, slope
-
-
-def first_kernel(owner_ref, rows_ref, cot_ref, other_ref, router_ref, up_ref, *refs, chunk, index, local_count):
-    act_ref, slope_ref, down_grad_ref, grad_ref = refs[-4:]
-    owners, capacity, width = rows_ref.shape
+    half = 0.5 * jnp.tanh(v * (np.float32(0.044715) * c * square + c)) + 0.5
+    return half, square
+
+
+def gelu_slope(v):
+    c = np.float32(np.sqrt(2.0 / np.pi))
+    half, square = gelu_half(v)
+    return half + v * half * (1.0 - half) * (np.float32(6.0 * 0.044715) * c * square + 2.0 * c)
+
+
+def arrived_spec(arrived):
+    return pl.BlockSpec(arrived.shape, lambda i: (0, 0, 0))
+
+
+def first_kernel(owner_ref, rows_ref, other_ref, router_ref, up_ref, *refs, index, local_count, capacity, pieces):
+    act_ref, pre_ref, down_grad_ref, grad_ref = refs[-4:]
+    owners, _, width = rows_ref.shape
     rows = owners * capacity
+    chunk = rows // 2
     @pl.when(pl.program_id(0) == 0)
     def _():
-        logits = dot_nt(router_ref[...], rows_ref[...].reshape(rows, width))
+        logits = dot_nt(router_ref[...], rows_ref[:, :capacity].reshape(rows, width))
         expert = lax.broadcasted_iota(jnp.int32, logits.shape, 0)
         mine = owner_ref[0] * local_count + index
         own = jnp.sum(jnp.where(expert == mine, logits, 0.0), axis=0, keepdims=True)
@@ -135,53 +149,46 @@
         gate = own / (own + jnp.exp(other - top))
         column = jnp.broadcast_to(gate, (128, rows)).T
         for start in range(0, width, 128):
-            part = cot_ref[:, :, start:start + 128].reshape(rows, 128).astype(jnp.float32) * column
+            parts = [refs[place][:, low:low + size, start:start + 128] for place, low, size in pieces]
+            part = parts[0] if len(parts) == 1 else jnp.concatenate(parts, axis=1)
+            part = part.reshape(rows, 128).astype(jnp.float32) * column
             grad_ref[:, start:start + 128] = part.astype(jnp.bfloat16)
     up = up_ref[0]
     for start in range(0, rows, chunk):
-        part = rows_ref[start // capacity:(start + chunk) // capacity].reshape(chunk, width)
+        part = rows_ref[start // capacity:(start + chunk) // capacity, :capacity].reshape(chunk, width)
         pre = dot_nn(part, up)
-        value, slope = gelu_pair(pre)
-        act_ref[start:start + chunk, :] = value.astype(jnp.bfloat16)
-        slope_ref[start:start + chunk, :] = slope.astype(jnp.bfloat16)
+        half, _ = gelu_half(pre)
+        act_ref[start:start + chunk, :] = (pre * half).astype(jnp.bfloat16)
+        pre_ref[start:start + chunk, :] = pre.astype(jnp.bfloat16)
     down_grad_ref[0] = dot_tn(act_ref[...], grad_ref[...]).astype(jnp.bfloat16)
 
 
-def arrived_spec(arrived, which):
-    if arrived.ndim == 3:
-        return pl.BlockSpec(arrived.shape, lambda i: (0, 0, 0))
-    owners, _, capacity, width = arrived.shape
-    return pl.BlockSpec((owners, None, capacity, width), lambda i: (0, which, 0, 0))
-
-
-def expert_first(owner, rows_in, cot, other, router, up, index, local_count, shards, into=None, after=()):
-    owners, capacity, width = rows_in.shape[0], *rows_in.shape[-2:]
+def expert_first(owner, rows_in, cots, pieces, other, router, up, index, local_count, capacity, shards, into=None):
+    owners, _, width = rows_in.shape
     rows = owners * capacity
     hidden = up.shape[2]
     tile = hidden // shards
-    chunk = rows // 2
     fixed = pl.BlockSpec((rows, width), lambda i: (0, 0))
     column = pl.BlockSpec((rows, tile), lambda i: (0, i))
-    operands = [owner, rows_in, cot, other, router, up]
+    operands = [owner, rows_in, other, router, up, *cots]
     place, aliases = 0, {}
     grad_shape = jax.ShapeDtypeStruct((shards, tile, width), jnp.bfloat16)
     if into is not None:
         aliases = {len(operands): 2}
         operands.append(into)
         place, grad_shape = 2, jax.ShapeDtypeStruct(into.shape, into.dtype)
-    operands += list(after)
-    return pl.pallas_call(
-        partial(first_kernel, chunk=chunk, index=index, local_count=local_count),
+    return pl.pallas_call(
+        partial(first_kernel, index=index, local_count=local_count, capacity=capacity, pieces=pieces),
         grid=(shards,),
         in_specs=[
             pl.BlockSpec(memory_space=pltpu.SMEM),
-            arrived_spec(rows_in, 0),
-            arrived_spec(cot, 1),
+            arrived_spec(rows_in),
             pl.BlockSpec((1, rows), lambda i: (0, 0)),
             pl.BlockSpec(router.shape, lambda i: (0, 0)),
             pl.BlockSpec((1, width, tile), lambda i: (index, 0, i)),
         ]
-        + [pl.BlockSpec(memory_space=pl.ANY)] * (len(operands) - 6),
+        + [arrived_spec(cot) for cot in cots]
+        + [pl.BlockSpec(memory_space=pl.ANY)] * (into is not None),
         out_specs=[column, column, pl.BlockSpec((1, tile, width), lambda i: (i, place, 0)), fixed],
         out_shape=[jax.ShapeDtypeStruct((rows, hidden), jnp.bfloat16)] * 2 + [grad_shape, jax.ShapeDtypeStruct((rows, width), jnp.bfloat16)],
         input_output_aliases=aliases,
@@ -189,17 +196,19 @@
     )(*operands)
 
 
-def second_kernel(rows_ref, grad_ref, act_ref, slope_ref, up_ref, down_ref, *refs):
+def second_kernel(rows_ref, grad_ref, act_ref, pre_ref, up_ref, down_ref, *refs):
     made_ref, up_grad_ref, turned, made_acc, back_acc = refs[-5:]
     step = pl.program_id(0)
     owners, _, capacity, width = made_ref.shape
     @pl.when(step == 0)
     def _():
-        turned[...] = rows_ref[...].reshape(grad_ref.shape).T
+        rows, width = grad_ref.shape
+        owners = rows_ref.shape[0]
+        turned[...] = rows_ref[:, :rows // owners].reshape(rows, width).T
     up = up_ref[0]
     down = down_ref[0]
     grads = dot_nt(grad_ref[...], down)
-    low = (slope_ref[...].astype(jnp.float32) * grads).astype(jnp.bfloat16)
+    low = (gelu_slope(pre_ref[...].astype(jnp.float32)) * grads).astype(jnp.bfloat16)
     up_grad_ref[0] = dot_nn(turned[...], low).astype(jnp.bfloat16)
     back = dot_nt(low, up)
     made = dot_nn(act_ref[...], down)
@@ -218,7 +227,7 @@
         made_ref[:, 1] = (back_acc[...] + back).astype(jnp.bfloat16).reshape(owners, capacity, width)
 
 
-def expert_second(rows_in, grad, act, slope, up, down, index, owners, shards, wide, after=()):
+def expert_second(rows_in, grad, act, pre, up, down, index, owners, shards, wide, after=()):
     rows, width = grad.shape
     hidden = up.shape[2]
     tile = hidden // shards
@@ -228,42 +237,44 @@
     return pl.pallas_call(
         second_kernel,
         grid=(shards,),
-        in_specs=[arrived_spec(rows_in, 0), fixed, column, column, pl.BlockSpec((1, width, tile), lambda i: (index, 0, i)), pl.BlockSpec((1, tile, width), lambda i: (index, i, 0))]
+        in_specs=[arrived_spec(rows_in), fixed, column, column, pl.BlockSpec((1, width, tile), lambda i: (index, 0, i)), pl.BlockSpec((1, tile, width), lambda i: (index, i, 0))]
         + [pl.BlockSpec(memory_space=pl.ANY)] * len(after),
         out_specs=[pl.BlockSpec(made_shape, lambda i: (0, 0, 0, 0)), pl.BlockSpec((1, width, tile), lambda i: (i, 0, 0))],
         out_shape=[jax.ShapeDtypeStruct(made_shape, jnp.bfloat16), jax.ShapeDtypeStruct((shards, wide, tile), jnp.bfloat16)],
         scratch_shapes=[pltpu.VMEM((width, rows), jnp.bfloat16), pltpu.VMEM((rows, width), jnp.float32), pltpu.VMEM((rows, width), jnp.float32)],
         compiler_params=pltpu.CompilerParams(vmem_limit_bytes=62 << 20),
-    )(rows_in, grad, act, slope, up, down, *after)
-
-
-def slope_kernel(rows_ref, grad_ref, slope_ref, down_ref, into_ref, low_ref, up_grad_ref, turned):
+    )(rows_in, grad, act, pre, up, down, *after)
+
+
+def slope_kernel(rows_ref, grad_ref, pre_ref, down_ref, into_ref, low_ref, up_grad_ref, turned):
     del into_ref
     @pl.when(pl.program_id(0) == 0)
     def _():
-        turned[...] = rows_ref[...].reshape(grad_ref.shape).T
+        rows, width = grad_ref.shape
+        owners = rows_ref.shape[0]
+        turned[...] = rows_ref[:, :rows // owners].reshape(rows, width).T
     grads = dot_nt(grad_ref[...], down_ref[0])
-    low = (slope_ref[...].astype(jnp.float32) * grads).astype(jnp.bfloat16)
+    low = (gelu_slope(pre_ref[...].astype(jnp.float32)) * grads).astype(jnp.bfloat16)
     low_ref[...] = low
     up_grad_ref[0] = dot_nn(turned[...], low).astype(jnp.bfloat16)
 
 
-def expert_slope(rows_in, grad, slope, down, index, shards, into, place):
+def expert_slope(rows_in, grad, pre, down, index, shards, into, place):
     rows, width = grad.shape
-    hidden = slope.shape[1]
+    hidden = pre.shape[1]
     tile = hidden // shards
     fixed = pl.BlockSpec((rows, width), lambda i: (0, 0))
     column = pl.BlockSpec((rows, tile), lambda i: (0, i))
     return pl.pallas_call(
         slope_kernel,
         grid=(shards,),
-        in_specs=[arrived_spec(rows_in, 0), fixed, column, pl.BlockSpec((1, tile, width), lambda i: (index, i, 0)), pl.BlockSpec(memory_space=pl.ANY)],
+        in_specs=[arrived_spec(rows_in), fixed, column, pl.BlockSpec((1, tile, width), lambda i: (index, i, 0)), pl.BlockSpec(memory_space=pl.ANY)],
         out_specs=[column, pl.BlockSpec((1, width, tile), lambda i: (i, place, 0))],
         out_shape=[jax.ShapeDtypeStruct((rows, hidden), jnp.bfloat16), jax.ShapeDtypeStruct(into.shape, into.dtype)],
         input_output_aliases={4: 1},
         scratch_shapes=[pltpu.VMEM((width, rows), jnp.bfloat16)],
         compiler_params=pltpu.CompilerParams(vmem_limit_bytes=62 << 20),
-    )(rows_in, grad, slope, down, into)
+    )(rows_in, grad, pre, down, into)
 
 
 def last_kernel(act_ref, low_ref, up_ref, down_ref, made_ref, made_acc, back_acc):
@@ -923,6 +934,7 @@
     capacity = -(-capacity // 16) * 16
     rows = owners * capacity
     assert local_count == 2 and hidden // shards == width
+    early = -(-capacity // 32) * 16
 
     router_at = 2 + local_heads + (-(2 + local_heads)) % 8
 
@@ -958,10 +970,9 @@
     router_full = router_full.transpose(1, 0, 2).reshape(experts, width)
 
     routes_line = routes.T
-    base = (routes_line % local_count * owners + routes_line // local_count) * capacity
-    slots = find_slots(routes_line, base, experts)
+    slots, routes_float = find_slots(routes_line, experts, local_count, owners, capacity)
     cot_rows, other = dispatch_first(
-        slots, routes_line.astype(f32), cotangent, owners, capacity
+        slots, routes_float, cotangent, owners, capacity, early
     )
     other = share_rows(other).reshape(owners, local_count, capacity)
 
@@ -985,19 +996,21 @@
     others = [other[:, index].reshape(1, rows) for index in range(local_count)]
     rows_in = share_large(send.reshape(owners, capacity, width))
     joint = dispatch_both(
-        slots, low_two, cotangent, rows, owners, capacity, after=others
+        slots, low_two, cotangent, rows, owners, capacity, early, after=others
     )
     joint_in = share_large(joint)
-    act, slope, first_down, grad_in = expert_first(
-    owner, rows_in, cot_in, others[0], router_full, up_weight, 0, local_count, shards,
+    act, pre, first_down, grad_in = expert_first(
+        owner, rows_in, [cot_in], [(0, 0, capacity)], others[0], router_full, up_weight,
+        0, local_count, capacity, shards,
     )
     first_sum = scatter_sum(first_down)
-    first_made, pair = expert_second(rows_in, grad_in, act, slope, up_weight, down_weight, 0, owners, shards, 3 * width)
-    act, slope, pair, grad_in = expert_first(
-        owner, joint_in, joint_in, others[1], router_full, up_weight, 1, local_count, shards,
-        into=pair,
-    )
-    low, pair = expert_slope(joint_in, grad_in, slope, down_weight, 1, shards, pair, 1)
+    first_made, pair = expert_second(rows_in, grad_in, act, pre, up_weight, down_weight, 0, owners, shards, 3 * width)
+    late = capacity - early
+    act, pre, pair, grad_in = expert_first(
+        owner, joint_in, [cot_in, joint_in], [(0, capacity, early), (1, capacity, late)],
+        others[1], router_full, up_weight, 1, local_count, capacity, shards, into=pair,
+    )
+    low, pair = expert_slope(joint_in, grad_in, pre, down_weight, 1, shards, pair, 1)
     pair_sum = scatter_sum(pair)
     second_made = expert_last(act, low, up_weight, down_weight, 1, owners, shards)
     returned = share_rows(first_made)

time: 570 us -> 561 us (0.984)
  blocking collectives: 9.92 us -> 0 us
    ppermute x17, waiting for transfers between devices: 57.9 us -> 74.1 us  [exchange(): return lax.ppermute(rows, OWNER, [(i, i ^ bit) for i in range(count)])]
    ppermute x6, waiting for transfers between devices: 40 us -> 25.5 us  [shift(): lax.ppermute(rows, LINE, [(i, (i + step) % count) for i in range(count)])]
    all_to_all x1 -> x0, blocking collectives: 9.92 us -> none  [share_rows(): return lax.all_to_all(rows, OWNER, 0, 0, tiled=True)]
    all_to_all x5 -> x6, waiting for transfers between devices: 78.6 us -> 76.2 us  [share_rows(): return lax.all_to_all(rows, OWNER, 0, 0, tiled=True)]
    all_to_all x5 -> x6, starting transfers between devices: 33.9 us -> 35.6 us  [share_rows(): return lax.all_to_all(rows, OWNER, 0, 0, tiled=True)]
  transfers between devices with their start and end apart: 31 -> 32, of which waited for: 20 -> 19; matrix products, arithmetic and copies ran while one was open for 4% -> 4% of each run, Pallas kernels for 43% -> 44%
where the time goes in v7:
time: 561 us; the launch traced here: 553 us
  Pallas kernels  270 us (48%)
  waiting for transfers between devices  176 us (31%)
  starting transfers between devices  66.5 us (12%)
  local copies, waits for them, and re-layouts  16.2 us (3%)
  between operations  14.5 us (3%)
  other arithmetic  10 us (2%)
    all_to_all x6, waiting for transfers between devices, share_rows(): return lax.all_to_all(rows, OWNER, 0, 0, tiled=True)  76.2 us
    ppermute x17, waiting for transfers between devices, exchange(): return lax.ppermute(rows, OWNER, [(i, i ^ bit) for i in range(count)])  74.1 us
    pallas_call x2, Pallas kernels, expert_first(): pl.pallas_call(partial(first_kernel, index=index, local_count=local_count...  39 us
    pallas_call x1, Pallas kernels, expert_second(): pl.pallas_call(second_kernel, grid=(shards,), in_specs=[arrived_spec(rows...  37.5 us
    pallas_call x1, Pallas kernels, attend_back(): pl.pallas_call(partial(attend_back_kernel, block=block, size=size, scale=...  35.6 us
    all_to_all x6, starting transfers between devices, share_rows(): return lax.all_to_all(rows, OWNER, 0, 0, tiled=True)  35.6 us
    ppermute x6, waiting for transfers between devices, shift(): lax.ppermute(rows, LINE, [(i, (i + step) % count) for i in range(count)])  25.5 us
    ppermute x17, starting transfers between devices, exchange(): return lax.ppermute(rows, OWNER, [(i, i ^ bit) for i in range(count)])  22.8 us
  transfers between devices with their start and end apart: 32, of which 19 were waited for; matrix products, arithmetic and copies ran while one was open for 4% of the time, Pallas kernels for 44%

profile of v7, /device:TPU:9, one launch (start us, length us, event | category | flops | bytes accessed | tf_op | source)
XLA Modules:
  0.0 553.4 jit_solution(6036648421105327234)
XLA Ops:
  16.3 8.0 %shard_map.251 = (bf16[8,240,768]{2,1,0:T(8,128)(2,1)}, f32[8,1,320]{2,1,0:T(1,128)}) custom-call(s32[2,1024]{1,0:T(2,128)} %get-tuple-element.56.slots_ref, f32[2,1024]{1,0:T(2,128)} %get-tuple-element.64.routes_ref, bf16[1024,768]{1,0:T(8,128)(2,1)} %cot_ref.7), custom_call_target="tpu_custom_call" | custom-call | tf_op jit(solution)/shard_map/pallas_call | solution.py:108
  24.3 5.2 all-to-all-start.1
  29.6 3.9 all-to-all-done.1
  33.5 5.0 all-to-all-start.2
  41.4 35.8 %collective-permute-done.6 = bf16[1,2,72,768]{3,2,1,0:T(8,128)(2,1)S(1)} collective-permute-done((bf16[1,2,72,768]{3,2,1,0:T(8,128)(2,1)S(1)}, bf16[1,2,72,768]{3,2,1,0:T(8,128)(2,1)S(1)}, u32[]{:S(2)}, u32[]{:S(2)}) %collective-permute-start.6) | collective-permute-done | bytes 221216 | tf_op jit(solution)/shard_map/ppermute | solution.py:825
  79.2 9.3 %collective-permute-done.7 = bf16[2,2,72,768]{3,2,1,0:T(8,128)(2,1)S(1)} collective-permute-done((bf16[2,2,72,768]{3,2,1,0:T(8,128)(2,1)S(1)}, bf16[2,2,72,768]{3,2,1,0:T(8,128)(2,1)S(1)}, u32[]{:S(2)}, u32[]{:S(2)}) %collective-permute-start.7) | collective-permute-done | bytes 442400 | tf_op jit(solution)/shard_map/ppermute | solution.py:825
  94.8 8.4 %shard_map.248 = (bf16[768,768]{1,0:T(8,128)(2,1)}, bf16[768,768]{1,0:T(8,128)(2,1)}, bf16[768,768]{1,0:T(8,128)(2,1)}, bf16[1024,768]{1,0:T(8,128)(2,1)}, bf16[...) custom-call(s32[1]{0:T(128)} %bitcast.1.owner_ref, bf16[1024,768]{1,0:T(8,128)(2,1)} %inputs_ref.5, ...), custom_call_target="tpu_custom_call" | custom-call | tf_op jit(solution)/shard_map/pallas_call | solution.py:658
  103.2 17.3 %shard_map.249 = (bf16[1024,768]{1,0:T(8,128)(2,1)}, f32[6,2,1024]{2,1,0:T(2,128)}) custom-call(bf16[1024,768]{1,0:T(8,128)(2,1)} %get-tuple-element.57.query_ref, bf16[1024,768]{1,0:T(8,128)(2,1)} %get-tuple-element.58.key_ref, bf16[1024,768]{1,0:T(8,128)(2,1)} %get-tuple-element.59.value_ref, f32[6,2,256]{2,1,0:T(2,128)} %copy.40.refs_4_.near_ref), custom_call_target="tpu_custom_call" | custom-call | tf_op jit(solution)/shard_map/pallas_call | solution.py:526
  120.6 10.9 %shard_map.250 = (f32[1024,768]{1,0:T(8,128)}, bf16[1024,768]{1,0:T(8,128)(2,1)}, f32[2,1024]{1,0:T(2,128)}, bf16[1280,768]{1,0:T(8,128)(2,1)}) custom-call(bf16[1024,768]{1,0:T(8,128)(2,1)} %get-tuple-element.60.mixed_ref.out_ref, bf16[768,768]{1,0:T(8,128)(2,1)} %all-gather.2.cloned.1.call-done.merge_ref, bf16[1024,768]{1,0:T(8,128)(2,1)} %inputs_ref.5, ...), custom_call_target="tpu_custom_call" | custom-call | tf_op jit(solution)/shard_map/pallas_call | solution.py:702
  131.4 4.3 all-to-all-start
  136.8 20.7 %all-to-all-done.rows_ref = bf16[8,160,768]{2,1,0:T(8,128)(2,1)} async-done(((bf16[8,160,768]{2,1,0:T(8,128)(2,1)}), bf16[8,160,768]{2,1,0:T(8,128)(2,1)}, u32[]{:S(2)}, u32[]{:S(2)}) %all-to-all-start) | async-done | bytes 1966112 | tf_op jit(solution)/shard_map/all_to_all | solution.py:899
  157.5 18.8 %shard_map.252 = (bf16[1280,3072]{1,0:T(8,128)(2,1)}, bf16[1280,3072]{1,0:T(8,128)(2,1)}, bf16[4,768,768]{2,1,0:T(8,128)(2,1)}, bf16[1280,768]{1,0:T(8,128)(2,1)}) custom-call(s32[1]{0:T(128)} %bitcast.1.owner_ref, bf16[8,160,768]{2,1,0:T(8,128)(2,1)} %all-to-all-done.rows_ref, f32[1,1280]{1,0:T(1,128)} %reshape_squeeze.8.other_ref.refs_0_, ...), custom_call_target="tpu_custom_call" | custom-call | tf_op jit(solution)/shard_map/pallas_call | solution.py:180
  176.9 8.3 %shard_map.255 = bf16[8,240,768]{2,1,0:T(8,128)(2,1)} custom-call(s32[2,1024]{1,0:T(2,128)} %get-tuple-element.56.slots_ref, bf16[1024,768]{1,0:T(8,128)(2,1)} %get-tuple-element.73.rows_ref, bf16[1024,768]{1,0:T(8,128)(2,1)} %cot_ref.7, f32[1,1280]{1,0:T(1,128)} %reshape_squeeze.8.other_ref.refs_0_, f32[1,1280]{1,0:T(1,128)} %reshape_squeeze.9.refs_1_.other_ref), custom_call_target="tpu_custom_call" | custom-call | tf_op jit(solution)/shard_map/pallas_call | solution.py:81
  185.2 7.9 %all-to-all-start.4 = ((bf16[8,240,768]{2,1,0:T(8,128)(2,1)}), bf16[8,240,768]{2,1,0:T(8,128)(2,1)}, u32[]{:S(2)}, u32[]{:S(2)}) async-start(bf16[8,240,768]{2,1,0:T(8,128)(2,1)} %shard_map.255), calls=%async_computation.4 | async-start | bytes 5898240 | tf_op jit(solution)/shard_map/all_to_all | solution.py:899
  193.1 37.5 %shard_map.253 = (bf16[8,2,160,768]{3,2,1,0:T(8,128)(2,1)}, bf16[4,2304,768]{2,1,0:T(8,128)(2,1)}) custom-call(bf16[8,160,768]{2,1,0:T(8,128)(2,1)} %all-to-all-done.rows_ref, bf16[1280,768]{1,0:T(8,128)(2,1)} %get-tuple-element.67.grad_ref, bf16[1280,3072]{1,0:T(8,128)(2,1)} %get-tuple-element.68.act_ref, bf16[1280,3072]{1,0:T(8,128)(2,1)} %get-tuple-element.69.pre_ref, ...), custom_call_target="tpu_custom_call" | custom-call | tf_op jit(solution)/shard_map/pallas_call | solution.py:237
  230.6 20.3 %shard_map.256 = (bf16[1280,3072]{1,0:T(8,128)(2,1)}, bf16[1280,3072]{1,0:T(8,128)(2,1)}, bf16[4,2304,768]{2,1,0:T(8,128)(2,1)}, bf16[1280,768]{1,0:T(8,128)(2,1)}) custom-call(s32[1]{0:T(128)} %bitcast.1.owner_ref, bf16[8,240,768]{2,1,0:T(8,128)(2,1)} %all-to-all-done.4.rows_ref.refs_1_, ...), custom_call_target="tpu_custom_call", output_to_operand_aliasing={{2}: (7, {})} | custom-call | tf_op jit(solution)/shard_map/pallas_call | solution.py:180
  250.9 20.0 %shard_map.257 = (bf16[1280,3072]{1,0:T(8,128)(2,1)}, bf16[4,2304,768]{2,1,0:T(8,128)(2,1)}) custom-call(bf16[8,240,768]{2,1,0:T(8,128)(2,1)} %all-to-all-done.4.rows_ref.refs_1_, bf16[1280,768]{1,0:T(8,128)(2,1)} %get-tuple-element.76.grad_ref, bf16[1280,3072]{1,0:T(8,128)(2,1)} %get-tuple-element.77.pre_ref, ...), custom_call_target="tpu_custom_call", output_to_operand_aliasing={{1}: (4, {})} | custom-call | tf_op jit(solution)/shard_map/pallas_call | solution.py:268
  270.9 4.6 all-to-all-start.3
  275.6 22.0 %shard_map.258 = bf16[8,2,160,768]{3,2,1,0:T(8,128)(2,1)} custom-call(bf16[1280,3072]{1,0:T(8,128)(2,1)} %get-tuple-element.75.act_ref, bf16[1280,3072]{1,0:T(8,128)(2,1)} %get-tuple-element.79.low_ref, bf16[2,768,3072]{2,1,0:T(8,128)(2,1)} %up_ref.7, bf16[2,3072,768]{2,1,0:T(8,128)(2,1)} %down_ref.5), custom_call_target="tpu_custom_call" | custom-call | tf_op jit(solution)/shard_map/pallas_call | solution.py:306
  297.5 20.8 %all-to-all-done.3.made_ref.back_ref = bf16[8,2,160,768]{3,2,1,0:T(8,128)(2,1)} async-done(((bf16[8,2,160,768]{3,2,1,0:T(8,128)(2,1)}), bf16[8,2,160,768]{3,2,1,0:T(8,128)(2,1)}, u32[]{:S(2)}, u32[]{:S(2)}) %all-to-all-start.3) | async-done | bytes 3932192 | tf_op jit(solution)/shard_map/all_to_all | solution.py:899
  318.4 8.5 %all-to-all-start.5 = ((bf16[8,2,160,768]{3,2,1,0:T(8,128)(2,1)}), bf16[8,2,160,768]{3,2,1,0:T(8,128)(2,1)}, u32[]{:S(2)}, u32[]{:S(2)}) async-start(bf16[8,2,160,768]{3,2,1,0:T(8,128)(2,1)} %shard_map.258), calls=%async_computation.5 | async-start | bytes 7864320 | tf_op jit(solution)/shard_map/all_to_all | solution.py:899
  327.6 11.2 %shard_map.254 = (f32[1024,768]{1,0:T(8,128)}, f32[1024,128]{1,0:T(8,128)}, f32[1024,768]{1,0:T(8,128)}) custom-call(s32[2,1024]{1,0:T(2,128)} %get-tuple-element.56.slots_ref, f32[2,1024]{1,0:T(2,128)} %get-tuple-element.61.gates_ref, f32[1024,768]{1,0:T(8,128)} %get-tuple-element.62.resid_ref, bf16[1024,768]{1,0:T(8,128)(2,1)} %cot_ref.7, ...), custom_call_target="tpu_custom_call" | custom-call | tf_op jit(solution)/shard_map/pallas_call | solution.py:356
  338.8 30.8 %all-to-all-done.5.made_ref.back_ref = bf16[8,2,160,768]{3,2,1,0:T(8,128)(2,1)} async-done(((bf16[8,2,160,768]{3,2,1,0:T(8,128)(2,1)}), bf16[8,2,160,768]{3,2,1,0:T(8,128)(2,1)}, u32[]{:S(2)}, u32[]{:S(2)}) %all-to-all-start.5) | async-done | bytes 3932192 | tf_op jit(solution)/shard_map/all_to_all | solution.py:899
  369.6 9.4 %shard_map.259 = (bf16[1024,768]{1,0:T(8,128)(2,1)}, bf16[1024,128]{1,0:T(8,128)(2,1)}) custom-call(s32[2,1024]{1,0:T(2,128)} %get-tuple-element.56.slots_ref, s32[2,1024]{1,0:T(2,128)} %bitcast.56, f32[2,1024]{1,0:T(2,128)} %get-tuple-element.61.gates_ref, f32[1024,768]{1,0:T(8,128)} %get-tuple-element.71.result_ref, ...), custom_call_target="tpu_custom_call" | custom-call | tf_op jit(solution)/shard_map/pallas_call | solution.py:397
  379.0 10.6 %shard_map.260 = (f32[1024,768]{1,0:T(8,128)}, bf16[1024,768]{1,0:T(8,128)(2,1)}, bf16[1024,768]{1,0:T(8,128)(2,1)}, f32[1,768]{1,0:T(1,128)}) custom-call(s32[2,1024]{1,0:T(2,128)} %get-tuple-element.56.slots_ref, bf16[1024,128]{1,0:T(8,128)(2,1)} %get-tuple-element.81.logit_ref, bf16[128,768]{1,0:T(8,128)(2,1)} %pad.35.router_ref, ...), custom_call_target="tpu_custom_call" | custom-call | tf_op jit(solution)/shard_map/pallas_call | solution.py:433
  389.5 35.6 %shard_map.261 = (bf16[3,1024,768]{2,1,0:T(8,128)(2,1)}, f32[6,4,256]{2,1,0:T(4,128)}) custom-call(bf16[1024,768]{1,0:T(8,128)(2,1)} %get-tuple-element.57.query_ref, bf16[1024,768]{1,0:T(8,128)(2,1)} %get-tuple-element.58.key_ref, bf16[1024,768]{1,0:T(8,128)(2,1)} %get-tuple-element.59.value_ref, bf16[1024,768]{1,0:T(8,128)(2,1)} %get-tuple-element.83.grad_ref, ...), custom_call_target="tpu_custom_call" | custom-call | tf_op jit(solution)/shard_map/pallas_call | solution.py:607
  425.2 11.4 %shard_map.263 = bf16[4,768,768]{2,1,0:T(8,128)(2,1)} custom-call(bf16[1024,768]{1,0:T(8,128)(2,1)} %get-tuple-element.91.left_ref, bf16[1024,768]{1,0:T(8,128)(2,1)} %get-tuple-element.60.mixed_ref.out_ref, bf16[3,1024,768]{2,1,0:T(8,128)(2,1)} %get-tuple-element.85.heads_ref, bf16[1024,768]{1,0:T(8,128)(2,1)} %get-tuple-element.92.branch_ref), custom_call_target="tpu_custom_call" | custom-call | tf_op jit(solution)/shard_map/pallas_call | solution.py:764
  443.8 9.9 %shard_map.262 = (f32[1024,768]{1,0:T(8,128)}, f32[1,768]{1,0:T(1,128)}) custom-call(bf16[3,1024,768]{2,1,0:T(8,128)(2,1)} %get-tuple-element.85.heads_ref, bf16[768,768]{1,0:T(8,128)(2,1)} %get-tuple-element.86.query_ref, bf16[768,768]{1,0:T(8,128)(2,1)} %get-tuple-element.87.key_ref, bf16[768,768]{1,0:T(8,128)(2,1)} %get-tuple-element.88.value_ref, ...), custom_call_target="tpu_custom_call" | custom-call | tf_op jit(solution)/shard_map/pallas_call | solution.py:731
  463.0 12.2 %collective-permute-done.13 = bf16[4,96,768]{2,1,0:T(8,128)(2,1)} collective-permute-done((bf16[4,96,768]{2,1,0:T(8,128)(2,1)S(1)}, bf16[4,96,768]{2,1,0:T(8,128)(2,1)}, u32[]{:S(2)}, u32[]{:S(2)}) %collective-permute-start.13) | collective-permute-done | bytes 589856 | tf_op jit(solution)/shard_map/ppermute | solution.py:825
  492.9 8.7 %collective-permute-done.15 = bf16[104,768]{1,0:T(8,128)(2,1)S(1)} collective-permute-done((bf16[104,768]{1,0:T(8,128)(2,1)S(1)}, bf16[104,768]{1,0:T(8,128)(2,1)S(1)}, u32[]{:S(2)}, u32[]{:S(2)}) %collective-permute-start.15) | collective-permute-done | bytes 159776 | tf_op jit(solution)/shard_map/ppermute | solution.py:830
  501.6 15.5 %collective-permute-done.16 = bf16[104,768]{1,0:T(8,128)(2,1)S(1)} collective-permute-done((bf16[104,768]{1,0:T(8,128)(2,1)S(1)}, bf16[104,768]{1,0:T(8,128)(2,1)S(1)}, u32[]{:S(2)}, u32[]{:S(2)}) %collective-permute-start.16) | collective-permute-done | bytes 159776 | tf_op jit(solution)/shard_map/ppermute | solution.py:830
  540.7 6.1 %shard_map.265 = (f32[1536,768]{1,0:T(8,128)}, f32[1536,768]{1,0:T(8,128)}) custom-call(bf16[2304,768]{1,0:T(8,128)(2,1)} %reduce-scatter.3.cloned.1.call-done.rows_ref, f32[1536,768]{1,0:T(8,128)} %shard_map.264.into_ref), custom_call_target="tpu_custom_call", output_to_operand_aliasing={{1}: (1, {})} | custom-call | tf_op jit(solution)/shard_map/pallas_call | solution.py:808
  (164 shorter events, 80.1 us)
Async XLA Ops:
  10.8 18.8 %collective-permute-start = (bf16[96,768]{1,0:T(8,128)(2,1)S(1)}, bf16[96,768]{1,0:T(8,128)(2,1)S(1)}, u32[]{:S(2)}, u32[]{:S(2)}) collective-permute-start(bf16[96,768]{1,0:T(8,128)(2,1)S(1)} %concatenate.74), channel_id=1, source_target_pairs={{0,1},{1,2},{2,3},{3,0},{4,5},{5,6},{6,7},{7,4},{8,9},{9,10},{10,1... | collective-permute-start | bytes 442376 | tf_op jit(solution)/shard_map/ppermute | solution.py:830
  12.2 26.4 %collective-permute-start.1 = (bf16[96,768]{1,0:T(8,128)(2,1)S(1)}, bf16[96,768]{1,0:T(8,128)(2,1)S(1)}, u32[]{:S(2)}, u32[]{:S(2)}) collective-permute-start(bf16[96,768]{1,0:T(8,128)(2,1)S(1)} %concatenate.74), channel_id=1, source_target_pairs={{0,2},{1,3},{2,0},{3,1},{4,6},{5,7},{6,4},{7,5},{8,10},{9,11},{10,... | collective-permute-start | bytes 442376 | tf_op jit(solution)/shard_map/ppermute | solution.py:830
  13.3 25.4 %collective-permute-start.2 = (bf16[96,768]{1,0:T(8,128)(2,1)S(1)}, bf16[96,768]{1,0:T(8,128)(2,1)S(1)}, u32[]{:S(2)}, u32[]{:S(2)}) collective-permute-start(bf16[96,768]{1,0:T(8,128)(2,1)S(1)} %concatenate.74), channel_id=1, source_target_pairs={{0,3},{1,0},{2,1},{3,2},{4,7},{5,4},{6,5},{7,6},{8,11},{9,8},{10,9... | collective-permute-start | bytes 442376 | tf_op jit(solution)/shard_map/ppermute | solution.py:830
  24.3 9.3 %all-to-all-start.1 = ((f32[8,1,320]{2,1,0:T(1,128)}), f32[8,1,320]{2,1,0:T(1,128)S(1)}, u32[]{:S(2)}, u32[]{:S(2)}) async-start(f32[8,1,320]{2,1,0:T(1,128)} %get-tuple-element.65), calls=%async_computation.1 | async-start | bytes 24576 | tf_op jit(solution)/shard_map/all_to_all | solution.py:899
  33.5 97.9 %all-to-all-start.2 = ((bf16[8,240,768]{2,1,0:T(8,128)(2,1)}), bf16[8,240,768]{2,1,0:T(8,128)(2,1)}, u32[]{:S(2)}, u32[]{:S(2)}) async-start(bf16[8,240,768]{2,1,0:T(8,128)(2,1)} %get-tuple-element.66), calls=%async_computation.2 | async-start | bytes 5898240 | tf_op jit(solution)/shard_map/all_to_all | solution.py:899
  38.6 82.0 %all-gather.2.cloned.1.call-start = ((), (), s32[]{:S(2)}) async-start(), calls=%async_computation.8 | async-start | bytes 1474560 | tf_op jit(solution)/shard_map/all_gather | solution.py:964
  38.7 38.5 %collective-permute-start.6 = (bf16[1,2,72,768]{3,2,1,0:T(8,128)(2,1)S(1)}, bf16[1,2,72,768]{3,2,1,0:T(8,128)(2,1)S(1)}, u32[]{:S(2)}, u32[]{:S(2)}) collective-permute-start(bf16[1,2,72,768]{3,2,1,0:T(8,128)(2,1)S(1)} %get-tuple-element.115), channel_id=1, source_target_pairs={{0,16},{4,20},{8,24},{12,28},{16,0},{20,4},{24,8},{28,12},{1,17},{... | collective-permute-start | bytes 663560 | tf_op jit(solution)/shard_map/ppermute | solution.py:825
  40.1 38.9 %collective-permute-start.3 = (bf16[1,2,72,768]{3,2,1,0:T(8,128)(2,1)S(1)}, bf16[1,2,72,768]{3,2,1,0:T(8,128)(2,1)S(1)}, u32[]{:S(2)}, u32[]{:S(2)}) collective-permute-start(bf16[1,2,72,768]{3,2,1,0:T(8,128)(2,1)S(1)} %get-tuple-element.116), channel_id=1, source_target_pairs={{0,8},{4,12},{8,0},{12,4},{16,24},{20,28},{24,16},{28,20},{1,9},{5... | collective-permute-start | bytes 663560 | tf_op jit(solution)/shard_map/ppermute | solution.py:825
  77.2 11.3 %collective-permute-start.7 = (bf16[2,2,72,768]{3,2,1,0:T(8,128)(2,1)S(1)}, bf16[2,2,72,768]{3,2,1,0:T(8,128)(2,1)S(1)}, u32[]{:S(2)}, u32[]{:S(2)}) collective-permute-start(bf16[2,2,72,768]{3,2,1,0:T(8,128)(2,1)S(1)} %pad_maximum_fusion.4), channel_id=1, source_target_pairs={{0,8},{4,12},{8,0},{12,4},{16,24},{20,28},{24,16},{28,20},{1,9},{5... | collective-permute-start | bytes 1327112 | tf_op jit(solution)/shard_map/ppermute | solution.py:825
  79.1 11.2 %collective-permute-start.4 = (bf16[2,2,72,768]{3,2,1,0:T(8,128)(2,1)S(1)}, bf16[2,2,72,768]{3,2,1,0:T(8,128)(2,1)S(1)}, u32[]{:S(2)}, u32[]{:S(2)}) collective-permute-start(bf16[2,2,72,768]{3,2,1,0:T(8,128)(2,1)S(1)} %pad_maximum_fusion.3), channel_id=1, source_target_pairs={{0,16},{4,20},{8,24},{12,28},{16,0},{20,4},{24,8},{28,12},{1,17},{... | collective-permute-start | bytes 1327112 | tf_op jit(solution)/shard_map/ppermute | solution.py:825
  88.6 6.1 %collective-permute-start.8 = (bf16[4,2,72,768]{3,2,1,0:T(8,128)(2,1)S(1)}, bf16[4,2,72,768]{3,2,1,0:T(8,128)(2,1)}, u32[]{:S(2)}, u32[]{:S(2)}) collective-permute-start(bf16[4,2,72,768]{3,2,1,0:T(8,128)(2,1)S(1)} %pad_maximum_fusion.1.refs_2_), channel_id=1, source_target_pairs={{0,4},{4,0},{8,12},{12,8},{16,20},{20,16},{24,28},{28,24},{1,5},{5... | collective-permute-start | bytes 2654216 | tf_op jit(solution)/shard_map/ppermute | solution.py:825
  90.4 4.4 collective-permute-start.5
  131.4 26.0 %all-to-all-start = ((bf16[8,160,768]{2,1,0:T(8,128)(2,1)}), bf16[8,160,768]{2,1,0:T(8,128)(2,1)}, u32[]{:S(2)}, u32[]{:S(2)}) async-start(bf16[8,160,768]{2,1,0:T(8,128)(2,1)} %bitcast.52), calls=%async_computation | async-start | bytes 3932160 | tf_op jit(solution)/shard_map/all_to_all | solution.py:899
  135.7 402.3 %reduce-scatter.5.cloned.1.call-start = ((), (), s32[]{:S(2)}) async-start(), calls=%async_computation.10 | async-start | bytes 5898240 | tf_op jit(solution)/shard_map/reduce_scatter | solution.py:895
  185.2 45.4 %all-to-all-start.4 = ((bf16[8,240,768]{2,1,0:T(8,128)(2,1)}), bf16[8,240,768]{2,1,0:T(8,128)(2,1)}, u32[]{:S(2)}, u32[]{:S(2)}) async-start(bf16[8,240,768]{2,1,0:T(8,128)(2,1)} %shard_map.255), calls=%async_computation.4 | async-start | bytes 5898240 | tf_op jit(solution)/shard_map/all_to_all | solution.py:899
  193.1 347.6 %reduce-scatter.3.cloned.1.call-start = ((), (), s32[]{:S(2)}) async-start(), calls=%async_computation.9 | async-start | bytes 17694720 | tf_op jit(solution)/shard_map/reduce_scatter | solution.py:895
  270.9 47.4 %all-to-all-start.3 = ((bf16[8,2,160,768]{3,2,1,0:T(8,128)(2,1)}), bf16[8,2,160,768]{3,2,1,0:T(8,128)(2,1)}, u32[]{:S(2)}, u32[]{:S(2)}) async-start(bf16[8,2,160,768]{3,2,1,0:T(8,128)(2,1)} %get-tuple-element.70), calls=%async_computation.3 | async-start | bytes 7864320 | tf_op jit(solution)/shard_map/all_to_all | solution.py:899
  318.4 51.2 %all-to-all-start.5 = ((bf16[8,2,160,768]{3,2,1,0:T(8,128)(2,1)}), bf16[8,2,160,768]{3,2,1,0:T(8,128)(2,1)}, u32[]{:S(2)}, u32[]{:S(2)}) async-start(bf16[8,2,160,768]{3,2,1,0:T(8,128)(2,1)} %shard_map.258), calls=%async_computation.5 | async-start | bytes 7864320 | tf_op jit(solution)/shard_map/all_to_all | solution.py:899
  439.8 17.4 %collective-permute-start.9 = (bf16[4,384,768]{2,1,0:T(8,128)(2,1)}, bf16[4,384,768]{2,1,0:T(8,128)(2,1)}, u32[]{:S(2)}, u32[]{:S(2)}) collective-permute-start(bf16[4,384,768]{2,1,0:T(8,128)(2,1)} %constant_dynamic-slice_fusion.3), channel_id=1, source_target_pairs={{0,4},{4,0},{8,12},{12,8},{16,20},{20,16},{24,28},{28,24},{1,5},{5... | collective-permute-start | bytes 7077896 | tf_op jit(solution)/shard_map/ppermute | solution.py:825
  455.7 1.5 collective-permute-start.12
  460.4 14.8 %collective-permute-start.13 = (bf16[4,96,768]{2,1,0:T(8,128)(2,1)S(1)}, bf16[4,96,768]{2,1,0:T(8,128)(2,1)}, u32[]{:S(2)}, u32[]{:S(2)}) collective-permute-start(bf16[4,96,768]{2,1,0:T(8,128)(2,1)S(1)} %fusion.1), channel_id=1, source_target_pairs={{0,16},{4,20},{8,24},{12,28},{16,0},{20,4},{24,8},{28,12},{1,17},{... | collective-permute-start | bytes 1769480 | tf_op jit(solution)/shard_map/ppermute | solution.py:825
  462.7 17.0 %collective-permute-start.10 = (bf16[4,112,768]{2,1,0:T(8,128)(2,1)}, bf16[4,112,768]{2,1,0:T(8,128)(2,1)}, u32[]{:S(2)}, u32[]{:S(2)}) collective-permute-start(bf16[4,112,768]{2,1,0:T(8,128)(2,1)} %constant_dynamic-slice_fusion.2), channel_id=1, source_target_pairs={{0,8},{4,12},{8,0},{12,4},{16,24},{20,28},{24,16},{28,20},{1,9},{5... | collective-permute-start | bytes 2064392 | tf_op jit(solution)/shard_map/ppermute | solution.py:825
  476.6 9.3 %collective-permute-start.14 = (bf16[4,48,768]{2,1,0:T(8,128)(2,1)S(1)}, bf16[4,48,768]{2,1,0:T(8,128)(2,1)S(1)}, u32[]{:S(2)}, u32[]{:S(2)}) collective-permute-start(bf16[4,48,768]{2,1,0:T(8,128)(2,1)S(1)} %constant_dynamic-slice_fusion), channel_id=1, source_target_pairs={{0,8},{4,12},{8,0},{12,4},{16,24},{20,28},{24,16},{28,20},{1,9},{5... | collective-permute-start | bytes 884744 | tf_op jit(solution)/shard_map/ppermute | solution.py:825
  480.9 7.8 %collective-permute-start.11 = (bf16[4,56,768]{2,1,0:T(8,128)(2,1)S(1)}, bf16[4,56,768]{2,1,0:T(8,128)(2,1)S(1)}, u32[]{:S(2)}, u32[]{:S(2)}) collective-permute-start(bf16[4,56,768]{2,1,0:T(8,128)(2,1)S(1)} %constant_dynamic-slice_fusion.1), channel_id=1, source_target_pairs={{0,16},{4,20},{8,24},{12,28},{16,0},{20,4},{24,8},{28,12},{1,17},{... | collective-permute-start | bytes 1032200 | tf_op jit(solution)/shard_map/ppermute | solution.py:825
  488.9 12.8 %collective-permute-start.15 = (bf16[104,768]{1,0:T(8,128)(2,1)S(1)}, bf16[104,768]{1,0:T(8,128)(2,1)S(1)}, u32[]{:S(2)}, u32[]{:S(2)}) collective-permute-start(bf16[104,768]{1,0:T(8,128)(2,1)S(1)} %get-tuple-element.112), channel_id=1, source_target_pairs={{0,1},{1,2},{2,3},{3,0},{4,5},{5,6},{6,7},{7,4},{8,9},{9,10},{10,1... | collective-permute-start | bytes 479240 | tf_op jit(solution)/shard_map/ppermute | solution.py:830
  489.1 28.1 %collective-permute-start.16 = (bf16[104,768]{1,0:T(8,128)(2,1)S(1)}, bf16[104,768]{1,0:T(8,128)(2,1)S(1)}, u32[]{:S(2)}, u32[]{:S(2)}) collective-permute-start(bf16[104,768]{1,0:T(8,128)(2,1)S(1)} %get-tuple-element.113), channel_id=1, source_target_pairs={{0,2},{1,3},{2,0},{3,1},{4,6},{5,7},{6,4},{7,5},{8,10},{9,11},{10,... | collective-permute-start | bytes 479240 | tf_op jit(solution)/shard_map/ppermute | solution.py:830
  492.9 25.5 %collective-permute-start.17 = (bf16[104,768]{1,0:T(8,128)(2,1)S(1)}, bf16[104,768]{1,0:T(8,128)(2,1)S(1)}, u32[]{:S(2)}, u32[]{:S(2)}) collective-permute-start(bf16[104,768]{1,0:T(8,128)(2,1)S(1)} %get-tuple-element.114), channel_id=1, source_target_pairs={{0,3},{1,0},{2,1},{3,2},{4,7},{5,4},{6,5},{7,6},{8,11},{9,8},{10,9... | collective-permute-start | bytes 479240 | tf_op jit(solution)/shard_map/ppermute | solution.py:830
  518.6 3.3 collective-permute-start.20
  520.1 3.6 collective-permute-start.18
  521.9 4.9 collective-permute-start.21
  523.8 4.6 collective-permute-start.19
  528.5 5.5 collective-permute-start.22
  (14 other events, 150.3 us)
Sparse Core Ops, SparseCore 0:
  41.5 27.9 all-gather.1
  176.4 85.4 reduce-scatter.4
  271.0 249.2 reduce-scatter.2

commit v8 on v7

--- a/solution.py
+++ b/solution.py
@@ -127,8 +127,9 @@
     return half + v * half * (1.0 - half) * (np.float32(6.0 * 0.044715) * c * square + 2.0 * c)
 
 
-def arrived_spec(arrived):
-    return pl.BlockSpec(arrived.shape, lambda i: (0, 0, 0))
+def arrived_spec(arrived, used=None):
+    owners, count, width = arrived.shape
+    return pl.BlockSpec((owners, used or count, width), lambda i: (0, 0, 0))
 
 
 def first_kernel(owner_ref, rows_ref, other_ref, router_ref, up_ref, *refs, index, local_count, capacity, pieces):
@@ -182,12 +183,12 @@
         grid=(shards,),
         in_specs=[
             pl.BlockSpec(memory_space=pltpu.SMEM),
-            arrived_spec(rows_in),
+            arrived_spec(rows_in, capacity),
             pl.BlockSpec((1, rows), lambda i: (0, 0)),
             pl.BlockSpec(router.shape, lambda i: (0, 0)),
             pl.BlockSpec((1, width, tile), lambda i: (index, 0, i)),
         ]
-        + [arrived_spec(cot) for cot in cots]
+        + [arrived_spec(cot, low + size) for cot, (_, low, size) in zip(cots, pieces)]
         + [pl.BlockSpec(memory_space=pl.ANY)] * (into is not None),
         out_specs=[column, column, pl.BlockSpec((1, tile, width), lambda i: (i, place, 0)), fixed],
         out_shape=[jax.ShapeDtypeStruct((rows, hidden), jnp.bfloat16)] * 2 + [grad_shape, jax.ShapeDtypeStruct((rows, width), jnp.bfloat16)],
@@ -237,7 +238,7 @@
     return pl.pallas_call(
         second_kernel,
         grid=(shards,),
-        in_specs=[arrived_spec(rows_in), fixed, column, column, pl.BlockSpec((1, width, tile), lambda i: (index, 0, i)), pl.BlockSpec((1, tile, width), lambda i: (index, i, 0))]
+        in_specs=[arrived_spec(rows_in, rows // rows_in.shape[0]), fixed, column, column, pl.BlockSpec((1, width, tile), lambda i: (index, 0, i)), pl.BlockSpec((1, tile, width), lambda i: (index, i, 0))]
         + [pl.BlockSpec(memory_space=pl.ANY)] * len(after),
         out_specs=[pl.BlockSpec(made_shape, lambda i: (0, 0, 0, 0)), pl.BlockSpec((1, width, tile), lambda i: (i, 0, 0))],
         out_shape=[jax.ShapeDtypeStruct(made_shape, jnp.bfloat16), jax.ShapeDtypeStruct((shards, wide, tile), jnp.bfloat16)],
@@ -268,7 +269,7 @@
     return pl.pallas_call(
         slope_kernel,
         grid=(shards,),
-        in_specs=[arrived_spec(rows_in), fixed, column, pl.BlockSpec((1, tile, width), lambda i: (index, i, 0)), pl.BlockSpec(memory_space=pl.ANY)],
+        in_specs=[arrived_spec(rows_in, rows // rows_in.shape[0]), fixed, column, pl.BlockSpec((1, tile, width), lambda i: (index, i, 0)), pl.BlockSpec(memory_space=pl.ANY)],
         out_specs=[column, pl.BlockSpec((1, width, tile), lambda i: (i, place, 0))],
         out_shape=[jax.ShapeDtypeStruct((rows, hidden), jnp.bfloat16), jax.ShapeDtypeStruct(into.shape, into.dtype)],
         input_output_aliases={4: 1},
@@ -650,7 +651,7 @@
         out_ref[...] = dot_nn(low, weight_ref[...]).astype(jnp.bfloat16)
 
 
-def project(owner, inputs, gain, pieces, eps, after=(), block=256):
+def project(owner, inputs, gain, pieces, eps, after=(), block=512):
     tokens, width = inputs.shape
     rows = pl.BlockSpec((block, width), lambda i: (i, 0))
     whole = lambda shape: pl.BlockSpec(shape, lambda i: (0,) * len(shape))
@@ -667,7 +668,7 @@
 
 def settle_kernel(mixed_ref, merge_ref, inputs_ref, gain_ref, router_ref, routes_ref, slots_ref, resid_ref, low_ref, gates_ref, out_ref, held, *, eps, settling):
     step = pl.program_id(0)
-    block = mixed_ref.shape[0]
+    block, picking = mixed_ref.shape[0], out_ref.shape[0]
     @pl.when(step < settling)
     def _():
         resid = inputs_ref[...].astype(jnp.float32) + dot_nn(mixed_ref[...], merge_ref[...])
@@ -687,13 +688,14 @@
     @pl.when(step >= settling)
     def _():
         tokens = held.shape[0]
-        slot = lax.broadcasted_iota(jnp.int32, (block, tokens), 0) + (step - settling) * block
+        slot = lax.broadcasted_iota(jnp.int32, (picking, tokens), 0) + (step - settling) * picking
         hot = jnp.where((slot == slots_ref[0:1, :]) | (slot == slots_ref[1:2, :]), 1.0, 0.0)
         out_ref[...] = dot_nn(hot.astype(jnp.bfloat16), held[...]).astype(out_ref.dtype)
 
 
-def settle(mixed, merge, inputs, gain, router, routes, slots, count, eps, block=256):
+def settle(mixed, merge, inputs, gain, router, routes, slots, count, eps, block=512):
     tokens, width = inputs.shape
+    picking = count // 4
     settling = tokens // block
     early = lambda i: jnp.minimum(i, settling - 1)
     rows = pl.BlockSpec((block, width), lambda i: (early(i), 0))
@@ -701,9 +703,9 @@
     small = pl.BlockSpec((2, block), lambda i: (0, early(i)))
     return pl.pallas_call(
         partial(settle_kernel, eps=eps, settling=settling),
-        grid=(settling + count // block,),
+        grid=(settling + 4,),
         in_specs=[rows, whole(merge.shape), rows, whole(gain.shape), whole(router.shape), small, whole(slots.shape)],
-        out_specs=[rows, rows, small, pl.BlockSpec((block, width), lambda i: (jnp.maximum(i - settling, 0), 0))],
+        out_specs=[rows, rows, small, pl.BlockSpec((picking, width), lambda i: (jnp.maximum(i - settling, 0), 0))],
         out_shape=[jax.ShapeDtypeStruct((tokens, width), jnp.float32), jax.ShapeDtypeStruct((tokens, width), jnp.bfloat16), jax.ShapeDtypeStruct((2, tokens), jnp.float32), jax.ShapeDtypeStruct((count, width), jnp.bfloat16)],
         scratch_shapes=[pltpu.VMEM((tokens, width), jnp.bfloat16)],
         compiler_params=pltpu.CompilerParams(vmem_limit_bytes=62 << 20),
@@ -814,6 +816,40 @@
         input_output_aliases={1: 1},
         compiler_params=pltpu.CompilerParams(vmem_limit_bytes=62 << 20),
     )(rows, into)
+
+
+def smalls_kernel(small_ref, near_ref, gain_one_ref, gain_two_ref, router_ref, table_ref, *, part, heads, router_at):
+    shards, _, width = small_ref.shape
+    group = table_ref.shape[1]
+    lanes = -(-part // 128) * 128
+    row = lax.broadcasted_iota(jnp.int32, (lanes, width), 0)
+    column = lax.broadcasted_iota(jnp.int32, (lanes, width), 1)
+    wide = None
+    for shard in range(shards):
+        place = jnp.where((column == row + shard * part) & (row < part), 1.0, 0.0).astype(jnp.bfloat16)
+        rows = dot_nn(small_ref[shard][:, :lanes], place)
+        wide = rows if wide is None else wide + rows
+        near = dot_nn(small_ref[shard][:8, :128], near_ref[...])
+        for head in range(heads):
+            at = shard * heads + head
+            table_ref[at // group, at % group:at % group + 1, :] = near[2 + head:3 + head, :]
+    gain_one_ref[...] = wide[0:1]
+    gain_two_ref[...] = wide[1:2]
+    router_ref[...] = wide[router_at:router_at + router_ref.shape[0]].astype(jnp.bfloat16)
+
+
+def spread_smalls(small, near, part, heads, group, experts, router_at):
+    shards, _, width = small.shape
+    f32 = jnp.float32
+    return pl.pallas_call(
+        partial(smalls_kernel, part=part, heads=heads, router_at=router_at),
+        out_shape=[
+            jax.ShapeDtypeStruct((1, width), f32),
+            jax.ShapeDtypeStruct((1, width), f32),
+            jax.ShapeDtypeStruct((experts, width), jnp.bfloat16),
+            jax.ShapeDtypeStruct((shards * heads // group, group, near.shape[1]), f32),
+        ],
+    )(small, near)
 
 
 OWNER = "expert"
@@ -963,11 +999,15 @@
         pieces += [held, exchange(held, bits[0])]
     merge_full = lax.all_gather(merge_weight, LINE, axis=0, tiled=True)
 
-    gain_one = small_full[:, 0, :part].reshape(1, width).astype(f32)
-    gain_two = small_full[:, 1, :part].reshape(1, width).astype(f32)
-    table_full = small_full[:, 2 : 2 + local_heads, :BUCKETS].reshape(heads, BUCKETS).astype(f32)
-    router_full = small_full[:, router_at : router_at + experts, :part]
-    router_full = router_full.transpose(1, 0, 2).reshape(experts, width)
+    block = 256
+    hot = bucket_hot(tokens)
+    assert hot[block:, -1].all()
+    near_hot = np.zeros((128, block), np.float32)
+    near_hot[:BUCKETS] = (hot[:block] - hot[-1:]).T
+    group = 128 // size
+    gain_one, gain_two, router_full, near = spread_smalls(
+        small_full, jnp.asarray(near_hot, bf16), part, local_heads, group, experts, router_at
+    )
 
     routes_line = routes.T
     slots, routes_float = find_slots(routes_line, experts, local_count, owners, capacity)
@@ -977,13 +1017,6 @@
     other = share_rows(other).reshape(owners, local_count, capacity)
 
     owner = me.astype(jnp.int32).reshape(1)
-    block = 256
-    hot = bucket_hot(tokens)
-    assert hot[block:, -1].all()
-    near_hot = jnp.asarray((hot[:block] - hot[-1:]).T, dtype=f32)
-    group = 128 // size
-    near = jnp.dot(table_full, near_hot, precision=lax.Precision.HIGHEST)
-    near = near.reshape(heads // group, group, block)
     query_full, key_full, value_full, low_one, queries, keys, values = project(
         owner, inputs, gain_one, pieces, epsilon, after=(near, router_full)
     )

time: 561 us -> 558 us (level)
  no operation moved by 1% of the time
where the time goes in v8:
time: 558 us; the launch traced here: 550 us
  Pallas kernels  269 us (48%)
  waiting for transfers between devices  176 us (32%)
  starting transfers between devices  66.4 us (12%)
  between operations  14.4 us (3%)
  local copies, waits for them, and re-layouts  14.1 us (3%)
  other arithmetic  9.98 us (2%)
    all_to_all x6, waiting for transfers between devices, share_rows(): return lax.all_to_all(rows, OWNER, 0, 0, tiled=True)  76.3 us
    ppermute x17, waiting for transfers between devices, exchange(): return lax.ppermute(rows, OWNER, [(i, i ^ bit) for i in range(count)])  74 us
    pallas_call x2, Pallas kernels, expert_first(): pl.pallas_call(partial(first_kernel, index=index, local_count=local_count...  38.4 us
    pallas_call x1, Pallas kernels, expert_second(): pl.pallas_call(second_kernel, grid=(shards,), in_specs=[arrived_spec(rows...  37.6 us
    pallas_call x1, Pallas kernels, attend_back(): pl.pallas_call(partial(attend_back_kernel, block=block, size=size, scale=...  35.6 us
    all_to_all x6, starting transfers between devices, share_rows(): return lax.all_to_all(rows, OWNER, 0, 0, tiled=True)  35.6 us
    ppermute x6, waiting for transfers between devices, shift(): lax.ppermute(rows, LINE, [(i, (i + step) % count) for i in range(count)])  25.6 us
    ppermute x17, starting transfers between devices, exchange(): return lax.ppermute(rows, OWNER, [(i, i ^ bit) for i in range(count)])  22.9 us
  transfers between devices with their start and end apart: 32, of which 19 were waited for; matrix products, arithmetic and copies ran while one was open for 4% of the time, Pallas kernels for 44%

profile of v8, /device:TPU:9, one launch (start us, length us, event | category | flops | bytes accessed | tf_op | source)
XLA Modules:
  0.0 550.4 jit_solution(10562702427283368657)
XLA Ops:
  16.3 8.0 %shard_map.252 = (bf16[8,240,768]{2,1,0:T(8,128)(2,1)}, f32[8,1,320]{2,1,0:T(1,128)}) custom-call(s32[2,1024]{1,0:T(2,128)} %get-tuple-element.60.slots_ref, f32[2,1024]{1,0:T(2,128)} %get-tuple-element.72.routes_ref, bf16[1024,768]{1,0:T(8,128)(2,1)} %cot_ref.7), custom_call_target="tpu_custom_call" | custom-call | tf_op jit(solution)/shard_map/pallas_call | solution.py:108
  24.3 5.2 all-to-all-start.1
  29.6 3.9 all-to-all-done.1
  33.5 5.0 all-to-all-start.2
  41.3 35.8 %collective-permute-done.6 = bf16[1,2,72,768]{3,2,1,0:T(8,128)(2,1)S(1)} collective-permute-done((bf16[1,2,72,768]{3,2,1,0:T(8,128)(2,1)S(1)}, bf16[1,2,72,768]{3,2,1,0:T(8,128)(2,1)S(1)}, u32[]{:S(2)}, u32[]{:S(2)}) %collective-permute-start.6) | collective-permute-done | bytes 221216 | tf_op jit(solution)/shard_map/ppermute | solution.py:861
  79.2 9.3 %collective-permute-done.7 = bf16[2,2,72,768]{3,2,1,0:T(8,128)(2,1)S(1)} collective-permute-done((bf16[2,2,72,768]{3,2,1,0:T(8,128)(2,1)S(1)}, bf16[2,2,72,768]{3,2,1,0:T(8,128)(2,1)S(1)}, u32[]{:S(2)}, u32[]{:S(2)}) %collective-permute-start.7) | collective-permute-done | bytes 442400 | tf_op jit(solution)/shard_map/ppermute | solution.py:861
  94.3 7.9 %shard_map.249 = (bf16[768,768]{1,0:T(8,128)(2,1)}, bf16[768,768]{1,0:T(8,128)(2,1)}, bf16[768,768]{1,0:T(8,128)(2,1)}, bf16[1024,768]{1,0:T(8,128)(2,1)}, bf16[...) custom-call(s32[1]{0:T(128)} %bitcast.1.owner_ref, bf16[1024,768]{1,0:T(8,128)(2,1)} %inputs_ref.5, ...), custom_call_target="tpu_custom_call" | custom-call | tf_op jit(solution)/shard_map/pallas_call | solution.py:659
  102.2 17.3 %shard_map.250 = (bf16[1024,768]{1,0:T(8,128)(2,1)}, f32[6,2,1024]{2,1,0:T(2,128)}) custom-call(bf16[1024,768]{1,0:T(8,128)(2,1)} %get-tuple-element.64.query_ref, bf16[1024,768]{1,0:T(8,128)(2,1)} %get-tuple-element.65.key_ref, bf16[1024,768]{1,0:T(8,128)(2,1)} %get-tuple-element.66.value_ref, f32[6,2,256]{2,1,0:T(2,128)} %get-tuple-element.62.refs_4_.near_ref), custom_call_target="tpu_custom_call" | custom-call | tf_op jit(solution)/shard_map/pallas_call | solution.py:527
  119.5 10.0 %shard_map.251 = (f32[1024,768]{1,0:T(8,128)}, bf16[1024,768]{1,0:T(8,128)(2,1)}, f32[2,1024]{1,0:T(2,128)}, bf16[1280,768]{1,0:T(8,128)(2,1)}) custom-call(bf16[1024,768]{1,0:T(8,128)(2,1)} %get-tuple-element.67.mixed_ref.out_ref, bf16[768,768]{1,0:T(8,128)(2,1)} %all-gather.2.cloned.1.call-done.merge_ref, bf16[1024,768]{1,0:T(8,128)(2,1)} %inputs_ref.5, ...), custom_call_target="tpu_custom_call" | custom-call | tf_op jit(solution)/shard_map/pallas_call | solution.py:704
  129.6 4.3 all-to-all-start
  134.9 20.7 %all-to-all-done.rows_ref = bf16[8,160,768]{2,1,0:T(8,128)(2,1)} async-done(((bf16[8,160,768]{2,1,0:T(8,128)(2,1)}), bf16[8,160,768]{2,1,0:T(8,128)(2,1)}, u32[]{:S(2)}, u32[]{:S(2)}) %all-to-all-start) | async-done | bytes 1966112 | tf_op jit(solution)/shard_map/all_to_all | solution.py:935
  155.7 18.5 %shard_map.253 = (bf16[1280,3072]{1,0:T(8,128)(2,1)}, bf16[1280,3072]{1,0:T(8,128)(2,1)}, bf16[4,768,768]{2,1,0:T(8,128)(2,1)}, bf16[1280,768]{1,0:T(8,128)(2,1)}) custom-call(s32[1]{0:T(128)} %bitcast.1.owner_ref, bf16[8,160,768]{2,1,0:T(8,128)(2,1)} %all-to-all-done.rows_ref, f32[1,1280]{1,0:T(1,128)} %reshape_squeeze.6.other_ref.refs_0_, ...), custom_call_target="tpu_custom_call" | custom-call | tf_op jit(solution)/shard_map/pallas_call | solution.py:181
  174.8 8.2 %shard_map.256 = bf16[8,240,768]{2,1,0:T(8,128)(2,1)} custom-call(s32[2,1024]{1,0:T(2,128)} %get-tuple-element.60.slots_ref, bf16[1024,768]{1,0:T(8,128)(2,1)} %get-tuple-element.81.rows_ref, bf16[1024,768]{1,0:T(8,128)(2,1)} %cot_ref.7, f32[1,1280]{1,0:T(1,128)} %reshape_squeeze.6.other_ref.refs_0_, f32[1,1280]{1,0:T(1,128)} %reshape_squeeze.7.refs_1_.other_ref), custom_call_target="tpu_custom_call" | custom-call | tf_op jit(solution)/shard_map/pallas_call | solution.py:81
  183.1 7.9 %all-to-all-start.4 = ((bf16[8,240,768]{2,1,0:T(8,128)(2,1)}), bf16[8,240,768]{2,1,0:T(8,128)(2,1)}, u32[]{:S(2)}, u32[]{:S(2)}) async-start(bf16[8,240,768]{2,1,0:T(8,128)(2,1)} %shard_map.256), calls=%async_computation.4 | async-start | bytes 5898240 | tf_op jit(solution)/shard_map/all_to_all | solution.py:935
  191.0 37.6 %shard_map.254 = (bf16[8,2,160,768]{3,2,1,0:T(8,128)(2,1)}, bf16[4,2304,768]{2,1,0:T(8,128)(2,1)}) custom-call(bf16[8,160,768]{2,1,0:T(8,128)(2,1)} %all-to-all-done.rows_ref, bf16[1280,768]{1,0:T(8,128)(2,1)} %get-tuple-element.75.grad_ref, bf16[1280,3072]{1,0:T(8,128)(2,1)} %get-tuple-element.76.act_ref, bf16[1280,3072]{1,0:T(8,128)(2,1)} %get-tuple-element.77.pre_ref, ...), custom_call_target="tpu_custom_call" | custom-call | tf_op jit(solution)/shard_map/pallas_call | solution.py:238
  228.6 19.9 %shard_map.257 = (bf16[1280,3072]{1,0:T(8,128)(2,1)}, bf16[1280,3072]{1,0:T(8,128)(2,1)}, bf16[4,2304,768]{2,1,0:T(8,128)(2,1)}, bf16[1280,768]{1,0:T(8,128)(2,1)}) custom-call(s32[1]{0:T(128)} %bitcast.1.owner_ref, bf16[8,240,768]{2,1,0:T(8,128)(2,1)} %all-to-all-done.4.rows_ref.refs_1_, ...), custom_call_target="tpu_custom_call", output_to_operand_aliasing={{2}: (7, {})} | custom-call | tf_op jit(solution)/shard_map/pallas_call | solution.py:181
  248.5 19.4 %shard_map.258 = (bf16[1280,3072]{1,0:T(8,128)(2,1)}, bf16[4,2304,768]{2,1,0:T(8,128)(2,1)}) custom-call(bf16[8,240,768]{2,1,0:T(8,128)(2,1)} %all-to-all-done.4.rows_ref.refs_1_, bf16[1280,768]{1,0:T(8,128)(2,1)} %get-tuple-element.84.grad_ref, bf16[1280,3072]{1,0:T(8,128)(2,1)} %get-tuple-element.85.pre_ref, ...), custom_call_target="tpu_custom_call", output_to_operand_aliasing={{1}: (4, {})} | custom-call | tf_op jit(solution)/shard_map/pallas_call | solution.py:269
  267.9 4.6 all-to-all-start.3
  272.5 22.0 %shard_map.259 = bf16[8,2,160,768]{3,2,1,0:T(8,128)(2,1)} custom-call(bf16[1280,3072]{1,0:T(8,128)(2,1)} %get-tuple-element.83.act_ref, bf16[1280,3072]{1,0:T(8,128)(2,1)} %get-tuple-element.87.low_ref, bf16[2,768,3072]{2,1,0:T(8,128)(2,1)} %up_ref.7, bf16[2,3072,768]{2,1,0:T(8,128)(2,1)} %down_ref.5), custom_call_target="tpu_custom_call" | custom-call | tf_op jit(solution)/shard_map/pallas_call | solution.py:307
  294.5 20.8 %all-to-all-done.3.made_ref.back_ref = bf16[8,2,160,768]{3,2,1,0:T(8,128)(2,1)} async-done(((bf16[8,2,160,768]{3,2,1,0:T(8,128)(2,1)}), bf16[8,2,160,768]{3,2,1,0:T(8,128)(2,1)}, u32[]{:S(2)}, u32[]{:S(2)}) %all-to-all-start.3) | async-done | bytes 3932192 | tf_op jit(solution)/shard_map/all_to_all | solution.py:935
  315.3 8.5 %all-to-all-start.5 = ((bf16[8,2,160,768]{3,2,1,0:T(8,128)(2,1)}), bf16[8,2,160,768]{3,2,1,0:T(8,128)(2,1)}, u32[]{:S(2)}, u32[]{:S(2)}) async-start(bf16[8,2,160,768]{3,2,1,0:T(8,128)(2,1)} %shard_map.259), calls=%async_computation.5 | async-start | bytes 7864320 | tf_op jit(solution)/shard_map/all_to_all | solution.py:935
  324.5 11.2 %shard_map.255 = (f32[1024,768]{1,0:T(8,128)}, f32[1024,128]{1,0:T(8,128)}, f32[1024,768]{1,0:T(8,128)}) custom-call(s32[2,1024]{1,0:T(2,128)} %get-tuple-element.60.slots_ref, f32[2,1024]{1,0:T(2,128)} %get-tuple-element.69.gates_ref, f32[1024,768]{1,0:T(8,128)} %get-tuple-element.70.resid_ref, bf16[1024,768]{1,0:T(8,128)(2,1)} %cot_ref.7, ...), custom_call_target="tpu_custom_call" | custom-call | tf_op jit(solution)/shard_map/pallas_call | solution.py:357
  335.8 30.8 %all-to-all-done.5.made_ref.back_ref = bf16[8,2,160,768]{3,2,1,0:T(8,128)(2,1)} async-done(((bf16[8,2,160,768]{3,2,1,0:T(8,128)(2,1)}), bf16[8,2,160,768]{3,2,1,0:T(8,128)(2,1)}, u32[]{:S(2)}, u32[]{:S(2)}) %all-to-all-start.5) | async-done | bytes 3932192 | tf_op jit(solution)/shard_map/all_to_all | solution.py:935
  366.6 9.4 %shard_map.260 = (bf16[1024,768]{1,0:T(8,128)(2,1)}, bf16[1024,128]{1,0:T(8,128)(2,1)}) custom-call(s32[2,1024]{1,0:T(2,128)} %get-tuple-element.60.slots_ref, s32[2,1024]{1,0:T(2,128)} %bitcast.52, f32[2,1024]{1,0:T(2,128)} %get-tuple-element.69.gates_ref, f32[1024,768]{1,0:T(8,128)} %get-tuple-element.79.result_ref, ...), custom_call_target="tpu_custom_call" | custom-call | tf_op jit(solution)/shard_map/pallas_call | solution.py:398
  376.0 10.6 %shard_map.261 = (f32[1024,768]{1,0:T(8,128)}, bf16[1024,768]{1,0:T(8,128)(2,1)}, bf16[1024,768]{1,0:T(8,128)(2,1)}, f32[1,768]{1,0:T(1,128)}) custom-call(s32[2,1024]{1,0:T(2,128)} %get-tuple-element.60.slots_ref, bf16[1024,128]{1,0:T(8,128)(2,1)} %get-tuple-element.89.logit_ref, bf16[128,768]{1,0:T(8,128)(2,1)} %pad.35.router_ref, ...), custom_call_target="tpu_custom_call" | custom-call | tf_op jit(solution)/shard_map/pallas_call | solution.py:434
  386.5 35.6 %shard_map.262 = (bf16[3,1024,768]{2,1,0:T(8,128)(2,1)}, f32[6,4,256]{2,1,0:T(4,128)}) custom-call(bf16[1024,768]{1,0:T(8,128)(2,1)} %get-tuple-element.64.query_ref, bf16[1024,768]{1,0:T(8,128)(2,1)} %get-tuple-element.65.key_ref, bf16[1024,768]{1,0:T(8,128)(2,1)} %get-tuple-element.66.value_ref, bf16[1024,768]{1,0:T(8,128)(2,1)} %get-tuple-element.91.grad_ref, ...), custom_call_target="tpu_custom_call" | custom-call | tf_op jit(solution)/shard_map/pallas_call | solution.py:608
  422.1 11.4 %shard_map.264 = bf16[4,768,768]{2,1,0:T(8,128)(2,1)} custom-call(bf16[1024,768]{1,0:T(8,128)(2,1)} %get-tuple-element.99.left_ref, bf16[1024,768]{1,0:T(8,128)(2,1)} %get-tuple-element.67.mixed_ref.out_ref, bf16[3,1024,768]{2,1,0:T(8,128)(2,1)} %get-tuple-element.93.heads_ref, bf16[1024,768]{1,0:T(8,128)(2,1)} %get-tuple-element.100.branch_ref), custom_call_target="tpu_custom_call" | custom-call | tf_op jit(solution)/shard_map/pallas_call | solution.py:766
  440.8 9.9 %shard_map.263 = (f32[1024,768]{1,0:T(8,128)}, f32[1,768]{1,0:T(1,128)}) custom-call(bf16[3,1024,768]{2,1,0:T(8,128)(2,1)} %get-tuple-element.93.heads_ref, bf16[768,768]{1,0:T(8,128)(2,1)} %get-tuple-element.94.query_ref, bf16[768,768]{1,0:T(8,128)(2,1)} %get-tuple-element.95.key_ref, bf16[768,768]{1,0:T(8,128)(2,1)} %get-tuple-element.96.value_ref, ...), custom_call_target="tpu_custom_call" | custom-call | tf_op jit(solution)/shard_map/pallas_call | solution.py:733
  460.0 12.2 %collective-permute-done.13 = bf16[4,96,768]{2,1,0:T(8,128)(2,1)} collective-permute-done((bf16[4,96,768]{2,1,0:T(8,128)(2,1)S(1)}, bf16[4,96,768]{2,1,0:T(8,128)(2,1)}, u32[]{:S(2)}, u32[]{:S(2)}) %collective-permute-start.13) | collective-permute-done | bytes 589856 | tf_op jit(solution)/shard_map/ppermute | solution.py:861
  489.8 9.4 %collective-permute-done.15 = bf16[104,768]{1,0:T(8,128)(2,1)S(1)} collective-permute-done((bf16[104,768]{1,0:T(8,128)(2,1)S(1)}, bf16[104,768]{1,0:T(8,128)(2,1)S(1)}, u32[]{:S(2)}, u32[]{:S(2)}) %collective-permute-start.15) | collective-permute-done | bytes 159776 | tf_op jit(solution)/shard_map/ppermute | solution.py:866
  499.1 15.0 %collective-permute-done.16 = bf16[104,768]{1,0:T(8,128)(2,1)S(1)} collective-permute-done((bf16[104,768]{1,0:T(8,128)(2,1)S(1)}, bf16[104,768]{1,0:T(8,128)(2,1)S(1)}, u32[]{:S(2)}, u32[]{:S(2)}) %collective-permute-start.16) | collective-permute-done | bytes 159776 | tf_op jit(solution)/shard_map/ppermute | solution.py:866
  537.7 6.1 %shard_map.266 = (f32[1536,768]{1,0:T(8,128)}, f32[1536,768]{1,0:T(8,128)}) custom-call(bf16[2304,768]{1,0:T(8,128)(2,1)} %reduce-scatter.3.cloned.1.call-done.rows_ref, f32[1536,768]{1,0:T(8,128)} %shard_map.265.into_ref), custom_call_target="tpu_custom_call", output_to_operand_aliasing={{1}: (1, {})} | custom-call | tf_op jit(solution)/shard_map/pallas_call | solution.py:810
  (154 shorter events, 79.5 us)
Async XLA Ops:
  10.8 18.8 %collective-permute-start = (bf16[96,768]{1,0:T(8,128)(2,1)S(1)}, bf16[96,768]{1,0:T(8,128)(2,1)S(1)}, u32[]{:S(2)}, u32[]{:S(2)}) collective-permute-start(bf16[96,768]{1,0:T(8,128)(2,1)S(1)} %concatenate.74), channel_id=1, source_target_pairs={{0,1},{1,2},{2,3},{3,0},{4,5},{5,6},{6,7},{7,4},{8,9},{9,10},{10,1... | collective-permute-start | bytes 442376 | tf_op jit(solution)/shard_map/ppermute | solution.py:866
  12.2 26.4 %collective-permute-start.1 = (bf16[96,768]{1,0:T(8,128)(2,1)S(1)}, bf16[96,768]{1,0:T(8,128)(2,1)S(1)}, u32[]{:S(2)}, u32[]{:S(2)}) collective-permute-start(bf16[96,768]{1,0:T(8,128)(2,1)S(1)} %concatenate.74), channel_id=1, source_target_pairs={{0,2},{1,3},{2,0},{3,1},{4,6},{5,7},{6,4},{7,5},{8,10},{9,11},{10,... | collective-permute-start | bytes 442376 | tf_op jit(solution)/shard_map/ppermute | solution.py:866
  13.3 25.3 %collective-permute-start.2 = (bf16[96,768]{1,0:T(8,128)(2,1)S(1)}, bf16[96,768]{1,0:T(8,128)(2,1)S(1)}, u32[]{:S(2)}, u32[]{:S(2)}) collective-permute-start(bf16[96,768]{1,0:T(8,128)(2,1)S(1)} %concatenate.74), channel_id=1, source_target_pairs={{0,3},{1,0},{2,1},{3,2},{4,7},{5,4},{6,5},{7,6},{8,11},{9,8},{10,9... | collective-permute-start | bytes 442376 | tf_op jit(solution)/shard_map/ppermute | solution.py:866
  24.3 9.3 %all-to-all-start.1 = ((f32[8,1,320]{2,1,0:T(1,128)}), f32[8,1,320]{2,1,0:T(1,128)S(1)}, u32[]{:S(2)}, u32[]{:S(2)}) async-start(f32[8,1,320]{2,1,0:T(1,128)} %get-tuple-element.73), calls=%async_computation.1 | async-start | bytes 24576 | tf_op jit(solution)/shard_map/all_to_all | solution.py:935
  33.5 96.0 %all-to-all-start.2 = ((bf16[8,240,768]{2,1,0:T(8,128)(2,1)}), bf16[8,240,768]{2,1,0:T(8,128)(2,1)}, u32[]{:S(2)}, u32[]{:S(2)}) async-start(bf16[8,240,768]{2,1,0:T(8,128)(2,1)} %get-tuple-element.74), calls=%async_computation.2 | async-start | bytes 5898240 | tf_op jit(solution)/shard_map/all_to_all | solution.py:935
  38.6 81.0 %all-gather.2.cloned.1.call-start = ((), (), s32[]{:S(2)}) async-start(), calls=%async_computation.8 | async-start | bytes 1474560 | tf_op jit(solution)/shard_map/all_gather | solution.py:1000
  38.7 38.5 %collective-permute-start.6 = (bf16[1,2,72,768]{3,2,1,0:T(8,128)(2,1)S(1)}, bf16[1,2,72,768]{3,2,1,0:T(8,128)(2,1)S(1)}, u32[]{:S(2)}, u32[]{:S(2)}) collective-permute-start(bf16[1,2,72,768]{3,2,1,0:T(8,128)(2,1)S(1)} %get-tuple-element.121), channel_id=1, source_target_pairs={{0,16},{4,20},{8,24},{12,28},{16,0},{20,4},{24,8},{28,12},{1,17},{... | collective-permute-start | bytes 663560 | tf_op jit(solution)/shard_map/ppermute | solution.py:861
  40.1 38.9 %collective-permute-start.3 = (bf16[1,2,72,768]{3,2,1,0:T(8,128)(2,1)S(1)}, bf16[1,2,72,768]{3,2,1,0:T(8,128)(2,1)S(1)}, u32[]{:S(2)}, u32[]{:S(2)}) collective-permute-start(bf16[1,2,72,768]{3,2,1,0:T(8,128)(2,1)S(1)} %get-tuple-element.122), channel_id=1, source_target_pairs={{0,8},{4,12},{8,0},{12,4},{16,24},{20,28},{24,16},{28,20},{1,9},{5... | collective-permute-start | bytes 663560 | tf_op jit(solution)/shard_map/ppermute | solution.py:861
  77.2 11.3 %collective-permute-start.7 = (bf16[2,2,72,768]{3,2,1,0:T(8,128)(2,1)S(1)}, bf16[2,2,72,768]{3,2,1,0:T(8,128)(2,1)S(1)}, u32[]{:S(2)}, u32[]{:S(2)}) collective-permute-start(bf16[2,2,72,768]{3,2,1,0:T(8,128)(2,1)S(1)} %pad_maximum_fusion.4), channel_id=1, source_target_pairs={{0,8},{4,12},{8,0},{12,4},{16,24},{20,28},{24,16},{28,20},{1,9},{5... | collective-permute-start | bytes 1327112 | tf_op jit(solution)/shard_map/ppermute | solution.py:861
  79.0 11.2 %collective-permute-start.4 = (bf16[2,2,72,768]{3,2,1,0:T(8,128)(2,1)S(1)}, bf16[2,2,72,768]{3,2,1,0:T(8,128)(2,1)S(1)}, u32[]{:S(2)}, u32[]{:S(2)}) collective-permute-start(bf16[2,2,72,768]{3,2,1,0:T(8,128)(2,1)S(1)} %pad_maximum_fusion.3), channel_id=1, source_target_pairs={{0,16},{4,20},{8,24},{12,28},{16,0},{20,4},{24,8},{28,12},{1,17},{... | collective-permute-start | bytes 1327112 | tf_op jit(solution)/shard_map/ppermute | solution.py:861
  88.6 5.7 %collective-permute-start.8 = (bf16[4,2,72,768]{3,2,1,0:T(8,128)(2,1)S(1)}, bf16[4,2,72,768]{3,2,1,0:T(8,128)(2,1)}, u32[]{:S(2)}, u32[]{:S(2)}) collective-permute-start(bf16[4,2,72,768]{3,2,1,0:T(8,128)(2,1)S(1)} %pad_maximum_fusion.1.refs_2_), channel_id=1, source_target_pairs={{0,4},{4,0},{8,12},{12,8},{16,20},{20,16},{24,28},{28,24},{1,5},{5... | collective-permute-start | bytes 2654216 | tf_op jit(solution)/shard_map/ppermute | solution.py:861
  90.4 3.9 collective-permute-start.5
  129.6 26.1 %all-to-all-start = ((bf16[8,160,768]{2,1,0:T(8,128)(2,1)}), bf16[8,160,768]{2,1,0:T(8,128)(2,1)}, u32[]{:S(2)}, u32[]{:S(2)}) async-start(bf16[8,160,768]{2,1,0:T(8,128)(2,1)} %bitcast.48), calls=%async_computation | async-start | bytes 3932160 | tf_op jit(solution)/shard_map/all_to_all | solution.py:935
  133.9 401.1 %reduce-scatter.5.cloned.1.call-start = ((), (), s32[]{:S(2)}) async-start(), calls=%async_computation.10 | async-start | bytes 5898240 | tf_op jit(solution)/shard_map/reduce_scatter | solution.py:931
  183.1 45.5 %all-to-all-start.4 = ((bf16[8,240,768]{2,1,0:T(8,128)(2,1)}), bf16[8,240,768]{2,1,0:T(8,128)(2,1)}, u32[]{:S(2)}, u32[]{:S(2)}) async-start(bf16[8,240,768]{2,1,0:T(8,128)(2,1)} %shard_map.256), calls=%async_computation.4 | async-start | bytes 5898240 | tf_op jit(solution)/shard_map/all_to_all | solution.py:935
  191.0 346.6 %reduce-scatter.3.cloned.1.call-start = ((), (), s32[]{:S(2)}) async-start(), calls=%async_computation.9 | async-start | bytes 17694720 | tf_op jit(solution)/shard_map/reduce_scatter | solution.py:931
  267.9 47.4 %all-to-all-start.3 = ((bf16[8,2,160,768]{3,2,1,0:T(8,128)(2,1)}), bf16[8,2,160,768]{3,2,1,0:T(8,128)(2,1)}, u32[]{:S(2)}, u32[]{:S(2)}) async-start(bf16[8,2,160,768]{3,2,1,0:T(8,128)(2,1)} %get-tuple-element.78), calls=%async_computation.3 | async-start | bytes 7864320 | tf_op jit(solution)/shard_map/all_to_all | solution.py:935
  315.3 51.2 %all-to-all-start.5 = ((bf16[8,2,160,768]{3,2,1,0:T(8,128)(2,1)}), bf16[8,2,160,768]{3,2,1,0:T(8,128)(2,1)}, u32[]{:S(2)}, u32[]{:S(2)}) async-start(bf16[8,2,160,768]{3,2,1,0:T(8,128)(2,1)} %shard_map.259), calls=%async_computation.5 | async-start | bytes 7864320 | tf_op jit(solution)/shard_map/all_to_all | solution.py:935
  436.8 17.4 %collective-permute-start.9 = (bf16[4,384,768]{2,1,0:T(8,128)(2,1)}, bf16[4,384,768]{2,1,0:T(8,128)(2,1)}, u32[]{:S(2)}, u32[]{:S(2)}) collective-permute-start(bf16[4,384,768]{2,1,0:T(8,128)(2,1)} %constant_dynamic-slice_fusion.3), channel_id=1, source_target_pairs={{0,4},{4,0},{8,12},{12,8},{16,20},{20,16},{24,28},{28,24},{1,5},{5... | collective-permute-start | bytes 7077896 | tf_op jit(solution)/shard_map/ppermute | solution.py:861
  452.7 1.5 collective-permute-start.12
  457.4 14.8 %collective-permute-start.13 = (bf16[4,96,768]{2,1,0:T(8,128)(2,1)S(1)}, bf16[4,96,768]{2,1,0:T(8,128)(2,1)}, u32[]{:S(2)}, u32[]{:S(2)}) collective-permute-start(bf16[4,96,768]{2,1,0:T(8,128)(2,1)S(1)} %fusion.1), channel_id=1, source_target_pairs={{0,16},{4,20},{8,24},{12,28},{16,0},{20,4},{24,8},{28,12},{1,17},{... | collective-permute-start | bytes 1769480 | tf_op jit(solution)/shard_map/ppermute | solution.py:861
  459.6 17.0 %collective-permute-start.10 = (bf16[4,112,768]{2,1,0:T(8,128)(2,1)}, bf16[4,112,768]{2,1,0:T(8,128)(2,1)}, u32[]{:S(2)}, u32[]{:S(2)}) collective-permute-start(bf16[4,112,768]{2,1,0:T(8,128)(2,1)} %constant_dynamic-slice_fusion.2), channel_id=1, source_target_pairs={{0,8},{4,12},{8,0},{12,4},{16,24},{20,28},{24,16},{28,20},{1,9},{5... | collective-permute-start | bytes 2064392 | tf_op jit(solution)/shard_map/ppermute | solution.py:861
  473.6 9.3 %collective-permute-start.14 = (bf16[4,48,768]{2,1,0:T(8,128)(2,1)S(1)}, bf16[4,48,768]{2,1,0:T(8,128)(2,1)S(1)}, u32[]{:S(2)}, u32[]{:S(2)}) collective-permute-start(bf16[4,48,768]{2,1,0:T(8,128)(2,1)S(1)} %constant_dynamic-slice_fusion), channel_id=1, source_target_pairs={{0,8},{4,12},{8,0},{12,4},{16,24},{20,28},{24,16},{28,20},{1,9},{5... | collective-permute-start | bytes 884744 | tf_op jit(solution)/shard_map/ppermute | solution.py:861
  477.9 7.8 %collective-permute-start.11 = (bf16[4,56,768]{2,1,0:T(8,128)(2,1)S(1)}, bf16[4,56,768]{2,1,0:T(8,128)(2,1)S(1)}, u32[]{:S(2)}, u32[]{:S(2)}) collective-permute-start(bf16[4,56,768]{2,1,0:T(8,128)(2,1)S(1)} %constant_dynamic-slice_fusion.1), channel_id=1, source_target_pairs={{0,16},{4,20},{8,24},{12,28},{16,0},{20,4},{24,8},{28,12},{1,17},{... | collective-permute-start | bytes 1032200 | tf_op jit(solution)/shard_map/ppermute | solution.py:861
  485.8 13.3 %collective-permute-start.15 = (bf16[104,768]{1,0:T(8,128)(2,1)S(1)}, bf16[104,768]{1,0:T(8,128)(2,1)S(1)}, u32[]{:S(2)}, u32[]{:S(2)}) collective-permute-start(bf16[104,768]{1,0:T(8,128)(2,1)S(1)} %get-tuple-element.118), channel_id=1, source_target_pairs={{0,1},{1,2},{2,3},{3,0},{4,5},{5,6},{6,7},{7,4},{8,9},{9,10},{10,1... | collective-permute-start | bytes 479240 | tf_op jit(solution)/shard_map/ppermute | solution.py:866
  486.2 27.9 %collective-permute-start.16 = (bf16[104,768]{1,0:T(8,128)(2,1)S(1)}, bf16[104,768]{1,0:T(8,128)(2,1)S(1)}, u32[]{:S(2)}, u32[]{:S(2)}) collective-permute-start(bf16[104,768]{1,0:T(8,128)(2,1)S(1)} %get-tuple-element.119), channel_id=1, source_target_pairs={{0,2},{1,3},{2,0},{3,1},{4,6},{5,7},{6,4},{7,5},{8,10},{9,11},{10,... | collective-permute-start | bytes 479240 | tf_op jit(solution)/shard_map/ppermute | solution.py:866
  489.8 25.6 %collective-permute-start.17 = (bf16[104,768]{1,0:T(8,128)(2,1)S(1)}, bf16[104,768]{1,0:T(8,128)(2,1)S(1)}, u32[]{:S(2)}, u32[]{:S(2)}) collective-permute-start(bf16[104,768]{1,0:T(8,128)(2,1)S(1)} %get-tuple-element.120), channel_id=1, source_target_pairs={{0,3},{1,0},{2,1},{3,2},{4,7},{5,4},{6,5},{7,6},{8,11},{9,8},{10,9... | collective-permute-start | bytes 479240 | tf_op jit(solution)/shard_map/ppermute | solution.py:866
  515.5 3.3 collective-permute-start.20
  517.1 3.6 collective-permute-start.18
  518.9 4.9 collective-permute-start.21
  520.8 4.6 collective-permute-start.19
  525.5 5.6 %collective-permute-start.22 = (bf16[416,768]{1,0:T(8,128)(2,1)S(1)}, bf16[416,768]{1,0:T(8,128)(2,1)S(1)}, u32[]{:S(2)}, u32[]{:S(2)}) collective-permute-start(bf16[416,768]{1,0:T(8,128)(2,1)S(1)} %pad_maximum_fusion.2), channel_id=1, source_target_pairs={{0,4},{4,0},{8,12},{12,8},{16,20},{20,16},{24,28},{28,24},{1,5},{5... | collective-permute-start | bytes 1916936 | tf_op jit(solution)/shard_map/ppermute | solution.py:861
  (13 other events, 133.9 us)
Sparse Core Ops, SparseCore 0:
  41.5 27.9 all-gather.1
  174.3 85.4 reduce-scatter.4
  268.1 249.2 reduce-scatter.2

commit v9 on v8

--- a/solution.py
+++ b/solution.py
@@ -64,8 +64,7 @@
     )(routes)
 
 
-def dispatch_both_kernel(slots_ref, rows_ref, cot_ref, *refs, start, capacity, early):
-    out_ref = refs[-1]
+def dispatch_both_kernel(slots_ref, rows_ref, cot_ref, out_ref, *, start, capacity, early):
     block, tokens = capacity, rows_ref.shape[0]
     slot = lax.broadcasted_iota(jnp.int32, (block, tokens), 0) + (pl.program_id(0) * block + start)
     hot = jnp.where((slot == slots_ref[0:1, :]) | (slot == slots_ref[1:2, :]), 1.0, 0.0)
@@ -74,43 +73,58 @@
     out_ref[0, capacity:] = dot_nn(hot[early:], cot_ref[...]).astype(out_ref.dtype)
 
 
-def dispatch_both(slots, rows, cot, start, owners, capacity, early, after=()):
+def dispatch_both(slots, rows, cot, start, owners, capacity, early):
     width = rows.shape[1]
     total = 2 * capacity - early
     whole = lambda shape: pl.BlockSpec(shape, lambda i: (0, 0))
     return pl.pallas_call(
         partial(dispatch_both_kernel, start=start, capacity=capacity, early=early),
         grid=(owners,),
-        in_specs=[whole(slots.shape), whole(rows.shape), whole(cot.shape)] + [pl.BlockSpec(memory_space=pl.ANY)] * len(after),
+        in_specs=[whole(slots.shape), whole(rows.shape), whole(cot.shape)],
         out_specs=pl.BlockSpec((1, total, width), lambda i: (i, 0, 0)),
         out_shape=jax.ShapeDtypeStruct((owners, total, width), rows.dtype),
         compiler_params=pltpu.CompilerParams(vmem_limit_bytes=62 << 20),
-    )(slots, rows, cot, *after)
-
-
-def dispatch_first_kernel(slots_ref, routes_ref, rows_ref, out_ref, other_ref, *, owners, capacity):
-    block, tokens = other_ref.shape[2], rows_ref.shape[0]
+    )(slots, rows, cot)
+
+
+def padded(count):
+    return -(-count // 128) * 128
+
+
+def dispatch_first_kernel(slots_ref, routes_ref, rows_ref, out_ref, *, owners, capacity, early):
+    per, _, width = out_ref.shape
+    block, tokens, total = 2 * capacity, rows_ref.shape[0], capacity + early
+    wide = padded(capacity)
     row = lax.broadcasted_iota(jnp.int32, (block, tokens), 0)
-    slot = row + pl.program_id(0) * capacity
-    slot = slot + jnp.where(row >= capacity, (owners - 1) * capacity, 0)
-    hits = [slot == slots_ref[c:c + 1, :] for c in range(2)]
-    hot = jnp.where(hits[0] | hits[1], 1.0, 0.0)[:out_ref.shape[1]]
-    out_ref[0] = dot_nn(hot.astype(jnp.bfloat16), rows_ref[...]).astype(out_ref.dtype)
-    other = jnp.where(hits[0], routes_ref[1:2, :], jnp.where(hits[1], routes_ref[0:1, :], 0.0))
-    column = jnp.sum(other, axis=1, keepdims=True)
-    other_ref[0] = jnp.broadcast_to(column, (block, 128)).T[0:1, :]
-
-
-def dispatch_first(slots, routes, rows, owners, capacity, early):
+    row = row + jnp.where(row >= capacity, (owners - 1) * capacity, 0)
+    hots = []
+    for index in range(per):
+        slot = row + (pl.program_id(0) * per + index) * capacity
+        hits = [slot == slots_ref[c:c + 1, :] for c in range(2)]
+        hots.append(jnp.where(hits[0] | hits[1], 1.0, 0.0)[:total].astype(jnp.bfloat16))
+        other = jnp.where(hits[0], routes_ref[1:2, :], jnp.where(hits[1], routes_ref[0:1, :], 0.0))
+        column = jnp.broadcast_to(jnp.sum(other, axis=1, keepdims=True), (block, 128))
+        gap = jnp.zeros((wide - capacity, 128), jnp.float32)
+        for local in range(2):
+            part = jnp.concatenate([column[local * capacity:(local + 1) * capacity], gap], axis=0)
+            out_ref[index, total:, local * wide:(local + 1) * wide] = part.T[:16].astype(out_ref.dtype)
+        out_ref[index, total:, 2 * wide:] = jnp.zeros((16, width - 2 * wide), out_ref.dtype)
+    picked = dot_nn(jnp.concatenate(hots, axis=0), rows_ref[...]).astype(out_ref.dtype)
+    for index in range(per):
+        out_ref[index, :total] = picked[index * total:(index + 1) * total]
+
+
+def dispatch_first(slots, routes, rows, owners, capacity, early, per=4):
     width = rows.shape[1]
-    total = capacity + early
+    total = capacity + early + 16
     whole = lambda shape: pl.BlockSpec(shape, lambda i: (0, 0))
     return pl.pallas_call(
-        partial(dispatch_first_kernel, owners=owners, capacity=capacity),
-        grid=(owners,),
+        partial(dispatch_first_kernel, owners=owners, capacity=capacity, early=early),
+        grid=(owners // per,),
         in_specs=[whole(slots.shape), whole(routes.shape), whole(rows.shape)],
-        out_specs=[pl.BlockSpec((1, total, width), lambda i: (i, 0, 0)), pl.BlockSpec((1, 1, 2 * capacity), lambda i: (i, 0, 0))],
-        out_shape=[jax.ShapeDtypeStruct((owners, total, width), rows.dtype), jax.ShapeDtypeStruct((owners, 1, 2 * capacity), jnp.float32)],
+        out_specs=pl.BlockSpec((per, total, width), lambda i: (i, 0, 0)),
+        out_shape=jax.ShapeDtypeStruct((owners, total, width), rows.dtype),
+        compiler_params=pltpu.CompilerParams(vmem_limit_bytes=62 << 20),
     )(slots, routes, rows)
 
 
@@ -132,28 +146,32 @@
     return pl.BlockSpec((owners, used or count, width), lambda i: (0, 0, 0))
 
 
-def first_kernel(owner_ref, rows_ref, other_ref, router_ref, up_ref, *refs, index, local_count, capacity, pieces):
+def first_kernel(owner_ref, rows_ref, router_ref, up_ref, *refs, index, local_count, capacity, pieces):
     act_ref, pre_ref, down_grad_ref, grad_ref = refs[-4:]
     owners, _, width = rows_ref.shape
     rows = owners * capacity
     chunk = rows // 2
     @pl.when(pl.program_id(0) == 0)
     def _():
-        logits = dot_nt(router_ref[...], rows_ref[:, :capacity].reshape(rows, width))
-        expert = lax.broadcasted_iota(jnp.int32, logits.shape, 0)
+        wide = padded(capacity)
+        expert = lax.broadcasted_iota(jnp.int32, (router_ref.shape[0], capacity), 0)
         mine = owner_ref[0] * local_count + index
-        own = jnp.sum(jnp.where(expert == mine, logits, 0.0), axis=0, keepdims=True)
-        other = other_ref[...].astype(jnp.int32)
-        other = jnp.sum(jnp.where(expert == other, logits, 0.0), axis=0, keepdims=True)
-        top = jnp.maximum(own, other)
-        own = jnp.exp(own - top)
-        gate = own / (own + jnp.exp(other - top))
-        column = jnp.broadcast_to(gate, (128, rows)).T
-        for start in range(0, width, 128):
-            parts = [refs[place][:, low:low + size, start:start + 128] for place, low, size in pieces]
-            part = parts[0] if len(parts) == 1 else jnp.concatenate(parts, axis=1)
-            part = part.reshape(rows, 128).astype(jnp.float32) * column
-            grad_ref[:, start:start + 128] = part.astype(jnp.bfloat16)
+        for owner in range(owners):
+            logits = dot_nt(router_ref[...], rows_ref[owner, :capacity])
+            other = refs[0][owner, -16:, index * wide:(index + 1) * wide].astype(jnp.float32)
+            other = other[0:1, :capacity].astype(jnp.int32)
+            own = jnp.sum(jnp.where(expert == mine, logits, 0.0), axis=0, keepdims=True)
+            other = jnp.sum(jnp.where(expert == other, logits, 0.0), axis=0, keepdims=True)
+            top = jnp.maximum(own, other)
+            own = jnp.exp(own - top)
+            gate = own / (own + jnp.exp(other - top))
+            column = jnp.broadcast_to(gate, (128, capacity)).T
+            at = owner * capacity
+            for start in range(0, width, 128):
+                parts = [refs[place][owner, low:low + size, start:start + 128] for place, low, size in pieces]
+                part = parts[0] if len(parts) == 1 else jnp.concatenate(parts, axis=0)
+                part = part.astype(jnp.float32) * column
+                grad_ref[at:at + capacity, start:start + 128] = part.astype(jnp.bfloat16)
     up = up_ref[0]
     for start in range(0, rows, chunk):
         part = rows_ref[start // capacity:(start + chunk) // capacity, :capacity].reshape(chunk, width)
@@ -164,14 +182,14 @@
     down_grad_ref[0] = dot_tn(act_ref[...], grad_ref[...]).astype(jnp.bfloat16)
 
 
-def expert_first(owner, rows_in, cots, pieces, other, router, up, index, local_count, capacity, shards, into=None):
+def expert_first(owner, rows_in, cots, pieces, router, up, index, local_count, capacity, shards, into=None):
     owners, _, width = rows_in.shape
     rows = owners * capacity
     hidden = up.shape[2]
     tile = hidden // shards
     fixed = pl.BlockSpec((rows, width), lambda i: (0, 0))
     column = pl.BlockSpec((rows, tile), lambda i: (0, i))
-    operands = [owner, rows_in, other, router, up, *cots]
+    operands = [owner, rows_in, router, up, *cots]
     place, aliases = 0, {}
     grad_shape = jax.ShapeDtypeStruct((shards, tile, width), jnp.bfloat16)
     if into is not None:
@@ -184,11 +202,10 @@
         in_specs=[
             pl.BlockSpec(memory_space=pltpu.SMEM),
             arrived_spec(rows_in, capacity),
-            pl.BlockSpec((1, rows), lambda i: (0, 0)),
             pl.BlockSpec(router.shape, lambda i: (0, 0)),
             pl.BlockSpec((1, width, tile), lambda i: (index, 0, i)),
         ]
-        + [arrived_spec(cot, low + size) for cot, (_, low, size) in zip(cots, pieces)]
+        + [arrived_spec(cot) for cot in cots]
         + [pl.BlockSpec(memory_space=pl.ANY)] * (into is not None),
         out_specs=[column, column, pl.BlockSpec((1, tile, width), lambda i: (i, place, 0)), fixed],
         out_shape=[jax.ShapeDtypeStruct((rows, hidden), jnp.bfloat16)] * 2 + [grad_shape, jax.ShapeDtypeStruct((rows, width), jnp.bfloat16)],
@@ -695,7 +712,7 @@
 
 def settle(mixed, merge, inputs, gain, router, routes, slots, count, eps, block=512):
     tokens, width = inputs.shape
-    picking = count // 4
+    picking = count // 2
     settling = tokens // block
     early = lambda i: jnp.minimum(i, settling - 1)
     rows = pl.BlockSpec((block, width), lambda i: (early(i), 0))
@@ -703,7 +720,7 @@
     small = pl.BlockSpec((2, block), lambda i: (0, early(i)))
     return pl.pallas_call(
         partial(settle_kernel, eps=eps, settling=settling),
-        grid=(settling + 4,),
+        grid=(settling + 2,),
         in_specs=[rows, whole(merge.shape), rows, whole(gain.shape), whole(router.shape), small, whole(slots.shape)],
         out_specs=[rows, rows, small, pl.BlockSpec((picking, width), lambda i: (jnp.maximum(i - settling, 0), 0))],
         out_shape=[jax.ShapeDtypeStruct((tokens, width), jnp.float32), jax.ShapeDtypeStruct((tokens, width), jnp.bfloat16), jax.ShapeDtypeStruct((2, tokens), jnp.float32), jax.ShapeDtypeStruct((count, width), jnp.bfloat16)],
@@ -970,7 +987,7 @@
     capacity = -(-capacity // 16) * 16
     rows = owners * capacity
     assert local_count == 2 and hidden // shards == width
-    early = -(-capacity // 32) * 16
+    early = max(16, 2 * capacity // 5 // 16 * 16)
 
     router_at = 2 + local_heads + (-(2 + local_heads)) % 8
 
@@ -1011,10 +1028,9 @@
 
     routes_line = routes.T
     slots, routes_float = find_slots(routes_line, experts, local_count, owners, capacity)
-    cot_rows, other = dispatch_first(
+    cot_rows = dispatch_first(
         slots, routes_float, cotangent, owners, capacity, early
     )
-    other = share_rows(other).reshape(owners, local_count, capacity)
 
     owner = me.astype(jnp.int32).reshape(1)
     query_full, key_full, value_full, low_one, queries, keys, values = project(
@@ -1026,22 +1042,21 @@
         attended, merge_full, inputs, gain_two, router_full, routes_line, slots, rows, epsilon
     )
 
-    others = [other[:, index].reshape(1, rows) for index in range(local_count)]
     rows_in = share_large(send.reshape(owners, capacity, width))
     joint = dispatch_both(
-        slots, low_two, cotangent, rows, owners, capacity, early, after=others
+        slots, low_two, cotangent, rows, owners, capacity, early
     )
     joint_in = share_large(joint)
     act, pre, first_down, grad_in = expert_first(
-        owner, rows_in, [cot_in], [(0, 0, capacity)], others[0], router_full, up_weight,
-        0, local_count, capacity, shards,
+        owner, rows_in, [cot_in], [(0, 0, capacity)], router_full, up_weight, 0,
+        local_count, capacity, shards,
     )
     first_sum = scatter_sum(first_down)
     first_made, pair = expert_second(rows_in, grad_in, act, pre, up_weight, down_weight, 0, owners, shards, 3 * width)
     late = capacity - early
     act, pre, pair, grad_in = expert_first(
         owner, joint_in, [cot_in, joint_in], [(0, capacity, early), (1, capacity, late)],
-        others[1], router_full, up_weight, 1, local_count, capacity, shards, into=pair,
+        router_full, up_weight, 1, local_count, capacity, shards, into=pair,
     )
     low, pair = expert_slope(joint_in, grad_in, pre, down_weight, 1, shards, pair, 1)
     pair_sum = scatter_sum(pair)

time: 558 us -> 550 us (0.986)
  blocking collectives: 0 us -> 29 us
  waiting for transfers between devices: 176 us -> 151 us
  starting transfers between devices: 66.4 us -> 54.9 us
    all_to_all x0 -> x1, blocking collectives: none -> 29 us  [share_rows(): return lax.all_to_all(rows, OWNER, 0, 0, tiled=True)]
    all_to_all x6 -> x4, waiting for transfers between devices: 76.3 us -> 51.7 us  [share_rows(): return lax.all_to_all(rows, OWNER, 0, 0, tiled=True)]
    all_to_all x6 -> x4, starting transfers between devices: 35.6 us -> 24.2 us  [share_rows(): return lax.all_to_all(rows, OWNER, 0, 0, tiled=True)]
  transfers between devices with their start and end apart: 32 -> 30, of which waited for: 19 -> 17; matrix products, arithmetic and copies ran while one was open for 4% -> 3% of each run, Pallas kernels for 44% -> 45%
where the time goes in v9:
time: 550 us; the launch traced here: 541 us
  Pallas kernels  268 us (49%)
  waiting for transfers between devices  151 us (27%)
  starting transfers between devices  54.9 us (10%)
  blocking collectives  29 us (5%)
  between operations  14.7 us (3%)
  local copies, waits for them, and re-layouts  12.6 us (2%)
  other arithmetic  9.95 us (2%)
    ppermute x17, waiting for transfers between devices, exchange(): return lax.ppermute(rows, OWNER, [(i, i ^ bit) for i in range(count)])  73.9 us
    all_to_all x4, waiting for transfers between devices, share_rows(): return lax.all_to_all(rows, OWNER, 0, 0, tiled=True)  51.7 us
    pallas_call x2, Pallas kernels, expert_first(): pl.pallas_call(partial(first_kernel, index=index, local_count=local_count...  38.4 us
    pallas_call x1, Pallas kernels, expert_second(): pl.pallas_call(second_kernel, grid=(shards,), in_specs=[arrived_spec(rows...  37.6 us
    pallas_call x1, Pallas kernels, attend_back(): pl.pallas_call(partial(attend_back_kernel, block=block, size=size, scale=...  35.6 us
    all_to_all x1, blocking collectives, share_rows(): return lax.all_to_all(rows, OWNER, 0, 0, tiled=True)  29 us
    ppermute x6, waiting for transfers between devices, shift(): lax.ppermute(rows, LINE, [(i, (i + step) % count) for i in range(count)])  25.5 us
    all_to_all x4, starting transfers between devices, share_rows(): return lax.all_to_all(rows, OWNER, 0, 0, tiled=True)  24.2 us
  transfers between devices with their start and end apart: 30, of which 17 were waited for; matrix products, arithmetic and copies ran while one was open for 3% of the time, Pallas kernels for 45%

profile of v9, /device:TPU:9, one launch (start us, length us, event | category | flops | bytes accessed | tf_op | source)
XLA Modules:
  0.0 540.6 jit_solution(13317472381745702055)
XLA Ops:
  16.3 6.8 %shard_map.252 = bf16[8,240,768]{2,1,0:T(8,128)(2,1)} custom-call(s32[2,1024]{1,0:T(2,128)} %get-tuple-element.58.slots_ref, f32[2,1024]{1,0:T(2,128)} %get-tuple-element.70.routes_ref, bf16[1024,768]{1,0:T(8,128)(2,1)} %cot_ref.7), custom_call_target="tpu_custom_call" | custom-call | tf_op jit(solution)/shard_map/pallas_call | solution.py:121
  23.1 5.8 %all-to-all-start.1 = ((bf16[8,240,768]{2,1,0:T(8,128)(2,1)}), bf16[8,240,768]{2,1,0:T(8,128)(2,1)}, u32[]{:S(2)}, u32[]{:S(2)}) async-start(bf16[8,240,768]{2,1,0:T(8,128)(2,1)} %shard_map.252), calls=%async_computation.1 | async-start | bytes 5898240 | tf_op jit(solution)/shard_map/all_to_all | solution.py:952
  31.9 35.7 %collective-permute-done.6 = bf16[1,2,72,768]{3,2,1,0:T(8,128)(2,1)S(1)} collective-permute-done((bf16[1,2,72,768]{3,2,1,0:T(8,128)(2,1)S(1)}, bf16[1,2,72,768]{3,2,1,0:T(8,128)(2,1)S(1)}, u32[]{:S(2)}, u32[]{:S(2)}) %collective-permute-start.6) | collective-permute-done | bytes 221216 | tf_op jit(solution)/shard_map/ppermute | solution.py:878
  69.5 9.3 %collective-permute-done.7 = bf16[2,2,72,768]{3,2,1,0:T(8,128)(2,1)S(1)} collective-permute-done((bf16[2,2,72,768]{3,2,1,0:T(8,128)(2,1)S(1)}, bf16[2,2,72,768]{3,2,1,0:T(8,128)(2,1)S(1)}, u32[]{:S(2)}, u32[]{:S(2)}) %collective-permute-start.7) | collective-permute-done | bytes 442400 | tf_op jit(solution)/shard_map/ppermute | solution.py:878
  84.7 7.9 %shard_map.249 = (bf16[768,768]{1,0:T(8,128)(2,1)}, bf16[768,768]{1,0:T(8,128)(2,1)}, bf16[768,768]{1,0:T(8,128)(2,1)}, bf16[1024,768]{1,0:T(8,128)(2,1)}, bf16[...) custom-call(s32[1]{0:T(128)} %bitcast.1.owner_ref, bf16[1024,768]{1,0:T(8,128)(2,1)} %inputs_ref.5, ...), custom_call_target="tpu_custom_call" | custom-call | tf_op jit(solution)/shard_map/pallas_call | solution.py:676
  92.5 17.3 %shard_map.250 = (bf16[1024,768]{1,0:T(8,128)(2,1)}, f32[6,2,1024]{2,1,0:T(2,128)}) custom-call(bf16[1024,768]{1,0:T(8,128)(2,1)} %get-tuple-element.62.query_ref, bf16[1024,768]{1,0:T(8,128)(2,1)} %get-tuple-element.63.key_ref, bf16[1024,768]{1,0:T(8,128)(2,1)} %get-tuple-element.64.value_ref, f32[6,2,256]{2,1,0:T(2,128)} %get-tuple-element.60.refs_4_.near_ref), custom_call_target="tpu_custom_call" | custom-call | tf_op jit(solution)/shard_map/pallas_call | solution.py:544
  109.9 9.7 %shard_map.251 = (f32[1024,768]{1,0:T(8,128)}, bf16[1024,768]{1,0:T(8,128)(2,1)}, f32[2,1024]{1,0:T(2,128)}, bf16[1280,768]{1,0:T(8,128)(2,1)}) custom-call(bf16[1024,768]{1,0:T(8,128)(2,1)} %get-tuple-element.65.mixed_ref.out_ref, bf16[768,768]{1,0:T(8,128)(2,1)} %all-gather.2.cloned.1.call-done.merge_ref, bf16[1024,768]{1,0:T(8,128)(2,1)} %inputs_ref.5, ...), custom_call_target="tpu_custom_call" | custom-call | tf_op jit(solution)/shard_map/pallas_call | solution.py:721
  119.6 29.0 %all_to_all.25.rows_ref = bf16[8,160,768]{2,1,0:T(8,128)(2,1)} all-to-all(bf16[8,160,768]{2,1,0:T(8,128)(2,1)} %bitcast.48), channel_id=1, replica_groups=mesh['expert'=8,'shard'=4] {'expert'}, dimensions={0} | all-to-all | bytes 3932160 | tf_op jit(solution)/shard_map/all_to_all | solution.py:952
  148.7 18.7 %shard_map.253 = (bf16[1280,3072]{1,0:T(8,128)(2,1)}, bf16[1280,3072]{1,0:T(8,128)(2,1)}, bf16[4,768,768]{2,1,0:T(8,128)(2,1)}, bf16[1280,768]{1,0:T(8,128)(2,1)}) custom-call(s32[1]{0:T(128)} %bitcast.1.owner_ref, bf16[8,160,768]{2,1,0:T(8,128)(2,1)} %all_to_all.25.rows_ref, bf16[16,768]{1,0:T(8,128)(2,1)} %get-tuple-element.61.refs_5_.router_ref, ...), custom_call_target="tpu_custom_call" | custom-call | tf_op jit(solution)/shard_map/pallas_call | solution.py:199
  167.3 8.3 %shard_map.256 = bf16[8,256,768]{2,1,0:T(8,128)(2,1)} custom-call(s32[2,1024]{1,0:T(2,128)} %get-tuple-element.58.slots_ref, bf16[1024,768]{1,0:T(8,128)(2,1)} %get-tuple-element.77.rows_ref, bf16[1024,768]{1,0:T(8,128)(2,1)} %cot_ref.7), custom_call_target="tpu_custom_call" | custom-call | tf_op jit(solution)/shard_map/pallas_call | solution.py:80
  175.6 5.3 all-to-all-start.3
  180.9 37.6 %shard_map.254 = (bf16[8,2,160,768]{3,2,1,0:T(8,128)(2,1)}, bf16[4,2304,768]{2,1,0:T(8,128)(2,1)}) custom-call(bf16[8,160,768]{2,1,0:T(8,128)(2,1)} %all_to_all.25.rows_ref, bf16[1280,768]{1,0:T(8,128)(2,1)} %get-tuple-element.71.grad_ref, bf16[1280,3072]{1,0:T(8,128)(2,1)} %get-tuple-element.72.act_ref, bf16[1280,3072]{1,0:T(8,128)(2,1)} %get-tuple-element.73.pre_ref, ...), custom_call_target="tpu_custom_call" | custom-call | tf_op jit(solution)/shard_map/pallas_call | solution.py:255
  218.5 19.7 %shard_map.257 = (bf16[1280,3072]{1,0:T(8,128)(2,1)}, bf16[1280,3072]{1,0:T(8,128)(2,1)}, bf16[4,2304,768]{2,1,0:T(8,128)(2,1)}, bf16[1280,768]{1,0:T(8,128)(2,1)}) custom-call(s32[1]{0:T(128)} %bitcast.1.owner_ref, bf16[8,256,768]{2,1,0:T(8,128)(2,1)} %all-to-all-done.3.rows_ref.refs_1_, ...), custom_call_target="tpu_custom_call", output_to_operand_aliasing={{2}: (6, {})} | custom-call | tf_op jit(solution)/shard_map/pallas_call | solution.py:199
  238.2 19.6 %shard_map.258 = (bf16[1280,3072]{1,0:T(8,128)(2,1)}, bf16[4,2304,768]{2,1,0:T(8,128)(2,1)}) custom-call(bf16[8,256,768]{2,1,0:T(8,128)(2,1)} %all-to-all-done.3.rows_ref.refs_1_, bf16[1280,768]{1,0:T(8,128)(2,1)} %get-tuple-element.80.grad_ref, bf16[1280,3072]{1,0:T(8,128)(2,1)} %get-tuple-element.81.pre_ref, ...), custom_call_target="tpu_custom_call", output_to_operand_aliasing={{1}: (4, {})} | custom-call | tf_op jit(solution)/shard_map/pallas_call | solution.py:286
  257.8 4.8 all-to-all-start.2
  262.6 21.9 %shard_map.259 = bf16[8,2,160,768]{3,2,1,0:T(8,128)(2,1)} custom-call(bf16[1280,3072]{1,0:T(8,128)(2,1)} %get-tuple-element.79.act_ref, bf16[1280,3072]{1,0:T(8,128)(2,1)} %get-tuple-element.83.low_ref, bf16[2,768,3072]{2,1,0:T(8,128)(2,1)} %up_ref.7, bf16[2,3072,768]{2,1,0:T(8,128)(2,1)} %down_ref.5), custom_call_target="tpu_custom_call" | custom-call | tf_op jit(solution)/shard_map/pallas_call | solution.py:324
  284.6 20.9 %all-to-all-done.2.made_ref.back_ref = bf16[8,2,160,768]{3,2,1,0:T(8,128)(2,1)} async-done(((bf16[8,2,160,768]{3,2,1,0:T(8,128)(2,1)}), bf16[8,2,160,768]{3,2,1,0:T(8,128)(2,1)}, u32[]{:S(2)}, u32[]{:S(2)}) %all-to-all-start.2) | async-done | bytes 3932192 | tf_op jit(solution)/shard_map/all_to_all | solution.py:952
  305.4 8.3 %all-to-all-start.4 = ((bf16[8,2,160,768]{3,2,1,0:T(8,128)(2,1)}), bf16[8,2,160,768]{3,2,1,0:T(8,128)(2,1)}, u32[]{:S(2)}, u32[]{:S(2)}) async-start(bf16[8,2,160,768]{3,2,1,0:T(8,128)(2,1)} %shard_map.259), calls=%async_computation.4 | async-start | bytes 7864320 | tf_op jit(solution)/shard_map/all_to_all | solution.py:952
  314.4 11.2 %shard_map.255 = (f32[1024,768]{1,0:T(8,128)}, f32[1024,128]{1,0:T(8,128)}, f32[1024,768]{1,0:T(8,128)}) custom-call(s32[2,1024]{1,0:T(2,128)} %get-tuple-element.58.slots_ref, f32[2,1024]{1,0:T(2,128)} %get-tuple-element.67.gates_ref, f32[1024,768]{1,0:T(8,128)} %get-tuple-element.68.resid_ref, bf16[1024,768]{1,0:T(8,128)(2,1)} %cot_ref.7, ...), custom_call_target="tpu_custom_call" | custom-call | tf_op jit(solution)/shard_map/pallas_call | solution.py:374
  325.7 30.8 %all-to-all-done.4.made_ref.back_ref = bf16[8,2,160,768]{3,2,1,0:T(8,128)(2,1)} async-done(((bf16[8,2,160,768]{3,2,1,0:T(8,128)(2,1)}), bf16[8,2,160,768]{3,2,1,0:T(8,128)(2,1)}, u32[]{:S(2)}, u32[]{:S(2)}) %all-to-all-start.4) | async-done | bytes 3932192 | tf_op jit(solution)/shard_map/all_to_all | solution.py:952
  356.5 9.4 %shard_map.260 = (bf16[1024,768]{1,0:T(8,128)(2,1)}, bf16[1024,128]{1,0:T(8,128)(2,1)}) custom-call(s32[2,1024]{1,0:T(2,128)} %get-tuple-element.58.slots_ref, s32[2,1024]{1,0:T(2,128)} %bitcast.52, f32[2,1024]{1,0:T(2,128)} %get-tuple-element.67.gates_ref, f32[1024,768]{1,0:T(8,128)} %get-tuple-element.75.result_ref, ...), custom_call_target="tpu_custom_call" | custom-call | tf_op jit(solution)/shard_map/pallas_call | solution.py:415
  365.9 10.6 %shard_map.261 = (f32[1024,768]{1,0:T(8,128)}, bf16[1024,768]{1,0:T(8,128)(2,1)}, bf16[1024,768]{1,0:T(8,128)(2,1)}, f32[1,768]{1,0:T(1,128)}) custom-call(s32[2,1024]{1,0:T(2,128)} %get-tuple-element.58.slots_ref, bf16[1024,128]{1,0:T(8,128)(2,1)} %get-tuple-element.85.logit_ref, bf16[128,768]{1,0:T(8,128)(2,1)} %pad.35.router_ref, ...), custom_call_target="tpu_custom_call" | custom-call | tf_op jit(solution)/shard_map/pallas_call | solution.py:451
  376.4 35.6 %shard_map.262 = (bf16[3,1024,768]{2,1,0:T(8,128)(2,1)}, f32[6,4,256]{2,1,0:T(4,128)}) custom-call(bf16[1024,768]{1,0:T(8,128)(2,1)} %get-tuple-element.62.query_ref, bf16[1024,768]{1,0:T(8,128)(2,1)} %get-tuple-element.63.key_ref, bf16[1024,768]{1,0:T(8,128)(2,1)} %get-tuple-element.64.value_ref, bf16[1024,768]{1,0:T(8,128)(2,1)} %get-tuple-element.87.grad_ref, ...), custom_call_target="tpu_custom_call" | custom-call | tf_op jit(solution)/shard_map/pallas_call | solution.py:625
  412.1 11.4 %shard_map.264 = bf16[4,768,768]{2,1,0:T(8,128)(2,1)} custom-call(bf16[1024,768]{1,0:T(8,128)(2,1)} %get-tuple-element.95.left_ref, bf16[1024,768]{1,0:T(8,128)(2,1)} %get-tuple-element.65.mixed_ref.out_ref, bf16[3,1024,768]{2,1,0:T(8,128)(2,1)} %get-tuple-element.89.heads_ref, bf16[1024,768]{1,0:T(8,128)(2,1)} %get-tuple-element.96.branch_ref), custom_call_target="tpu_custom_call" | custom-call | tf_op jit(solution)/shard_map/pallas_call | solution.py:783
  426.8 3.8 collective-permute-start.9
  430.7 9.9 %shard_map.263 = (f32[1024,768]{1,0:T(8,128)}, f32[1,768]{1,0:T(1,128)}) custom-call(bf16[3,1024,768]{2,1,0:T(8,128)(2,1)} %get-tuple-element.89.heads_ref, bf16[768,768]{1,0:T(8,128)(2,1)} %get-tuple-element.90.query_ref, bf16[768,768]{1,0:T(8,128)(2,1)} %get-tuple-element.91.key_ref, bf16[768,768]{1,0:T(8,128)(2,1)} %get-tuple-element.92.value_ref, ...), custom_call_target="tpu_custom_call" | custom-call | tf_op jit(solution)/shard_map/pallas_call | solution.py:750
  450.0 12.1 %collective-permute-done.13 = bf16[4,96,768]{2,1,0:T(8,128)(2,1)} collective-permute-done((bf16[4,96,768]{2,1,0:T(8,128)(2,1)S(1)}, bf16[4,96,768]{2,1,0:T(8,128)(2,1)}, u32[]{:S(2)}, u32[]{:S(2)}) %collective-permute-start.13) | collective-permute-done | bytes 589856 | tf_op jit(solution)/shard_map/ppermute | solution.py:878
  469.0 3.8 collective-permute-done.14
  475.9 4.1 collective-permute-start.16
  480.0 8.2 %collective-permute-done.15 = bf16[104,768]{1,0:T(8,128)(2,1)S(1)} collective-permute-done((bf16[104,768]{1,0:T(8,128)(2,1)S(1)}, bf16[104,768]{1,0:T(8,128)(2,1)S(1)}, u32[]{:S(2)}, u32[]{:S(2)}) %collective-permute-start.15) | collective-permute-done | bytes 159776 | tf_op jit(solution)/shard_map/ppermute | solution.py:883
  488.2 15.9 %collective-permute-done.16 = bf16[104,768]{1,0:T(8,128)(2,1)S(1)} collective-permute-done((bf16[104,768]{1,0:T(8,128)(2,1)S(1)}, bf16[104,768]{1,0:T(8,128)(2,1)S(1)}, u32[]{:S(2)}, u32[]{:S(2)}) %collective-permute-start.16) | collective-permute-done | bytes 159776 | tf_op jit(solution)/shard_map/ppermute | solution.py:883
  527.5 6.1 %shard_map.266 = (f32[1536,768]{1,0:T(8,128)}, f32[1536,768]{1,0:T(8,128)}) custom-call(bf16[2304,768]{1,0:T(8,128)(2,1)} %reduce-scatter.3.cloned.1.call-done.rows_ref, f32[1536,768]{1,0:T(8,128)} %shard_map.265.into_ref), custom_call_target="tpu_custom_call", output_to_operand_aliasing={{1}: (1, {})} | custom-call | tf_op jit(solution)/shard_map/pallas_call | solution.py:827
  (146 shorter events, 66.4 us)
Async XLA Ops:
  10.8 18.2 %collective-permute-start = (bf16[96,768]{1,0:T(8,128)(2,1)S(1)}, bf16[96,768]{1,0:T(8,128)(2,1)S(1)}, u32[]{:S(2)}, u32[]{:S(2)}) collective-permute-start(bf16[96,768]{1,0:T(8,128)(2,1)S(1)} %concatenate.74), channel_id=1, source_target_pairs={{0,1},{1,2},{2,3},{3,0},{4,5},{5,6},{6,7},{7,4},{8,9},{9,10},{10,1... | collective-permute-start | bytes 442376 | tf_op jit(solution)/shard_map/ppermute | solution.py:883
  12.2 16.9 %collective-permute-start.1 = (bf16[96,768]{1,0:T(8,128)(2,1)S(1)}, bf16[96,768]{1,0:T(8,128)(2,1)S(1)}, u32[]{:S(2)}, u32[]{:S(2)}) collective-permute-start(bf16[96,768]{1,0:T(8,128)(2,1)S(1)} %concatenate.74), channel_id=1, source_target_pairs={{0,2},{1,3},{2,0},{3,1},{4,6},{5,7},{6,4},{7,5},{8,10},{9,11},{10,... | collective-permute-start | bytes 442376 | tf_op jit(solution)/shard_map/ppermute | solution.py:883
  13.3 15.8 %collective-permute-start.2 = (bf16[96,768]{1,0:T(8,128)(2,1)S(1)}, bf16[96,768]{1,0:T(8,128)(2,1)S(1)}, u32[]{:S(2)}, u32[]{:S(2)}) collective-permute-start(bf16[96,768]{1,0:T(8,128)(2,1)S(1)} %concatenate.74), channel_id=1, source_target_pairs={{0,3},{1,0},{2,1},{3,2},{4,7},{5,4},{6,5},{7,6},{8,11},{9,8},{10,9... | collective-permute-start | bytes 442376 | tf_op jit(solution)/shard_map/ppermute | solution.py:883
  23.1 96.5 %all-to-all-start.1 = ((bf16[8,240,768]{2,1,0:T(8,128)(2,1)}), bf16[8,240,768]{2,1,0:T(8,128)(2,1)}, u32[]{:S(2)}, u32[]{:S(2)}) async-start(bf16[8,240,768]{2,1,0:T(8,128)(2,1)} %shard_map.252), calls=%async_computation.1 | async-start | bytes 5898240 | tf_op jit(solution)/shard_map/all_to_all | solution.py:952
  28.9 81.0 %all-gather.2.cloned.1.call-start = ((), (), s32[]{:S(2)}) async-start(), calls=%async_computation.7 | async-start | bytes 1474560 | tf_op jit(solution)/shard_map/all_gather | solution.py:1017
  29.1 38.4 %collective-permute-start.6 = (bf16[1,2,72,768]{3,2,1,0:T(8,128)(2,1)S(1)}, bf16[1,2,72,768]{3,2,1,0:T(8,128)(2,1)S(1)}, u32[]{:S(2)}, u32[]{:S(2)}) collective-permute-start(bf16[1,2,72,768]{3,2,1,0:T(8,128)(2,1)S(1)} %get-tuple-element.115), channel_id=1, source_target_pairs={{0,16},{4,20},{8,24},{12,28},{16,0},{20,4},{24,8},{28,12},{1,17},{... | collective-permute-start | bytes 663560 | tf_op jit(solution)/shard_map/ppermute | solution.py:878
  30.6 38.7 %collective-permute-start.3 = (bf16[1,2,72,768]{3,2,1,0:T(8,128)(2,1)S(1)}, bf16[1,2,72,768]{3,2,1,0:T(8,128)(2,1)S(1)}, u32[]{:S(2)}, u32[]{:S(2)}) collective-permute-start(bf16[1,2,72,768]{3,2,1,0:T(8,128)(2,1)S(1)} %get-tuple-element.116), channel_id=1, source_target_pairs={{0,8},{4,12},{8,0},{12,4},{16,24},{20,28},{24,16},{28,20},{1,9},{5... | collective-permute-start | bytes 663560 | tf_op jit(solution)/shard_map/ppermute | solution.py:878
  31.8 493.1 %reduce-scatter.5.cloned.1.call-start = ((), (), s32[]{:S(2)}) async-start(), calls=%async_computation.9 | async-start | bytes 5898240 | tf_op jit(solution)/shard_map/reduce_scatter | solution.py:948
  67.6 11.3 %collective-permute-start.7 = (bf16[2,2,72,768]{3,2,1,0:T(8,128)(2,1)S(1)}, bf16[2,2,72,768]{3,2,1,0:T(8,128)(2,1)S(1)}, u32[]{:S(2)}, u32[]{:S(2)}) collective-permute-start(bf16[2,2,72,768]{3,2,1,0:T(8,128)(2,1)S(1)} %pad_maximum_fusion.4), channel_id=1, source_target_pairs={{0,8},{4,12},{8,0},{12,4},{16,24},{20,28},{24,16},{28,20},{1,9},{5... | collective-permute-start | bytes 1327112 | tf_op jit(solution)/shard_map/ppermute | solution.py:878
  69.4 11.2 %collective-permute-start.4 = (bf16[2,2,72,768]{3,2,1,0:T(8,128)(2,1)S(1)}, bf16[2,2,72,768]{3,2,1,0:T(8,128)(2,1)S(1)}, u32[]{:S(2)}, u32[]{:S(2)}) collective-permute-start(bf16[2,2,72,768]{3,2,1,0:T(8,128)(2,1)S(1)} %pad_maximum_fusion.3), channel_id=1, source_target_pairs={{0,16},{4,20},{8,24},{12,28},{16,0},{20,4},{24,8},{28,12},{1,17},{... | collective-permute-start | bytes 1327112 | tf_op jit(solution)/shard_map/ppermute | solution.py:878
  79.0 5.7 %collective-permute-start.8 = (bf16[4,2,72,768]{3,2,1,0:T(8,128)(2,1)S(1)}, bf16[4,2,72,768]{3,2,1,0:T(8,128)(2,1)}, u32[]{:S(2)}, u32[]{:S(2)}) collective-permute-start(bf16[4,2,72,768]{3,2,1,0:T(8,128)(2,1)S(1)} %pad_maximum_fusion.1.refs_2_), channel_id=1, source_target_pairs={{0,4},{4,0},{8,12},{12,8},{16,20},{20,16},{24,28},{28,24},{1,5},{5... | collective-permute-start | bytes 2654216 | tf_op jit(solution)/shard_map/ppermute | solution.py:878
  80.7 3.9 collective-permute-start.5
  175.6 42.8 %all-to-all-start.3 = ((bf16[8,256,768]{2,1,0:T(8,128)(2,1)}), bf16[8,256,768]{2,1,0:T(8,128)(2,1)}, u32[]{:S(2)}, u32[]{:S(2)}) async-start(bf16[8,256,768]{2,1,0:T(8,128)(2,1)} %shard_map.256), calls=%async_computation.3 | async-start | bytes 6291456 | tf_op jit(solution)/shard_map/all_to_all | solution.py:952
  180.9 346.6 %reduce-scatter.3.cloned.1.call-start = ((), (), s32[]{:S(2)}) async-start(), calls=%async_computation.8 | async-start | bytes 17694720 | tf_op jit(solution)/shard_map/reduce_scatter | solution.py:948
  257.8 47.6 %all-to-all-start.2 = ((bf16[8,2,160,768]{3,2,1,0:T(8,128)(2,1)}), bf16[8,2,160,768]{3,2,1,0:T(8,128)(2,1)}, u32[]{:S(2)}, u32[]{:S(2)}) async-start(bf16[8,2,160,768]{3,2,1,0:T(8,128)(2,1)} %get-tuple-element.74), calls=%async_computation.2 | async-start | bytes 7864320 | tf_op jit(solution)/shard_map/all_to_all | solution.py:952
  284.6 29.2 %copy-start.8 = (bf16[16,768]{1,0:T(8,128)(2,1)S(1)}, bf16[16,768]{1,0:T(8,128)(2,1)}, u32[]{:S(2)}) copy-start(bf16[16,768]{1,0:T(8,128)(2,1)} %get-tuple-element.61.refs_5_.router_ref) | copy-start | bytes 73732
  305.4 51.0 %all-to-all-start.4 = ((bf16[8,2,160,768]{3,2,1,0:T(8,128)(2,1)}), bf16[8,2,160,768]{3,2,1,0:T(8,128)(2,1)}, u32[]{:S(2)}, u32[]{:S(2)}) async-start(bf16[8,2,160,768]{3,2,1,0:T(8,128)(2,1)} %shard_map.259), calls=%async_computation.4 | async-start | bytes 7864320 | tf_op jit(solution)/shard_map/all_to_all | solution.py:952
  426.8 17.3 %collective-permute-start.9 = (bf16[4,384,768]{2,1,0:T(8,128)(2,1)}, bf16[4,384,768]{2,1,0:T(8,128)(2,1)}, u32[]{:S(2)}, u32[]{:S(2)}) collective-permute-start(bf16[4,384,768]{2,1,0:T(8,128)(2,1)} %constant_dynamic-slice_fusion.3), channel_id=1, source_target_pairs={{0,4},{4,0},{8,12},{12,8},{16,20},{20,16},{24,28},{28,24},{1,5},{5... | collective-permute-start | bytes 7077896 | tf_op jit(solution)/shard_map/ppermute | solution.py:878
  442.6 1.5 collective-permute-start.12
  447.3 14.8 %collective-permute-start.13 = (bf16[4,96,768]{2,1,0:T(8,128)(2,1)S(1)}, bf16[4,96,768]{2,1,0:T(8,128)(2,1)}, u32[]{:S(2)}, u32[]{:S(2)}) collective-permute-start(bf16[4,96,768]{2,1,0:T(8,128)(2,1)S(1)} %fusion.1), channel_id=1, source_target_pairs={{0,16},{4,20},{8,24},{12,28},{16,0},{20,4},{24,8},{28,12},{1,17},{... | collective-permute-start | bytes 1769480 | tf_op jit(solution)/shard_map/ppermute | solution.py:878
  449.6 17.0 %collective-permute-start.10 = (bf16[4,112,768]{2,1,0:T(8,128)(2,1)}, bf16[4,112,768]{2,1,0:T(8,128)(2,1)}, u32[]{:S(2)}, u32[]{:S(2)}) collective-permute-start(bf16[4,112,768]{2,1,0:T(8,128)(2,1)} %constant_dynamic-slice_fusion.2), channel_id=1, source_target_pairs={{0,8},{4,12},{8,0},{12,4},{16,24},{20,28},{24,16},{28,20},{1,9},{5... | collective-permute-start | bytes 2064392 | tf_op jit(solution)/shard_map/ppermute | solution.py:878
  450.0 16.6 %copy-start.4 = (bf16[4,224,768]{2,1,0:T(8,128)(2,1)S(1)}, bf16[4,224,768]{2,1,0:T(8,128)(2,1)}, u32[]{:S(2)}) copy-start(bf16[4,224,768]{2,1,0:T(8,128)(2,1)} %copy-done.3) | copy-start | bytes 4128772
  463.5 9.4 %collective-permute-start.14 = (bf16[4,48,768]{2,1,0:T(8,128)(2,1)S(1)}, bf16[4,48,768]{2,1,0:T(8,128)(2,1)S(1)}, u32[]{:S(2)}, u32[]{:S(2)}) collective-permute-start(bf16[4,48,768]{2,1,0:T(8,128)(2,1)S(1)} %constant_dynamic-slice_fusion), channel_id=1, source_target_pairs={{0,8},{4,12},{8,0},{12,4},{16,24},{20,28},{24,16},{28,20},{1,9},{5... | collective-permute-start | bytes 884744 | tf_op jit(solution)/shard_map/ppermute | solution.py:878
  467.9 7.8 %collective-permute-start.11 = (bf16[4,56,768]{2,1,0:T(8,128)(2,1)S(1)}, bf16[4,56,768]{2,1,0:T(8,128)(2,1)S(1)}, u32[]{:S(2)}, u32[]{:S(2)}) collective-permute-start(bf16[4,56,768]{2,1,0:T(8,128)(2,1)S(1)} %constant_dynamic-slice_fusion.1), channel_id=1, source_target_pairs={{0,16},{4,20},{8,24},{12,28},{16,0},{20,4},{24,8},{28,12},{1,17},{... | collective-permute-start | bytes 1032200 | tf_op jit(solution)/shard_map/ppermute | solution.py:878
  475.8 12.4 %collective-permute-start.15 = (bf16[104,768]{1,0:T(8,128)(2,1)S(1)}, bf16[104,768]{1,0:T(8,128)(2,1)S(1)}, u32[]{:S(2)}, u32[]{:S(2)}) collective-permute-start(bf16[104,768]{1,0:T(8,128)(2,1)S(1)} %get-tuple-element.112), channel_id=1, source_target_pairs={{0,1},{1,2},{2,3},{3,0},{4,5},{5,6},{6,7},{7,4},{8,9},{9,10},{10,1... | collective-permute-start | bytes 479240 | tf_op jit(solution)/shard_map/ppermute | solution.py:883
  475.9 28.2 %collective-permute-start.16 = (bf16[104,768]{1,0:T(8,128)(2,1)S(1)}, bf16[104,768]{1,0:T(8,128)(2,1)S(1)}, u32[]{:S(2)}, u32[]{:S(2)}) collective-permute-start(bf16[104,768]{1,0:T(8,128)(2,1)S(1)} %get-tuple-element.113), channel_id=1, source_target_pairs={{0,2},{1,3},{2,0},{3,1},{4,6},{5,7},{6,4},{7,5},{8,10},{9,11},{10,... | collective-permute-start | bytes 479240 | tf_op jit(solution)/shard_map/ppermute | solution.py:883
  480.0 25.5 %collective-permute-start.17 = (bf16[104,768]{1,0:T(8,128)(2,1)S(1)}, bf16[104,768]{1,0:T(8,128)(2,1)S(1)}, u32[]{:S(2)}, u32[]{:S(2)}) collective-permute-start(bf16[104,768]{1,0:T(8,128)(2,1)S(1)} %get-tuple-element.114), channel_id=1, source_target_pairs={{0,3},{1,0},{2,1},{3,2},{4,7},{5,4},{6,5},{7,6},{8,11},{9,8},{10,9... | collective-permute-start | bytes 479240 | tf_op jit(solution)/shard_map/ppermute | solution.py:883
  505.6 3.3 collective-permute-start.20
  507.1 3.6 collective-permute-start.18
  508.9 4.8 collective-permute-start.21
  510.7 4.6 collective-permute-start.19
  515.5 5.5 %collective-permute-start.22 = (bf16[416,768]{1,0:T(8,128)(2,1)S(1)}, bf16[416,768]{1,0:T(8,128)(2,1)S(1)}, u32[]{:S(2)}, u32[]{:S(2)}) collective-permute-start(bf16[416,768]{1,0:T(8,128)(2,1)S(1)} %pad_maximum_fusion.2), channel_id=1, source_target_pairs={{0,4},{4,0},{8,12},{12,8},{16,20},{20,16},{24,28},{28,24},{1,5},{5... | collective-permute-start | bytes 1916936 | tf_op jit(solution)/shard_map/ppermute | solution.py:878
  (11 other events, 88.0 us)
Sparse Core Ops, SparseCore 0:
  31.9 27.8 all-gather.1
  167.5 82.8 reduce-scatter.4
  257.9 249.2 reduce-scatter.2

commit v10 on v8

--- a/solution.py
+++ b/solution.py
@@ -473,7 +473,7 @@
     ones = jnp.ones((16, length), jnp.bfloat16)
     flipped = [jnp.concatenate([turned[head * size:(head + 1) * size], ones], axis=0) for head in range(heads)]
     tiles = [near_tiles(near_ref, head, block) for head in range(heads)]
-    units = [(i, head) for i in range(count) for head in range(heads)]
+    units = [(i, head) for i in reversed(range(count)) for head in range(heads)]
     def fold(tile, op):
         parts = [tile[k:k + 8] for k in range(0, tile.shape[0], 8)]
         while len(parts) > 1:
@@ -491,7 +491,8 @@
     def part_of(unit):
         i, head = unit
         return head_part(query_ref[pl.ds(i * block, block), :] * jnp.bfloat16(scale), head, size)
-    tops = {0: [score_tile(units[0], part_of(units[0]), 0, 0)]}
+    first = part_of(units[0])
+    tops = {0: [score_tile(units[0], first, j, 0) for j in range(units[0][0] + 1)]}
     outs = []
     for n, (i, head) in enumerate(units):
         top = jnp.max(reduce(jnp.maximum, tops[n]), axis=0, keepdims=True)
@@ -695,7 +696,7 @@
 
 def settle(mixed, merge, inputs, gain, router, routes, slots, count, eps, block=512):
     tokens, width = inputs.shape
-    picking = count // 4
+    picking = count // 2
     settling = tokens // block
     early = lambda i: jnp.minimum(i, settling - 1)
     rows = pl.BlockSpec((block, width), lambda i: (early(i), 0))
@@ -703,7 +704,7 @@
     small = pl.BlockSpec((2, block), lambda i: (0, early(i)))
     return pl.pallas_call(
         partial(settle_kernel, eps=eps, settling=settling),
-        grid=(settling + 4,),
+        grid=(settling + 2,),
         in_specs=[rows, whole(merge.shape), rows, whole(gain.shape), whole(router.shape), small, whole(slots.shape)],
         out_specs=[rows, rows, small, pl.BlockSpec((picking, width), lambda i: (jnp.maximum(i - settling, 0), 0))],
         out_shape=[jax.ShapeDtypeStruct((tokens, width), jnp.float32), jax.ShapeDtypeStruct((tokens, width), jnp.bfloat16), jax.ShapeDtypeStruct((2, tokens), jnp.float32), jax.ShapeDtypeStruct((count, width), jnp.bfloat16)],
@@ -970,7 +971,7 @@
     capacity = -(-capacity // 16) * 16
     rows = owners * capacity
     assert local_count == 2 and hidden // shards == width
-    early = -(-capacity // 32) * 16
+    early = max(16, 2 * capacity // 5 // 16 * 16)
 
     router_at = 2 + local_heads + (-(2 + local_heads)) % 8
 

time: 558 us -> 554 us (level)
  the two profiles are of different devices: /device:TPU:9 before, /device:TPU:13 now
where the time goes in v10:
time: 554 us; the launch traced here: 545 us
  Pallas kernels  266 us (48%)
  waiting for transfers between devices  175 us (32%)
  starting transfers between devices  65.4 us (12%)
  between operations  14.5 us (3%)
  local copies, waits for them, and re-layouts  14.1 us (3%)
  other arithmetic  10.1 us (2%)
    ppermute x17, waiting for transfers between devices, exchange(): return lax.ppermute(rows, OWNER, [(i, i ^ bit) for i in range(count)])  74.8 us
    all_to_all x6, waiting for transfers between devices, share_rows(): return lax.all_to_all(rows, OWNER, 0, 0, tiled=True)  74.6 us
    all_to_all x6, starting transfers between devices, share_rows(): return lax.all_to_all(rows, OWNER, 0, 0, tiled=True)  38.7 us
    pallas_call x2, Pallas kernels, expert_first(): pl.pallas_call(partial(first_kernel, index=index, local_count=local_count...  38.5 us
    pallas_call x1, Pallas kernels, expert_second(): pl.pallas_call(second_kernel, grid=(shards,), in_specs=[arrived_spec(rows...  37.6 us
    pallas_call x1, Pallas kernels, attend_back(): pl.pallas_call(partial(attend_back_kernel, block=block, size=size, scale=...  35.6 us
    ppermute x6, waiting for transfers between devices, shift(): lax.ppermute(rows, LINE, [(i, (i + step) % count) for i in range(count)])  25.5 us
    pallas_call x1, Pallas kernels, expert_last(): pl.pallas_call(last_kernel, grid=(shards,), in_specs=[column, column, pl....  21.8 us
  transfers between devices with their start and end apart: 32, of which 19 were waited for; matrix products, arithmetic and copies ran while one was open for 4% of the time, Pallas kernels for 44%

profile of v10, /device:TPU:13, one launch (start us, length us, event | category | flops | bytes accessed | tf_op | source)
XLA Modules:
  0.0 545.4 jit_solution(15363279534884211646)
XLA Ops:
  16.3 7.8 %shard_map.252 = (bf16[8,224,768]{2,1,0:T(8,128)(2,1)}, f32[8,1,320]{2,1,0:T(1,128)}) custom-call(s32[2,1024]{1,0:T(2,128)} %get-tuple-element.60.slots_ref, f32[2,1024]{1,0:T(2,128)} %get-tuple-element.72.routes_ref, bf16[1024,768]{1,0:T(8,128)(2,1)} %cot_ref.7), custom_call_target="tpu_custom_call" | custom-call | tf_op jit(solution)/shard_map/pallas_call | solution.py:108
  24.0 5.4 all-to-all-start.1
  32.6 5.8 %all-to-all-start.2 = ((bf16[8,224,768]{2,1,0:T(8,128)(2,1)}), bf16[8,224,768]{2,1,0:T(8,128)(2,1)}, u32[]{:S(2)}, u32[]{:S(2)}) async-start(bf16[8,224,768]{2,1,0:T(8,128)(2,1)} %get-tuple-element.74), calls=%async_computation.2 | async-start | bytes 5505024 | tf_op jit(solution)/shard_map/all_to_all | solution.py:936
  40.1 33.9 %collective-permute-done.6 = bf16[1,2,72,768]{3,2,1,0:T(8,128)(2,1)S(1)} collective-permute-done((bf16[1,2,72,768]{3,2,1,0:T(8,128)(2,1)S(1)}, bf16[1,2,72,768]{3,2,1,0:T(8,128)(2,1)S(1)}, u32[]{:S(2)}, u32[]{:S(2)}) %collective-permute-start.6) | collective-permute-done | bytes 221216 | tf_op jit(solution)/shard_map/ppermute | solution.py:862
  77.0 8.1 %collective-permute-done.7 = bf16[2,2,72,768]{3,2,1,0:T(8,128)(2,1)S(1)} collective-permute-done((bf16[2,2,72,768]{3,2,1,0:T(8,128)(2,1)S(1)}, bf16[2,2,72,768]{3,2,1,0:T(8,128)(2,1)S(1)}, u32[]{:S(2)}, u32[]{:S(2)}) %collective-permute-start.7) | collective-permute-done | bytes 442400 | tf_op jit(solution)/shard_map/ppermute | solution.py:862
  90.8 7.9 %shard_map.249 = (bf16[768,768]{1,0:T(8,128)(2,1)}, bf16[768,768]{1,0:T(8,128)(2,1)}, bf16[768,768]{1,0:T(8,128)(2,1)}, bf16[1024,768]{1,0:T(8,128)(2,1)}, bf16[...) custom-call(s32[1]{0:T(128)} %bitcast.1.owner_ref, bf16[1024,768]{1,0:T(8,128)(2,1)} %inputs_ref.5, ...), custom_call_target="tpu_custom_call" | custom-call | tf_op jit(solution)/shard_map/pallas_call | solution.py:660
  98.7 14.8 %shard_map.250 = (bf16[1024,768]{1,0:T(8,128)(2,1)}, f32[6,2,1024]{2,1,0:T(2,128)}) custom-call(bf16[1024,768]{1,0:T(8,128)(2,1)} %get-tuple-element.64.query_ref, bf16[1024,768]{1,0:T(8,128)(2,1)} %get-tuple-element.65.key_ref, bf16[1024,768]{1,0:T(8,128)(2,1)} %get-tuple-element.66.value_ref, f32[6,2,256]{2,1,0:T(2,128)} %get-tuple-element.62.refs_4_.near_ref), custom_call_target="tpu_custom_call" | custom-call | tf_op jit(solution)/shard_map/pallas_call | solution.py:528
  113.5 9.7 %shard_map.251 = (f32[1024,768]{1,0:T(8,128)}, bf16[1024,768]{1,0:T(8,128)(2,1)}, f32[2,1024]{1,0:T(2,128)}, bf16[1280,768]{1,0:T(8,128)(2,1)}) custom-call(bf16[1024,768]{1,0:T(8,128)(2,1)} %get-tuple-element.67.mixed_ref.out_ref, bf16[768,768]{1,0:T(8,128)(2,1)} %all-gather.2.cloned.1.call-done.merge_ref, bf16[1024,768]{1,0:T(8,128)(2,1)} %inputs_ref.5, ...), custom_call_target="tpu_custom_call" | custom-call | tf_op jit(solution)/shard_map/pallas_call | solution.py:705
  123.2 5.6 %all-to-all-start = ((bf16[8,160,768]{2,1,0:T(8,128)(2,1)}), bf16[8,160,768]{2,1,0:T(8,128)(2,1)}, u32[]{:S(2)}, u32[]{:S(2)}) async-start(bf16[8,160,768]{2,1,0:T(8,128)(2,1)} %bitcast.48), calls=%async_computation | async-start | bytes 3932160 | tf_op jit(solution)/shard_map/all_to_all | solution.py:936
  129.9 20.4 %all-to-all-done.rows_ref = bf16[8,160,768]{2,1,0:T(8,128)(2,1)} async-done(((bf16[8,160,768]{2,1,0:T(8,128)(2,1)}), bf16[8,160,768]{2,1,0:T(8,128)(2,1)}, u32[]{:S(2)}, u32[]{:S(2)}) %all-to-all-start) | async-done | bytes 1966112 | tf_op jit(solution)/shard_map/all_to_all | solution.py:936
  150.2 18.5 %shard_map.253 = (bf16[1280,3072]{1,0:T(8,128)(2,1)}, bf16[1280,3072]{1,0:T(8,128)(2,1)}, bf16[4,768,768]{2,1,0:T(8,128)(2,1)}, bf16[1280,768]{1,0:T(8,128)(2,1)}) custom-call(s32[1]{0:T(128)} %bitcast.1.owner_ref, bf16[8,160,768]{2,1,0:T(8,128)(2,1)} %all-to-all-done.rows_ref, f32[1,1280]{1,0:T(1,128)} %reshape_squeeze.6.other_ref.refs_0_, ...), custom_call_target="tpu_custom_call" | custom-call | tf_op jit(solution)/shard_map/pallas_call | solution.py:181
  169.4 8.3 %shard_map.256 = bf16[8,256,768]{2,1,0:T(8,128)(2,1)} custom-call(s32[2,1024]{1,0:T(2,128)} %get-tuple-element.60.slots_ref, bf16[1024,768]{1,0:T(8,128)(2,1)} %get-tuple-element.81.rows_ref, bf16[1024,768]{1,0:T(8,128)(2,1)} %cot_ref.7, f32[1,1280]{1,0:T(1,128)} %reshape_squeeze.6.other_ref.refs_0_, f32[1,1280]{1,0:T(1,128)} %reshape_squeeze.7.refs_1_.other_ref), custom_call_target="tpu_custom_call" | custom-call | tf_op jit(solution)/shard_map/pallas_call | solution.py:81
  177.7 8.3 %all-to-all-start.4 = ((bf16[8,256,768]{2,1,0:T(8,128)(2,1)}), bf16[8,256,768]{2,1,0:T(8,128)(2,1)}, u32[]{:S(2)}, u32[]{:S(2)}) async-start(bf16[8,256,768]{2,1,0:T(8,128)(2,1)} %shard_map.256), calls=%async_computation.4 | async-start | bytes 6291456 | tf_op jit(solution)/shard_map/all_to_all | solution.py:936
  186.0 37.6 %shard_map.254 = (bf16[8,2,160,768]{3,2,1,0:T(8,128)(2,1)}, bf16[4,2304,768]{2,1,0:T(8,128)(2,1)}) custom-call(bf16[8,160,768]{2,1,0:T(8,128)(2,1)} %all-to-all-done.rows_ref, bf16[1280,768]{1,0:T(8,128)(2,1)} %get-tuple-element.75.grad_ref, bf16[1280,3072]{1,0:T(8,128)(2,1)} %get-tuple-element.76.act_ref, bf16[1280,3072]{1,0:T(8,128)(2,1)} %get-tuple-element.77.pre_ref, ...), custom_call_target="tpu_custom_call" | custom-call | tf_op jit(solution)/shard_map/pallas_call | solution.py:238
  223.6 20.0 %shard_map.257 = (bf16[1280,3072]{1,0:T(8,128)(2,1)}, bf16[1280,3072]{1,0:T(8,128)(2,1)}, bf16[4,2304,768]{2,1,0:T(8,128)(2,1)}, bf16[1280,768]{1,0:T(8,128)(2,1)}) custom-call(s32[1]{0:T(128)} %bitcast.1.owner_ref, bf16[8,256,768]{2,1,0:T(8,128)(2,1)} %all-to-all-done.4.rows_ref.refs_1_, ...), custom_call_target="tpu_custom_call", output_to_operand_aliasing={{2}: (7, {})} | custom-call | tf_op jit(solution)/shard_map/pallas_call | solution.py:181
  243.6 19.4 %shard_map.258 = (bf16[1280,3072]{1,0:T(8,128)(2,1)}, bf16[4,2304,768]{2,1,0:T(8,128)(2,1)}) custom-call(bf16[8,256,768]{2,1,0:T(8,128)(2,1)} %all-to-all-done.4.rows_ref.refs_1_, bf16[1280,768]{1,0:T(8,128)(2,1)} %get-tuple-element.84.grad_ref, bf16[1280,3072]{1,0:T(8,128)(2,1)} %get-tuple-element.85.pre_ref, ...), custom_call_target="tpu_custom_call", output_to_operand_aliasing={{1}: (4, {})} | custom-call | tf_op jit(solution)/shard_map/pallas_call | solution.py:269
  263.0 4.8 all-to-all-start.3
  267.7 21.8 %shard_map.259 = bf16[8,2,160,768]{3,2,1,0:T(8,128)(2,1)} custom-call(bf16[1280,3072]{1,0:T(8,128)(2,1)} %get-tuple-element.83.act_ref, bf16[1280,3072]{1,0:T(8,128)(2,1)} %get-tuple-element.87.low_ref, bf16[2,768,3072]{2,1,0:T(8,128)(2,1)} %up_ref.7, bf16[2,3072,768]{2,1,0:T(8,128)(2,1)} %down_ref.5), custom_call_target="tpu_custom_call" | custom-call | tf_op jit(solution)/shard_map/pallas_call | solution.py:307
  289.6 20.6 %all-to-all-done.3.made_ref.back_ref = bf16[8,2,160,768]{3,2,1,0:T(8,128)(2,1)} async-done(((bf16[8,2,160,768]{3,2,1,0:T(8,128)(2,1)}), bf16[8,2,160,768]{3,2,1,0:T(8,128)(2,1)}, u32[]{:S(2)}, u32[]{:S(2)}) %all-to-all-start.3) | async-done | bytes 3932192 | tf_op jit(solution)/shard_map/all_to_all | solution.py:936
  310.2 8.8 %all-to-all-start.5 = ((bf16[8,2,160,768]{3,2,1,0:T(8,128)(2,1)}), bf16[8,2,160,768]{3,2,1,0:T(8,128)(2,1)}, u32[]{:S(2)}, u32[]{:S(2)}) async-start(bf16[8,2,160,768]{3,2,1,0:T(8,128)(2,1)} %shard_map.259), calls=%async_computation.5 | async-start | bytes 7864320 | tf_op jit(solution)/shard_map/all_to_all | solution.py:936
  319.7 11.2 %shard_map.255 = (f32[1024,768]{1,0:T(8,128)}, f32[1024,128]{1,0:T(8,128)}, f32[1024,768]{1,0:T(8,128)}) custom-call(s32[2,1024]{1,0:T(2,128)} %get-tuple-element.60.slots_ref, f32[2,1024]{1,0:T(2,128)} %get-tuple-element.69.gates_ref, f32[1024,768]{1,0:T(8,128)} %get-tuple-element.70.resid_ref, bf16[1024,768]{1,0:T(8,128)(2,1)} %cot_ref.7, ...), custom_call_target="tpu_custom_call" | custom-call | tf_op jit(solution)/shard_map/pallas_call | solution.py:357
  331.0 30.5 %all-to-all-done.5.made_ref.back_ref = bf16[8,2,160,768]{3,2,1,0:T(8,128)(2,1)} async-done(((bf16[8,2,160,768]{3,2,1,0:T(8,128)(2,1)}), bf16[8,2,160,768]{3,2,1,0:T(8,128)(2,1)}, u32[]{:S(2)}, u32[]{:S(2)}) %all-to-all-start.5) | async-done | bytes 3932192 | tf_op jit(solution)/shard_map/all_to_all | solution.py:936
  361.5 9.4 %shard_map.260 = (bf16[1024,768]{1,0:T(8,128)(2,1)}, bf16[1024,128]{1,0:T(8,128)(2,1)}) custom-call(s32[2,1024]{1,0:T(2,128)} %get-tuple-element.60.slots_ref, s32[2,1024]{1,0:T(2,128)} %bitcast.52, f32[2,1024]{1,0:T(2,128)} %get-tuple-element.69.gates_ref, f32[1024,768]{1,0:T(8,128)} %get-tuple-element.79.result_ref, ...), custom_call_target="tpu_custom_call" | custom-call | tf_op jit(solution)/shard_map/pallas_call | solution.py:398
  370.8 10.6 %shard_map.261 = (f32[1024,768]{1,0:T(8,128)}, bf16[1024,768]{1,0:T(8,128)(2,1)}, bf16[1024,768]{1,0:T(8,128)(2,1)}, f32[1,768]{1,0:T(1,128)}) custom-call(s32[2,1024]{1,0:T(2,128)} %get-tuple-element.60.slots_ref, bf16[1024,128]{1,0:T(8,128)(2,1)} %get-tuple-element.89.logit_ref, bf16[128,768]{1,0:T(8,128)(2,1)} %pad.35.router_ref, ...), custom_call_target="tpu_custom_call" | custom-call | tf_op jit(solution)/shard_map/pallas_call | solution.py:434
  381.4 35.6 %shard_map.262 = (bf16[3,1024,768]{2,1,0:T(8,128)(2,1)}, f32[6,4,256]{2,1,0:T(4,128)}) custom-call(bf16[1024,768]{1,0:T(8,128)(2,1)} %get-tuple-element.64.query_ref, bf16[1024,768]{1,0:T(8,128)(2,1)} %get-tuple-element.65.key_ref, bf16[1024,768]{1,0:T(8,128)(2,1)} %get-tuple-element.66.value_ref, bf16[1024,768]{1,0:T(8,128)(2,1)} %get-tuple-element.91.grad_ref, ...), custom_call_target="tpu_custom_call" | custom-call | tf_op jit(solution)/shard_map/pallas_call | solution.py:609
  417.0 11.4 %shard_map.264 = bf16[4,768,768]{2,1,0:T(8,128)(2,1)} custom-call(bf16[1024,768]{1,0:T(8,128)(2,1)} %get-tuple-element.99.left_ref, bf16[1024,768]{1,0:T(8,128)(2,1)} %get-tuple-element.67.mixed_ref.out_ref, bf16[3,1024,768]{2,1,0:T(8,128)(2,1)} %get-tuple-element.93.heads_ref, bf16[1024,768]{1,0:T(8,128)(2,1)} %get-tuple-element.100.branch_ref), custom_call_target="tpu_custom_call" | custom-call | tf_op jit(solution)/shard_map/pallas_call | solution.py:767
  434.5 9.9 %shard_map.263 = (f32[1024,768]{1,0:T(8,128)}, f32[1,768]{1,0:T(1,128)}) custom-call(bf16[3,1024,768]{2,1,0:T(8,128)(2,1)} %get-tuple-element.93.heads_ref, bf16[768,768]{1,0:T(8,128)(2,1)} %get-tuple-element.94.query_ref, bf16[768,768]{1,0:T(8,128)(2,1)} %get-tuple-element.95.key_ref, bf16[768,768]{1,0:T(8,128)(2,1)} %get-tuple-element.96.value_ref, ...), custom_call_target="tpu_custom_call" | custom-call | tf_op jit(solution)/shard_map/pallas_call | solution.py:734
  455.1 11.6 %collective-permute-done.13 = bf16[4,96,768]{2,1,0:T(8,128)(2,1)} collective-permute-done((bf16[4,96,768]{2,1,0:T(8,128)(2,1)S(1)}, bf16[4,96,768]{2,1,0:T(8,128)(2,1)}, u32[]{:S(2)}, u32[]{:S(2)}) %collective-permute-start.13) | collective-permute-done | bytes 589856 | tf_op jit(solution)/shard_map/ppermute | solution.py:862
  473.7 4.6 collective-permute-done.14
  484.6 9.1 %collective-permute-done.15 = bf16[104,768]{1,0:T(8,128)(2,1)S(1)} collective-permute-done((bf16[104,768]{1,0:T(8,128)(2,1)S(1)}, bf16[104,768]{1,0:T(8,128)(2,1)S(1)}, u32[]{:S(2)}, u32[]{:S(2)}) %collective-permute-start.15) | collective-permute-done | bytes 159776 | tf_op jit(solution)/shard_map/ppermute | solution.py:867
  493.7 15.2 %collective-permute-done.16 = bf16[104,768]{1,0:T(8,128)(2,1)S(1)} collective-permute-done((bf16[104,768]{1,0:T(8,128)(2,1)S(1)}, bf16[104,768]{1,0:T(8,128)(2,1)S(1)}, u32[]{:S(2)}, u32[]{:S(2)}) %collective-permute-start.16) | collective-permute-done | bytes 159776 | tf_op jit(solution)/shard_map/ppermute | solution.py:867
  532.6 6.1 %shard_map.266 = (f32[1536,768]{1,0:T(8,128)}, f32[1536,768]{1,0:T(8,128)}) custom-call(bf16[2304,768]{1,0:T(8,128)(2,1)} %reduce-scatter.3.cloned.1.call-done.rows_ref, f32[1536,768]{1,0:T(8,128)} %shard_map.265.into_ref), custom_call_target="tpu_custom_call", output_to_operand_aliasing={{1}: (1, {})} | custom-call | tf_op jit(solution)/shard_map/pallas_call | solution.py:811
  (154 shorter events, 78.5 us)
Async XLA Ops:
  10.8 18.6 %collective-permute-start = (bf16[96,768]{1,0:T(8,128)(2,1)S(1)}, bf16[96,768]{1,0:T(8,128)(2,1)S(1)}, u32[]{:S(2)}, u32[]{:S(2)}) collective-permute-start(bf16[96,768]{1,0:T(8,128)(2,1)S(1)} %concatenate.74), channel_id=1, source_target_pairs={{0,1},{1,2},{2,3},{3,0},{4,5},{5,6},{6,7},{7,4},{8,9},{9,10},{10,1... | collective-permute-start | bytes 442376 | tf_op jit(solution)/shard_map/ppermute | solution.py:867
  12.2 17.3 %collective-permute-start.1 = (bf16[96,768]{1,0:T(8,128)(2,1)S(1)}, bf16[96,768]{1,0:T(8,128)(2,1)S(1)}, u32[]{:S(2)}, u32[]{:S(2)}) collective-permute-start(bf16[96,768]{1,0:T(8,128)(2,1)S(1)} %concatenate.74), channel_id=1, source_target_pairs={{0,2},{1,3},{2,0},{3,1},{4,6},{5,7},{6,4},{7,5},{8,10},{9,11},{10,... | collective-permute-start | bytes 442376 | tf_op jit(solution)/shard_map/ppermute | solution.py:867
  13.3 25.2 %collective-permute-start.2 = (bf16[96,768]{1,0:T(8,128)(2,1)S(1)}, bf16[96,768]{1,0:T(8,128)(2,1)S(1)}, u32[]{:S(2)}, u32[]{:S(2)}) collective-permute-start(bf16[96,768]{1,0:T(8,128)(2,1)S(1)} %concatenate.74), channel_id=1, source_target_pairs={{0,3},{1,0},{2,1},{3,2},{4,7},{5,4},{6,5},{7,6},{8,11},{9,8},{10,9... | collective-permute-start | bytes 442376 | tf_op jit(solution)/shard_map/ppermute | solution.py:867
  24.0 8.6 %all-to-all-start.1 = ((f32[8,1,320]{2,1,0:T(1,128)}), f32[8,1,320]{2,1,0:T(1,128)S(1)}, u32[]{:S(2)}, u32[]{:S(2)}) async-start(f32[8,1,320]{2,1,0:T(1,128)} %get-tuple-element.73), calls=%async_computation.1 | async-start | bytes 24576 | tf_op jit(solution)/shard_map/all_to_all | solution.py:936
  32.6 90.6 %all-to-all-start.2 = ((bf16[8,224,768]{2,1,0:T(8,128)(2,1)}), bf16[8,224,768]{2,1,0:T(8,128)(2,1)}, u32[]{:S(2)}, u32[]{:S(2)}) async-start(bf16[8,224,768]{2,1,0:T(8,128)(2,1)} %get-tuple-element.74), calls=%async_computation.2 | async-start | bytes 5505024 | tf_op jit(solution)/shard_map/all_to_all | solution.py:936
  38.5 75.0 %all-gather.2.cloned.1.call-start = ((), (), s32[]{:S(2)}) async-start(), calls=%async_computation.8 | async-start | bytes 1474560 | tf_op jit(solution)/shard_map/all_gather | solution.py:1001
  38.5 35.4 %collective-permute-start.6 = (bf16[1,2,72,768]{3,2,1,0:T(8,128)(2,1)S(1)}, bf16[1,2,72,768]{3,2,1,0:T(8,128)(2,1)S(1)}, u32[]{:S(2)}, u32[]{:S(2)}) collective-permute-start(bf16[1,2,72,768]{3,2,1,0:T(8,128)(2,1)S(1)} %get-tuple-element.121), channel_id=1, source_target_pairs={{0,16},{4,20},{8,24},{12,28},{16,0},{20,4},{24,8},{28,12},{1,17},{... | collective-permute-start | bytes 663560 | tf_op jit(solution)/shard_map/ppermute | solution.py:862
  38.7 36.8 %collective-permute-start.3 = (bf16[1,2,72,768]{3,2,1,0:T(8,128)(2,1)S(1)}, bf16[1,2,72,768]{3,2,1,0:T(8,128)(2,1)S(1)}, u32[]{:S(2)}, u32[]{:S(2)}) collective-permute-start(bf16[1,2,72,768]{3,2,1,0:T(8,128)(2,1)S(1)} %get-tuple-element.122), channel_id=1, source_target_pairs={{0,8},{4,12},{8,0},{12,4},{16,24},{20,28},{24,16},{28,20},{1,9},{5... | collective-permute-start | bytes 663560 | tf_op jit(solution)/shard_map/ppermute | solution.py:862
  74.0 11.1 %collective-permute-start.7 = (bf16[2,2,72,768]{3,2,1,0:T(8,128)(2,1)S(1)}, bf16[2,2,72,768]{3,2,1,0:T(8,128)(2,1)S(1)}, u32[]{:S(2)}, u32[]{:S(2)}) collective-permute-start(bf16[2,2,72,768]{3,2,1,0:T(8,128)(2,1)S(1)} %pad_maximum_fusion.4), channel_id=1, source_target_pairs={{0,8},{4,12},{8,0},{12,4},{16,24},{20,28},{24,16},{28,20},{1,9},{5... | collective-permute-start | bytes 1327112 | tf_op jit(solution)/shard_map/ppermute | solution.py:862
  75.5 11.3 %collective-permute-start.4 = (bf16[2,2,72,768]{3,2,1,0:T(8,128)(2,1)S(1)}, bf16[2,2,72,768]{3,2,1,0:T(8,128)(2,1)S(1)}, u32[]{:S(2)}, u32[]{:S(2)}) collective-permute-start(bf16[2,2,72,768]{3,2,1,0:T(8,128)(2,1)S(1)} %pad_maximum_fusion.3), channel_id=1, source_target_pairs={{0,16},{4,20},{8,24},{12,28},{16,0},{20,4},{24,8},{28,12},{1,17},{... | collective-permute-start | bytes 1327112 | tf_op jit(solution)/shard_map/ppermute | solution.py:862
  85.2 5.6 %collective-permute-start.8 = (bf16[4,2,72,768]{3,2,1,0:T(8,128)(2,1)S(1)}, bf16[4,2,72,768]{3,2,1,0:T(8,128)(2,1)}, u32[]{:S(2)}, u32[]{:S(2)}) collective-permute-start(bf16[4,2,72,768]{3,2,1,0:T(8,128)(2,1)S(1)} %pad_maximum_fusion.1.refs_2_), channel_id=1, source_target_pairs={{0,4},{4,0},{8,12},{12,8},{16,20},{20,16},{24,28},{28,24},{1,5},{5... | collective-permute-start | bytes 2654216 | tf_op jit(solution)/shard_map/ppermute | solution.py:862
  86.9 3.9 collective-permute-start.5
  123.2 27.0 %all-to-all-start = ((bf16[8,160,768]{2,1,0:T(8,128)(2,1)}), bf16[8,160,768]{2,1,0:T(8,128)(2,1)}, u32[]{:S(2)}, u32[]{:S(2)}) async-start(bf16[8,160,768]{2,1,0:T(8,128)(2,1)} %bitcast.48), calls=%async_computation | async-start | bytes 3932160 | tf_op jit(solution)/shard_map/all_to_all | solution.py:936
  128.8 401.2 %reduce-scatter.5.cloned.1.call-start = ((), (), s32[]{:S(2)}) async-start(), calls=%async_computation.10 | async-start | bytes 5898240 | tf_op jit(solution)/shard_map/reduce_scatter | solution.py:932
  177.7 45.8 %all-to-all-start.4 = ((bf16[8,256,768]{2,1,0:T(8,128)(2,1)}), bf16[8,256,768]{2,1,0:T(8,128)(2,1)}, u32[]{:S(2)}, u32[]{:S(2)}) async-start(bf16[8,256,768]{2,1,0:T(8,128)(2,1)} %shard_map.256), calls=%async_computation.4 | async-start | bytes 6291456 | tf_op jit(solution)/shard_map/all_to_all | solution.py:936
  186.0 346.6 %reduce-scatter.3.cloned.1.call-start = ((), (), s32[]{:S(2)}) async-start(), calls=%async_computation.9 | async-start | bytes 17694720 | tf_op jit(solution)/shard_map/reduce_scatter | solution.py:932
  263.0 47.2 %all-to-all-start.3 = ((bf16[8,2,160,768]{3,2,1,0:T(8,128)(2,1)}), bf16[8,2,160,768]{3,2,1,0:T(8,128)(2,1)}, u32[]{:S(2)}, u32[]{:S(2)}) async-start(bf16[8,2,160,768]{3,2,1,0:T(8,128)(2,1)} %get-tuple-element.78), calls=%async_computation.3 | async-start | bytes 7864320 | tf_op jit(solution)/shard_map/all_to_all | solution.py:936
  310.2 51.3 %all-to-all-start.5 = ((bf16[8,2,160,768]{3,2,1,0:T(8,128)(2,1)}), bf16[8,2,160,768]{3,2,1,0:T(8,128)(2,1)}, u32[]{:S(2)}, u32[]{:S(2)}) async-start(bf16[8,2,160,768]{3,2,1,0:T(8,128)(2,1)} %shard_map.259), calls=%async_computation.5 | async-start | bytes 7864320 | tf_op jit(solution)/shard_map/all_to_all | solution.py:936
  431.7 16.3 %collective-permute-start.9 = (bf16[4,384,768]{2,1,0:T(8,128)(2,1)}, bf16[4,384,768]{2,1,0:T(8,128)(2,1)}, u32[]{:S(2)}, u32[]{:S(2)}) collective-permute-start(bf16[4,384,768]{2,1,0:T(8,128)(2,1)} %constant_dynamic-slice_fusion.3), channel_id=1, source_target_pairs={{0,4},{4,0},{8,12},{12,8},{16,20},{20,16},{24,28},{28,24},{1,5},{5... | collective-permute-start | bytes 7077896 | tf_op jit(solution)/shard_map/ppermute | solution.py:862
  446.4 1.5 collective-permute-start.12
  451.3 15.4 %collective-permute-start.13 = (bf16[4,96,768]{2,1,0:T(8,128)(2,1)S(1)}, bf16[4,96,768]{2,1,0:T(8,128)(2,1)}, u32[]{:S(2)}, u32[]{:S(2)}) collective-permute-start(bf16[4,96,768]{2,1,0:T(8,128)(2,1)S(1)} %fusion.1), channel_id=1, source_target_pairs={{0,16},{4,20},{8,24},{12,28},{16,0},{20,4},{24,8},{28,12},{1,17},{... | collective-permute-start | bytes 1769480 | tf_op jit(solution)/shard_map/ppermute | solution.py:862
  455.1 16.8 %collective-permute-start.10 = (bf16[4,112,768]{2,1,0:T(8,128)(2,1)}, bf16[4,112,768]{2,1,0:T(8,128)(2,1)}, u32[]{:S(2)}, u32[]{:S(2)}) collective-permute-start(bf16[4,112,768]{2,1,0:T(8,128)(2,1)} %constant_dynamic-slice_fusion.2), channel_id=1, source_target_pairs={{0,8},{4,12},{8,0},{12,4},{16,24},{20,28},{24,16},{28,20},{1,9},{5... | collective-permute-start | bytes 2064392 | tf_op jit(solution)/shard_map/ppermute | solution.py:862
  468.1 10.2 %collective-permute-start.14 = (bf16[4,48,768]{2,1,0:T(8,128)(2,1)S(1)}, bf16[4,48,768]{2,1,0:T(8,128)(2,1)S(1)}, u32[]{:S(2)}, u32[]{:S(2)}) collective-permute-start(bf16[4,48,768]{2,1,0:T(8,128)(2,1)S(1)} %constant_dynamic-slice_fusion), channel_id=1, source_target_pairs={{0,8},{4,12},{8,0},{12,4},{16,24},{20,28},{24,16},{28,20},{1,9},{5... | collective-permute-start | bytes 884744 | tf_op jit(solution)/shard_map/ppermute | solution.py:862
  473.3 7.6 %collective-permute-start.11 = (bf16[4,56,768]{2,1,0:T(8,128)(2,1)S(1)}, bf16[4,56,768]{2,1,0:T(8,128)(2,1)S(1)}, u32[]{:S(2)}, u32[]{:S(2)}) collective-permute-start(bf16[4,56,768]{2,1,0:T(8,128)(2,1)S(1)} %constant_dynamic-slice_fusion.1), channel_id=1, source_target_pairs={{0,16},{4,20},{8,24},{12,28},{16,0},{20,4},{24,8},{28,12},{1,17},{... | collective-permute-start | bytes 1032200 | tf_op jit(solution)/shard_map/ppermute | solution.py:862
  481.0 12.7 %collective-permute-start.15 = (bf16[104,768]{1,0:T(8,128)(2,1)S(1)}, bf16[104,768]{1,0:T(8,128)(2,1)S(1)}, u32[]{:S(2)}, u32[]{:S(2)}) collective-permute-start(bf16[104,768]{1,0:T(8,128)(2,1)S(1)} %get-tuple-element.118), channel_id=1, source_target_pairs={{0,1},{1,2},{2,3},{3,0},{4,5},{5,6},{6,7},{7,4},{8,9},{9,10},{10,1... | collective-permute-start | bytes 479240 | tf_op jit(solution)/shard_map/ppermute | solution.py:867
  481.1 27.8 %collective-permute-start.16 = (bf16[104,768]{1,0:T(8,128)(2,1)S(1)}, bf16[104,768]{1,0:T(8,128)(2,1)S(1)}, u32[]{:S(2)}, u32[]{:S(2)}) collective-permute-start(bf16[104,768]{1,0:T(8,128)(2,1)S(1)} %get-tuple-element.119), channel_id=1, source_target_pairs={{0,2},{1,3},{2,0},{3,1},{4,6},{5,7},{6,4},{7,5},{8,10},{9,11},{10,... | collective-permute-start | bytes 479240 | tf_op jit(solution)/shard_map/ppermute | solution.py:867
  484.6 25.5 %collective-permute-start.17 = (bf16[104,768]{1,0:T(8,128)(2,1)S(1)}, bf16[104,768]{1,0:T(8,128)(2,1)S(1)}, u32[]{:S(2)}, u32[]{:S(2)}) collective-permute-start(bf16[104,768]{1,0:T(8,128)(2,1)S(1)} %get-tuple-element.120), channel_id=1, source_target_pairs={{0,3},{1,0},{2,1},{3,2},{4,7},{5,4},{6,5},{7,6},{8,11},{9,8},{10,9... | collective-permute-start | bytes 479240 | tf_op jit(solution)/shard_map/ppermute | solution.py:867
  510.2 3.4 collective-permute-start.20
  511.9 3.6 collective-permute-start.18
  513.6 5.0 collective-permute-start.21
  515.5 4.6 collective-permute-start.19
  520.3 5.8 %collective-permute-start.22 = (bf16[416,768]{1,0:T(8,128)(2,1)S(1)}, bf16[416,768]{1,0:T(8,128)(2,1)S(1)}, u32[]{:S(2)}, u32[]{:S(2)}) collective-permute-start(bf16[416,768]{1,0:T(8,128)(2,1)S(1)} %pad_maximum_fusion.2), channel_id=1, source_target_pairs={{0,4},{4,0},{8,12},{12,8},{16,20},{20,16},{24,28},{28,24},{1,5},{5... | collective-permute-start | bytes 1916936 | tf_op jit(solution)/shard_map/ppermute | solution.py:862
  (13 other events, 134.3 us)
Sparse Core Ops, SparseCore 0:
  40.8 28.2 all-gather.1
  168.9 85.5 reduce-scatter.4
  263.1 248.9 reduce-scatter.2

commit v11 on v10

--- a/solution.py
+++ b/solution.py
@@ -84,7 +84,7 @@
         in_specs=[whole(slots.shape), whole(rows.shape), whole(cot.shape)] + [pl.BlockSpec(memory_space=pl.ANY)] * len(after),
         out_specs=pl.BlockSpec((1, total, width), lambda i: (i, 0, 0)),
         out_shape=jax.ShapeDtypeStruct((owners, total, width), rows.dtype),
-        compiler_params=pltpu.CompilerParams(vmem_limit_bytes=62 << 20),
+        compiler_params=pltpu.CompilerParams(vmem_limit_bytes=48 << 20),
     )(slots, rows, cot, *after)
 
 
@@ -853,6 +853,42 @@
     )(small, near)
 
 
+def pack_kernel(owner_ref, query_ref, key_ref, value_ref, one_ref, two_ref, table_ref, router_ref, out_ref, tall, *, router_at):
+    del owner_ref
+    piece = query_ref.shape[0]
+    experts, part = router_ref.shape
+    heads, buckets = table_ref.shape
+    tall[...] = jnp.zeros_like(tall)
+    tall[0:1, :part] = one_ref[...].astype(jnp.float32).reshape(1, part)
+    tall[1:2, :part] = two_ref[...].astype(jnp.float32).reshape(1, part)
+    tall[2:2 + heads, :buckets] = table_ref[...].astype(jnp.float32)
+    tall[router_at:router_at + experts, :part] = router_ref[...].astype(jnp.float32)
+    for index, ref in enumerate((query_ref, key_ref, value_ref)):
+        out_ref[index * piece:(index + 1) * piece, :] = ref[...]
+    out_ref[3 * piece:, :] = tall[...].astype(out_ref.dtype)
+
+
+def pack_first(owner, weights, one, two, table, router, piece, small_rows, router_at):
+    width = weights[0].shape[1]
+    if piece % 8 == 0:
+        rows = pl.BlockSpec((piece, width), lambda i, owner: (owner[0], 0))
+    else:
+        weights = [lax.dynamic_slice_in_dim(weight, owner[0] * piece, piece, 0) for weight in weights]
+        rows = pl.BlockSpec((piece, width), lambda i, owner: (0, 0))
+    whole = lambda shape: pl.BlockSpec(shape, lambda i, owner: (0,) * len(shape))
+    return pl.pallas_call(
+        partial(pack_kernel, router_at=router_at),
+        grid_spec=pltpu.PrefetchScalarGridSpec(
+            num_scalar_prefetch=1,
+            grid=(1,),
+            in_specs=[rows, rows, rows, whole(one.shape), whole(two.shape), whole(table.shape), whole(router.shape)],
+            out_specs=whole((3 * piece + small_rows, width)),
+            scratch_shapes=[pltpu.VMEM((small_rows, width), jnp.float32)],
+        ),
+        out_shape=jax.ShapeDtypeStruct((3 * piece + small_rows, width), weights[0].dtype),
+    )(owner, *weights, one, two, table, router)
+
+
 OWNER = "expert"
 LINE = "shard"
 
@@ -983,12 +1019,12 @@
         gap = jnp.zeros((router_at - 2 - local_heads, width), bf16)
         return jnp.concatenate([widen(head), widen(table), gap, widen(router)], axis=0)
 
-    small = pack(norm_gain[None], expert_gain[None], bias_table.T, router_weight.T)
-    slices = [
-        lax.dynamic_slice_in_dim(weight, me * piece, piece, 0)
-        for weight in (query_weight, key_weight, value_weight)
-    ]
-    lined = gather_line(jnp.concatenate(slices + [small]))
+    owner = me.astype(jnp.int32).reshape(1)
+    first = pack_first(
+        owner, [query_weight, key_weight, value_weight], norm_gain, expert_gain,
+        bias_table.T, router_weight.T, piece, router_at + experts, router_at,
+    )
+    lined = gather_line(first)
     small_full = lined[:, 3 * piece :]
     bits = [1 << level for level in range(owners.bit_length() - 1)]
     pieces = []
@@ -1017,7 +1053,6 @@
     )
     other = share_rows(other).reshape(owners, local_count, capacity)
 
-    owner = me.astype(jnp.int32).reshape(1)
     query_full, key_full, value_full, low_one, queries, keys, values = project(
         owner, inputs, gain_one, pieces, epsilon, after=(near, router_full)
     )

time: 554 us -> 553 us (level)
  the two profiles are of different devices: /device:TPU:13 before, /device:TPU:9 now
where the time goes in v11:
time: 553 us; the launch traced here: 545 us
  Pallas kernels  265 us (48%)
  waiting for transfers between devices  174 us (31%)
  starting transfers between devices  65.4 us (12%)
  local copies, waits for them, and re-layouts  14.8 us (3%)
  between operations  14.4 us (3%)
  other arithmetic  9.97 us (2%)
    all_to_all x6, waiting for transfers between devices, share_rows(): return lax.all_to_all(rows, OWNER, 0, 0, tiled=True)  76.2 us
    ppermute x17, waiting for transfers between devices, exchange(): return lax.ppermute(rows, OWNER, [(i, i ^ bit) for i in range(count)])  72 us
    pallas_call x2, Pallas kernels, expert_first(): pl.pallas_call(partial(first_kernel, index=index, local_count=local_count...  38.4 us
    pallas_call x1, Pallas kernels, expert_second(): pl.pallas_call(second_kernel, grid=(shards,), in_specs=[arrived_spec(rows...  37.5 us
    pallas_call x1, Pallas kernels, attend_back(): pl.pallas_call(partial(attend_back_kernel, block=block, size=size, scale=...  35.6 us
    all_to_all x6, starting transfers between devices, share_rows(): return lax.all_to_all(rows, OWNER, 0, 0, tiled=True)  35 us
    ppermute x6, waiting for transfers between devices, shift(): lax.ppermute(rows, LINE, [(i, (i + step) % count) for i in range(count)])  26 us
    ppermute x17, starting transfers between devices, exchange(): return lax.ppermute(rows, OWNER, [(i, i ^ bit) for i in range(count)])  22.9 us
  transfers between devices with their start and end apart: 32, of which 19 were waited for; matrix products, arithmetic and copies ran while one was open for 4% of the time, Pallas kernels for 44%

profile of v11, /device:TPU:9, one launch (start us, length us, event | category | flops | bytes accessed | tf_op | source)
XLA Modules:
  0.0 544.9 jit_solution(198646943068186931)
XLA Ops:
  14.1 7.8 %shard_map.253 = (bf16[8,224,768]{2,1,0:T(8,128)(2,1)}, f32[8,1,320]{2,1,0:T(1,128)}) custom-call(s32[2,1024]{1,0:T(2,128)} %get-tuple-element.60.slots_ref, f32[2,1024]{1,0:T(2,128)} %get-tuple-element.72.routes_ref, bf16[1024,768]{1,0:T(8,128)(2,1)} %cot_ref.7), custom_call_target="tpu_custom_call" | custom-call | tf_op jit(solution)/shard_map/pallas_call | solution.py:108
  21.9 5.2 all-to-all-start.1
  27.3 3.9 all-to-all-done.1
  31.1 5.0 all-to-all-start.2
  38.9 33.8 %collective-permute-done.6 = bf16[1,2,72,768]{3,2,1,0:T(8,128)(2,1)S(1)} collective-permute-done((bf16[1,2,72,768]{3,2,1,0:T(8,128)(2,1)S(1)}, bf16[1,2,72,768]{3,2,1,0:T(8,128)(2,1)S(1)}, u32[]{:S(2)}, u32[]{:S(2)}) %collective-permute-start.6) | collective-permute-done | bytes 221216 | tf_op jit(solution)/shard_map/ppermute | solution.py:898
  74.6 9.3 %collective-permute-done.7 = bf16[2,2,72,768]{3,2,1,0:T(8,128)(2,1)S(1)} collective-permute-done((bf16[2,2,72,768]{3,2,1,0:T(8,128)(2,1)S(1)}, bf16[2,2,72,768]{3,2,1,0:T(8,128)(2,1)S(1)}, u32[]{:S(2)}, u32[]{:S(2)}) %collective-permute-start.7) | collective-permute-done | bytes 442400 | tf_op jit(solution)/shard_map/ppermute | solution.py:898
  90.7 7.8 %shard_map.250 = (bf16[768,768]{1,0:T(8,128)(2,1)}, bf16[768,768]{1,0:T(8,128)(2,1)}, bf16[768,768]{1,0:T(8,128)(2,1)}, bf16[1024,768]{1,0:T(8,128)(2,1)}, bf16[...) custom-call(s32[1]{0:T(128)} %bitcast.1.owner_ref, bf16[1024,768]{1,0:T(8,128)(2,1)} %inputs_ref.5, ...), custom_call_target="tpu_custom_call" | custom-call | tf_op jit(solution)/shard_map/pallas_call | solution.py:660
  98.5 14.8 %shard_map.251 = (bf16[1024,768]{1,0:T(8,128)(2,1)}, f32[6,2,1024]{2,1,0:T(2,128)}) custom-call(bf16[1024,768]{1,0:T(8,128)(2,1)} %get-tuple-element.64.query_ref, bf16[1024,768]{1,0:T(8,128)(2,1)} %get-tuple-element.65.key_ref, bf16[1024,768]{1,0:T(8,128)(2,1)} %get-tuple-element.66.value_ref, f32[6,2,256]{2,1,0:T(2,128)} %get-tuple-element.62.refs_4_.near_ref), custom_call_target="tpu_custom_call" | custom-call | tf_op jit(solution)/shard_map/pallas_call | solution.py:528
  113.4 9.7 %shard_map.252 = (f32[1024,768]{1,0:T(8,128)}, bf16[1024,768]{1,0:T(8,128)(2,1)}, f32[2,1024]{1,0:T(2,128)}, bf16[1280,768]{1,0:T(8,128)(2,1)}) custom-call(bf16[1024,768]{1,0:T(8,128)(2,1)} %get-tuple-element.67.mixed_ref.out_ref, bf16[768,768]{1,0:T(8,128)(2,1)} %all-gather.2.cloned.1.call-done.merge_ref, bf16[1024,768]{1,0:T(8,128)(2,1)} %inputs_ref.5, ...), custom_call_target="tpu_custom_call" | custom-call | tf_op jit(solution)/shard_map/pallas_call | solution.py:705
  127.8 20.7 %all-to-all-done.rows_ref = bf16[8,160,768]{2,1,0:T(8,128)(2,1)S(1)} async-done(((bf16[8,160,768]{2,1,0:T(8,128)(2,1)}), bf16[8,160,768]{2,1,0:T(8,128)(2,1)S(1)}, u32[]{:S(2)}, u32[]{:S(2)}) %all-to-all-start) | async-done | bytes 1966112 | tf_op jit(solution)/shard_map/all_to_all | solution.py:972
  149.7 18.5 %shard_map.254 = (bf16[1280,3072]{1,0:T(8,128)(2,1)}, bf16[1280,3072]{1,0:T(8,128)(2,1)}, bf16[4,768,768]{2,1,0:T(8,128)(2,1)}, bf16[1280,768]{1,0:T(8,128)(2,1)}) custom-call(s32[1]{0:T(128)} %bitcast.1.owner_ref, bf16[8,160,768]{2,1,0:T(8,128)(2,1)} %copy-done.6, f32[1,1280]{1,0:T(1,128)} %reshape_squeeze.6.other_ref.refs_0_, ...), custom_call_target="tpu_custom_call" | custom-call | tf_op jit(solution)/shard_map/pallas_call | solution.py:181
  171.0 6.3 %shard_map.257 = bf16[8,256,768]{2,1,0:T(8,128)(2,1)} custom-call(s32[2,1024]{1,0:T(2,128)S(1)} %copy-done.3, bf16[1024,768]{1,0:T(8,128)(2,1)S(1)} %copy-done.1, bf16[1024,768]{1,0:T(8,128)(2,1)S(1)} %copy-done, f32[1,1280]{1,0:T(1,128)S(1)} %copy-done.5, f32[1,1280]{1,0:T(1,128)S(1)} %reshape_squeeze.7.refs_1_.other_ref), custom_call_target="tpu_custom_call" | custom-call | tf_op jit(solution)/shard_map/pallas_call | solution.py:81
  177.3 7.8 %all-to-all-start.4 = ((bf16[8,256,768]{2,1,0:T(8,128)(2,1)}), bf16[8,256,768]{2,1,0:T(8,128)(2,1)}, u32[]{:S(2)}, u32[]{:S(2)}) async-start(bf16[8,256,768]{2,1,0:T(8,128)(2,1)} %shard_map.257), calls=%async_computation.4 | async-start | bytes 6291456 | tf_op jit(solution)/shard_map/all_to_all | solution.py:972
  185.1 37.5 %shard_map.255 = (bf16[8,2,160,768]{3,2,1,0:T(8,128)(2,1)}, bf16[4,2304,768]{2,1,0:T(8,128)(2,1)}) custom-call(bf16[8,160,768]{2,1,0:T(8,128)(2,1)} %copy-done.6, bf16[1280,768]{1,0:T(8,128)(2,1)} %get-tuple-element.75.grad_ref, bf16[1280,3072]{1,0:T(8,128)(2,1)} %get-tuple-element.76.act_ref, bf16[1280,3072]{1,0:T(8,128)(2,1)} %get-tuple-element.77.pre_ref, ...), custom_call_target="tpu_custom_call" | custom-call | tf_op jit(solution)/shard_map/pallas_call | solution.py:238
  222.7 20.0 %shard_map.258 = (bf16[1280,3072]{1,0:T(8,128)(2,1)}, bf16[1280,3072]{1,0:T(8,128)(2,1)}, bf16[4,2304,768]{2,1,0:T(8,128)(2,1)}, bf16[1280,768]{1,0:T(8,128)(2,1)}) custom-call(s32[1]{0:T(128)} %bitcast.1.owner_ref, bf16[8,256,768]{2,1,0:T(8,128)(2,1)} %all-to-all-done.4.rows_ref.refs_1_, f32[1,1280]{1,0:T(1,128)} %copy-done.4, ...), custom_call_target="tpu_custom_call", output_to_operand_aliasing={{2}: (7, {})} | custom-call | tf_op jit(solution)/shard_map/pallas_call | solution.py:181
  242.6 19.4 %shard_map.259 = (bf16[1280,3072]{1,0:T(8,128)(2,1)}, bf16[4,2304,768]{2,1,0:T(8,128)(2,1)}) custom-call(bf16[8,256,768]{2,1,0:T(8,128)(2,1)} %all-to-all-done.4.rows_ref.refs_1_, bf16[1280,768]{1,0:T(8,128)(2,1)} %get-tuple-element.84.grad_ref, bf16[1280,3072]{1,0:T(8,128)(2,1)} %get-tuple-element.85.pre_ref, ...), custom_call_target="tpu_custom_call", output_to_operand_aliasing={{1}: (4, {})} | custom-call | tf_op jit(solution)/shard_map/pallas_call | solution.py:269
  262.1 4.8 all-to-all-start.3
  266.9 22.0 %shard_map.260 = bf16[8,2,160,768]{3,2,1,0:T(8,128)(2,1)} custom-call(bf16[1280,3072]{1,0:T(8,128)(2,1)} %get-tuple-element.83.act_ref, bf16[1280,3072]{1,0:T(8,128)(2,1)} %get-tuple-element.87.low_ref, bf16[2,768,3072]{2,1,0:T(8,128)(2,1)} %up_ref.7, bf16[2,3072,768]{2,1,0:T(8,128)(2,1)} %down_ref.5), custom_call_target="tpu_custom_call" | custom-call | tf_op jit(solution)/shard_map/pallas_call | solution.py:307
  288.8 20.8 %all-to-all-done.3.made_ref.back_ref = bf16[8,2,160,768]{3,2,1,0:T(8,128)(2,1)} async-done(((bf16[8,2,160,768]{3,2,1,0:T(8,128)(2,1)}), bf16[8,2,160,768]{3,2,1,0:T(8,128)(2,1)}, u32[]{:S(2)}, u32[]{:S(2)}) %all-to-all-start.3) | async-done | bytes 3932192 | tf_op jit(solution)/shard_map/all_to_all | solution.py:972
  309.7 8.5 %all-to-all-start.5 = ((bf16[8,2,160,768]{3,2,1,0:T(8,128)(2,1)}), bf16[8,2,160,768]{3,2,1,0:T(8,128)(2,1)}, u32[]{:S(2)}, u32[]{:S(2)}) async-start(bf16[8,2,160,768]{3,2,1,0:T(8,128)(2,1)} %shard_map.260), calls=%async_computation.5 | async-start | bytes 7864320 | tf_op jit(solution)/shard_map/all_to_all | solution.py:972
  318.9 11.2 %shard_map.256 = (f32[1024,768]{1,0:T(8,128)}, f32[1024,128]{1,0:T(8,128)}, f32[1024,768]{1,0:T(8,128)}) custom-call(s32[2,1024]{1,0:T(2,128)} %get-tuple-element.60.slots_ref, f32[2,1024]{1,0:T(2,128)} %get-tuple-element.69.gates_ref, f32[1024,768]{1,0:T(8,128)} %get-tuple-element.70.resid_ref, bf16[1024,768]{1,0:T(8,128)(2,1)} %cot_ref.7, ...), custom_call_target="tpu_custom_call" | custom-call | tf_op jit(solution)/shard_map/pallas_call | solution.py:357
  330.1 30.8 %all-to-all-done.5.made_ref.back_ref = bf16[8,2,160,768]{3,2,1,0:T(8,128)(2,1)} async-done(((bf16[8,2,160,768]{3,2,1,0:T(8,128)(2,1)}), bf16[8,2,160,768]{3,2,1,0:T(8,128)(2,1)}, u32[]{:S(2)}, u32[]{:S(2)}) %all-to-all-start.5) | async-done | bytes 3932192 | tf_op jit(solution)/shard_map/all_to_all | solution.py:972
  360.9 9.4 %shard_map.261 = (bf16[1024,768]{1,0:T(8,128)(2,1)}, bf16[1024,128]{1,0:T(8,128)(2,1)}) custom-call(s32[2,1024]{1,0:T(2,128)} %get-tuple-element.60.slots_ref, s32[2,1024]{1,0:T(2,128)} %bitcast.52, f32[2,1024]{1,0:T(2,128)} %get-tuple-element.69.gates_ref, f32[1024,768]{1,0:T(8,128)} %get-tuple-element.79.result_ref, ...), custom_call_target="tpu_custom_call" | custom-call | tf_op jit(solution)/shard_map/pallas_call | solution.py:398
  370.3 10.6 %shard_map.262 = (f32[1024,768]{1,0:T(8,128)}, bf16[1024,768]{1,0:T(8,128)(2,1)}, bf16[1024,768]{1,0:T(8,128)(2,1)}, f32[1,768]{1,0:T(1,128)}) custom-call(s32[2,1024]{1,0:T(2,128)} %get-tuple-element.60.slots_ref, bf16[1024,128]{1,0:T(8,128)(2,1)} %get-tuple-element.89.logit_ref, bf16[128,768]{1,0:T(8,128)(2,1)} %pad.20.router_ref, ...), custom_call_target="tpu_custom_call" | custom-call | tf_op jit(solution)/shard_map/pallas_call | solution.py:434
  380.9 35.6 %shard_map.263 = (bf16[3,1024,768]{2,1,0:T(8,128)(2,1)}, f32[6,4,256]{2,1,0:T(4,128)}) custom-call(bf16[1024,768]{1,0:T(8,128)(2,1)} %get-tuple-element.64.query_ref, bf16[1024,768]{1,0:T(8,128)(2,1)} %get-tuple-element.65.key_ref, bf16[1024,768]{1,0:T(8,128)(2,1)} %get-tuple-element.66.value_ref, bf16[1024,768]{1,0:T(8,128)(2,1)} %get-tuple-element.91.grad_ref, ...), custom_call_target="tpu_custom_call" | custom-call | tf_op jit(solution)/shard_map/pallas_call | solution.py:609
  416.5 11.4 %shard_map.265 = bf16[4,768,768]{2,1,0:T(8,128)(2,1)} custom-call(bf16[1024,768]{1,0:T(8,128)(2,1)} %get-tuple-element.99.left_ref, bf16[1024,768]{1,0:T(8,128)(2,1)} %get-tuple-element.67.mixed_ref.out_ref, bf16[3,1024,768]{2,1,0:T(8,128)(2,1)} %get-tuple-element.93.heads_ref, bf16[1024,768]{1,0:T(8,128)(2,1)} %get-tuple-element.100.branch_ref), custom_call_target="tpu_custom_call" | custom-call | tf_op jit(solution)/shard_map/pallas_call | solution.py:767
  435.1 9.9 %shard_map.264 = (f32[1024,768]{1,0:T(8,128)}, f32[1,768]{1,0:T(1,128)}) custom-call(bf16[3,1024,768]{2,1,0:T(8,128)(2,1)} %get-tuple-element.93.heads_ref, bf16[768,768]{1,0:T(8,128)(2,1)} %get-tuple-element.94.query_ref, bf16[768,768]{1,0:T(8,128)(2,1)} %get-tuple-element.95.key_ref, bf16[768,768]{1,0:T(8,128)(2,1)} %get-tuple-element.96.value_ref, ...), custom_call_target="tpu_custom_call" | custom-call | tf_op jit(solution)/shard_map/pallas_call | solution.py:734
  454.4 12.2 %collective-permute-done.13 = bf16[4,96,768]{2,1,0:T(8,128)(2,1)} collective-permute-done((bf16[4,96,768]{2,1,0:T(8,128)(2,1)S(1)}, bf16[4,96,768]{2,1,0:T(8,128)(2,1)}, u32[]{:S(2)}, u32[]{:S(2)}) %collective-permute-start.13) | collective-permute-done | bytes 589856 | tf_op jit(solution)/shard_map/ppermute | solution.py:898
  483.8 9.3 %collective-permute-done.15 = bf16[104,768]{1,0:T(8,128)(2,1)S(1)} collective-permute-done((bf16[104,768]{1,0:T(8,128)(2,1)S(1)}, bf16[104,768]{1,0:T(8,128)(2,1)S(1)}, u32[]{:S(2)}, u32[]{:S(2)}) %collective-permute-start.15) | collective-permute-done | bytes 159776 | tf_op jit(solution)/shard_map/ppermute | solution.py:903
  493.0 15.4 %collective-permute-done.16 = bf16[104,768]{1,0:T(8,128)(2,1)S(1)} collective-permute-done((bf16[104,768]{1,0:T(8,128)(2,1)S(1)}, bf16[104,768]{1,0:T(8,128)(2,1)S(1)}, u32[]{:S(2)}, u32[]{:S(2)}) %collective-permute-start.16) | collective-permute-done | bytes 159776 | tf_op jit(solution)/shard_map/ppermute | solution.py:903
  519.8 4.0 collective-permute-start.22
  532.1 6.1 %shard_map.267 = (f32[1536,768]{1,0:T(8,128)}, f32[1536,768]{1,0:T(8,128)}) custom-call(bf16[2304,768]{1,0:T(8,128)(2,1)} %reduce-scatter.3.cloned.1.call-done.rows_ref, f32[1536,768]{1,0:T(8,128)} %shard_map.266.into_ref), custom_call_target="tpu_custom_call", output_to_operand_aliasing={{1}: (1, {})} | custom-call | tf_op jit(solution)/shard_map/pallas_call | solution.py:811
  (158 shorter events, 81.1 us)
Async XLA Ops:
  8.7 18.5 %collective-permute-start = (bf16[96,768]{1,0:T(8,128)(2,1)}, bf16[96,768]{1,0:T(8,128)(2,1)S(1)}, u32[]{:S(2)}, u32[]{:S(2)}) collective-permute-start(bf16[96,768]{1,0:T(8,128)(2,1)} %shard_map.248), channel_id=1, source_target_pairs={{0,1},{1,2},{2,3},{3,0},{4,5},{5,6},{6,7},{7,4},{8,9},{9,10},{10,1... | collective-permute-start | bytes 442376 | tf_op jit(solution)/shard_map/ppermute | solution.py:903
  10.0 17.2 %collective-permute-start.1 = (bf16[96,768]{1,0:T(8,128)(2,1)}, bf16[96,768]{1,0:T(8,128)(2,1)S(1)}, u32[]{:S(2)}, u32[]{:S(2)}) collective-permute-start(bf16[96,768]{1,0:T(8,128)(2,1)} %shard_map.248), channel_id=1, source_target_pairs={{0,2},{1,3},{2,0},{3,1},{4,6},{5,7},{6,4},{7,5},{8,10},{9,11},{10,... | collective-permute-start | bytes 442376 | tf_op jit(solution)/shard_map/ppermute | solution.py:903
  11.0 25.1 %collective-permute-start.2 = (bf16[96,768]{1,0:T(8,128)(2,1)}, bf16[96,768]{1,0:T(8,128)(2,1)S(1)}, u32[]{:S(2)}, u32[]{:S(2)}) collective-permute-start(bf16[96,768]{1,0:T(8,128)(2,1)} %shard_map.248), channel_id=1, source_target_pairs={{0,3},{1,0},{2,1},{3,2},{4,7},{5,4},{6,5},{7,6},{8,11},{9,8},{10,9... | collective-permute-start | bytes 442376 | tf_op jit(solution)/shard_map/ppermute | solution.py:903
  21.9 9.3 %all-to-all-start.1 = ((f32[8,1,320]{2,1,0:T(1,128)}), f32[8,1,320]{2,1,0:T(1,128)S(1)}, u32[]{:S(2)}, u32[]{:S(2)}) async-start(f32[8,1,320]{2,1,0:T(1,128)} %get-tuple-element.73), calls=%async_computation.1 | async-start | bytes 24576 | tf_op jit(solution)/shard_map/all_to_all | solution.py:972
  31.1 92.0 %all-to-all-start.2 = ((bf16[8,224,768]{2,1,0:T(8,128)(2,1)}), bf16[8,224,768]{2,1,0:T(8,128)(2,1)}, u32[]{:S(2)}, u32[]{:S(2)}) async-start(bf16[8,224,768]{2,1,0:T(8,128)(2,1)} %get-tuple-element.74), calls=%async_computation.2 | async-start | bytes 5505024 | tf_op jit(solution)/shard_map/all_to_all | solution.py:972
  36.1 77.2 %all-gather.2.cloned.1.call-start = ((), (), s32[]{:S(2)}) async-start(), calls=%async_computation.8 | async-start | bytes 1474560 | tf_op jit(solution)/shard_map/all_gather | solution.py:1037
  36.2 36.4 %collective-permute-start.6 = (bf16[1,2,72,768]{3,2,1,0:T(8,128)(2,1)S(1)}, bf16[1,2,72,768]{3,2,1,0:T(8,128)(2,1)S(1)}, u32[]{:S(2)}, u32[]{:S(2)}) collective-permute-start(bf16[1,2,72,768]{3,2,1,0:T(8,128)(2,1)S(1)} %get-tuple-element.121), channel_id=1, source_target_pairs={{0,16},{4,20},{8,24},{12,28},{16,0},{20,4},{24,8},{28,12},{1,17},{... | collective-permute-start | bytes 663560 | tf_op jit(solution)/shard_map/ppermute | solution.py:898
  37.7 36.8 %collective-permute-start.3 = (bf16[1,2,72,768]{3,2,1,0:T(8,128)(2,1)S(1)}, bf16[1,2,72,768]{3,2,1,0:T(8,128)(2,1)S(1)}, u32[]{:S(2)}, u32[]{:S(2)}) collective-permute-start(bf16[1,2,72,768]{3,2,1,0:T(8,128)(2,1)S(1)} %get-tuple-element.122), channel_id=1, source_target_pairs={{0,8},{4,12},{8,0},{12,4},{16,24},{20,28},{24,16},{28,20},{1,9},{5... | collective-permute-start | bytes 663560 | tf_op jit(solution)/shard_map/ppermute | solution.py:898
  72.7 11.3 %collective-permute-start.7 = (bf16[2,2,72,768]{3,2,1,0:T(8,128)(2,1)S(1)}, bf16[2,2,72,768]{3,2,1,0:T(8,128)(2,1)S(1)}, u32[]{:S(2)}, u32[]{:S(2)}) collective-permute-start(bf16[2,2,72,768]{3,2,1,0:T(8,128)(2,1)S(1)} %pad_maximum_fusion.4), channel_id=1, source_target_pairs={{0,8},{4,12},{8,0},{12,4},{16,24},{20,28},{24,16},{28,20},{1,9},{5... | collective-permute-start | bytes 1327112 | tf_op jit(solution)/shard_map/ppermute | solution.py:898
  74.5 11.2 %collective-permute-start.4 = (bf16[2,2,72,768]{3,2,1,0:T(8,128)(2,1)S(1)}, bf16[2,2,72,768]{3,2,1,0:T(8,128)(2,1)S(1)}, u32[]{:S(2)}, u32[]{:S(2)}) collective-permute-start(bf16[2,2,72,768]{3,2,1,0:T(8,128)(2,1)S(1)} %pad_maximum_fusion.3), channel_id=1, source_target_pairs={{0,16},{4,20},{8,24},{12,28},{16,0},{20,4},{24,8},{28,12},{1,17},{... | collective-permute-start | bytes 1327112 | tf_op jit(solution)/shard_map/ppermute | solution.py:898
  84.1 5.7 %collective-permute-start.8 = (bf16[4,2,72,768]{3,2,1,0:T(8,128)(2,1)S(1)}, bf16[4,2,72,768]{3,2,1,0:T(8,128)(2,1)}, u32[]{:S(2)}, u32[]{:S(2)}) collective-permute-start(bf16[4,2,72,768]{3,2,1,0:T(8,128)(2,1)S(1)} %pad_maximum_fusion.1.refs_2_), channel_id=1, source_target_pairs={{0,4},{4,0},{8,12},{12,8},{16,20},{20,16},{24,28},{28,24},{1,5},{5... | collective-permute-start | bytes 2654216 | tf_op jit(solution)/shard_map/ppermute | solution.py:898
  85.8 3.9 collective-permute-start.5
  123.1 25.4 %all-to-all-start = ((bf16[8,160,768]{2,1,0:T(8,128)(2,1)}), bf16[8,160,768]{2,1,0:T(8,128)(2,1)S(1)}, u32[]{:S(2)}, u32[]{:S(2)}) async-start(bf16[8,160,768]{2,1,0:T(8,128)(2,1)} %bitcast.48), calls=%async_computation | async-start | bytes 3932160 | tf_op jit(solution)/shard_map/all_to_all | solution.py:972
  126.7 402.8 %reduce-scatter.5.cloned.1.call-start = ((), (), s32[]{:S(2)}) async-start(), calls=%async_computation.10 | async-start | bytes 5898240 | tf_op jit(solution)/shard_map/reduce_scatter | solution.py:968
  177.3 45.4 %all-to-all-start.4 = ((bf16[8,256,768]{2,1,0:T(8,128)(2,1)}), bf16[8,256,768]{2,1,0:T(8,128)(2,1)}, u32[]{:S(2)}, u32[]{:S(2)}) async-start(bf16[8,256,768]{2,1,0:T(8,128)(2,1)} %shard_map.257), calls=%async_computation.4 | async-start | bytes 6291456 | tf_op jit(solution)/shard_map/all_to_all | solution.py:972
  185.1 346.9 %reduce-scatter.3.cloned.1.call-start = ((), (), s32[]{:S(2)}) async-start(), calls=%async_computation.9 | async-start | bytes 17694720 | tf_op jit(solution)/shard_map/reduce_scatter | solution.py:968
  262.1 47.6 %all-to-all-start.3 = ((bf16[8,2,160,768]{3,2,1,0:T(8,128)(2,1)}), bf16[8,2,160,768]{3,2,1,0:T(8,128)(2,1)}, u32[]{:S(2)}, u32[]{:S(2)}) async-start(bf16[8,2,160,768]{3,2,1,0:T(8,128)(2,1)} %get-tuple-element.78), calls=%async_computation.3 | async-start | bytes 7864320 | tf_op jit(solution)/shard_map/all_to_all | solution.py:972
  309.7 51.2 %all-to-all-start.5 = ((bf16[8,2,160,768]{3,2,1,0:T(8,128)(2,1)}), bf16[8,2,160,768]{3,2,1,0:T(8,128)(2,1)}, u32[]{:S(2)}, u32[]{:S(2)}) async-start(bf16[8,2,160,768]{3,2,1,0:T(8,128)(2,1)} %shard_map.260), calls=%async_computation.5 | async-start | bytes 7864320 | tf_op jit(solution)/shard_map/all_to_all | solution.py:972
  431.2 17.4 %collective-permute-start.9 = (bf16[4,384,768]{2,1,0:T(8,128)(2,1)}, bf16[4,384,768]{2,1,0:T(8,128)(2,1)}, u32[]{:S(2)}, u32[]{:S(2)}) collective-permute-start(bf16[4,384,768]{2,1,0:T(8,128)(2,1)} %constant_dynamic-slice_fusion.3), channel_id=1, source_target_pairs={{0,4},{4,0},{8,12},{12,8},{16,20},{20,16},{24,28},{28,24},{1,5},{5... | collective-permute-start | bytes 7077896 | tf_op jit(solution)/shard_map/ppermute | solution.py:898
  447.0 1.5 collective-permute-start.12
  451.7 14.8 %collective-permute-start.13 = (bf16[4,96,768]{2,1,0:T(8,128)(2,1)S(1)}, bf16[4,96,768]{2,1,0:T(8,128)(2,1)}, u32[]{:S(2)}, u32[]{:S(2)}) collective-permute-start(bf16[4,96,768]{2,1,0:T(8,128)(2,1)S(1)} %fusion.1), channel_id=1, source_target_pairs={{0,16},{4,20},{8,24},{12,28},{16,0},{20,4},{24,8},{28,12},{1,17},{... | collective-permute-start | bytes 1769480 | tf_op jit(solution)/shard_map/ppermute | solution.py:898
  454.0 17.0 %collective-permute-start.10 = (bf16[4,112,768]{2,1,0:T(8,128)(2,1)}, bf16[4,112,768]{2,1,0:T(8,128)(2,1)}, u32[]{:S(2)}, u32[]{:S(2)}) collective-permute-start(bf16[4,112,768]{2,1,0:T(8,128)(2,1)} %constant_dynamic-slice_fusion.2), channel_id=1, source_target_pairs={{0,8},{4,12},{8,0},{12,4},{16,24},{20,28},{24,16},{28,20},{1,9},{5... | collective-permute-start | bytes 2064392 | tf_op jit(solution)/shard_map/ppermute | solution.py:898
  467.9 9.4 %collective-permute-start.14 = (bf16[4,48,768]{2,1,0:T(8,128)(2,1)S(1)}, bf16[4,48,768]{2,1,0:T(8,128)(2,1)S(1)}, u32[]{:S(2)}, u32[]{:S(2)}) collective-permute-start(bf16[4,48,768]{2,1,0:T(8,128)(2,1)S(1)} %constant_dynamic-slice_fusion), channel_id=1, source_target_pairs={{0,8},{4,12},{8,0},{12,4},{16,24},{20,28},{24,16},{28,20},{1,9},{5... | collective-permute-start | bytes 884744 | tf_op jit(solution)/shard_map/ppermute | solution.py:898
  472.3 7.8 %collective-permute-start.11 = (bf16[4,56,768]{2,1,0:T(8,128)(2,1)S(1)}, bf16[4,56,768]{2,1,0:T(8,128)(2,1)S(1)}, u32[]{:S(2)}, u32[]{:S(2)}) collective-permute-start(bf16[4,56,768]{2,1,0:T(8,128)(2,1)S(1)} %constant_dynamic-slice_fusion.1), channel_id=1, source_target_pairs={{0,16},{4,20},{8,24},{12,28},{16,0},{20,4},{24,8},{28,12},{1,17},{... | collective-permute-start | bytes 1032200 | tf_op jit(solution)/shard_map/ppermute | solution.py:898
  480.2 12.8 %collective-permute-start.15 = (bf16[104,768]{1,0:T(8,128)(2,1)S(1)}, bf16[104,768]{1,0:T(8,128)(2,1)S(1)}, u32[]{:S(2)}, u32[]{:S(2)}) collective-permute-start(bf16[104,768]{1,0:T(8,128)(2,1)S(1)} %get-tuple-element.118), channel_id=1, source_target_pairs={{0,1},{1,2},{2,3},{3,0},{4,5},{5,6},{6,7},{7,4},{8,9},{9,10},{10,1... | collective-permute-start | bytes 479240 | tf_op jit(solution)/shard_map/ppermute | solution.py:903
  480.3 28.1 %collective-permute-start.16 = (bf16[104,768]{1,0:T(8,128)(2,1)S(1)}, bf16[104,768]{1,0:T(8,128)(2,1)S(1)}, u32[]{:S(2)}, u32[]{:S(2)}) collective-permute-start(bf16[104,768]{1,0:T(8,128)(2,1)S(1)} %get-tuple-element.119), channel_id=1, source_target_pairs={{0,2},{1,3},{2,0},{3,1},{4,6},{5,7},{6,4},{7,5},{8,10},{9,11},{10,... | collective-permute-start | bytes 479240 | tf_op jit(solution)/shard_map/ppermute | solution.py:903
  483.8 26.0 %collective-permute-start.17 = (bf16[104,768]{1,0:T(8,128)(2,1)S(1)}, bf16[104,768]{1,0:T(8,128)(2,1)S(1)}, u32[]{:S(2)}, u32[]{:S(2)}) collective-permute-start(bf16[104,768]{1,0:T(8,128)(2,1)S(1)} %get-tuple-element.120), channel_id=1, source_target_pairs={{0,3},{1,0},{2,1},{3,2},{4,7},{5,4},{6,5},{7,6},{8,11},{9,8},{10,9... | collective-permute-start | bytes 479240 | tf_op jit(solution)/shard_map/ppermute | solution.py:903
  509.9 3.3 collective-permute-start.20
  511.4 3.6 collective-permute-start.18
  513.2 4.9 collective-permute-start.21
  515.1 4.6 collective-permute-start.19
  519.8 5.7 %collective-permute-start.22 = (bf16[416,768]{1,0:T(8,128)(2,1)S(1)}, bf16[416,768]{1,0:T(8,128)(2,1)S(1)}, u32[]{:S(2)}, u32[]{:S(2)}) collective-permute-start(bf16[416,768]{1,0:T(8,128)(2,1)S(1)} %pad_maximum_fusion.2), channel_id=1, source_target_pairs={{0,4},{4,0},{8,12},{12,8},{16,20},{20,16},{24,28},{28,24},{1,5},{5... | collective-permute-start | bytes 1916936 | tf_op jit(solution)/shard_map/ppermute | solution.py:898
  (19 other events, 159.6 us)
Sparse Core Ops, SparseCore 0:
  39.0 27.9 all-gather.1
  168.4 85.3 reduce-scatter.4
  262.2 249.5 reduce-scatter.2

commit v12 on v11

--- a/solution.py
+++ b/solution.py
@@ -89,27 +89,32 @@
 
 
 def dispatch_first_kernel(slots_ref, routes_ref, rows_ref, out_ref, other_ref, *, owners, capacity):
+    per, total, _ = out_ref.shape
     block, tokens = other_ref.shape[2], rows_ref.shape[0]
     row = lax.broadcasted_iota(jnp.int32, (block, tokens), 0)
-    slot = row + pl.program_id(0) * capacity
-    slot = slot + jnp.where(row >= capacity, (owners - 1) * capacity, 0)
-    hits = [slot == slots_ref[c:c + 1, :] for c in range(2)]
-    hot = jnp.where(hits[0] | hits[1], 1.0, 0.0)[:out_ref.shape[1]]
-    out_ref[0] = dot_nn(hot.astype(jnp.bfloat16), rows_ref[...]).astype(out_ref.dtype)
-    other = jnp.where(hits[0], routes_ref[1:2, :], jnp.where(hits[1], routes_ref[0:1, :], 0.0))
-    column = jnp.sum(other, axis=1, keepdims=True)
-    other_ref[0] = jnp.broadcast_to(column, (block, 128)).T[0:1, :]
-
-
-def dispatch_first(slots, routes, rows, owners, capacity, early):
+    row = row + jnp.where(row >= capacity, (owners - 1) * capacity, 0)
+    hots = []
+    for index in range(per):
+        slot = row + (pl.program_id(0) * per + index) * capacity
+        hits = [slot == slots_ref[c:c + 1, :] for c in range(2)]
+        hots.append(jnp.where(hits[0] | hits[1], 1.0, 0.0)[:total].astype(jnp.bfloat16))
+        other = jnp.where(hits[0], routes_ref[1:2, :], jnp.where(hits[1], routes_ref[0:1, :], 0.0))
+        column = jnp.sum(other, axis=1, keepdims=True)
+        other_ref[index] = jnp.broadcast_to(column, (block, 128)).T[0:1, :]
+    picked = dot_nn(jnp.concatenate(hots, axis=0), rows_ref[...]).astype(out_ref.dtype)
+    for index in range(per):
+        out_ref[index] = picked[index * total:(index + 1) * total]
+
+
+def dispatch_first(slots, routes, rows, owners, capacity, early, per=4):
     width = rows.shape[1]
     total = capacity + early
     whole = lambda shape: pl.BlockSpec(shape, lambda i: (0, 0))
     return pl.pallas_call(
         partial(dispatch_first_kernel, owners=owners, capacity=capacity),
-        grid=(owners,),
+        grid=(owners // per,),
         in_specs=[whole(slots.shape), whole(routes.shape), whole(rows.shape)],
-        out_specs=[pl.BlockSpec((1, total, width), lambda i: (i, 0, 0)), pl.BlockSpec((1, 1, 2 * capacity), lambda i: (i, 0, 0))],
+        out_specs=[pl.BlockSpec((per, total, width), lambda i: (i, 0, 0)), pl.BlockSpec((per, 1, 2 * capacity), lambda i: (i, 0, 0))],
         out_shape=[jax.ShapeDtypeStruct((owners, total, width), rows.dtype), jax.ShapeDtypeStruct((owners, 1, 2 * capacity), jnp.float32)],
     )(slots, routes, rows)
 

time: 553 us -> 553 us (level)
  no operation moved by 1% of the time
where the time goes in v12:
time: 553 us; the launch traced here: 544 us
  Pallas kernels  265 us (48%)
  waiting for transfers between devices  174 us (31%)
  starting transfers between devices  65.3 us (12%)
  local copies, waits for them, and re-layouts  14.8 us (3%)
  between operations  14.7 us (3%)
  other arithmetic  10 us (2%)
    all_to_all x6, waiting for transfers between devices, share_rows(): return lax.all_to_all(rows, OWNER, 0, 0, tiled=True)  76 us
    ppermute x17, waiting for transfers between devices, exchange(): return lax.ppermute(rows, OWNER, [(i, i ^ bit) for i in range(count)])  72.1 us
    pallas_call x2, Pallas kernels, expert_first(): pl.pallas_call(partial(first_kernel, index=index, local_count=local_count...  38.4 us
    pallas_call x1, Pallas kernels, expert_second(): pl.pallas_call(second_kernel, grid=(shards,), in_specs=[arrived_spec(rows...  37.5 us
    pallas_call x1, Pallas kernels, attend_back(): pl.pallas_call(partial(attend_back_kernel, block=block, size=size, scale=...  35.6 us
    all_to_all x6, starting transfers between devices, share_rows(): return lax.all_to_all(rows, OWNER, 0, 0, tiled=True)  34.8 us
    ppermute x6, waiting for transfers between devices, shift(): lax.ppermute(rows, LINE, [(i, (i + step) % count) for i in range(count)])  25.8 us
    ppermute x17, starting transfers between devices, exchange(): return lax.ppermute(rows, OWNER, [(i, i ^ bit) for i in range(count)])  22.6 us
  transfers between devices with their start and end apart: 32, of which 19 were waited for; matrix products, arithmetic and copies ran while one was open for 4% of the time, Pallas kernels for 44%

profile of v12, /device:TPU:9, one launch (start us, length us, event | category | flops | bytes accessed | tf_op | source)
XLA Modules:
  0.0 544.0 jit_solution(12405646850152469681)
XLA Ops:
  14.1 6.8 %shard_map.253 = (bf16[8,224,768]{2,1,0:T(8,128)(2,1)}, f32[8,1,320]{2,1,0:T(1,128)}) custom-call(s32[2,1024]{1,0:T(2,128)} %get-tuple-element.60.slots_ref, f32[2,1024]{1,0:T(2,128)} %get-tuple-element.72.routes_ref, bf16[1024,768]{1,0:T(8,128)(2,1)} %cot_ref.7), custom_call_target="tpu_custom_call" | custom-call | tf_op jit(solution)/shard_map/pallas_call | solution.py:113
  20.9 5.2 all-to-all-start.1
  26.3 3.9 all-to-all-done.1
  30.2 5.0 all-to-all-start.2
  38.0 33.8 %collective-permute-done.6 = bf16[1,2,72,768]{3,2,1,0:T(8,128)(2,1)S(1)} collective-permute-done((bf16[1,2,72,768]{3,2,1,0:T(8,128)(2,1)S(1)}, bf16[1,2,72,768]{3,2,1,0:T(8,128)(2,1)S(1)}, u32[]{:S(2)}, u32[]{:S(2)}) %collective-permute-start.6) | collective-permute-done | bytes 221216 | tf_op jit(solution)/shard_map/ppermute | solution.py:903
  73.7 9.3 %collective-permute-done.7 = bf16[2,2,72,768]{3,2,1,0:T(8,128)(2,1)S(1)} collective-permute-done((bf16[2,2,72,768]{3,2,1,0:T(8,128)(2,1)S(1)}, bf16[2,2,72,768]{3,2,1,0:T(8,128)(2,1)S(1)}, u32[]{:S(2)}, u32[]{:S(2)}) %collective-permute-start.7) | collective-permute-done | bytes 442400 | tf_op jit(solution)/shard_map/ppermute | solution.py:903
  89.8 7.8 %shard_map.250 = (bf16[768,768]{1,0:T(8,128)(2,1)}, bf16[768,768]{1,0:T(8,128)(2,1)}, bf16[768,768]{1,0:T(8,128)(2,1)}, bf16[1024,768]{1,0:T(8,128)(2,1)}, bf16[...) custom-call(s32[1]{0:T(128)} %bitcast.1.owner_ref, bf16[1024,768]{1,0:T(8,128)(2,1)} %inputs_ref.5, ...), custom_call_target="tpu_custom_call" | custom-call | tf_op jit(solution)/shard_map/pallas_call | solution.py:665
  97.6 14.8 %shard_map.251 = (bf16[1024,768]{1,0:T(8,128)(2,1)}, f32[6,2,1024]{2,1,0:T(2,128)}) custom-call(bf16[1024,768]{1,0:T(8,128)(2,1)} %get-tuple-element.64.query_ref, bf16[1024,768]{1,0:T(8,128)(2,1)} %get-tuple-element.65.key_ref, bf16[1024,768]{1,0:T(8,128)(2,1)} %get-tuple-element.66.value_ref, f32[6,2,256]{2,1,0:T(2,128)} %get-tuple-element.62.refs_4_.near_ref), custom_call_target="tpu_custom_call" | custom-call | tf_op jit(solution)/shard_map/pallas_call | solution.py:533
  112.4 9.7 %shard_map.252 = (f32[1024,768]{1,0:T(8,128)}, bf16[1024,768]{1,0:T(8,128)(2,1)}, f32[2,1024]{1,0:T(2,128)}, bf16[1280,768]{1,0:T(8,128)(2,1)}) custom-call(bf16[1024,768]{1,0:T(8,128)(2,1)} %get-tuple-element.67.mixed_ref.out_ref, bf16[768,768]{1,0:T(8,128)(2,1)} %all-gather.2.cloned.1.call-done.merge_ref, bf16[1024,768]{1,0:T(8,128)(2,1)} %inputs_ref.5, ...), custom_call_target="tpu_custom_call" | custom-call | tf_op jit(solution)/shard_map/pallas_call | solution.py:710
  127.0 20.5 %all-to-all-done.rows_ref = bf16[8,160,768]{2,1,0:T(8,128)(2,1)S(1)} async-done(((bf16[8,160,768]{2,1,0:T(8,128)(2,1)}), bf16[8,160,768]{2,1,0:T(8,128)(2,1)S(1)}, u32[]{:S(2)}, u32[]{:S(2)}) %all-to-all-start) | async-done | bytes 1966112 | tf_op jit(solution)/shard_map/all_to_all | solution.py:977
  148.8 18.5 %shard_map.254 = (bf16[1280,3072]{1,0:T(8,128)(2,1)}, bf16[1280,3072]{1,0:T(8,128)(2,1)}, bf16[4,768,768]{2,1,0:T(8,128)(2,1)}, bf16[1280,768]{1,0:T(8,128)(2,1)}) custom-call(s32[1]{0:T(128)} %bitcast.1.owner_ref, bf16[8,160,768]{2,1,0:T(8,128)(2,1)} %copy-done.6, f32[1,1280]{1,0:T(1,128)} %reshape_squeeze.6.other_ref.refs_0_, ...), custom_call_target="tpu_custom_call" | custom-call | tf_op jit(solution)/shard_map/pallas_call | solution.py:186
  170.1 6.3 %shard_map.257 = bf16[8,256,768]{2,1,0:T(8,128)(2,1)} custom-call(s32[2,1024]{1,0:T(2,128)S(1)} %copy-done.3, bf16[1024,768]{1,0:T(8,128)(2,1)S(1)} %copy-done.1, bf16[1024,768]{1,0:T(8,128)(2,1)S(1)} %copy-done, f32[1,1280]{1,0:T(1,128)S(1)} %copy-done.5, f32[1,1280]{1,0:T(1,128)S(1)} %reshape_squeeze.7.refs_1_.other_ref), custom_call_target="tpu_custom_call" | custom-call | tf_op jit(solution)/shard_map/pallas_call | solution.py:81
  176.4 7.8 %all-to-all-start.4 = ((bf16[8,256,768]{2,1,0:T(8,128)(2,1)}), bf16[8,256,768]{2,1,0:T(8,128)(2,1)}, u32[]{:S(2)}, u32[]{:S(2)}) async-start(bf16[8,256,768]{2,1,0:T(8,128)(2,1)} %shard_map.257), calls=%async_computation.4 | async-start | bytes 6291456 | tf_op jit(solution)/shard_map/all_to_all | solution.py:977
  184.2 37.5 %shard_map.255 = (bf16[8,2,160,768]{3,2,1,0:T(8,128)(2,1)}, bf16[4,2304,768]{2,1,0:T(8,128)(2,1)}) custom-call(bf16[8,160,768]{2,1,0:T(8,128)(2,1)} %copy-done.6, bf16[1280,768]{1,0:T(8,128)(2,1)} %get-tuple-element.75.grad_ref, bf16[1280,3072]{1,0:T(8,128)(2,1)} %get-tuple-element.76.act_ref, bf16[1280,3072]{1,0:T(8,128)(2,1)} %get-tuple-element.77.pre_ref, ...), custom_call_target="tpu_custom_call" | custom-call | tf_op jit(solution)/shard_map/pallas_call | solution.py:243
  221.8 19.9 %shard_map.258 = (bf16[1280,3072]{1,0:T(8,128)(2,1)}, bf16[1280,3072]{1,0:T(8,128)(2,1)}, bf16[4,2304,768]{2,1,0:T(8,128)(2,1)}, bf16[1280,768]{1,0:T(8,128)(2,1)}) custom-call(s32[1]{0:T(128)} %bitcast.1.owner_ref, bf16[8,256,768]{2,1,0:T(8,128)(2,1)} %all-to-all-done.4.rows_ref.refs_1_, f32[1,1280]{1,0:T(1,128)} %copy-done.4, ...), custom_call_target="tpu_custom_call", output_to_operand_aliasing={{2}: (7, {})} | custom-call | tf_op jit(solution)/shard_map/pallas_call | solution.py:186
  241.7 19.4 %shard_map.259 = (bf16[1280,3072]{1,0:T(8,128)(2,1)}, bf16[4,2304,768]{2,1,0:T(8,128)(2,1)}) custom-call(bf16[8,256,768]{2,1,0:T(8,128)(2,1)} %all-to-all-done.4.rows_ref.refs_1_, bf16[1280,768]{1,0:T(8,128)(2,1)} %get-tuple-element.84.grad_ref, bf16[1280,3072]{1,0:T(8,128)(2,1)} %get-tuple-element.85.pre_ref, ...), custom_call_target="tpu_custom_call", output_to_operand_aliasing={{1}: (4, {})} | custom-call | tf_op jit(solution)/shard_map/pallas_call | solution.py:274
  261.1 4.8 all-to-all-start.3
  265.9 22.0 %shard_map.260 = bf16[8,2,160,768]{3,2,1,0:T(8,128)(2,1)} custom-call(bf16[1280,3072]{1,0:T(8,128)(2,1)} %get-tuple-element.83.act_ref, bf16[1280,3072]{1,0:T(8,128)(2,1)} %get-tuple-element.87.low_ref, bf16[2,768,3072]{2,1,0:T(8,128)(2,1)} %up_ref.7, bf16[2,3072,768]{2,1,0:T(8,128)(2,1)} %down_ref.5), custom_call_target="tpu_custom_call" | custom-call | tf_op jit(solution)/shard_map/pallas_call | solution.py:312
  287.8 20.9 %all-to-all-done.3.made_ref.back_ref = bf16[8,2,160,768]{3,2,1,0:T(8,128)(2,1)} async-done(((bf16[8,2,160,768]{3,2,1,0:T(8,128)(2,1)}), bf16[8,2,160,768]{3,2,1,0:T(8,128)(2,1)}, u32[]{:S(2)}, u32[]{:S(2)}) %all-to-all-start.3) | async-done | bytes 3932192 | tf_op jit(solution)/shard_map/all_to_all | solution.py:977
  308.7 8.3 %all-to-all-start.5 = ((bf16[8,2,160,768]{3,2,1,0:T(8,128)(2,1)}), bf16[8,2,160,768]{3,2,1,0:T(8,128)(2,1)}, u32[]{:S(2)}, u32[]{:S(2)}) async-start(bf16[8,2,160,768]{3,2,1,0:T(8,128)(2,1)} %shard_map.260), calls=%async_computation.5 | async-start | bytes 7864320 | tf_op jit(solution)/shard_map/all_to_all | solution.py:977
  317.7 11.3 %shard_map.256 = (f32[1024,768]{1,0:T(8,128)}, f32[1024,128]{1,0:T(8,128)}, f32[1024,768]{1,0:T(8,128)}) custom-call(s32[2,1024]{1,0:T(2,128)} %get-tuple-element.60.slots_ref, f32[2,1024]{1,0:T(2,128)} %get-tuple-element.69.gates_ref, f32[1024,768]{1,0:T(8,128)} %get-tuple-element.70.resid_ref, bf16[1024,768]{1,0:T(8,128)(2,1)} %cot_ref.7, ...), custom_call_target="tpu_custom_call" | custom-call | tf_op jit(solution)/shard_map/pallas_call | solution.py:362
  329.0 30.8 %all-to-all-done.5.made_ref.back_ref = bf16[8,2,160,768]{3,2,1,0:T(8,128)(2,1)} async-done(((bf16[8,2,160,768]{3,2,1,0:T(8,128)(2,1)}), bf16[8,2,160,768]{3,2,1,0:T(8,128)(2,1)}, u32[]{:S(2)}, u32[]{:S(2)}) %all-to-all-start.5) | async-done | bytes 3932192 | tf_op jit(solution)/shard_map/all_to_all | solution.py:977
  359.8 9.4 %shard_map.261 = (bf16[1024,768]{1,0:T(8,128)(2,1)}, bf16[1024,128]{1,0:T(8,128)(2,1)}) custom-call(s32[2,1024]{1,0:T(2,128)} %get-tuple-element.60.slots_ref, s32[2,1024]{1,0:T(2,128)} %bitcast.52, f32[2,1024]{1,0:T(2,128)} %get-tuple-element.69.gates_ref, f32[1024,768]{1,0:T(8,128)} %get-tuple-element.79.result_ref, ...), custom_call_target="tpu_custom_call" | custom-call | tf_op jit(solution)/shard_map/pallas_call | solution.py:403
  369.1 10.6 %shard_map.262 = (f32[1024,768]{1,0:T(8,128)}, bf16[1024,768]{1,0:T(8,128)(2,1)}, bf16[1024,768]{1,0:T(8,128)(2,1)}, f32[1,768]{1,0:T(1,128)}) custom-call(s32[2,1024]{1,0:T(2,128)} %get-tuple-element.60.slots_ref, bf16[1024,128]{1,0:T(8,128)(2,1)} %get-tuple-element.89.logit_ref, bf16[128,768]{1,0:T(8,128)(2,1)} %pad.20.router_ref, ...), custom_call_target="tpu_custom_call" | custom-call | tf_op jit(solution)/shard_map/pallas_call | solution.py:439
  379.8 35.6 %shard_map.263 = (bf16[3,1024,768]{2,1,0:T(8,128)(2,1)}, f32[6,4,256]{2,1,0:T(4,128)}) custom-call(bf16[1024,768]{1,0:T(8,128)(2,1)} %get-tuple-element.64.query_ref, bf16[1024,768]{1,0:T(8,128)(2,1)} %get-tuple-element.65.key_ref, bf16[1024,768]{1,0:T(8,128)(2,1)} %get-tuple-element.66.value_ref, bf16[1024,768]{1,0:T(8,128)(2,1)} %get-tuple-element.91.grad_ref, ...), custom_call_target="tpu_custom_call" | custom-call | tf_op jit(solution)/shard_map/pallas_call | solution.py:614
  415.4 11.4 %shard_map.265 = bf16[4,768,768]{2,1,0:T(8,128)(2,1)} custom-call(bf16[1024,768]{1,0:T(8,128)(2,1)} %get-tuple-element.99.left_ref, bf16[1024,768]{1,0:T(8,128)(2,1)} %get-tuple-element.67.mixed_ref.out_ref, bf16[3,1024,768]{2,1,0:T(8,128)(2,1)} %get-tuple-element.93.heads_ref, bf16[1024,768]{1,0:T(8,128)(2,1)} %get-tuple-element.100.branch_ref), custom_call_target="tpu_custom_call" | custom-call | tf_op jit(solution)/shard_map/pallas_call | solution.py:772
  433.8 9.9 %shard_map.264 = (f32[1024,768]{1,0:T(8,128)}, f32[1,768]{1,0:T(1,128)}) custom-call(bf16[3,1024,768]{2,1,0:T(8,128)(2,1)} %get-tuple-element.93.heads_ref, bf16[768,768]{1,0:T(8,128)(2,1)} %get-tuple-element.94.query_ref, bf16[768,768]{1,0:T(8,128)(2,1)} %get-tuple-element.95.key_ref, bf16[768,768]{1,0:T(8,128)(2,1)} %get-tuple-element.96.value_ref, ...), custom_call_target="tpu_custom_call" | custom-call | tf_op jit(solution)/shard_map/pallas_call | solution.py:739
  453.3 11.9 %collective-permute-done.13 = bf16[4,96,768]{2,1,0:T(8,128)(2,1)} collective-permute-done((bf16[4,96,768]{2,1,0:T(8,128)(2,1)S(1)}, bf16[4,96,768]{2,1,0:T(8,128)(2,1)}, u32[]{:S(2)}, u32[]{:S(2)}) %collective-permute-start.13) | collective-permute-done | bytes 589856 | tf_op jit(solution)/shard_map/ppermute | solution.py:903
  472.2 4.1 collective-permute-done.14
  483.0 8.7 %collective-permute-done.15 = bf16[104,768]{1,0:T(8,128)(2,1)S(1)} collective-permute-done((bf16[104,768]{1,0:T(8,128)(2,1)S(1)}, bf16[104,768]{1,0:T(8,128)(2,1)S(1)}, u32[]{:S(2)}, u32[]{:S(2)}) %collective-permute-start.15) | collective-permute-done | bytes 159776 | tf_op jit(solution)/shard_map/ppermute | solution.py:908
  491.7 15.7 %collective-permute-done.16 = bf16[104,768]{1,0:T(8,128)(2,1)S(1)} collective-permute-done((bf16[104,768]{1,0:T(8,128)(2,1)S(1)}, bf16[104,768]{1,0:T(8,128)(2,1)S(1)}, u32[]{:S(2)}, u32[]{:S(2)}) %collective-permute-start.16) | collective-permute-done | bytes 159776 | tf_op jit(solution)/shard_map/ppermute | solution.py:908
  530.9 6.1 %shard_map.267 = (f32[1536,768]{1,0:T(8,128)}, f32[1536,768]{1,0:T(8,128)}) custom-call(bf16[2304,768]{1,0:T(8,128)(2,1)} %reduce-scatter.3.cloned.1.call-done.rows_ref, f32[1536,768]{1,0:T(8,128)} %shard_map.266.into_ref), custom_call_target="tpu_custom_call", output_to_operand_aliasing={{1}: (1, {})} | custom-call | tf_op jit(solution)/shard_map/pallas_call | solution.py:816
  (158 shorter events, 81.5 us)
Async XLA Ops:
  8.7 17.6 %collective-permute-start = (bf16[96,768]{1,0:T(8,128)(2,1)}, bf16[96,768]{1,0:T(8,128)(2,1)S(1)}, u32[]{:S(2)}, u32[]{:S(2)}) collective-permute-start(bf16[96,768]{1,0:T(8,128)(2,1)} %shard_map.248), channel_id=1, source_target_pairs={{0,1},{1,2},{2,3},{3,0},{4,5},{5,6},{6,7},{7,4},{8,9},{9,10},{10,1... | collective-permute-start | bytes 442376 | tf_op jit(solution)/shard_map/ppermute | solution.py:908
  10.0 16.3 %collective-permute-start.1 = (bf16[96,768]{1,0:T(8,128)(2,1)}, bf16[96,768]{1,0:T(8,128)(2,1)S(1)}, u32[]{:S(2)}, u32[]{:S(2)}) collective-permute-start(bf16[96,768]{1,0:T(8,128)(2,1)} %shard_map.248), channel_id=1, source_target_pairs={{0,2},{1,3},{2,0},{3,1},{4,6},{5,7},{6,4},{7,5},{8,10},{9,11},{10,... | collective-permute-start | bytes 442376 | tf_op jit(solution)/shard_map/ppermute | solution.py:908
  11.0 24.2 %collective-permute-start.2 = (bf16[96,768]{1,0:T(8,128)(2,1)}, bf16[96,768]{1,0:T(8,128)(2,1)S(1)}, u32[]{:S(2)}, u32[]{:S(2)}) collective-permute-start(bf16[96,768]{1,0:T(8,128)(2,1)} %shard_map.248), channel_id=1, source_target_pairs={{0,3},{1,0},{2,1},{3,2},{4,7},{5,4},{6,5},{7,6},{8,11},{9,8},{10,9... | collective-permute-start | bytes 442376 | tf_op jit(solution)/shard_map/ppermute | solution.py:908
  20.9 9.3 %all-to-all-start.1 = ((f32[8,1,320]{2,1,0:T(1,128)}), f32[8,1,320]{2,1,0:T(1,128)S(1)}, u32[]{:S(2)}, u32[]{:S(2)}) async-start(f32[8,1,320]{2,1,0:T(1,128)} %get-tuple-element.73), calls=%async_computation.1 | async-start | bytes 24576 | tf_op jit(solution)/shard_map/all_to_all | solution.py:977
  30.2 92.0 %all-to-all-start.2 = ((bf16[8,224,768]{2,1,0:T(8,128)(2,1)}), bf16[8,224,768]{2,1,0:T(8,128)(2,1)}, u32[]{:S(2)}, u32[]{:S(2)}) async-start(bf16[8,224,768]{2,1,0:T(8,128)(2,1)} %get-tuple-element.74), calls=%async_computation.2 | async-start | bytes 5505024 | tf_op jit(solution)/shard_map/all_to_all | solution.py:977
  35.2 77.2 %all-gather.2.cloned.1.call-start = ((), (), s32[]{:S(2)}) async-start(), calls=%async_computation.8 | async-start | bytes 1474560 | tf_op jit(solution)/shard_map/all_gather | solution.py:1042
  35.3 36.4 %collective-permute-start.6 = (bf16[1,2,72,768]{3,2,1,0:T(8,128)(2,1)S(1)}, bf16[1,2,72,768]{3,2,1,0:T(8,128)(2,1)S(1)}, u32[]{:S(2)}, u32[]{:S(2)}) collective-permute-start(bf16[1,2,72,768]{3,2,1,0:T(8,128)(2,1)S(1)} %get-tuple-element.121), channel_id=1, source_target_pairs={{0,16},{4,20},{8,24},{12,28},{16,0},{20,4},{24,8},{28,12},{1,17},{... | collective-permute-start | bytes 663560 | tf_op jit(solution)/shard_map/ppermute | solution.py:903
  36.7 36.8 %collective-permute-start.3 = (bf16[1,2,72,768]{3,2,1,0:T(8,128)(2,1)S(1)}, bf16[1,2,72,768]{3,2,1,0:T(8,128)(2,1)S(1)}, u32[]{:S(2)}, u32[]{:S(2)}) collective-permute-start(bf16[1,2,72,768]{3,2,1,0:T(8,128)(2,1)S(1)} %get-tuple-element.122), channel_id=1, source_target_pairs={{0,8},{4,12},{8,0},{12,4},{16,24},{20,28},{24,16},{28,20},{1,9},{5... | collective-permute-start | bytes 663560 | tf_op jit(solution)/shard_map/ppermute | solution.py:903
  71.8 11.3 %collective-permute-start.7 = (bf16[2,2,72,768]{3,2,1,0:T(8,128)(2,1)S(1)}, bf16[2,2,72,768]{3,2,1,0:T(8,128)(2,1)S(1)}, u32[]{:S(2)}, u32[]{:S(2)}) collective-permute-start(bf16[2,2,72,768]{3,2,1,0:T(8,128)(2,1)S(1)} %pad_maximum_fusion.4), channel_id=1, source_target_pairs={{0,8},{4,12},{8,0},{12,4},{16,24},{20,28},{24,16},{28,20},{1,9},{5... | collective-permute-start | bytes 1327112 | tf_op jit(solution)/shard_map/ppermute | solution.py:903
  73.6 11.2 %collective-permute-start.4 = (bf16[2,2,72,768]{3,2,1,0:T(8,128)(2,1)S(1)}, bf16[2,2,72,768]{3,2,1,0:T(8,128)(2,1)S(1)}, u32[]{:S(2)}, u32[]{:S(2)}) collective-permute-start(bf16[2,2,72,768]{3,2,1,0:T(8,128)(2,1)S(1)} %pad_maximum_fusion.3), channel_id=1, source_target_pairs={{0,16},{4,20},{8,24},{12,28},{16,0},{20,4},{24,8},{28,12},{1,17},{... | collective-permute-start | bytes 1327112 | tf_op jit(solution)/shard_map/ppermute | solution.py:903
  83.2 5.7 %collective-permute-start.8 = (bf16[4,2,72,768]{3,2,1,0:T(8,128)(2,1)S(1)}, bf16[4,2,72,768]{3,2,1,0:T(8,128)(2,1)}, u32[]{:S(2)}, u32[]{:S(2)}) collective-permute-start(bf16[4,2,72,768]{3,2,1,0:T(8,128)(2,1)S(1)} %pad_maximum_fusion.1.refs_2_), channel_id=1, source_target_pairs={{0,4},{4,0},{8,12},{12,8},{16,20},{20,16},{24,28},{28,24},{1,5},{5... | collective-permute-start | bytes 2654216 | tf_op jit(solution)/shard_map/ppermute | solution.py:903
  84.9 3.9 collective-permute-start.5
  122.2 25.4 %all-to-all-start = ((bf16[8,160,768]{2,1,0:T(8,128)(2,1)}), bf16[8,160,768]{2,1,0:T(8,128)(2,1)S(1)}, u32[]{:S(2)}, u32[]{:S(2)}) async-start(bf16[8,160,768]{2,1,0:T(8,128)(2,1)} %bitcast.48), calls=%async_computation | async-start | bytes 3932160 | tf_op jit(solution)/shard_map/all_to_all | solution.py:977
  125.8 402.6 %reduce-scatter.5.cloned.1.call-start = ((), (), s32[]{:S(2)}) async-start(), calls=%async_computation.10 | async-start | bytes 5898240 | tf_op jit(solution)/shard_map/reduce_scatter | solution.py:973
  176.4 45.4 %all-to-all-start.4 = ((bf16[8,256,768]{2,1,0:T(8,128)(2,1)}), bf16[8,256,768]{2,1,0:T(8,128)(2,1)}, u32[]{:S(2)}, u32[]{:S(2)}) async-start(bf16[8,256,768]{2,1,0:T(8,128)(2,1)} %shard_map.257), calls=%async_computation.4 | async-start | bytes 6291456 | tf_op jit(solution)/shard_map/all_to_all | solution.py:977
  184.2 346.7 %reduce-scatter.3.cloned.1.call-start = ((), (), s32[]{:S(2)}) async-start(), calls=%async_computation.9 | async-start | bytes 17694720 | tf_op jit(solution)/shard_map/reduce_scatter | solution.py:973
  261.1 47.6 %all-to-all-start.3 = ((bf16[8,2,160,768]{3,2,1,0:T(8,128)(2,1)}), bf16[8,2,160,768]{3,2,1,0:T(8,128)(2,1)}, u32[]{:S(2)}, u32[]{:S(2)}) async-start(bf16[8,2,160,768]{3,2,1,0:T(8,128)(2,1)} %get-tuple-element.78), calls=%async_computation.3 | async-start | bytes 7864320 | tf_op jit(solution)/shard_map/all_to_all | solution.py:977
  308.7 51.1 %all-to-all-start.5 = ((bf16[8,2,160,768]{3,2,1,0:T(8,128)(2,1)}), bf16[8,2,160,768]{3,2,1,0:T(8,128)(2,1)}, u32[]{:S(2)}, u32[]{:S(2)}) async-start(bf16[8,2,160,768]{3,2,1,0:T(8,128)(2,1)} %shard_map.260), calls=%async_computation.5 | async-start | bytes 7864320 | tf_op jit(solution)/shard_map/all_to_all | solution.py:977
  430.1 17.1 %collective-permute-start.9 = (bf16[4,384,768]{2,1,0:T(8,128)(2,1)}, bf16[4,384,768]{2,1,0:T(8,128)(2,1)}, u32[]{:S(2)}, u32[]{:S(2)}) collective-permute-start(bf16[4,384,768]{2,1,0:T(8,128)(2,1)} %constant_dynamic-slice_fusion.3), channel_id=1, source_target_pairs={{0,4},{4,0},{8,12},{12,8},{16,20},{20,16},{24,28},{28,24},{1,5},{5... | collective-permute-start | bytes 7077896 | tf_op jit(solution)/shard_map/ppermute | solution.py:903
  445.6 1.5 collective-permute-start.12
  450.4 14.8 %collective-permute-start.13 = (bf16[4,96,768]{2,1,0:T(8,128)(2,1)S(1)}, bf16[4,96,768]{2,1,0:T(8,128)(2,1)}, u32[]{:S(2)}, u32[]{:S(2)}) collective-permute-start(bf16[4,96,768]{2,1,0:T(8,128)(2,1)S(1)} %fusion.1), channel_id=1, source_target_pairs={{0,16},{4,20},{8,24},{12,28},{16,0},{20,4},{24,8},{28,12},{1,17},{... | collective-permute-start | bytes 1769480 | tf_op jit(solution)/shard_map/ppermute | solution.py:903
  452.9 17.0 %collective-permute-start.10 = (bf16[4,112,768]{2,1,0:T(8,128)(2,1)}, bf16[4,112,768]{2,1,0:T(8,128)(2,1)}, u32[]{:S(2)}, u32[]{:S(2)}) collective-permute-start(bf16[4,112,768]{2,1,0:T(8,128)(2,1)} %constant_dynamic-slice_fusion.2), channel_id=1, source_target_pairs={{0,8},{4,12},{8,0},{12,4},{16,24},{20,28},{24,16},{28,20},{1,9},{5... | collective-permute-start | bytes 2064392 | tf_op jit(solution)/shard_map/ppermute | solution.py:903
  466.6 9.6 %collective-permute-start.14 = (bf16[4,48,768]{2,1,0:T(8,128)(2,1)S(1)}, bf16[4,48,768]{2,1,0:T(8,128)(2,1)S(1)}, u32[]{:S(2)}, u32[]{:S(2)}) collective-permute-start(bf16[4,48,768]{2,1,0:T(8,128)(2,1)S(1)} %constant_dynamic-slice_fusion), channel_id=1, source_target_pairs={{0,8},{4,12},{8,0},{12,4},{16,24},{20,28},{24,16},{28,20},{1,9},{5... | collective-permute-start | bytes 884744 | tf_op jit(solution)/shard_map/ppermute | solution.py:903
  471.2 7.8 %collective-permute-start.11 = (bf16[4,56,768]{2,1,0:T(8,128)(2,1)S(1)}, bf16[4,56,768]{2,1,0:T(8,128)(2,1)S(1)}, u32[]{:S(2)}, u32[]{:S(2)}) collective-permute-start(bf16[4,56,768]{2,1,0:T(8,128)(2,1)S(1)} %constant_dynamic-slice_fusion.1), channel_id=1, source_target_pairs={{0,16},{4,20},{8,24},{12,28},{16,0},{20,4},{24,8},{28,12},{1,17},{... | collective-permute-start | bytes 1032200 | tf_op jit(solution)/shard_map/ppermute | solution.py:903
  479.2 12.5 %collective-permute-start.15 = (bf16[104,768]{1,0:T(8,128)(2,1)S(1)}, bf16[104,768]{1,0:T(8,128)(2,1)S(1)}, u32[]{:S(2)}, u32[]{:S(2)}) collective-permute-start(bf16[104,768]{1,0:T(8,128)(2,1)S(1)} %get-tuple-element.118), channel_id=1, source_target_pairs={{0,1},{1,2},{2,3},{3,0},{4,5},{5,6},{6,7},{7,4},{8,9},{9,10},{10,1... | collective-permute-start | bytes 479240 | tf_op jit(solution)/shard_map/ppermute | solution.py:908
  479.3 28.2 %collective-permute-start.16 = (bf16[104,768]{1,0:T(8,128)(2,1)S(1)}, bf16[104,768]{1,0:T(8,128)(2,1)S(1)}, u32[]{:S(2)}, u32[]{:S(2)}) collective-permute-start(bf16[104,768]{1,0:T(8,128)(2,1)S(1)} %get-tuple-element.119), channel_id=1, source_target_pairs={{0,2},{1,3},{2,0},{3,1},{4,6},{5,7},{6,4},{7,5},{8,10},{9,11},{10,... | collective-permute-start | bytes 479240 | tf_op jit(solution)/shard_map/ppermute | solution.py:908
  483.0 25.8 %collective-permute-start.17 = (bf16[104,768]{1,0:T(8,128)(2,1)S(1)}, bf16[104,768]{1,0:T(8,128)(2,1)S(1)}, u32[]{:S(2)}, u32[]{:S(2)}) collective-permute-start(bf16[104,768]{1,0:T(8,128)(2,1)S(1)} %get-tuple-element.120), channel_id=1, source_target_pairs={{0,3},{1,0},{2,1},{3,2},{4,7},{5,4},{6,5},{7,6},{8,11},{9,8},{10,9... | collective-permute-start | bytes 479240 | tf_op jit(solution)/shard_map/ppermute | solution.py:908
  509.0 3.3 collective-permute-start.20
  510.6 3.6 collective-permute-start.18
  512.3 4.8 collective-permute-start.21
  514.2 4.6 collective-permute-start.19
  519.0 5.4 %collective-permute-start.22 = (bf16[416,768]{1,0:T(8,128)(2,1)S(1)}, bf16[416,768]{1,0:T(8,128)(2,1)S(1)}, u32[]{:S(2)}, u32[]{:S(2)}) collective-permute-start(bf16[416,768]{1,0:T(8,128)(2,1)S(1)} %pad_maximum_fusion.2), channel_id=1, source_target_pairs={{0,4},{4,0},{8,12},{12,8},{16,20},{20,16},{24,28},{28,24},{1,5},{5... | collective-permute-start | bytes 1916936 | tf_op jit(solution)/shard_map/ppermute | solution.py:903
  (19 other events, 158.5 us)
Sparse Core Ops, SparseCore 0:
  38.1 27.9 all-gather.1
  167.4 85.3 reduce-scatter.4
  261.3 249.5 reduce-scatter.2
